TPU v7x, 32 devices: a whole 2x2x4 slice. The times are simulated.
32 devices in a mesh: dp: 4 (over y, x), chan: 4 (over z), row: 2 (over core).
Axes of the slice: x: 2, y: 2, z: 4, core: 2. Of those that a mesh axis runs over, the one named last changes fastest.
Arguments:
- images: bfloat16 [4, 128, 320, 128], P('dp', 'row', 'chan'), may hold values from -6 to 6
- kernel: bfloat16 [9, 320, 320], P(None, 'dp', 'chan'), may hold values from -0.109375 to 0.109375
- cotangent: bfloat16 [4, 128, 320, 128], P('dp', 'row', 'chan'), may hold values from -6 to 6
Outputs:
- activated: bfloat16 [4, 128, 320, 128], P('dp', 'row', 'chan')
- input_grad: float32 [4, 128, 320, 128], P('dp', 'row', 'chan')
- kernel_grad: float32 [9, 320, 320], P(None, 'dp', 'chan')
All inputs are finite; a program needn't handle non-finite values.
Results may differ from a plain program's by a relative error of at most 0.0029.
Values may be sent and summed in bfloat16 or wider, within the bound.
No kernel may reach another device: no remote copies, remote signals or barrier semaphores. Data moves between devices by JAX's collectives and lax.ppermute only.
A program may use at most 192 MiB of HBM per device.

v0:
```python
import functools

import jax
import jax.numpy as jnp
from jax import lax
from jax.experimental import pallas as pl
from jax.experimental.pallas import tpu as pltpu
from jax.sharding import PartitionSpec as P

VMEM_LIMIT = 60 * 1024 * 1024


def receive(block, axis, ahead):
    count = lax.axis_size(axis)
    return lax.ppermute(block, axis, [(i, (i - ahead) % count) for i in range(count)])


def home_of(row, chan, chans):
    return jnp.where(row % 2 == 0, chan, chans - 1 - chan)


def part(array, index, size, axis):
    return lax.dynamic_slice_in_dim(array, index * size, size, axis=axis)


def rotated(array, start, axis):
    twice = jnp.concatenate([array, array], axis=axis)
    return lax.dynamic_slice_in_dim(twice, start, array.shape[axis], axis=axis)


def columns_moved(block, step):
    width = block.shape[-1]
    lane = lax.broadcasted_iota(jnp.int32, block.shape, block.ndim - 1)
    if step < 0:
        moved = pltpu.roll(block, 1, block.ndim - 1)
        return jnp.where(lane == 0, jnp.zeros_like(block), moved)
    moved = pltpu.roll(block, width - 1, block.ndim - 1)
    return jnp.where(lane == width - 1, jnp.zeros_like(block), moved)


def place(stacked, channel, row, block, channels):
    depth, width = block.shape
    lanes = pl.ds(pl.multiple_of(row * width, width), width)
    wide = block.astype(jnp.float32)
    stacked[pl.ds(channel, depth), lanes] = columns_moved(wide, -1).astype(block.dtype)
    stacked[pl.ds(channels + channel, depth), lanes] = block
    stacked[pl.ds(2 * channels + channel, depth), lanes] = columns_moved(wide, 1).astype(block.dtype)


def taps(kernels, stacked, first, rows, width):
    total = None
    for tap_row in range(3):
        start = pl.multiple_of((first + tap_row) * width, width)
        term = jnp.dot(
            kernels[tap_row],
            stacked[:, pl.ds(start, rows * width)],
            preferred_element_type=jnp.float32,
        )
        total = term if total is None else total + term
    return total


def forward_body(count, rows, *refs):
    pieces, rims, kernels = refs[:count], refs[count : 2 * count], refs[2 * count]
    outs = refs[2 * count + 1 : 3 * count + 1]
    factor, stacked = refs[3 * count + 1 :]
    height, depth, width = pieces[0].shape
    channels = count * depth
    step = pl.program_id(0)

    @pl.when(step == 0)
    def _():
        for j in range(count):
            place(stacked, j * depth, 0, rims[j][0], channels)
            place(stacked, j * depth, height + 1, rims[j][1], channels)

        def body(row, carry):
            for j in range(count):
                place(stacked, j * depth, row + 1, pieces[j][row], channels)
            return carry

        lax.fori_loop(0, height, body, 0)

    pre = taps(kernels, stacked, step * rows, rows, width)
    sigma = jax.nn.sigmoid(pre)
    activated = (pre * sigma).astype(jnp.bfloat16)
    slope = sigma * (1.0 + pre * (1.0 - sigma))
    for row in range(rows):
        lanes = slice(row * width, (row + 1) * width)
        factor[row] = slope[:, lanes]
        for j in range(count):
            outs[j][row] = activated[j * depth : (j + 1) * depth, lanes]


def whole(shape):
    return pl.BlockSpec(shape, lambda *_: (0,) * len(shape))


def forward(pieces, rims, kernels):
    count = len(pieces)
    height, depth, width = pieces[0].shape
    channels = count * depth
    rows = 4 if height % 4 == 0 else 1
    flops = 2 * 9 * channels * channels * height * width
    results = pl.pallas_call(
        functools.partial(forward_body, count, rows),
        grid=(height // rows,),
        in_specs=[whole(pieces[0].shape)] * count
        + [whole(rims[0].shape)] * count
        + [whole(kernels.shape)],
        out_specs=[pl.BlockSpec((rows, depth, width), lambda g: (g, 0, 0))] * count
        + [
            pl.BlockSpec((rows, channels, width), lambda g: (g, 0, 0)),
            whole((3 * channels, (height + 2) * width)),
        ],
        out_shape=[jax.ShapeDtypeStruct((height, depth, width), jnp.bfloat16)] * count
        + [
            jax.ShapeDtypeStruct((height, channels, width), jnp.float32),
            jax.ShapeDtypeStruct((3 * channels, (height + 2) * width), jnp.bfloat16),
        ],
        compiler_params=pltpu.CompilerParams(vmem_limit_bytes=VMEM_LIMIT),
        cost_estimate=pl.CostEstimate(
            flops=flops, bytes_accessed=16 * 1024 * 1024, transcendentals=0
        ),
        name="conv_forward",
    )(*pieces, *rims, kernels)
    return results[:count], results[count], results[count + 1]


def correlate_body(count, *refs):
    stacked, factor = refs[0], refs[1]
    pieces = refs[2 : 2 + count]
    grads, slope = refs[2 + count :]
    height, depth, width = pieces[0].shape
    channels = count * depth
    tap_row, tap_col = pl.program_id(0), pl.program_id(1)

    @pl.when((tap_row == 0) & (tap_col == 0))
    def _():
        def body(row, carry):
            lanes = pl.ds(pl.multiple_of(row * width, width), width)
            for j in range(count):
                part_of = pl.ds(j * depth, depth)
                value = pieces[j][row].astype(jnp.float32) * factor[row, part_of, :]
                slope[part_of, lanes] = value.astype(jnp.bfloat16)
            return carry

        lax.fori_loop(0, height, body, 0)

    source = stacked[
        pl.ds(pl.multiple_of(tap_col * channels, channels), channels),
        pl.ds(pl.multiple_of(tap_row * width, width), height * width),
    ]
    grads[0] = lax.dot_general(
        source, slope[...], (((1,), (1,)), ((), ())), preferred_element_type=jnp.float32
    )


def correlate(stacked, factor, pieces):
    count = len(pieces)
    height, depth, width = pieces[0].shape
    channels = count * depth
    flops = 2 * 9 * channels * channels * height * width
    return pl.pallas_call(
        functools.partial(correlate_body, count),
        grid=(3, 3),
        in_specs=[whole(stacked.shape), whole(factor.shape)] + [whole(pieces[0].shape)] * count,
        out_specs=[
            pl.BlockSpec((1, channels, channels), lambda a, b: (3 * a + b, 0, 0)),
            whole((channels, height * width)),
        ],
        out_shape=[
            jax.ShapeDtypeStruct((9, channels, channels), jnp.float32),
            jax.ShapeDtypeStruct((channels, height * width), jnp.bfloat16),
        ],
        compiler_params=pltpu.CompilerParams(vmem_limit_bytes=VMEM_LIMIT),
        cost_estimate=pl.CostEstimate(
            flops=flops, bytes_accessed=14 * 1024 * 1024, transcendentals=0
        ),
        name="kernel_grad",
    )(stacked, factor, *pieces)


def backward_body(count, rows, turns, slope, above, below, kernels, *refs):
    outs, stacked = refs[:count], refs[count]
    channels = slope.shape[0]
    _, _, width = above.shape
    height = slope.shape[1] // width
    depth = channels // count
    step = pl.program_id(0)

    @pl.when(step == 0)
    def _():
        for j in range(count):
            for side, rim, row in ((0, above, 0), (1, below, height + 1)):
                start = lax.rem(turns[side] + j, count) * depth
                block = rim[0, pl.ds(pl.multiple_of(start, depth), depth), :]
                place(stacked, j * depth, row, block, channels)

        def body(row, carry):
            lanes = pl.ds(pl.multiple_of(row * width, width), width)
            place(stacked, 0, row + 1, slope[:, lanes], channels)
            return carry

        lax.fori_loop(0, height, body, 0)

    grad = taps(kernels, stacked, step * rows, rows, width)
    for row in range(rows):
        lanes = slice(row * width, (row + 1) * width)
        for j in range(count):
            outs[j][row] = grad[j * depth : (j + 1) * depth, lanes].astype(outs[j].dtype)


def backward(turns, slope, above, below, kernels, count):
    channels = slope.shape[0]
    width = above.shape[2]
    height = slope.shape[1] // width
    depth = channels // count
    rows = 4 if height % 4 == 0 else 1
    flops = 2 * 9 * channels * channels * height * width
    return pl.pallas_call(
        functools.partial(backward_body, count, rows),
        grid=(height // rows,),
        in_specs=[
            pl.BlockSpec(memory_space=pltpu.SMEM),
            whole(slope.shape),
            whole(above.shape),
            whole(below.shape),
            whole(kernels.shape),
        ],
        out_specs=[pl.BlockSpec((rows, depth, width), lambda g: (g, 0, 0))] * count,
        out_shape=[
            jax.ShapeDtypeStruct((height, depth, width), jnp.bfloat16 if j else jnp.float32)
            for j in range(count)
        ],
        scratch_shapes=[pltpu.VMEM((3 * channels, (height + 2) * width), jnp.bfloat16)],
        compiler_params=pltpu.CompilerParams(vmem_limit_bytes=VMEM_LIMIT),
        cost_estimate=pl.CostEstimate(
            flops=flops, bytes_accessed=8 * 1024 * 1024, transcendentals=0
        ),
        name="conv_backward",
    )(turns, slope, above, below, kernels)


def gathered_kernel(kernel):
    dp, chan, row = (lax.axis_index(a) for a in ("dp", "chan", "row"))
    dps, chans, rows = (lax.axis_size(a) for a in ("dp", "chan", "row"))
    _, inner, outer = kernel.shape
    share = inner // rows
    mine = part(kernel, row, share, 1)
    mine = jnp.transpose(mine, (2, 0, 1)).reshape(outer, 9 * share)
    over_chan = jnp.concatenate([mine] + [receive(mine, "chan", j) for j in range(1, chans)], axis=0)
    over_dp = jnp.stack([over_chan] + [receive(over_chan, "dp", j) for j in range(1, dps)])
    over_row = jnp.stack([over_dp] + [receive(over_dp, "row", j) for j in range(1, rows)])
    placed = rotated(over_row, (rows - row) % rows, 0)
    placed = rotated(placed, (chan * (dps // chans) - dp) % dps, 1)
    channels = chans * outer
    taps_of = placed.reshape(rows, dps, channels, 3, 3, share)
    ahead = jnp.transpose(taps_of, (3, 2, 4, 1, 0, 5)).reshape(3, channels, 3 * channels)
    flipped = taps_of[:, :, :, ::-1, ::-1]
    back = jnp.transpose(flipped, (3, 1, 0, 5, 4, 2)).reshape(3, channels, 3 * channels)
    return ahead, back


def summed_kernel_grad(terms, inner, outer):
    dp, chan, row = (lax.axis_index(a) for a in ("dp", "chan", "row"))
    dps, chans, rows = (lax.axis_size(a) for a in ("dp", "chan", "row"))
    channels = terms.shape[1]
    share = inner // rows
    terms = terms.reshape(9, dps, rows, share, channels)

    def of_row(r):
        return lax.dynamic_index_in_dim(terms, r, 2, keepdims=False)

    halves = of_row(row)
    for j in range(1, rows):
        halves = halves + receive(of_row((row - j) % rows), "row", j)

    def of_dp(d):
        return lax.dynamic_index_in_dim(halves, (d - chan * (dps // chans)) % dps, 1, keepdims=False)

    total = of_dp(dp)
    for j in range(1, dps):
        total = total + receive(of_dp((dp - j) % dps), "dp", j)
    total = jnp.transpose(total, (2, 0, 1)).reshape(channels, 9 * share)
    own = total[:outer]
    for j in range(1, chans):
        own = own + receive(total[(chans - j) * outer : (chans - j + 1) * outer], "chan", j)
    both = jnp.stack([own] + [receive(own, "row", j) for j in range(1, rows)])
    both = rotated(both, (rows - row) % rows, 0).reshape(rows, outer, 9, share)
    return jnp.transpose(both, (2, 0, 3, 1)).reshape(9, inner, outer)


def shards(images, kernel, cotangent):
    row, chan = lax.axis_index("row"), lax.axis_index("chan")
    rows, chans = lax.axis_size("row"), lax.axis_size("chan")
    _, slab, depth, width = images.shape
    height = slab // chans
    images, cotangent = images[0], cotangent[0]

    def home(ahead):
        return home_of(row, (chan + ahead) % chans, chans)

    def to_homes(array, size):
        return [part(array, home(0), size, 0)] + [
            receive(part(array, home(-j), size, 0), "chan", j) for j in range(1, chans)
        ]

    ahead_kernel, back_kernel = gathered_kernel(kernel)
    pieces = to_homes(images, height)
    down = [(i, i + 1) for i in range(rows - 1)]
    up = [(i + 1, i) for i in range(rows - 1)]
    low = lax.ppermute(images[slab - 1 :], "row", down)
    high = lax.ppermute(images[:1], "row", up)
    tops = jnp.concatenate([low, images[height - 1 : slab - 1 : height]])
    bottoms = jnp.concatenate([images[height::height], high])
    rims = to_homes(jnp.stack([tops, bottoms], axis=1).reshape(2 * chans, depth, width), 2)
    cotangents = to_homes(cotangent, height)

    activated, factor, stacked = forward(pieces, rims, ahead_kernel)

    def edge(at):
        wide = jnp.concatenate([c[at] for c in cotangents]).astype(jnp.float32)
        return (wide * factor[at]).astype(jnp.bfloat16)[None]

    def snake(place_at):
        r, k = place_at // chans, place_at % chans
        return (k if r % 2 == 0 else chans - 1 - k) * rows + r

    line = [(snake(i), snake(i + 1)) for i in range(rows * chans - 1)]
    above = lax.ppermute(edge(height - 1), ("chan", "row"), line)
    below = lax.ppermute(edge(0), ("chan", "row"), [(b, a) for a, b in line])

    place_at = home(0)
    forth = jnp.where(row % 2 == 0, 1, chans - 1)
    turns = jnp.stack(
        [
            jnp.where(place_at == 0, 0, forth),
            jnp.where(place_at == chans - 1, 0, chans - forth),
        ]
    ).astype(jnp.int32)
    grads, slope = correlate(stacked, factor, cotangents)
    input_grads = backward(turns, slope, above, below, back_kernel, chans)
    kernel_grad = summed_kernel_grad(grads, kernel.shape[1], kernel.shape[2])

    def to_owners(blocks, dtype):
        out = jnp.zeros((slab, depth, width), dtype)
        for j in range(chans):
            arrived = receive(blocks[j], "chan", chans - j) if j else blocks[0]
            out = lax.dynamic_update_slice_in_dim(out, arrived.astype(dtype), home(-j) * height, 0)
        return out[None]

    return to_owners(activated, jnp.bfloat16), to_owners(input_grads, jnp.float32), kernel_grad


def solution(mesh):
    placed = (P("dp", "row", "chan", None), P(None, "dp", "chan"), P("dp", "row", "chan", None))
    return jax.shard_map(
        shards,
        mesh=mesh,
        in_specs=placed,
        out_specs=(
            P("dp", "row", "chan", None),
            P("dp", "row", "chan", None),
            P(None, "dp", "chan"),
        ),
        check_vma=False,
    )
```

profile of v0, /device:TPU:0, one launch (start us, length us, event | category | flops | bytes accessed | tf_op | source)
XLA Modules:
  0.0 214.4 jit_solution(12603447497698291918)
XLA Ops:
  0.7 0.9 copy-done
  1.6 3.1 %collective-permute-start.10 = (bf16[80,360]{0,1:T(8,128)(2,1)S(1)}, bf16[80,360]{0,1:T(8,128)(2,1)S(1)}, u32[]{:S(2)}, u32[]{:S(2)}) collective-permute-start(bf16[80,360]{0,1:T(8,128)(2,1)S(1)} %bitcast.112), channel_id=1, source_target_pairs={{0,2},{2,4},{4,6},{6,0},{1,3},{3,5},{5,7},{7,1},{8,10},{10,12},{12... | collective-permute-start | bytes 172808 | tf_op jit(solution)/shard_map/ppermute | solution.py:15
  4.7 2.1 collective-permute-start.8
  6.8 0.9 collective-permute-start.9
  7.7 1.4 slice_bitcast_fusion.1
  9.1 1.9 collective-permute-start.3
  11.0 1.3 collective-permute-start.4
  12.3 0.9 fusion.13
  13.2 2.4 %dynamic-slice_bitcast_fusion.8 = (bf16[16,80,128]{2,1,0:T(8,128)(2,1)}, bf16[16,80,128]{2,1,0:T(8,128)(2,1)}, bf16[16,80,128]{2,1,0:T(8,128)(2,1)}, bf16[16,80,128]{2,1,0:T(8,128)(2,1)}) fusion(bf16[1,64,80,128]{3,2,1,0:T(8,128)(2,1)} %param.3, s32[]{:T(128)S(6)} %select_n.259, s32[]{:T(128)S(6)} %select_n.256, s32[]{:T(128)S(6)} %select_n.253, ...), kind=kLoop, calls=%fused_computation.40 | loop fusion | bytes 2621456 | tf_op jit(solution)/shard_map/dynamic_slice | solution.py:23
  15.6 1.1 dynamic-slice_bitcast_fusion.4
  16.9 2.5 %collective-permute-start.11 = (bf16[320,360]{0,1:T(8,128)(2,1)S(1)}, bf16[320,360]{0,1:T(8,128)(2,1)S(1)}, u32[]{:S(2)}, u32[]{:S(2)}) collective-permute-start(bf16[320,360]{0,1:T(8,128)(2,1)S(1)} %pad_maximum_fusion.1), channel_id=1, source_target_pairs={{0,24},{8,0},{16,8},{24,16},{1,25},{9,1},{17,9},{25,17},{2,26},{10... | collective-permute-start | bytes 691208 | tf_op jit(solution)/shard_map/ppermute | solution.py:15
  19.9 0.6 collective-permute-start.13
  20.8 5.1 %collective-permute-done.11 = bf16[320,360]{0,1:T(8,128)(2,1)S(1)} collective-permute-done((bf16[320,360]{0,1:T(8,128)(2,1)S(1)}, bf16[320,360]{0,1:T(8,128)(2,1)S(1)}, u32[]{:S(2)}, u32[]{:S(2)}) %collective-permute-start.11) | collective-permute-done | bytes 230432 | tf_op jit(solution)/shard_map/ppermute | solution.py:15
  25.8 1.3 collective-permute-start
  27.2 7.3 %collective-permute-done.12 = bf16[320,360]{0,1:T(8,128)(2,1)S(1)} collective-permute-done((bf16[320,360]{0,1:T(8,128)(2,1)S(1)}, bf16[320,360]{0,1:T(8,128)(2,1)S(1)}, u32[]{:S(2)}, u32[]{:S(2)}) %collective-permute-start.12) | collective-permute-done | bytes 230432 | tf_op jit(solution)/shard_map/ppermute | solution.py:15
  34.5 2.1 collective-permute-start.1
  36.9 0.7 copy.18
  38.0 0.6 pad_add_fusion.turns
  38.6 1.8 collective-permute-start.18
  40.4 0.7 maximum_bitcast_fusion
  41.3 0.7 maximum_bitcast_fusion.1
  42.0 0.7 constant_dynamic-slice_fusion.1
  42.7 11.9 %collective-permute-done.18.refs_3_ = bf16[16,80,128]{2,1,0:T(8,128)(2,1)S(1)} collective-permute-done((bf16[16,80,128]{2,1,0:T(8,128)(2,1)}, bf16[16,80,128]{2,1,0:T(8,128)(2,1)S(1)}, u32[]{:S(2)}, u32[]{:S(2)}) %collective-permute-start.18) | collective-permute-done | bytes 327712 | tf_op jit(solution)/shard_map/ppermute | solution.py:15
  54.6 20.3 %collective-permute-start.2 = (bf16[16,80,128]{2,1,0:T(8,128)(2,1)}, bf16[16,80,128]{2,1,0:T(8,128)(2,1)}, u32[]{:S(2)}, u32[]{:S(2)}) collective-permute-start(bf16[16,80,128]{2,1,0:T(8,128)(2,1)} %get-tuple-element.42), channel_id=1, source_target_pairs={{0,2},{2,4},{4,6},{6,0},{1,3},{3,5},{5,7},{7,1},{8,10},{10,12},{12... | collective-permute-start | bytes 983048 | tf_op jit(solution)/shard_map/ppermute | solution.py:15
  74.9 6.1 %collective-permute-done.19.refs_4_ = bf16[16,80,128]{2,1,0:T(8,128)(2,1)S(1)} collective-permute-done((bf16[16,80,128]{2,1,0:T(8,128)(2,1)}, bf16[16,80,128]{2,1,0:T(8,128)(2,1)S(1)}, u32[]{:S(2)}, u32[]{:S(2)}) %collective-permute-start.19) | collective-permute-done | bytes 327712 | tf_op jit(solution)/shard_map/ppermute | solution.py:15
  81.0 0.7 copy-done.10
  81.7 0.7 copy.19
  82.4 2.0 fusion.3
  84.5 0.8 collective-permute-done.5.refs_5_
  85.3 0.6 collective-permute-start.7
  85.9 1.0 fusion
  86.9 1.6 copy.20
  88.6 4.1 %copy.21.refs_8_ = bf16[3,320,960]{2,1,0:T(8,128)(2,1)} copy(bf16[3,320,960]{1,2,0:T(8,128)(2,1)} %bitcast.106) | data formatting | bytes 3686400 | tf_op jit(solution)/shard_map/reshape | solution.py:259
  92.7 2.1 collective-permute-start.20
  94.8 0.6 copy-done.15
  95.4 11.8 %conv_forward.1 = (bf16[16,80,128]{2,1,0:T(8,128)(2,1)}, bf16[16,80,128]{2,1,0:T(8,128)(2,1)}, bf16[16,80,128]{2,1,0:T(8,128)(2,1)}, bf16[16,80,128]{2,1,0:T(8,1...) custom-call(bf16[16,80,128]{2,1,0:T(8,128)(2,1)} %get-tuple-element.45.refs_0_, ...), custom_call_target="tpu_custom_call" | custom-call | flops 3774873600 | bytes 16777216 | tf_op jit(solution)/shard_map/conv_forward/pallas_call | solution.py:105
  107.2 0.7 copy-done.11
  107.9 12.6 %kernel_grad.1 = (f32[9,320,320]{2,1,0:T(8,128)}, bf16[320,2048]{1,0:T(8,128)(2,1)}) custom-call(bf16[960,2304]{1,0:T(8,128)(2,1)} %get-tuple-element.19.refs_0_, f32[16,320,128]{2,1,0:T(8,128)} %get-tuple-element.20.refs_1_, bf16[16,80,128]{2,1,0:T(8,128)(2,1)} %get-tuple-element.36.refs_2_, bf16[16,80,128]{2,1,0:T(8,128)(2,1)} %copy-done.9, ...), custom_call_target="tpu_custom_call" | custom-call | flops 3774873600 | bytes 14680064 | tf_op jit(solution)/shard_map/kernel_grad/pallas_call | solution.py:164
  120.5 3.3 %dynamic-slice_bitcast_fusion = f32[9,4,40,320]{3,2,1,0:T(8,128)} fusion(f32[9,4,2,40,320]{4,3,2,1,0:T(8,128)} %bitcast.107, s32[]{:T(128)S(6)} %select_n.274), kind=kLoop, calls=%fused_computation.11 | loop fusion | bytes 3686404 | tf_op jit(solution)/shard_map/jit(dynamic_index_in_dim)/squeeze | solution.py:273
  123.8 0.7 fusion.17
  124.5 1.7 multiply_convert_fusion
  126.2 3.3 %collective-permute-start.21 = (bf16[1,320,128]{2,1,0:T(8,128)(2,1)}, bf16[1,320,128]{2,1,0:T(8,128)(2,1)S(1)}, u32[]{:S(2)}, u32[]{:S(2)}) collective-permute-start(bf16[1,320,128]{2,1,0:T(8,128)(2,1)} %get-tuple-element.28), channel_id=1, source_target_pairs={{0,2},{2,4},{4,6},{6,7},{7,5},{5,3},{3,1},{8,10},{10,12},{12,14},{... | collective-permute-start | bytes 245768 | tf_op jit(solution)/shard_map/ppermute | solution.py:331
  129.5 1.3 collective-permute-start.22
  130.8 2.9 %collective-permute-start.15 = (bf16[16,80,128]{2,1,0:T(8,128)(2,1)}, bf16[16,80,128]{2,1,0:T(8,128)(2,1)}, u32[]{:S(2)}, u32[]{:S(2)}) collective-permute-start(bf16[16,80,128]{2,1,0:T(8,128)(2,1)} %get-tuple-element.16), channel_id=1, source_target_pairs={{0,2},{2,4},{4,6},{6,0},{1,3},{3,5},{5,7},{7,1},{8,10},{10,12},{12... | collective-permute-start | bytes 983048 | tf_op jit(solution)/shard_map/ppermute | solution.py:15
  133.6 0.9 collective-permute-start.16
  134.8 1.0 copy-done.3
  136.1 1.4 copy.22
  137.5 3.6 %reshape.172.kernels = bf16[3,320,960]{2,1,0:T(8,128)(2,1)} reshape(bf16[3,4,2,40,3,320]{5,4,3,2,1,0:T(4,128)(2,1)S(1)} %copy.22) | data formatting | bytes 3686400 | tf_op jit(solution)/shard_map/reshape | solution.py:261
  141.1 2.3 %collective-permute-start.17 = (bf16[16,80,128]{2,1,0:T(8,128)(2,1)}, bf16[16,80,128]{2,1,0:T(8,128)(2,1)S(1)}, u32[]{:S(2)}, u32[]{:S(2)}) collective-permute-start(bf16[16,80,128]{2,1,0:T(8,128)(2,1)} %get-tuple-element.18), channel_id=1, source_target_pairs={{0,6},{2,0},{4,2},{6,4},{1,7},{3,1},{5,3},{7,5},{8,14},{10,8},{12,... | collective-permute-start | bytes 983048 | tf_op jit(solution)/shard_map/ppermute | solution.py:15
  143.4 9.7 %conv_backward.1 = (f32[16,80,128]{2,1,0:T(8,128)}, bf16[16,80,128]{2,1,0:T(8,128)(2,1)}, bf16[16,80,128]{2,1,0:T(8,128)(2,1)}, bf16[16,80,128]{2,1,0:T(8,128)(2,1)}) custom-call(s32[2]{0:T(128)} %pad_add_fusion.turns, bf16[320,2048]{1,0:T(8,128)(2,1)} %get-tuple-element.21.slope, bf16[1,320,128]{2,1,0:T(8,128)(2,1)} %copy-done.14, ...), custom_call_target="tpu_custom_call" | custom-call | flops 3774873600 | bytes 8388608 | tf_op jit(solution)/shard_map/conv_backward/pallas_call | solution.py:221
  153.4 0.8 copy-done.6
  154.3 4.0 %collective-permute-start.24 = (bf16[16,80,128]{2,1,0:T(8,128)(2,1)S(1)}, bf16[16,80,128]{2,1,0:T(8,128)(2,1)S(1)}, u32[]{:S(2)}, u32[]{:S(2)}) collective-permute-start(bf16[16,80,128]{2,1,0:T(8,128)(2,1)S(1)} %copy-done.13), channel_id=1, source_target_pairs={{0,4},{2,6},{4,0},{6,2},{1,5},{3,7},{5,1},{7,3},{8,12},{10,14},{12... | collective-permute-start | bytes 983048 | tf_op jit(solution)/shard_map/ppermute | solution.py:15
  158.3 1.0 bitcast_dynamic-update-slice_fusion.3
  159.4 2.5 %bitcast_add_fusion = f32[9,4,40,320]{3,2,1,0:T(8,128)S(1)} fusion(f32[9,4,40,320]{3,2,1,0:T(8,128)} %collective-permute-done.26, f32[9,4,2,40,320]{4,3,2,1,0:T(8,128)} %bitcast.108, s32[]{:T(128)S(6)} %select_n.272), kind=kLoop, calls=%fused_computation.10 | loop fusion | flops 460800 | bytes 5529604 | tf_op jit(solution)/shard_map/add | solution.py:277
  162.1 2.3 %collective-permute-start.27 = (f32[9,40,320]{2,1,0:T(8,128)S(1)}, f32[9,40,320]{2,1,0:T(8,128)S(1)}, u32[]{:S(2)}, u32[]{:S(2)}) collective-permute-start(f32[9,40,320]{2,1,0:T(8,128)S(1)} %get-tuple-element.29), channel_id=1, source_target_pairs={{0,24},{8,0},{16,8},{24,16},{1,25},{9,1},{17,9},{25,17},{2,26},{10... | collective-permute-start | bytes 1382408 | tf_op jit(solution)/shard_map/ppermute | solution.py:15
  164.9 0.9 collective-permute-start.29
  165.9 13.7 %collective-permute-start.25 = (bf16[16,80,128]{2,1,0:T(8,128)(2,1)S(1)}, bf16[16,80,128]{2,1,0:T(8,128)(2,1)S(1)}, u32[]{:S(2)}, u32[]{:S(2)}) collective-permute-start(bf16[16,80,128]{2,1,0:T(8,128)(2,1)S(1)} %copy-done.12), channel_id=1, source_target_pairs={{0,6},{2,0},{4,2},{6,4},{1,7},{3,1},{5,3},{7,5},{8,14},{10,8},{12,... | collective-permute-start | bytes 983048 | tf_op jit(solution)/shard_map/ppermute | solution.py:15
  179.7 9.1 %collective-permute-done.28 = f32[9,40,320]{2,1,0:T(8,128)S(1)} collective-permute-done((f32[9,40,320]{2,1,0:T(8,128)S(1)}, f32[9,40,320]{2,1,0:T(8,128)S(1)}, u32[]{:S(2)}, u32[]{:S(2)}) %collective-permute-start.28) | collective-permute-done | bytes 460832 | tf_op jit(solution)/shard_map/ppermute | solution.py:15
  189.2 7.3 %collective-permute-start.30 = (f32[80,360]{0,1:T(8,128)S(1)}, f32[80,360]{0,1:T(8,128)S(1)}, u32[]{:S(2)}, u32[]{:S(2)}) collective-permute-start(f32[80,360]{0,1:T(8,128)S(1)} %bitcast.125), channel_id=1, source_target_pairs={{0,6},{2,0},{4,2},{6,4},{1,7},{3,1},{5,3},{7,5},{8,14},{10,8},{12,... | collective-permute-start | bytes 345608 | tf_op jit(solution)/shard_map/ppermute | solution.py:15
  196.6 0.5 collective-permute-start.32
  197.2 4.3 %collective-permute-done.30 = f32[80,360]{0,1:T(8,128)S(1)} collective-permute-done((f32[80,360]{0,1:T(8,128)S(1)}, f32[80,360]{0,1:T(8,128)S(1)}, u32[]{:S(2)}, u32[]{:S(2)}) %collective-permute-start.30) | collective-permute-done | bytes 115232 | tf_op jit(solution)/shard_map/ppermute | solution.py:15
  201.4 10.6 %collective-permute-done.31 = f32[80,360]{0,1:T(8,128)S(1)} collective-permute-done((f32[80,360]{0,1:T(8,128)S(1)}, f32[80,360]{0,1:T(8,128)S(1)}, u32[]{:S(2)}, u32[]{:S(2)}) %collective-permute-start.31) | collective-permute-done | bytes 115232 | tf_op jit(solution)/shard_map/ppermute | solution.py:15
  212.2 1.3 collective-permute-done.33
  213.7 0.8 copy.23
  (85 shorter events, 4.3 us)
Async XLA Ops:
  0.6 0.9 copy-start
  0.6 15.0 %copy-start.2 = (bf16[1,64,80,128]{3,2,1,0:T(8,128)(2,1)S(1)}, bf16[1,64,80,128]{3,2,1,0:T(8,128)(2,1)}, u32[]{:S(2)}) copy-start(bf16[1,64,80,128]{3,2,1,0:T(8,128)(2,1)} %param.5) | copy-start | bytes 3932164
  1.6 15.1 %collective-permute-start.10 = (bf16[80,360]{0,1:T(8,128)(2,1)S(1)}, bf16[80,360]{0,1:T(8,128)(2,1)S(1)}, u32[]{:S(2)}, u32[]{:S(2)}) collective-permute-start(bf16[80,360]{0,1:T(8,128)(2,1)S(1)} %bitcast.112), channel_id=1, source_target_pairs={{0,2},{2,4},{4,6},{6,0},{1,3},{3,5},{5,7},{7,1},{8,10},{10,12},{12... | collective-permute-start | bytes 172808 | tf_op jit(solution)/shard_map/ppermute | solution.py:15
  4.7 12.0 %collective-permute-start.8 = (bf16[80,360]{0,1:T(8,128)(2,1)S(1)}, bf16[80,360]{0,1:T(8,128)(2,1)S(1)}, u32[]{:S(2)}, u32[]{:S(2)}) collective-permute-start(bf16[80,360]{0,1:T(8,128)(2,1)S(1)} %bitcast.113), channel_id=1, source_target_pairs={{0,6},{2,0},{4,2},{6,4},{1,7},{3,1},{5,3},{7,5},{8,14},{10,8},{12,... | collective-permute-start | bytes 172808 | tf_op jit(solution)/shard_map/ppermute | solution.py:15
  6.8 9.9 %collective-permute-start.9 = (bf16[80,360]{0,1:T(8,128)(2,1)S(1)}, bf16[80,360]{0,1:T(8,128)(2,1)S(1)}, u32[]{:S(2)}, u32[]{:S(2)}) collective-permute-start(bf16[80,360]{0,1:T(8,128)(2,1)S(1)} %bitcast.114), channel_id=1, source_target_pairs={{0,4},{2,6},{4,0},{6,2},{1,5},{3,7},{5,1},{7,3},{8,12},{10,14},{12... | collective-permute-start | bytes 172808 | tf_op jit(solution)/shard_map/ppermute | solution.py:15
  9.1 29.6 %collective-permute-start.3 = (bf16[1,80,128]{2,1,0:T(8,128)(2,1)}, bf16[1,80,128]{2,1,0:T(8,128)(2,1)}, u32[]{:S(2)}, u32[]{:S(2)}) collective-permute-start(bf16[1,80,128]{2,1,0:T(8,128)(2,1)} %get-tuple-element.38), channel_id=1, source_target_pairs={{0,1},{2,3},{4,5},{6,7},{8,9},{10,11},{12,13},{14,15},{16,17},{18,... | collective-permute-start | bytes 61448 | tf_op jit(solution)/shard_map/ppermute | solution.py:313
  11.0 30.2 %collective-permute-start.4 = (bf16[1,80,128]{2,1,0:T(8,128)(2,1)}, bf16[1,80,128]{2,1,0:T(8,128)(2,1)}, u32[]{:S(2)}, u32[]{:S(2)}) collective-permute-start(bf16[1,80,128]{2,1,0:T(8,128)(2,1)} %get-tuple-element.39), channel_id=1, source_target_pairs={{1,0},{3,2},{5,4},{7,6},{9,8},{11,10},{13,12},{15,14},{17,16},{19,... | collective-permute-start | bytes 61448 | tf_op jit(solution)/shard_map/ppermute | solution.py:314
  16.9 8.9 %collective-permute-start.11 = (bf16[320,360]{0,1:T(8,128)(2,1)S(1)}, bf16[320,360]{0,1:T(8,128)(2,1)S(1)}, u32[]{:S(2)}, u32[]{:S(2)}) collective-permute-start(bf16[320,360]{0,1:T(8,128)(2,1)S(1)} %pad_maximum_fusion.1), channel_id=1, source_target_pairs={{0,24},{8,0},{16,8},{24,16},{1,25},{9,1},{17,9},{25,17},{2,26},{10... | collective-permute-start | bytes 691208 | tf_op jit(solution)/shard_map/ppermute | solution.py:15
  19.4 15.1 %collective-permute-start.12 = (bf16[320,360]{0,1:T(8,128)(2,1)S(1)}, bf16[320,360]{0,1:T(8,128)(2,1)S(1)}, u32[]{:S(2)}, u32[]{:S(2)}) collective-permute-start(bf16[320,360]{0,1:T(8,128)(2,1)S(1)} %pad_maximum_fusion.1), channel_id=1, source_target_pairs={{0,16},{8,24},{16,0},{24,8},{1,17},{9,25},{17,1},{25,9},{2,18},{10... | collective-permute-start | bytes 691208 | tf_op jit(solution)/shard_map/ppermute | solution.py:15
  19.9 16.7 %collective-permute-start.13 = (bf16[320,360]{0,1:T(8,128)(2,1)S(1)}, bf16[320,360]{0,1:T(8,128)(2,1)S(1)}, u32[]{:S(2)}, u32[]{:S(2)}) collective-permute-start(bf16[320,360]{0,1:T(8,128)(2,1)S(1)} %pad_maximum_fusion.1), channel_id=1, source_target_pairs={{0,8},{8,16},{16,24},{24,0},{1,9},{9,17},{17,25},{25,1},{2,10},{10... | collective-permute-start | bytes 691208 | tf_op jit(solution)/shard_map/ppermute | solution.py:15
  25.8 68.9 %collective-permute-start = (bf16[16,80,128]{2,1,0:T(8,128)(2,1)}, bf16[16,80,128]{2,1,0:T(8,128)(2,1)}, u32[]{:S(2)}, u32[]{:S(2)}) collective-permute-start(bf16[16,80,128]{2,1,0:T(8,128)(2,1)} %get-tuple-element.44), channel_id=1, source_target_pairs={{0,6},{2,0},{4,2},{6,4},{1,7},{3,1},{5,3},{7,5},{8,14},{10,8},{12,... | collective-permute-start | bytes 983048 | tf_op jit(solution)/shard_map/ppermute | solution.py:15
  34.5 60.3 %collective-permute-start.1 = (bf16[16,80,128]{2,1,0:T(8,128)(2,1)}, bf16[16,80,128]{2,1,0:T(8,128)(2,1)}, u32[]{:S(2)}, u32[]{:S(2)}) collective-permute-start(bf16[16,80,128]{2,1,0:T(8,128)(2,1)} %get-tuple-element.43), channel_id=1, source_target_pairs={{0,4},{2,6},{4,0},{6,2},{1,5},{3,7},{5,1},{7,3},{8,12},{10,14},{12... | collective-permute-start | bytes 983048 | tf_op jit(solution)/shard_map/ppermute | solution.py:15
  37.6 43.3 %collective-permute-start.14 = (bf16[4,320,360]{2,1,0:T(8,128)(2,1)S(1)}, bf16[4,320,360]{2,1,0:T(8,128)(2,1)S(1)}, u32[]{:S(2)}, u32[]{:S(2)}) collective-permute-start(bf16[4,320,360]{2,1,0:T(8,128)(2,1)S(1)} %copy.18), channel_id=1, source_target_pairs={{0,1},{1,0},{2,3},{3,2},{4,5},{5,4},{6,7},{7,6},{8,9},{9,8},{10,11... | collective-permute-start | bytes 2764808 | tf_op jit(solution)/shard_map/ppermute | solution.py:15
  38.6 15.9 %collective-permute-start.18 = (bf16[16,80,128]{2,1,0:T(8,128)(2,1)}, bf16[16,80,128]{2,1,0:T(8,128)(2,1)S(1)}, u32[]{:S(2)}, u32[]{:S(2)}) collective-permute-start(bf16[16,80,128]{2,1,0:T(8,128)(2,1)} %get-tuple-element.35), channel_id=1, source_target_pairs={{0,6},{2,0},{4,2},{6,4},{1,7},{3,1},{5,3},{7,5},{8,14},{10,8},{12,... | collective-permute-start | bytes 983048 | tf_op jit(solution)/shard_map/ppermute | solution.py:15
  41.2 39.8 %collective-permute-start.19 = (bf16[16,80,128]{2,1,0:T(8,128)(2,1)}, bf16[16,80,128]{2,1,0:T(8,128)(2,1)S(1)}, u32[]{:S(2)}, u32[]{:S(2)}) collective-permute-start(bf16[16,80,128]{2,1,0:T(8,128)(2,1)} %get-tuple-element.37), channel_id=1, source_target_pairs={{0,4},{2,6},{4,0},{6,2},{1,5},{3,7},{5,1},{7,3},{8,12},{10,14},{12... | collective-permute-start | bytes 983048 | tf_op jit(solution)/shard_map/ppermute | solution.py:15
  54.6 26.4 %copy-start.9 = (bf16[16,80,128]{2,1,0:T(8,128)(2,1)}, bf16[16,80,128]{2,1,0:T(8,128)(2,1)S(1)}, u32[]{:S(2)}) copy-start(bf16[16,80,128]{2,1,0:T(8,128)(2,1)S(1)} %collective-permute-done.18.refs_3_) | copy-start | bytes 983044
  54.6 40.2 %collective-permute-start.2 = (bf16[16,80,128]{2,1,0:T(8,128)(2,1)}, bf16[16,80,128]{2,1,0:T(8,128)(2,1)}, u32[]{:S(2)}, u32[]{:S(2)}) collective-permute-start(bf16[16,80,128]{2,1,0:T(8,128)(2,1)} %get-tuple-element.42), channel_id=1, source_target_pairs={{0,2},{2,4},{4,6},{6,0},{1,3},{3,5},{5,7},{7,1},{8,10},{10,12},{12... | collective-permute-start | bytes 983048 | tf_op jit(solution)/shard_map/ppermute | solution.py:15
  80.9 0.8 copy-start.10
  80.9 4.3 %collective-permute-start.5 = (bf16[2,80,128]{2,1,0:T(8,128)(2,1)}, bf16[2,80,128]{2,1,0:T(8,128)(2,1)}, u32[]{:S(2)}, u32[]{:S(2)}) collective-permute-start(bf16[2,80,128]{2,1,0:T(8,128)(2,1)} %get-tuple-element.60), channel_id=1, source_target_pairs={{0,6},{2,0},{4,2},{6,4},{1,7},{3,1},{5,3},{7,5},{8,14},{10,8},{12,... | collective-permute-start | bytes 122888 | tf_op jit(solution)/shard_map/ppermute | solution.py:15
  81.7 11.0 %collective-permute-start.6 = (bf16[2,80,128]{2,1,0:T(8,128)(2,1)}, bf16[2,80,128]{2,1,0:T(8,128)(2,1)}, u32[]{:S(2)}, u32[]{:S(2)}) collective-permute-start(bf16[2,80,128]{2,1,0:T(8,128)(2,1)} %get-tuple-element.59), channel_id=1, source_target_pairs={{0,4},{2,6},{4,0},{6,2},{1,5},{3,7},{5,1},{7,3},{8,12},{10,14},{12... | collective-permute-start | bytes 122888 | tf_op jit(solution)/shard_map/ppermute | solution.py:15
  85.3 9.5 %collective-permute-start.7 = (bf16[2,80,128]{2,1,0:T(8,128)(2,1)S(1)}, bf16[2,80,128]{2,1,0:T(8,128)(2,1)S(1)}, u32[]{:S(2)}, u32[]{:S(2)}) collective-permute-start(bf16[2,80,128]{2,1,0:T(8,128)(2,1)S(1)} %get-tuple-element.58), channel_id=1, source_target_pairs={{0,2},{2,4},{4,6},{6,0},{1,3},{3,5},{5,7},{7,1},{8,10},{10,12},{12... | collective-permute-start | bytes 122888 | tf_op jit(solution)/shard_map/ppermute | solution.py:15
  88.6 4.1 %copy-start.7 = (bf16[16,80,128]{2,1,0:T(8,128)(2,1)S(1)}, bf16[16,80,128]{2,1,0:T(8,128)(2,1)}, u32[]{:S(2)}) copy-start(bf16[16,80,128]{2,1,0:T(8,128)(2,1)} %get-tuple-element.34) | copy-start | bytes 983044
  92.7 14.5 %collective-permute-start.20 = (bf16[16,80,128]{2,1,0:T(8,128)(2,1)S(1)}, bf16[16,80,128]{2,1,0:T(8,128)(2,1)S(1)}, u32[]{:S(2)}, u32[]{:S(2)}) collective-permute-start(bf16[16,80,128]{2,1,0:T(8,128)(2,1)S(1)} %copy-done.7), channel_id=1, source_target_pairs={{0,2},{2,4},{4,6},{6,0},{1,3},{3,5},{5,7},{7,1},{8,10},{10,12},{12... | collective-permute-start | bytes 983048 | tf_op jit(solution)/shard_map/ppermute | solution.py:15
  94.8 0.6 copy-start.15
  107.2 0.7 copy-start.11
  120.5 14.2 %copy-start.8 = (bf16[16,80,128]{2,1,0:T(8,128)(2,1)S(1)}, bf16[16,80,128]{2,1,0:T(8,128)(2,1)}, u32[]{:S(2)}) copy-start(bf16[16,80,128]{2,1,0:T(8,128)(2,1)} %get-tuple-element.15) | copy-start | bytes 983044
  123.8 35.6 %collective-permute-start.26 = (f32[9,4,40,320]{3,2,1,0:T(8,128)}, f32[9,4,40,320]{3,2,1,0:T(8,128)}, u32[]{:S(2)}, u32[]{:S(2)}) collective-permute-start(f32[9,4,40,320]{3,2,1,0:T(8,128)} %dynamic-slice_bitcast_fusion), channel_id=1, source_target_pairs={{0,1},{1,0},{2,3},{3,2},{4,5},{5,4},{6,7},{7,6},{8,9},{9,8},{10,11... | collective-permute-start | bytes 5529608 | tf_op jit(solution)/shard_map/ppermute | solution.py:15
  126.2 14.9 %collective-permute-start.21 = (bf16[1,320,128]{2,1,0:T(8,128)(2,1)}, bf16[1,320,128]{2,1,0:T(8,128)(2,1)S(1)}, u32[]{:S(2)}, u32[]{:S(2)}) collective-permute-start(bf16[1,320,128]{2,1,0:T(8,128)(2,1)} %get-tuple-element.28), channel_id=1, source_target_pairs={{0,2},{2,4},{4,6},{6,7},{7,5},{5,3},{3,1},{8,10},{10,12},{12,14},{... | collective-permute-start | bytes 245768 | tf_op jit(solution)/shard_map/ppermute | solution.py:331
  129.5 13.9 %collective-permute-start.22 = (bf16[1,320,128]{2,1,0:T(8,128)(2,1)}, bf16[1,320,128]{2,1,0:T(8,128)(2,1)}, u32[]{:S(2)}, u32[]{:S(2)}) collective-permute-start(bf16[1,320,128]{2,1,0:T(8,128)(2,1)} %get-tuple-element.27), channel_id=1, source_target_pairs={{2,0},{4,2},{6,4},{7,6},{5,7},{3,5},{1,3},{10,8},{12,10},{14,12},{... | collective-permute-start | bytes 245768 | tf_op jit(solution)/shard_map/ppermute | solution.py:332
  130.8 23.5 %collective-permute-start.15 = (bf16[16,80,128]{2,1,0:T(8,128)(2,1)}, bf16[16,80,128]{2,1,0:T(8,128)(2,1)}, u32[]{:S(2)}, u32[]{:S(2)}) collective-permute-start(bf16[16,80,128]{2,1,0:T(8,128)(2,1)} %get-tuple-element.16), channel_id=1, source_target_pairs={{0,2},{2,4},{4,6},{6,0},{1,3},{3,5},{5,7},{7,1},{8,10},{10,12},{12... | collective-permute-start | bytes 983048 | tf_op jit(solution)/shard_map/ppermute | solution.py:15
  133.6 25.7 %collective-permute-start.16 = (bf16[16,80,128]{2,1,0:T(8,128)(2,1)}, bf16[16,80,128]{2,1,0:T(8,128)(2,1)S(1)}, u32[]{:S(2)}, u32[]{:S(2)}) collective-permute-start(bf16[16,80,128]{2,1,0:T(8,128)(2,1)} %get-tuple-element.17), channel_id=1, source_target_pairs={{0,4},{2,6},{4,0},{6,2},{1,5},{3,7},{5,1},{7,3},{8,12},{10,14},{12... | collective-permute-start | bytes 983048 | tf_op jit(solution)/shard_map/ppermute | solution.py:15
  134.8 1.1 copy-start.3
  141.1 2.3 %copy-start.14 = (bf16[1,320,128]{2,1,0:T(8,128)(2,1)}, bf16[1,320,128]{2,1,0:T(8,128)(2,1)S(1)}, u32[]{:S(2)}) copy-start(bf16[1,320,128]{2,1,0:T(8,128)(2,1)S(1)} %collective-permute-done.21.above) | copy-start | bytes 245764
  141.1 23.8 %collective-permute-start.17 = (bf16[16,80,128]{2,1,0:T(8,128)(2,1)}, bf16[16,80,128]{2,1,0:T(8,128)(2,1)S(1)}, u32[]{:S(2)}, u32[]{:S(2)}) collective-permute-start(bf16[16,80,128]{2,1,0:T(8,128)(2,1)} %get-tuple-element.18), channel_id=1, source_target_pairs={{0,6},{2,0},{4,2},{6,4},{1,7},{3,1},{5,3},{7,5},{8,14},{10,8},{12,... | collective-permute-start | bytes 983048 | tf_op jit(solution)/shard_map/ppermute | solution.py:15
  153.1 1.1 copy-start.6
  153.1 1.2 copy-start.13
  153.1 5.1 %copy-start.4 = (bf16[1,64,80,128]{3,2,1,0:T(8,128)(2,1)S(1)}, bf16[1,64,80,128]{3,2,1,0:T(8,128)(2,1)}, u32[]{:S(2)}) copy-start(bf16[1,64,80,128]{3,2,1,0:T(8,128)(2,1)} %copy-done.3) | copy-start | bytes 3932164
  153.2 12.7 %collective-permute-start.23 = (bf16[16,80,128]{2,1,0:T(8,128)(2,1)}, bf16[16,80,128]{2,1,0:T(8,128)(2,1)S(1)}, u32[]{:S(2)}, u32[]{:S(2)}) collective-permute-start(bf16[16,80,128]{2,1,0:T(8,128)(2,1)} %get-tuple-element.23), channel_id=1, source_target_pairs={{0,2},{2,4},{4,6},{6,0},{1,3},{3,5},{5,7},{7,1},{8,10},{10,12},{12... | collective-permute-start | bytes 983048 | tf_op jit(solution)/shard_map/ppermute | solution.py:15
  154.3 42.8 %collective-permute-start.24 = (bf16[16,80,128]{2,1,0:T(8,128)(2,1)S(1)}, bf16[16,80,128]{2,1,0:T(8,128)(2,1)S(1)}, u32[]{:S(2)}, u32[]{:S(2)}) collective-permute-start(bf16[16,80,128]{2,1,0:T(8,128)(2,1)S(1)} %copy-done.13), channel_id=1, source_target_pairs={{0,4},{2,6},{4,0},{6,2},{1,5},{3,7},{5,1},{7,3},{8,12},{10,14},{12... | collective-permute-start | bytes 983048 | tf_op jit(solution)/shard_map/ppermute | solution.py:15
  161.9 4.0 %copy-start.12 = (bf16[16,80,128]{2,1,0:T(8,128)(2,1)S(1)}, bf16[16,80,128]{2,1,0:T(8,128)(2,1)}, u32[]{:S(2)}) copy-start(bf16[16,80,128]{2,1,0:T(8,128)(2,1)} %get-tuple-element.25) | copy-start | bytes 983044
  162.1 17.5 %collective-permute-start.27 = (f32[9,40,320]{2,1,0:T(8,128)S(1)}, f32[9,40,320]{2,1,0:T(8,128)S(1)}, u32[]{:S(2)}, u32[]{:S(2)}) collective-permute-start(f32[9,40,320]{2,1,0:T(8,128)S(1)} %get-tuple-element.29), channel_id=1, source_target_pairs={{0,24},{8,0},{16,8},{24,16},{1,25},{9,1},{17,9},{25,17},{2,26},{10... | collective-permute-start | bytes 1382408 | tf_op jit(solution)/shard_map/ppermute | solution.py:15
  164.4 24.4 %collective-permute-start.28 = (f32[9,40,320]{2,1,0:T(8,128)S(1)}, f32[9,40,320]{2,1,0:T(8,128)S(1)}, u32[]{:S(2)}, u32[]{:S(2)}) collective-permute-start(f32[9,40,320]{2,1,0:T(8,128)S(1)} %get-tuple-element.31), channel_id=1, source_target_pairs={{0,16},{8,24},{16,0},{24,8},{1,17},{9,25},{17,1},{25,9},{2,18},{10... | collective-permute-start | bytes 1382408 | tf_op jit(solution)/shard_map/ppermute | solution.py:15
  164.9 23.9 %collective-permute-start.29 = (f32[9,40,320]{2,1,0:T(8,128)S(1)}, f32[9,40,320]{2,1,0:T(8,128)S(1)}, u32[]{:S(2)}, u32[]{:S(2)}) collective-permute-start(f32[9,40,320]{2,1,0:T(8,128)S(1)} %get-tuple-element.30), channel_id=1, source_target_pairs={{0,8},{8,16},{16,24},{24,0},{1,9},{9,17},{17,25},{25,1},{2,10},{10... | collective-permute-start | bytes 1382408 | tf_op jit(solution)/shard_map/ppermute | solution.py:15
  165.8 48.6 %copy-start.5 = (bf16[1,64,80,128]{3,2,1,0:T(8,128)(2,1)}, bf16[1,64,80,128]{3,2,1,0:T(8,128)(2,1)S(1)}, u32[]{:S(2)}) copy-start(bf16[1,64,80,128]{3,2,1,0:T(8,128)(2,1)S(1)} %bitcast_dynamic-update-slice_fusion.1) | copy-start | bytes 3932164
  165.9 46.3 %collective-permute-start.25 = (bf16[16,80,128]{2,1,0:T(8,128)(2,1)S(1)}, bf16[16,80,128]{2,1,0:T(8,128)(2,1)S(1)}, u32[]{:S(2)}, u32[]{:S(2)}) collective-permute-start(bf16[16,80,128]{2,1,0:T(8,128)(2,1)S(1)} %copy-done.12), channel_id=1, source_target_pairs={{0,6},{2,0},{4,2},{6,4},{1,7},{3,1},{5,3},{7,5},{8,14},{10,8},{12,... | collective-permute-start | bytes 983048 | tf_op jit(solution)/shard_map/ppermute | solution.py:15
  189.2 12.3 %collective-permute-start.30 = (f32[80,360]{0,1:T(8,128)S(1)}, f32[80,360]{0,1:T(8,128)S(1)}, u32[]{:S(2)}, u32[]{:S(2)}) collective-permute-start(f32[80,360]{0,1:T(8,128)S(1)} %bitcast.125), channel_id=1, source_target_pairs={{0,6},{2,0},{4,2},{6,4},{1,7},{3,1},{5,3},{7,5},{8,14},{10,8},{12,... | collective-permute-start | bytes 345608 | tf_op jit(solution)/shard_map/ppermute | solution.py:15
  196.5 15.5 %collective-permute-start.31 = (f32[80,360]{0,1:T(8,128)S(1)}, f32[80,360]{0,1:T(8,128)S(1)}, u32[]{:S(2)}, u32[]{:S(2)}) collective-permute-start(f32[80,360]{0,1:T(8,128)S(1)} %bitcast.124), channel_id=1, source_target_pairs={{0,4},{2,6},{4,0},{6,2},{1,5},{3,7},{5,1},{7,3},{8,12},{10,14},{12... | collective-permute-start | bytes 345608 | tf_op jit(solution)/shard_map/ppermute | solution.py:15
  196.6 15.4 %collective-permute-start.32 = (f32[80,360]{0,1:T(8,128)S(1)}, f32[80,360]{0,1:T(8,128)S(1)}, u32[]{:S(2)}, u32[]{:S(2)}) collective-permute-start(f32[80,360]{0,1:T(8,128)S(1)} %bitcast.123), channel_id=1, source_target_pairs={{0,2},{2,4},{4,6},{6,0},{1,3},{3,5},{5,7},{7,1},{8,10},{10,12},{12... | collective-permute-start | bytes 345608 | tf_op jit(solution)/shard_map/ppermute | solution.py:15
  212.1 1.5 collective-permute-start.33
  212.2 2.2 %copy-start.1 = (f32[1,64,80,128]{3,2,1,0:T(8,128)}, f32[1,64,80,128]{3,2,1,0:T(8,128)S(1)}, u32[]{:S(2)}) copy-start(f32[1,64,80,128]{3,2,1,0:T(8,128)S(1)} %convert_dynamic-update-slice_fusion) | copy-start | bytes 7864324
where the time goes:
time: 215 us; the launch traced here: 214 us
  starting transfers between devices  81.7 us (38%)
  waiting for transfers between devices  56.5 us (26%)
  Pallas kernels  34.1 us (16%)
  local copies, waits for them, and re-layouts  30.3 us (14%)
  other arithmetic  10.6 us (5%)
    ppermute x30, starting transfers between devices, receive(): lax.ppermute(block, axis, [(i, (i - ahead) % count) for i in range(count)])  74 us
    ppermute x30, waiting for transfers between devices, receive(): lax.ppermute(block, axis, [(i, (i - ahead) % count) for i in range(count)])  56.5 us
    pallas_call x1, Pallas kernels, correlate(): pl.pallas_call(functools.partial(correlate_body, count), grid=(3, 3), in_...  12.6 us
    pallas_call x1, Pallas kernels, forward(): pl.pallas_call(functools.partial(forward_body, count, rows), grid=(height...  11.8 us
    pallas_call x1, Pallas kernels, backward(): pl.pallas_call(functools.partial(backward_body, count, rows), grid=(heigh...  9.72 us
    unnamed x32, local copies, waits for them, and re-layouts  4.87 us
  transfers between devices with their start and end apart: 34, of which 9 were waited for; matrix products, arithmetic and copies ran while one was open for 15% of the time, Pallas kernels for 10%

commit v1 on v0

--- a/solution.py
+++ b/solution.py
@@ -7,7 +7,8 @@
 from jax.experimental.pallas import tpu as pltpu
 from jax.sharding import PartitionSpec as P
 
-VMEM_LIMIT = 60 * 1024 * 1024
+
+VMEM_LIMIT = 36 * 1024 * 1024
 
 
 def receive(block, axis, ahead):
@@ -61,9 +62,10 @@
 
 
 def forward_body(count, rows, *refs):
-    pieces, rims, kernels = refs[:count], refs[count : 2 * count], refs[2 * count]
-    outs = refs[2 * count + 1 : 3 * count + 1]
-    factor, stacked = refs[3 * count + 1 :]
+    pieces, rims, ends = (refs[k * count : (k + 1) * count] for k in range(3))
+    kernels = refs[3 * count]
+    outs = refs[3 * count + 1 : 4 * count + 1]
+    factor, stacked, first, last = refs[4 * count + 1 :]
     height, depth, width = pieces[0].shape
     channels = count * depth
     step = pl.program_id(0)
@@ -91,94 +93,131 @@
         for j in range(count):
             outs[j][row] = activated[j * depth : (j + 1) * depth, lanes]
 
+    def end(out, side, row):
+        for j in range(count):
+            part_of = slice(j * depth, (j + 1) * depth)
+            value = ends[j][side].astype(jnp.float32) * factor[row, part_of, :]
+            out[0, part_of, :] = value.astype(jnp.bfloat16)
+
+    @pl.when(step == 0)
+    def _():
+        end(first, 0, 0)
+
+    @pl.when(step == pl.num_programs(0) - 1)
+    def _():
+        end(last, 1, rows - 1)
+
 
 def whole(shape):
-    return pl.BlockSpec(shape, lambda *_: (0,) * len(shape))
-
-
-def forward(pieces, rims, kernels):
+    return pl.BlockSpec(shape, lambda *_: (0,) * len(shape), pipeline_mode=pl.Buffered(1))
+
+
+def forward(pieces, rims, ends, kernels):
     count = len(pieces)
     height, depth, width = pieces[0].shape
     channels = count * depth
     rows = 4 if height % 4 == 0 else 1
     flops = 2 * 9 * channels * channels * height * width
-    results = pl.pallas_call(
+    call = pl.pallas_call(
         functools.partial(forward_body, count, rows),
         grid=(height // rows,),
         in_specs=[whole(pieces[0].shape)] * count
         + [whole(rims[0].shape)] * count
+        + [whole(ends[0].shape)] * count
         + [whole(kernels.shape)],
         out_specs=[pl.BlockSpec((rows, depth, width), lambda g: (g, 0, 0))] * count
         + [
             pl.BlockSpec((rows, channels, width), lambda g: (g, 0, 0)),
             whole((3 * channels, (height + 2) * width)),
+            whole((1, channels, width)),
+            whole((1, channels, width)),
         ],
         out_shape=[jax.ShapeDtypeStruct((height, depth, width), jnp.bfloat16)] * count
         + [
             jax.ShapeDtypeStruct((height, channels, width), jnp.float32),
             jax.ShapeDtypeStruct((3 * channels, (height + 2) * width), jnp.bfloat16),
+            jax.ShapeDtypeStruct((1, channels, width), jnp.bfloat16),
+            jax.ShapeDtypeStruct((1, channels, width), jnp.bfloat16),
         ],
         compiler_params=pltpu.CompilerParams(vmem_limit_bytes=VMEM_LIMIT),
         cost_estimate=pl.CostEstimate(
             flops=flops, bytes_accessed=16 * 1024 * 1024, transcendentals=0
         ),
         name="conv_forward",
-    )(*pieces, *rims, kernels)
-    return results[:count], results[count], results[count + 1]
-
-
-def correlate_body(count, *refs):
-    stacked, factor = refs[0], refs[1]
-    pieces = refs[2 : 2 + count]
-    grads, slope = refs[2 + count :]
-    height, depth, width = pieces[0].shape
+    )
+    results = call(*pieces, *rims, *ends, kernels)
+    return results[:count], *results[count:]
+
+
+def correlate_body(count, groups, rows, turn, stacked, factor, *refs):
+    pieces, ends = refs[:count], refs[count : 2 * count]
+    shares, slope = refs[2 * count : -1], refs[-1]
+    height, depth, width = factor.shape[0], pieces[0].shape[1], factor.shape[2]
     channels = count * depth
     tap_row, tap_col = pl.program_id(0), pl.program_id(1)
 
     @pl.when((tap_row == 0) & (tap_col == 0))
     def _():
-        def body(row, carry):
+        def put(row, blocks):
             lanes = pl.ds(pl.multiple_of(row * width, width), width)
             for j in range(count):
                 part_of = pl.ds(j * depth, depth)
-                value = pieces[j][row].astype(jnp.float32) * factor[row, part_of, :]
+                value = blocks[j].astype(jnp.float32) * factor[row, part_of, :]
                 slope[part_of, lanes] = value.astype(jnp.bfloat16)
+
+        def body(row, carry):
+            put(row + 1, [piece[row] for piece in pieces])
             return carry
 
-        lax.fori_loop(0, height, body, 0)
+        put(0, [end[0] for end in ends])
+        lax.fori_loop(0, height - 2, body, 0)
+        put(height - 1, [end[1] for end in ends])
 
     source = stacked[
         pl.ds(pl.multiple_of(tap_col * channels, channels), channels),
         pl.ds(pl.multiple_of(tap_row * width, width), height * width),
     ]
-    grads[0] = lax.dot_general(
+    grads = lax.dot_general(
         source, slope[...], (((1,), (1,)), ((), ())), preferred_element_type=jnp.float32
     )
-
-
-def correlate(stacked, factor, pieces):
+    size = channels // (groups * rows)
+    for own in range(rows):
+
+        @pl.when(turn[0] == own)
+        def _():
+            for j in range(rows):
+                for group in range(groups):
+                    start = (group * rows + (own - j) % rows) * size
+                    shares[j][0, group] = grads[start : start + size]
+
+
+def correlate(stacked, factor, pieces, ends):
     count = len(pieces)
-    height, depth, width = pieces[0].shape
-    channels = count * depth
+    height, channels, width = factor.shape
+    groups, rows = lax.axis_size("dp"), lax.axis_size("row")
+    size = channels // (groups * rows)
     flops = 2 * 9 * channels * channels * height * width
-    return pl.pallas_call(
-        functools.partial(correlate_body, count),
+    call = pl.pallas_call(
+        functools.partial(correlate_body, count, groups, rows),
         grid=(3, 3),
-        in_specs=[whole(stacked.shape), whole(factor.shape)] + [whole(pieces[0].shape)] * count,
-        out_specs=[
-            pl.BlockSpec((1, channels, channels), lambda a, b: (3 * a + b, 0, 0)),
-            whole((channels, height * width)),
-        ],
-        out_shape=[
-            jax.ShapeDtypeStruct((9, channels, channels), jnp.float32),
-            jax.ShapeDtypeStruct((channels, height * width), jnp.bfloat16),
-        ],
+        in_specs=[pl.BlockSpec(memory_space=pltpu.SMEM)]
+        + [whole(stacked.shape), whole(factor.shape)]
+        + [whole(pieces[0].shape)] * count
+        + [whole(ends[0].shape)] * count,
+        out_specs=[pl.BlockSpec((1, groups, size, channels), lambda a, b: (3 * a + b, 0, 0, 0))]
+        * rows
+        + [whole((channels, height * width))],
+        out_shape=[jax.ShapeDtypeStruct((9, groups, size, channels), jnp.float32)] * rows
+        + [jax.ShapeDtypeStruct((channels, height * width), jnp.bfloat16)],
         compiler_params=pltpu.CompilerParams(vmem_limit_bytes=VMEM_LIMIT),
         cost_estimate=pl.CostEstimate(
             flops=flops, bytes_accessed=14 * 1024 * 1024, transcendentals=0
         ),
         name="kernel_grad",
-    )(stacked, factor, *pieces)
+    )
+    turn = lax.axis_index("row").astype(jnp.int32)[None]
+    results = call(turn, stacked, factor, *pieces, *ends)
+    return results[:-1], results[-1]
 
 
 def backward_body(count, rows, turns, slope, above, below, kernels, *refs):
@@ -256,28 +295,32 @@
     placed = rotated(placed, (chan * (dps // chans) - dp) % dps, 1)
     channels = chans * outer
     taps_of = placed.reshape(rows, dps, channels, 3, 3, share)
-    ahead = jnp.transpose(taps_of, (3, 2, 4, 1, 0, 5)).reshape(3, channels, 3 * channels)
+    return taps_of
+
+
+def ahead_order(taps_of):
+    channels = taps_of.shape[2]
+    return jnp.transpose(taps_of, (3, 2, 4, 1, 0, 5)).reshape(3, channels, 3 * channels)
+
+
+def back_order(taps_of):
+    channels = taps_of.shape[2]
     flipped = taps_of[:, :, :, ::-1, ::-1]
-    back = jnp.transpose(flipped, (3, 1, 0, 5, 4, 2)).reshape(3, channels, 3 * channels)
-    return ahead, back
-
-
-def summed_kernel_grad(terms, inner, outer):
+    return jnp.transpose(flipped, (3, 1, 0, 5, 4, 2)).reshape(3, channels, 3 * channels)
+
+
+def summed_kernel_grad(shares, inner, outer):
     dp, chan, row = (lax.axis_index(a) for a in ("dp", "chan", "row"))
     dps, chans, rows = (lax.axis_size(a) for a in ("dp", "chan", "row"))
-    channels = terms.shape[1]
+    channels = shares[0].shape[3]
     share = inner // rows
-    terms = terms.reshape(9, dps, rows, share, channels)
-
-    def of_row(r):
-        return lax.dynamic_index_in_dim(terms, r, 2, keepdims=False)
-
-    halves = of_row(row)
+    halves = shares[0]
     for j in range(1, rows):
-        halves = halves + receive(of_row((row - j) % rows), "row", j)
+        halves = halves + receive(shares[j], "row", j)
 
     def of_dp(d):
-        return lax.dynamic_index_in_dim(halves, (d - chan * (dps // chans)) % dps, 1, keepdims=False)
+        at = (d - chan * (dps // chans)) % dps
+        return lax.dynamic_index_in_dim(halves, at, 1, keepdims=False)
 
     total = of_dp(dp)
     for j in range(1, dps):
@@ -285,7 +328,8 @@
     total = jnp.transpose(total, (2, 0, 1)).reshape(channels, 9 * share)
     own = total[:outer]
     for j in range(1, chans):
-        own = own + receive(total[(chans - j) * outer : (chans - j + 1) * outer], "chan", j)
+        start = (chans - j) * outer
+        own = own + receive(total[start : start + outer], "chan", j)
     both = jnp.stack([own] + [receive(own, "row", j) for j in range(1, rows)])
     both = rotated(both, (rows - row) % rows, 0).reshape(rows, outer, 9, share)
     return jnp.transpose(both, (2, 0, 3, 1)).reshape(9, inner, outer)
@@ -306,7 +350,7 @@
             receive(part(array, home(-j), size, 0), "chan", j) for j in range(1, chans)
         ]
 
-    ahead_kernel, back_kernel = gathered_kernel(kernel)
+    taps_of = gathered_kernel(kernel)
     pieces = to_homes(images, height)
     down = [(i, i + 1) for i in range(rows - 1)]
     up = [(i + 1, i) for i in range(rows - 1)]
@@ -314,22 +358,27 @@
     high = lax.ppermute(images[:1], "row", up)
     tops = jnp.concatenate([low, images[height - 1 : slab - 1 : height]])
     bottoms = jnp.concatenate([images[height::height], high])
-    rims = to_homes(jnp.stack([tops, bottoms], axis=1).reshape(2 * chans, depth, width), 2)
-    cotangents = to_homes(cotangent, height)
-
-    activated, factor, stacked = forward(pieces, rims, ahead_kernel)
-
-    def edge(at):
-        wide = jnp.concatenate([c[at] for c in cotangents]).astype(jnp.float32)
-        return (wide * factor[at]).astype(jnp.bfloat16)[None]
+    rims = jnp.stack([tops, bottoms], axis=1).reshape(2 * chans, depth, width)
+    rims = to_homes(rims, 2)
+    firsts, lasts = cotangent[::height], cotangent[height - 1 :: height]
+    ends = jnp.stack([firsts, lasts], axis=1).reshape(2 * chans, depth, width)
+    ends = to_homes(ends, 2)
+    inside = cotangent.reshape(chans, height, depth, width)[:, 1:-1]
+    inside = inside.reshape(slab - 2 * chans, depth, width)
+    cotangents = to_homes(inside, height - 2)
+
+    results = forward(pieces, rims, ends, ahead_order(taps_of))
+    activated, factor, stacked, first, last = results
+    taps_of, factor = lax.optimization_barrier((taps_of, factor))
+    back_kernel = back_order(taps_of)
 
     def snake(place_at):
         r, k = place_at // chans, place_at % chans
         return (k if r % 2 == 0 else chans - 1 - k) * rows + r
 
     line = [(snake(i), snake(i + 1)) for i in range(rows * chans - 1)]
-    above = lax.ppermute(edge(height - 1), ("chan", "row"), line)
-    below = lax.ppermute(edge(0), ("chan", "row"), [(b, a) for a, b in line])
+    above = lax.ppermute(last, ("chan", "row"), line)
+    below = lax.ppermute(first, ("chan", "row"), [(b, a) for a, b in line])
 
     place_at = home(0)
     forth = jnp.where(row % 2 == 0, 1, chans - 1)
@@ -339,7 +388,7 @@
             jnp.where(place_at == chans - 1, 0, chans - forth),
         ]
     ).astype(jnp.int32)
-    grads, slope = correlate(stacked, factor, cotangents)
+    grads, slope = correlate(stacked, factor, cotangents, ends)
     input_grads = backward(turns, slope, above, below, back_kernel, chans)
     kernel_grad = summed_kernel_grad(grads, kernel.shape[1], kernel.shape[2])
 

time: 215 us -> 212 us (0.986)
  starting transfers between devices: 81.7 us -> 55.3 us
  local copies, waits for them, and re-layouts: 30.3 us -> 48.2 us
  waiting for transfers between devices: 56.5 us -> 69.3 us
  Pallas kernels: 34.1 us -> 25.2 us
    ppermute x30 -> x33, starting transfers between devices: 74 us -> 49.1 us  [receive(): lax.ppermute(block, axis, [(i, (i - ahead) % count) for i in range(count)])]
    ppermute x30 -> x33, waiting for transfers between devices: 56.5 us -> 69.2 us  [receive(): lax.ppermute(block, axis, [(i, (i - ahead) % count) for i in range(count)])]
    unnamed x32 -> x56, local copies, waits for them, and re-layouts: 4.87 us -> 13.1 us
    pallas_call x2, Pallas kernels: 24.4 us -> 17.8 us  [the longest x1 9.34 us: correlate(): results = call(turn, stacked, factor, *pieces, *ends)]
    dynamic_update_slice x5, local copies, waits for them, and re-layouts: 1.2 us -> 4.98 us  [to_owners(): lax.dynamic_update_slice_in_dim(out, arrived.astype(dtype), home(-j) * he...]
    squeeze x2 -> x1, local copies, waits for them, and re-layouts: 3.43 us -> 0.17 us  [of_dp(): return lax.dynamic_index_in_dim(halves, at, 1, keepdims=False)]
    transpose x3, local copies, waits for them, and re-layouts: 3.29 us -> 6.52 us  [the longest x2 4.7 us: back_order(): jnp.transpose(flipped, (3, 1, 0, 5, 4, 2))]
    pallas_call x1, Pallas kernels: 9.72 us -> 7.46 us  [backward(): pl.pallas_call(functools.partial(backward_body, count, rows), grid=(heigh...]
  transfers between devices with their start and end apart: 34 -> 37, of which waited for: 9 -> 11; matrix products, arithmetic and copies ran while one was open for 15% -> 22% of each run, Pallas kernels for 10% -> 8%
where the time goes in v1:
time: 212 us; the launch traced here: 210 us
  waiting for transfers between devices  69.3 us (33%)
  starting transfers between devices  55.3 us (26%)
  local copies, waits for them, and re-layouts  48.2 us (23%)
  Pallas kernels  25.2 us (12%)
  other arithmetic  11.3 us (5%)
    ppermute x33, waiting for transfers between devices, receive(): lax.ppermute(block, axis, [(i, (i - ahead) % count) for i in range(count)])  69.2 us
    ppermute x33, starting transfers between devices, receive(): lax.ppermute(block, axis, [(i, (i - ahead) % count) for i in range(count)])  49.1 us
    unnamed x56, local copies, waits for them, and re-layouts  13.1 us
    pallas_call x1, Pallas kernels, correlate(): results = call(turn, stacked, factor, *pieces, *ends)  9.34 us
    pallas_call x1, Pallas kernels, forward(): results = call(*pieces, *rims, *ends, kernels)  8.45 us
    pallas_call x1, Pallas kernels, backward(): pl.pallas_call(functools.partial(backward_body, count, rows), grid=(heigh...  7.46 us
    reshape x1, local copies, waits for them, and re-layouts, back_order(): jnp.transpose(flipped, (3, 1, 0, 5, 4, 2))  6.81 us
    dynamic_update_slice x5, local copies, waits for them, and re-layouts, to_owners(): lax.dynamic_update_slice_in_dim(out, arrived.astype(dtype), home(-j) * he...  4.98 us
  transfers between devices with their start and end apart: 37, of which 11 were waited for; matrix products, arithmetic and copies ran while one was open for 22% of the time, Pallas kernels for 8%

profile of v1, /device:TPU:0, one launch (start us, length us, event | category | flops | bytes accessed | tf_op | source)
XLA Modules:
  0.0 210.5 jit_solution(4238256488644981487)
XLA Ops:
  0.7 0.9 copy-done
  1.6 5.1 %collective-permute-start.11 = (bf16[80,360]{0,1:T(8,128)(2,1)S(1)}, bf16[80,360]{0,1:T(8,128)(2,1)S(1)}, u32[]{:S(2)}, u32[]{:S(2)}) collective-permute-start(bf16[80,360]{0,1:T(8,128)(2,1)S(1)} %bitcast.105), channel_id=1, source_target_pairs={{0,6},{2,0},{4,2},{6,4},{1,7},{3,1},{5,3},{7,5},{8,14},{10,8},{12,... | collective-permute-start | bytes 172808 | tf_op jit(solution)/shard_map/ppermute | solution.py:16
  6.7 1.0 collective-permute-start.13
  7.7 1.4 slice_bitcast_fusion.3
  9.1 1.9 collective-permute-start.3
  11.0 1.3 collective-permute-start.4
  12.2 0.9 slice_bitcast_fusion.1
  13.5 1.5 collective-permute-done.12
  15.2 2.5 %collective-permute-start.14 = (bf16[320,360]{0,1:T(8,128)(2,1)S(1)}, bf16[320,360]{0,1:T(8,128)(2,1)S(1)}, u32[]{:S(2)}, u32[]{:S(2)}) collective-permute-start(bf16[320,360]{0,1:T(8,128)(2,1)S(1)} %pad_maximum_fusion.1), channel_id=1, source_target_pairs={{0,24},{8,0},{16,8},{24,16},{1,25},{9,1},{17,9},{25,17},{2,26},{10... | collective-permute-start | bytes 691208 | tf_op jit(solution)/shard_map/ppermute | solution.py:16
  19.5 1.1 fusion.15
  20.6 4.2 %collective-permute-done.14 = bf16[320,360]{0,1:T(8,128)(2,1)S(1)} collective-permute-done((bf16[320,360]{0,1:T(8,128)(2,1)S(1)}, bf16[320,360]{0,1:T(8,128)(2,1)S(1)}, u32[]{:S(2)}, u32[]{:S(2)}) %collective-permute-start.14) | collective-permute-done | bytes 230432 | tf_op jit(solution)/shard_map/ppermute | solution.py:16
  25.1 7.1 %collective-permute-done.15 = bf16[320,360]{0,1:T(8,128)(2,1)S(1)} collective-permute-done((bf16[320,360]{0,1:T(8,128)(2,1)S(1)}, bf16[320,360]{0,1:T(8,128)(2,1)S(1)}, u32[]{:S(2)}, u32[]{:S(2)}) %collective-permute-start.15) | collective-permute-done | bytes 230432 | tf_op jit(solution)/shard_map/ppermute | solution.py:16
  32.2 2.8 %collective-permute-start.8 = (bf16[2,80,128]{2,1,0:T(8,128)(2,1)}, bf16[2,80,128]{2,1,0:T(8,128)(2,1)S(1)}, u32[]{:S(2)}, u32[]{:S(2)}) collective-permute-start(bf16[2,80,128]{2,1,0:T(8,128)(2,1)} %get-tuple-element.62), channel_id=1, source_target_pairs={{0,6},{2,0},{4,2},{6,4},{1,7},{3,1},{5,3},{7,5},{8,14},{10,8},{12,... | collective-permute-start | bytes 122888 | tf_op jit(solution)/shard_map/ppermute | solution.py:16
  35.0 1.3 pad_maximum_fusion
  36.3 1.4 copy.22
  37.6 2.3 %dynamic-slice_bitcast_fusion.3 = (bf16[16,80,128]{2,1,0:T(8,128)(2,1)}, bf16[16,80,128]{2,1,0:T(8,128)(2,1)}, bf16[16,80,128]{2,1,0:T(8,128)(2,1)}, bf16[16,80,128]{2,1,0:T(8,128)(2,1)S(1)}) fusion(bf16[1,64,80,128]{3,2,1,0:T(8,128)(2,1)} %param.3, s32[]{:T(128)S(6)} %select_n.280, s32[]{:T(128)S(6)} %select_n.277, s32[]{:T(128)S(6)} %select_n.274, ...), kind=kLoop, calls=%fused_computation.34 | loop fusion | bytes 2621456 | tf_op jit(solution)/shard_map/dynamic_slice | solution.py:24
  39.9 0.9 fusion.13
  40.8 1.0 constant_dynamic-slice_fusion
  41.9 0.8 maximum_bitcast_fusion
  42.8 1.3 collective-permute-start
  45.5 1.4 collective-permute-start.1
  46.9 2.3 %copy.23 = bf16[4,320,360]{1,2,0:T(8,128)(2,1)} copy(bf16[4,320,360]{2,1,0:T(8,128)(2,1)} %collective-permute-done.17) | data formatting | bytes 1843200 | tf_op jit(solution)/shard_map/ppermute | solution.py:16
  49.2 2.0 collective-permute-start.2
  51.2 1.8 collective-permute-start.5
  53.0 3.6 %fusion.3 = bf16[2,4,320,360]{2,3,1,0:T(8,128)(2,1)S(1)} fusion(s32[]{:T(128)S(6)} %select_n.287, bf16[1,4,320,360]{2,3,1,0:T(8,128)(2,1)S(1)} %copy-done.24, bf16[1,4,320,360]{2,3,1,0:T(8,128)(2,1)} %bitcast.100), kind=kLoop, calls=%fused_computation.9 | loop fusion | flops 2764800 | bytes 3686404 | tf_op jit(solution)/shard_map/concatenate | solution.py:28
  56.7 10.4 %collective-permute-done.5.refs_5_ = bf16[2,80,128]{2,1,0:T(8,128)(2,1)S(1)} collective-permute-done((bf16[2,80,128]{2,1,0:T(8,128)(2,1)S(1)}, bf16[2,80,128]{2,1,0:T(8,128)(2,1)S(1)}, u32[]{:S(2)}, u32[]{:S(2)}) %collective-permute-start.5) | collective-permute-done | bytes 40992 | tf_op jit(solution)/shard_map/ppermute | solution.py:16
  67.1 11.4 %collective-permute-start.7 = (bf16[2,80,128]{2,1,0:T(8,128)(2,1)}, bf16[2,80,128]{2,1,0:T(8,128)(2,1)}, u32[]{:S(2)}, u32[]{:S(2)}) collective-permute-start(bf16[2,80,128]{2,1,0:T(8,128)(2,1)} %get-tuple-element.64), channel_id=1, source_target_pairs={{0,2},{2,4},{4,6},{6,0},{1,3},{3,5},{5,7},{7,1},{8,10},{10,12},{12... | collective-permute-start | bytes 122888 | tf_op jit(solution)/shard_map/ppermute | solution.py:16
  78.5 1.0 fusion
  79.5 1.8 copy.24
  81.6 2.8 %copy.25.refs_12_ = bf16[3,320,960]{2,1,0:T(8,128)(2,1)S(1)} copy(bf16[3,320,960]{1,2,0:T(8,128)(2,1)} %bitcast.98) | data formatting | bytes 3686400 | tf_op jit(solution)/shard_map/reshape | solution.py:303
  84.4 1.5 collective-permute-start.22
  87.9 1.0 copy-done.5
  88.9 1.0 copy-done.7
  89.8 0.8 copy-done.14
  92.2 8.5 %conv_forward.1 = (bf16[16,80,128]{2,1,0:T(8,128)(2,1)S(1)}, bf16[16,80,128]{2,1,0:T(8,128)(2,1)S(1)}, bf16[16,80,128]{2,1,0:T(8,128)(2,1)S(1)}, bf16[16,80,128]...) custom-call(bf16[16,80,128]{2,1,0:T(8,128)(2,1)S(1)} %get-tuple-elem, ...), custom_call_target="tpu_custom_call" | custom-call | flops 3774873600 | bytes 16777216 | tf_op jit(solution)/shard_map/conv_forward/pallas_call | solution.py:148
  101.3 9.3 %collective-permute-done.22.refs_2_ = bf16[14,80,128]{2,1,0:T(8,128)(2,1)S(1)} collective-permute-done((bf16[14,80,128]{2,1,0:T(8,128)(2,1)}, bf16[14,80,128]{2,1,0:T(8,128)(2,1)S(1)}, u32[]{:S(2)}, u32[]{:S(2)}) %collective-permute-start.22) | collective-permute-done | bytes 286752 | tf_op jit(solution)/shard_map/ppermute | solution.py:16
  110.7 9.3 %kernel_grad.1 = (f32[9,4,40,320]{3,2,1,0:T(8,128)S(1)}, f32[9,4,40,320]{3,2,1,0:T(8,128)}, bf16[320,2048]{1,0:T(8,128)(2,1)S(1)}) custom-call(s32[1]{0:T(128)} %bitcast.32.turn, bf16[960,2304]{1,0:T(8,128)(2,1)S(1)} %get-tuple-element.24.stacked, f32[16,320,128]{2,1,0:T(8,128)S(1)} %get-tuple-element.26.factor, ...), custom_call_target="tpu_custom_call" | custom-call | flops 3774873600 | bytes 14680064 | tf_op jit(solution)/shard_map/kernel_grad/pallas_call | solution.py:219
  120.0 1.2 copy-done.21
  121.2 1.7 collective-permute-start.24
  123.0 1.3 collective-permute-start.25
  124.3 3.2 %collective-permute-start.18 = (bf16[16,80,128]{2,1,0:T(8,128)(2,1)}, bf16[16,80,128]{2,1,0:T(8,128)(2,1)}, u32[]{:S(2)}, u32[]{:S(2)}) collective-permute-start(bf16[16,80,128]{2,1,0:T(8,128)(2,1)} %copy-done.3), channel_id=1, source_target_pairs={{0,2},{2,4},{4,6},{6,0},{1,3},{3,5},{5,7},{7,1},{8,10},{10,12},{12... | collective-permute-start | bytes 983048 | tf_op jit(solution)/shard_map/ppermute | solution.py:16
  127.6 1.5 collective-permute-start.19
  129.1 1.2 broadcast_in_dim.33
  131.1 1.8 reverse_bitcast_fusion
  132.9 2.9 %copy.26 = bf16[3,4,2,40,3,320]{5,4,3,2,1,0:T(4,128)(2,1)} copy(bf16[3,4,2,40,3,320]{5,3,4,0,1,2:T(8,128)(2,1)S(1)} %reverse_bitcast_fusion) | data formatting | bytes 3686400 | tf_op jit(solution)/shard_map/transpose | solution.py:309
  135.8 6.8 %reshape.69.kernels = bf16[3,320,960]{2,1,0:T(8,128)(2,1)} reshape(bf16[3,4,2,40,3,320]{5,4,3,2,1,0:T(4,128)(2,1)} %copy.26) | data formatting | bytes 3686400 | tf_op jit(solution)/shard_map/reshape | solution.py:309
  142.6 2.8 %collective-permute-start.20 = (bf16[16,80,128]{2,1,0:T(8,128)(2,1)S(1)}, bf16[16,80,128]{2,1,0:T(8,128)(2,1)S(1)}, u32[]{:S(2)}, u32[]{:S(2)}) collective-permute-start(bf16[16,80,128]{2,1,0:T(8,128)(2,1)S(1)} %get-tuple-element.23), channel_id=1, source_target_pairs={{0,6},{2,0},{4,2},{6,4},{1,7},{3,1},{5,3},{7,5},{8,14},{10,8},{12,... | collective-permute-start | bytes 983048 | tf_op jit(solution)/shard_map/ppermute | solution.py:16
  146.1 1.5 copy-done.1
  147.6 0.9 copy-done.12
  148.5 1.3 copy-done.22
  149.8 7.5 %conv_backward.1 = (f32[16,80,128]{2,1,0:T(8,128)S(1)}, bf16[16,80,128]{2,1,0:T(8,128)(2,1)S(1)}, bf16[16,80,128]{2,1,0:T(8,128)(2,1)S(1)}, bf16[16,80,128]{2,1,0:T(8,128)(2,1)S(1)}) custom-call(s32[2]{0:T(128)S(1)} %pad_add_fusion.turns, bf16[320,2048]{1,0:T(8,128)(2,1)S(1)} %copy-done.22, bf16[1,320,128]{2,1,0:T(8,128)(2,1)S(1)} %collective-permute-done.24.above, ...), custom_call_target="tpu_custom_call" | custom-call | flops 3774873600 | bytes 8388608 | tf_op jit(solution)/shard_map/conv_backward/pallas_call | solution.py:260
  157.3 0.8 collective-permute-start.26
  158.4 1.7 bitcast_dynamic-update-slice_fusion.3
  160.2 1.7 bitcast_dynamic-update-slice_fusion.2
  161.9 1.9 add.234
  165.1 1.5 collective-permute-start.32
  167.3 2.4 %collective-permute-done.26 = bf16[16,80,128]{2,1,0:T(8,128)(2,1)S(1)} collective-permute-done((bf16[16,80,128]{2,1,0:T(8,128)(2,1)S(1)}, bf16[16,80,128]{2,1,0:T(8,128)(2,1)S(1)}, u32[]{:S(2)}, u32[]{:S(2)}) %collective-permute-start.26) | collective-permute-done | bytes 327712 | tf_op jit(solution)/shard_map/ppermute | solution.py:16
  170.4 9.1 %collective-permute-done.30 = f32[9,40,320]{2,1,0:T(8,128)S(1)} collective-permute-done((f32[9,40,320]{2,1,0:T(8,128)S(1)}, f32[9,40,320]{2,1,0:T(8,128)S(1)}, u32[]{:S(2)}, u32[]{:S(2)}) %collective-permute-start.30) | collective-permute-done | bytes 460832 | tf_op jit(solution)/shard_map/ppermute | solution.py:16
  179.5 10.4 %collective-permute-done.31 = f32[9,40,320]{2,1,0:T(8,128)S(1)} collective-permute-done((f32[9,40,320]{2,1,0:T(8,128)S(1)}, f32[9,40,320]{2,1,0:T(8,128)S(1)}, u32[]{:S(2)}, u32[]{:S(2)}) %collective-permute-start.31) | collective-permute-done | bytes 460832 | tf_op jit(solution)/shard_map/ppermute | solution.py:16
  190.3 2.7 %collective-permute-start.33 = (f32[80,360]{0,1:T(8,128)S(1)}, f32[80,360]{0,1:T(8,128)S(1)}, u32[]{:S(2)}, u32[]{:S(2)}) collective-permute-start(f32[80,360]{0,1:T(8,128)S(1)} %bitcast.119), channel_id=1, source_target_pairs={{0,6},{2,0},{4,2},{6,4},{1,7},{3,1},{5,3},{7,5},{8,14},{10,8},{12,... | collective-permute-start | bytes 345608 | tf_op jit(solution)/shard_map/ppermute | solution.py:16
  192.9 1.5 collective-permute-start.34
  194.5 3.5 %collective-permute-done.33 = f32[80,360]{0,1:T(8,128)S(1)} collective-permute-done((f32[80,360]{0,1:T(8,128)S(1)}, f32[80,360]{0,1:T(8,128)S(1)}, u32[]{:S(2)}, u32[]{:S(2)}) %collective-permute-start.33) | collective-permute-done | bytes 115232 | tf_op jit(solution)/shard_map/ppermute | solution.py:16
  197.9 10.1 %collective-permute-done.34 = f32[80,360]{0,1:T(8,128)S(1)} collective-permute-done((f32[80,360]{0,1:T(8,128)S(1)}, f32[80,360]{0,1:T(8,128)S(1)}, u32[]{:S(2)}, u32[]{:S(2)}) %collective-permute-start.34) | collective-permute-done | bytes 115232 | tf_op jit(solution)/shard_map/ppermute | solution.py:16
  208.2 1.3 collective-permute-done.36
  (114 shorter events, 14.6 us)
Async XLA Ops:
  0.6 0.9 copy-start
  0.6 12.7 %copy-start.26 = (bf16[1,64,80,128]{3,2,1,0:T(8,128)(2,1)S(1)}, bf16[1,64,80,128]{3,2,1,0:T(8,128)(2,1)}, u32[]{:S(2)}) copy-start(bf16[1,64,80,128]{3,2,1,0:T(8,128)(2,1)} %param.5) | copy-start | bytes 3932164
  1.6 12.0 %collective-permute-start.11 = (bf16[80,360]{0,1:T(8,128)(2,1)S(1)}, bf16[80,360]{0,1:T(8,128)(2,1)S(1)}, u32[]{:S(2)}, u32[]{:S(2)}) collective-permute-start(bf16[80,360]{0,1:T(8,128)(2,1)S(1)} %bitcast.105), channel_id=1, source_target_pairs={{0,6},{2,0},{4,2},{6,4},{1,7},{3,1},{5,3},{7,5},{8,14},{10,8},{12,... | collective-permute-start | bytes 172808 | tf_op jit(solution)/shard_map/ppermute | solution.py:16
  6.7 8.3 %collective-permute-start.12 = (bf16[80,360]{0,1:T(8,128)(2,1)S(1)}, bf16[80,360]{0,1:T(8,128)(2,1)S(1)}, u32[]{:S(2)}, u32[]{:S(2)}) collective-permute-start(bf16[80,360]{0,1:T(8,128)(2,1)S(1)} %bitcast.106), channel_id=1, source_target_pairs={{0,4},{2,6},{4,0},{6,2},{1,5},{3,7},{5,1},{7,3},{8,12},{10,14},{12... | collective-permute-start | bytes 172808 | tf_op jit(solution)/shard_map/ppermute | solution.py:16
  6.7 8.3 %collective-permute-start.13 = (bf16[80,360]{0,1:T(8,128)(2,1)S(1)}, bf16[80,360]{0,1:T(8,128)(2,1)S(1)}, u32[]{:S(2)}, u32[]{:S(2)}) collective-permute-start(bf16[80,360]{0,1:T(8,128)(2,1)S(1)} %bitcast.107), channel_id=1, source_target_pairs={{0,2},{2,4},{4,6},{6,0},{1,3},{3,5},{5,7},{7,1},{8,10},{10,12},{12... | collective-permute-start | bytes 172808 | tf_op jit(solution)/shard_map/ppermute | solution.py:16
  9.1 32.6 %collective-permute-start.3 = (bf16[1,80,128]{2,1,0:T(8,128)(2,1)}, bf16[1,80,128]{2,1,0:T(8,128)(2,1)}, u32[]{:S(2)}, u32[]{:S(2)}) collective-permute-start(bf16[1,80,128]{2,1,0:T(8,128)(2,1)} %get-tuple-element.42), channel_id=1, source_target_pairs={{0,1},{2,3},{4,5},{6,7},{8,9},{10,11},{12,13},{14,15},{16,17},{18,... | collective-permute-start | bytes 61448 | tf_op jit(solution)/shard_map/ppermute | solution.py:357
  11.0 31.8 %collective-permute-start.4 = (bf16[1,80,128]{2,1,0:T(8,128)(2,1)}, bf16[1,80,128]{2,1,0:T(8,128)(2,1)}, u32[]{:S(2)}, u32[]{:S(2)}) collective-permute-start(bf16[1,80,128]{2,1,0:T(8,128)(2,1)} %get-tuple-element.43), channel_id=1, source_target_pairs={{1,0},{3,2},{5,4},{7,6},{9,8},{11,10},{13,12},{15,14},{17,16},{19,... | collective-permute-start | bytes 61448 | tf_op jit(solution)/shard_map/ppermute | solution.py:358
  15.0 3.8 %copy-start.27 = (bf16[80,360]{0,1:T(8,128)(2,1)}, bf16[80,360]{0,1:T(8,128)(2,1)S(1)}, u32[]{:S(2)}) copy-start(bf16[80,360]{0,1:T(8,128)(2,1)S(1)} %collective-permute-done.13) | copy-start | bytes 172804
  15.2 9.6 %collective-permute-start.14 = (bf16[320,360]{0,1:T(8,128)(2,1)S(1)}, bf16[320,360]{0,1:T(8,128)(2,1)S(1)}, u32[]{:S(2)}, u32[]{:S(2)}) collective-permute-start(bf16[320,360]{0,1:T(8,128)(2,1)S(1)} %pad_maximum_fusion.1), channel_id=1, source_target_pairs={{0,24},{8,0},{16,8},{24,16},{1,25},{9,1},{17,9},{25,17},{2,26},{10... | collective-permute-start | bytes 691208 | tf_op jit(solution)/shard_map/ppermute | solution.py:16
  17.7 14.4 %collective-permute-start.15 = (bf16[320,360]{0,1:T(8,128)(2,1)S(1)}, bf16[320,360]{0,1:T(8,128)(2,1)S(1)}, u32[]{:S(2)}, u32[]{:S(2)}) collective-permute-start(bf16[320,360]{0,1:T(8,128)(2,1)S(1)} %pad_maximum_fusion.1), channel_id=1, source_target_pairs={{0,16},{8,24},{16,0},{24,8},{1,17},{9,25},{17,1},{25,9},{2,18},{10... | collective-permute-start | bytes 691208 | tf_op jit(solution)/shard_map/ppermute | solution.py:16
  18.2 16.8 %collective-permute-start.16 = (bf16[320,360]{0,1:T(8,128)(2,1)S(1)}, bf16[320,360]{0,1:T(8,128)(2,1)S(1)}, u32[]{:S(2)}, u32[]{:S(2)}) collective-permute-start(bf16[320,360]{0,1:T(8,128)(2,1)S(1)} %pad_maximum_fusion.1), channel_id=1, source_target_pairs={{0,8},{8,16},{16,24},{24,0},{1,9},{9,17},{17,25},{25,1},{2,10},{10... | collective-permute-start | bytes 691208 | tf_op jit(solution)/shard_map/ppermute | solution.py:16
  24.8 24.4 %collective-permute-start.10 = (bf16[2,80,128]{2,1,0:T(8,128)(2,1)}, bf16[2,80,128]{2,1,0:T(8,128)(2,1)S(1)}, u32[]{:S(2)}, u32[]{:S(2)}) collective-permute-start(bf16[2,80,128]{2,1,0:T(8,128)(2,1)} %get-tuple-element.60), channel_id=1, source_target_pairs={{0,2},{2,4},{4,6},{6,0},{1,3},{3,5},{5,7},{7,1},{8,10},{10,12},{12... | collective-permute-start | bytes 122888 | tf_op jit(solution)/shard_map/ppermute | solution.py:16
  32.2 19.0 %collective-permute-start.8 = (bf16[2,80,128]{2,1,0:T(8,128)(2,1)}, bf16[2,80,128]{2,1,0:T(8,128)(2,1)S(1)}, u32[]{:S(2)}, u32[]{:S(2)}) collective-permute-start(bf16[2,80,128]{2,1,0:T(8,128)(2,1)} %get-tuple-element.62), channel_id=1, source_target_pairs={{0,6},{2,0},{4,2},{6,4},{1,7},{3,1},{5,3},{7,5},{8,14},{10,8},{12,... | collective-permute-start | bytes 122888 | tf_op jit(solution)/shard_map/ppermute | solution.py:16
  37.6 7.9 %collective-permute-start.17 = (bf16[4,320,360]{2,1,0:T(8,128)(2,1)}, bf16[4,320,360]{2,1,0:T(8,128)(2,1)}, u32[]{:S(2)}, u32[]{:S(2)}) collective-permute-start(bf16[4,320,360]{2,1,0:T(8,128)(2,1)} %copy.22), channel_id=1, source_target_pairs={{0,1},{1,0},{2,3},{3,2},{4,5},{5,4},{6,7},{7,6},{8,9},{9,8},{10,11... | collective-permute-start | bytes 2764808 | tf_op jit(solution)/shard_map/ppermute | solution.py:16
  41.7 11.3 %copy-start.24 = (bf16[1,4,320,360]{2,3,1,0:T(8,128)(2,1)S(1)}, bf16[1,4,320,360]{2,3,1,0:T(8,128)(2,1)}, u32[]{:S(2)}) copy-start(bf16[1,4,320,360]{2,3,1,0:T(8,128)(2,1)} %get-tuple-element.55) | copy-start | bytes 2764804
  41.7 14.9 %collective-permute-start.9 = (bf16[2,80,128]{2,1,0:T(8,128)(2,1)}, bf16[2,80,128]{2,1,0:T(8,128)(2,1)S(1)}, u32[]{:S(2)}, u32[]{:S(2)}) collective-permute-start(bf16[2,80,128]{2,1,0:T(8,128)(2,1)} %get-tuple-element.61), channel_id=1, source_target_pairs={{0,4},{2,6},{4,0},{6,2},{1,5},{3,7},{5,1},{7,3},{8,12},{10,14},{12... | collective-permute-start | bytes 122888 | tf_op jit(solution)/shard_map/ppermute | solution.py:16
  42.8 43.1 %collective-permute-start = (bf16[16,80,128]{2,1,0:T(8,128)(2,1)}, bf16[16,80,128]{2,1,0:T(8,128)(2,1)S(1)}, u32[]{:S(2)}, u32[]{:S(2)}) collective-permute-start(bf16[16,80,128]{2,1,0:T(8,128)(2,1)} %get-tuple-element.48), channel_id=1, source_target_pairs={{0,6},{2,0},{4,2},{6,4},{1,7},{3,1},{5,3},{7,5},{8,14},{10,8},{12,... | collective-permute-start | bytes 983048 | tf_op jit(solution)/shard_map/ppermute | solution.py:16
  45.5 41.6 %collective-permute-start.1 = (bf16[16,80,128]{2,1,0:T(8,128)(2,1)}, bf16[16,80,128]{2,1,0:T(8,128)(2,1)S(1)}, u32[]{:S(2)}, u32[]{:S(2)}) collective-permute-start(bf16[16,80,128]{2,1,0:T(8,128)(2,1)} %get-tuple-element.47), channel_id=1, source_target_pairs={{0,4},{2,6},{4,0},{6,2},{1,5},{3,7},{5,1},{7,3},{8,12},{10,14},{12... | collective-permute-start | bytes 983048 | tf_op jit(solution)/shard_map/ppermute | solution.py:16
  49.2 38.7 %collective-permute-start.2 = (bf16[16,80,128]{2,1,0:T(8,128)(2,1)}, bf16[16,80,128]{2,1,0:T(8,128)(2,1)}, u32[]{:S(2)}, u32[]{:S(2)}) collective-permute-start(bf16[16,80,128]{2,1,0:T(8,128)(2,1)} %get-tuple-element.46), channel_id=1, source_target_pairs={{0,2},{2,4},{4,6},{6,0},{1,3},{3,5},{5,7},{7,1},{8,10},{10,12},{12... | collective-permute-start | bytes 983048 | tf_op jit(solution)/shard_map/ppermute | solution.py:16
  51.2 5.4 %copy-start.13 = (bf16[2,80,128]{2,1,0:T(8,128)(2,1)}, bf16[2,80,128]{2,1,0:T(8,128)(2,1)S(1)}, u32[]{:S(2)}) copy-start(bf16[2,80,128]{2,1,0:T(8,128)(2,1)S(1)} %collective-permute-done.8.refs_9_.refs_5_) | copy-start | bytes 122884
  51.2 15.9 %collective-permute-start.5 = (bf16[2,80,128]{2,1,0:T(8,128)(2,1)S(1)}, bf16[2,80,128]{2,1,0:T(8,128)(2,1)S(1)}, u32[]{:S(2)}, u32[]{:S(2)}) collective-permute-start(bf16[2,80,128]{2,1,0:T(8,128)(2,1)S(1)} %get-tuple-element.66), channel_id=1, source_target_pairs={{0,6},{2,0},{4,2},{6,4},{1,7},{3,1},{5,3},{7,5},{8,14},{10,8},{12,... | collective-permute-start | bytes 122888 | tf_op jit(solution)/shard_map/ppermute | solution.py:16
  56.6 22.9 %copy-start.16 = (bf16[2,80,128]{2,1,0:T(8,128)(2,1)}, bf16[2,80,128]{2,1,0:T(8,128)(2,1)S(1)}, u32[]{:S(2)}) copy-start(bf16[2,80,128]{2,1,0:T(8,128)(2,1)S(1)} %collective-permute-done.9.refs_10_.refs_6_) | copy-start | bytes 122884
  56.6 27.7 %collective-permute-start.6 = (bf16[2,80,128]{2,1,0:T(8,128)(2,1)}, bf16[2,80,128]{2,1,0:T(8,128)(2,1)}, u32[]{:S(2)}, u32[]{:S(2)}) collective-permute-start(bf16[2,80,128]{2,1,0:T(8,128)(2,1)} %get-tuple-element.65), channel_id=1, source_target_pairs={{0,4},{2,6},{4,0},{6,2},{1,5},{3,7},{5,1},{7,3},{8,12},{10,14},{12... | collective-permute-start | bytes 122888 | tf_op jit(solution)/shard_map/ppermute | solution.py:16
  67.1 12.4 %copy-start.19 = (bf16[2,80,128]{2,1,0:T(8,128)(2,1)}, bf16[2,80,128]{2,1,0:T(8,128)(2,1)S(1)}, u32[]{:S(2)}) copy-start(bf16[2,80,128]{2,1,0:T(8,128)(2,1)S(1)} %collective-permute-done.5.refs_5_) | copy-start | bytes 122884
  67.1 17.3 %collective-permute-start.7 = (bf16[2,80,128]{2,1,0:T(8,128)(2,1)}, bf16[2,80,128]{2,1,0:T(8,128)(2,1)}, u32[]{:S(2)}, u32[]{:S(2)}) collective-permute-start(bf16[2,80,128]{2,1,0:T(8,128)(2,1)} %get-tuple-element.64), channel_id=1, source_target_pairs={{0,2},{2,4},{4,6},{6,0},{1,3},{3,5},{5,7},{7,1},{8,10},{10,12},{12... | collective-permute-start | bytes 122888 | tf_op jit(solution)/shard_map/ppermute | solution.py:16
  79.5 2.1 copy-start.23
  84.3 16.9 %collective-permute-start.21 = (bf16[14,80,128]{2,1,0:T(8,128)(2,1)}, bf16[14,80,128]{2,1,0:T(8,128)(2,1)S(1)}, u32[]{:S(2)}, u32[]{:S(2)}) collective-permute-start(bf16[14,80,128]{2,1,0:T(8,128)(2,1)} %get-tuple-element.52), channel_id=1, source_target_pairs={{0,6},{2,0},{4,2},{6,4},{1,7},{3,1},{5,3},{7,5},{8,14},{10,8},{12,... | collective-permute-start | bytes 860168 | tf_op jit(solution)/shard_map/ppermute | solution.py:16
  84.4 26.2 %collective-permute-start.22 = (bf16[14,80,128]{2,1,0:T(8,128)(2,1)}, bf16[14,80,128]{2,1,0:T(8,128)(2,1)S(1)}, u32[]{:S(2)}, u32[]{:S(2)}) collective-permute-start(bf16[14,80,128]{2,1,0:T(8,128)(2,1)} %get-tuple-element.51), channel_id=1, source_target_pairs={{0,4},{2,6},{4,0},{6,2},{1,5},{3,7},{5,1},{7,3},{8,12},{10,14},{12... | collective-permute-start | bytes 860168 | tf_op jit(solution)/shard_map/ppermute | solution.py:16
  85.9 0.7 copy-start.4
  86.6 24.0 %collective-permute-start.23 = (bf16[14,80,128]{2,1,0:T(8,128)(2,1)}, bf16[14,80,128]{2,1,0:T(8,128)(2,1)S(1)}, u32[]{:S(2)}, u32[]{:S(2)}) collective-permute-start(bf16[14,80,128]{2,1,0:T(8,128)(2,1)} %get-tuple-element.50), channel_id=1, source_target_pairs={{0,2},{2,4},{4,6},{6,0},{1,3},{3,5},{5,7},{7,1},{8,10},{10,12},{12... | collective-permute-start | bytes 860168 | tf_op jit(solution)/shard_map/ppermute | solution.py:16
  87.2 0.7 copy-start.6
  87.9 1.0 copy-start.5
  88.9 1.0 copy-start.7
  89.8 0.8 copy-start.14
  90.6 0.8 copy-start.17
  91.4 0.8 copy-start.20
  92.2 18.5 %copy-start.15 = (bf16[2,80,128]{2,1,0:T(8,128)(2,1)S(1)}, bf16[2,80,128]{2,1,0:T(8,128)(2,1)}, u32[]{:S(2)}) copy-start(bf16[2,80,128]{2,1,0:T(8,128)(2,1)} %copy-done.13) | copy-start | bytes 122884
  92.2 18.5 %copy-start.18 = (bf16[2,80,128]{2,1,0:T(8,128)(2,1)S(1)}, bf16[2,80,128]{2,1,0:T(8,128)(2,1)}, u32[]{:S(2)}) copy-start(bf16[2,80,128]{2,1,0:T(8,128)(2,1)} %copy-done.16) | copy-start | bytes 122884
  100.6 0.6 copy-start.8
  101.3 9.3 %copy-start.2 = (bf16[16,80,128]{2,1,0:T(8,128)(2,1)}, bf16[16,80,128]{2,1,0:T(8,128)(2,1)S(1)}, u32[]{:S(2)}) copy-start(bf16[16,80,128]{2,1,0:T(8,128)(2,1)S(1)} %get-tuple-element.22) | copy-start | bytes 983044
  101.3 9.3 %copy-start.3 = (bf16[16,80,128]{2,1,0:T(8,128)(2,1)}, bf16[16,80,128]{2,1,0:T(8,128)(2,1)S(1)}, u32[]{:S(2)}) copy-start(bf16[16,80,128]{2,1,0:T(8,128)(2,1)S(1)} %get-tuple-element.21) | copy-start | bytes 983044
  101.3 9.3 %copy-start.10 = (bf16[1,320,128]{2,1,0:T(8,128)(2,1)}, bf16[1,320,128]{2,1,0:T(8,128)(2,1)S(1)}, u32[]{:S(2)}) copy-start(bf16[1,320,128]{2,1,0:T(8,128)(2,1)S(1)} %get-tuple-element.28) | copy-start | bytes 245764
  110.7 12.3 %copy-start.9 = (bf16[1,320,128]{2,1,0:T(8,128)(2,1)S(1)}, bf16[1,320,128]{2,1,0:T(8,128)(2,1)}, u32[]{:S(2)}) copy-start(bf16[1,320,128]{2,1,0:T(8,128)(2,1)} %copy-done.8) | copy-start | bytes 245764
  120.0 1.2 copy-start.21
  121.2 40.7 %collective-permute-start.29 = (f32[9,4,40,320]{3,2,1,0:T(8,128)}, f32[9,4,40,320]{3,2,1,0:T(8,128)}, u32[]{:S(2)}, u32[]{:S(2)}) collective-permute-start(f32[9,4,40,320]{3,2,1,0:T(8,128)} %get-tuple-element.36), channel_id=1, source_target_pairs={{0,1},{1,0},{2,3},{3,2},{4,5},{5,4},{6,7},{7,6},{8,9},{9,8},{10,11... | collective-permute-start | bytes 5529608 | tf_op jit(solution)/shard_map/ppermute | solution.py:16
  121.2 21.3 %collective-permute-start.24 = (bf16[1,320,128]{2,1,0:T(8,128)(2,1)}, bf16[1,320,128]{2,1,0:T(8,128)(2,1)S(1)}, u32[]{:S(2)}, u32[]{:S(2)}) collective-permute-start(bf16[1,320,128]{2,1,0:T(8,128)(2,1)} %copy-done.10), channel_id=1, source_target_pairs={{0,2},{2,4},{4,6},{6,7},{7,5},{5,3},{3,1},{8,10},{10,12},{12,14},{... | collective-permute-start | bytes 245768 | tf_op jit(solution)/shard_map/ppermute | solution.py:380
  123.0 22.4 %collective-permute-start.25 = (bf16[1,320,128]{2,1,0:T(8,128)(2,1)S(1)}, bf16[1,320,128]{2,1,0:T(8,128)(2,1)S(1)}, u32[]{:S(2)}, u32[]{:S(2)}) collective-permute-start(bf16[1,320,128]{2,1,0:T(8,128)(2,1)S(1)} %copy-done.9), channel_id=1, source_target_pairs={{2,0},{4,2},{6,4},{7,6},{5,7},{3,5},{1,3},{10,8},{12,10},{14,12},{... | collective-permute-start | bytes 245768 | tf_op jit(solution)/shard_map/ppermute | solution.py:381
  124.3 34.0 %collective-permute-start.18 = (bf16[16,80,128]{2,1,0:T(8,128)(2,1)}, bf16[16,80,128]{2,1,0:T(8,128)(2,1)}, u32[]{:S(2)}, u32[]{:S(2)}) collective-permute-start(bf16[16,80,128]{2,1,0:T(8,128)(2,1)} %copy-done.3), channel_id=1, source_target_pairs={{0,2},{2,4},{4,6},{6,0},{1,3},{3,5},{5,7},{7,1},{8,10},{10,12},{12... | collective-permute-start | bytes 983048 | tf_op jit(solution)/shard_map/ppermute | solution.py:16
  127.6 32.6 %collective-permute-start.19 = (bf16[16,80,128]{2,1,0:T(8,128)(2,1)}, bf16[16,80,128]{2,1,0:T(8,128)(2,1)}, u32[]{:S(2)}, u32[]{:S(2)}) collective-permute-start(bf16[16,80,128]{2,1,0:T(8,128)(2,1)} %copy-done.2), channel_id=1, source_target_pairs={{0,4},{2,6},{4,0},{6,2},{1,5},{3,7},{5,1},{7,3},{8,12},{10,14},{12... | collective-permute-start | bytes 983048 | tf_op jit(solution)/shard_map/ppermute | solution.py:16
  142.6 22.5 %collective-permute-start.20 = (bf16[16,80,128]{2,1,0:T(8,128)(2,1)S(1)}, bf16[16,80,128]{2,1,0:T(8,128)(2,1)S(1)}, u32[]{:S(2)}, u32[]{:S(2)}) collective-permute-start(bf16[16,80,128]{2,1,0:T(8,128)(2,1)S(1)} %get-tuple-element.23), channel_id=1, source_target_pairs={{0,6},{2,0},{4,2},{6,4},{1,7},{3,1},{5,3},{7,5},{8,14},{10,8},{12,... | collective-permute-start | bytes 983048 | tf_op jit(solution)/shard_map/ppermute | solution.py:16
  146.1 1.5 copy-start.1
  147.6 0.9 copy-start.12
  148.5 1.3 copy-start.22
  157.3 12.5 %collective-permute-start.26 = (bf16[16,80,128]{2,1,0:T(8,128)(2,1)S(1)}, bf16[16,80,128]{2,1,0:T(8,128)(2,1)S(1)}, u32[]{:S(2)}, u32[]{:S(2)}) collective-permute-start(bf16[16,80,128]{2,1,0:T(8,128)(2,1)S(1)} %get-tuple-element.32), channel_id=1, source_target_pairs={{0,2},{2,4},{4,6},{6,0},{1,3},{3,5},{5,7},{7,1},{8,10},{10,12},{12... | collective-permute-start | bytes 983048 | tf_op jit(solution)/shard_map/ppermute | solution.py:16
  158.4 36.1 %collective-permute-start.27 = (bf16[16,80,128]{2,1,0:T(8,128)(2,1)S(1)}, bf16[16,80,128]{2,1,0:T(8,128)(2,1)S(1)}, u32[]{:S(2)}, u32[]{:S(2)}) collective-permute-start(bf16[16,80,128]{2,1,0:T(8,128)(2,1)S(1)} %get-tuple-element.33), channel_id=1, source_target_pairs={{0,4},{2,6},{4,0},{6,2},{1,5},{3,7},{5,1},{7,3},{8,12},{10,14},{12... | collective-permute-start | bytes 983048 | tf_op jit(solution)/shard_map/ppermute | solution.py:16
  164.0 15.5 %collective-permute-start.30 = (f32[9,40,320]{2,1,0:T(8,128)S(1)}, f32[9,40,320]{2,1,0:T(8,128)S(1)}, u32[]{:S(2)}, u32[]{:S(2)}) collective-permute-start(f32[9,40,320]{2,1,0:T(8,128)S(1)} %get-tuple-element.37), channel_id=1, source_target_pairs={{0,24},{8,0},{16,8},{24,16},{1,25},{9,1},{17,9},{25,17},{2,26},{10... | collective-permute-start | bytes 1382408 | tf_op jit(solution)/shard_map/ppermute | solution.py:16
  164.6 25.3 %collective-permute-start.31 = (f32[9,40,320]{2,1,0:T(8,128)S(1)}, f32[9,40,320]{2,1,0:T(8,128)S(1)}, u32[]{:S(2)}, u32[]{:S(2)}) collective-permute-start(f32[9,40,320]{2,1,0:T(8,128)S(1)} %get-tuple-element.39), channel_id=1, source_target_pairs={{0,16},{8,24},{16,0},{24,8},{1,17},{9,25},{17,1},{25,9},{2,18},{10... | collective-permute-start | bytes 1382408 | tf_op jit(solution)/shard_map/ppermute | solution.py:16
  165.1 24.8 %collective-permute-start.32 = (f32[9,40,320]{2,1,0:T(8,128)S(1)}, f32[9,40,320]{2,1,0:T(8,128)S(1)}, u32[]{:S(2)}, u32[]{:S(2)}) collective-permute-start(f32[9,40,320]{2,1,0:T(8,128)S(1)} %get-tuple-element.38), channel_id=1, source_target_pairs={{0,8},{8,16},{16,24},{24,0},{1,9},{9,17},{17,25},{25,1},{2,10},{10... | collective-permute-start | bytes 1382408 | tf_op jit(solution)/shard_map/ppermute | solution.py:16
  169.8 38.4 %collective-permute-start.28 = (bf16[16,80,128]{2,1,0:T(8,128)(2,1)S(1)}, bf16[16,80,128]{2,1,0:T(8,128)(2,1)S(1)}, u32[]{:S(2)}, u32[]{:S(2)}) collective-permute-start(bf16[16,80,128]{2,1,0:T(8,128)(2,1)S(1)} %get-tuple-element.34), channel_id=1, source_target_pairs={{0,6},{2,0},{4,2},{6,4},{1,7},{3,1},{5,3},{7,5},{8,14},{10,8},{12,... | collective-permute-start | bytes 983048 | tf_op jit(solution)/shard_map/ppermute | solution.py:16
  190.3 7.7 %collective-permute-start.33 = (f32[80,360]{0,1:T(8,128)S(1)}, f32[80,360]{0,1:T(8,128)S(1)}, u32[]{:S(2)}, u32[]{:S(2)}) collective-permute-start(f32[80,360]{0,1:T(8,128)S(1)} %bitcast.119), channel_id=1, source_target_pairs={{0,6},{2,0},{4,2},{6,4},{1,7},{3,1},{5,3},{7,5},{8,14},{10,8},{12,... | collective-permute-start | bytes 345608 | tf_op jit(solution)/shard_map/ppermute | solution.py:16
  192.9 15.1 %collective-permute-start.34 = (f32[80,360]{0,1:T(8,128)S(1)}, f32[80,360]{0,1:T(8,128)S(1)}, u32[]{:S(2)}, u32[]{:S(2)}) collective-permute-start(f32[80,360]{0,1:T(8,128)S(1)} %bitcast.118), channel_id=1, source_target_pairs={{0,4},{2,6},{4,0},{6,2},{1,5},{3,7},{5,1},{7,3},{8,12},{10,14},{12... | collective-permute-start | bytes 345608 | tf_op jit(solution)/shard_map/ppermute | solution.py:16
  194.4 13.6 %collective-permute-start.35 = (f32[80,360]{0,1:T(8,128)S(1)}, f32[80,360]{0,1:T(8,128)S(1)}, u32[]{:S(2)}, u32[]{:S(2)}) collective-permute-start(f32[80,360]{0,1:T(8,128)S(1)} %bitcast.117), channel_id=1, source_target_pairs={{0,2},{2,4},{4,6},{6,0},{1,3},{3,5},{5,7},{7,1},{8,10},{10,12},{12... | collective-permute-start | bytes 345608 | tf_op jit(solution)/shard_map/ppermute | solution.py:16
  208.1 1.5 collective-permute-start.36
  208.2 2.2 %copy-start.25 = (f32[1,64,80,128]{3,2,1,0:T(8,128)}, f32[1,64,80,128]{3,2,1,0:T(8,128)S(1)}, u32[]{:S(2)}) copy-start(f32[1,64,80,128]{3,2,1,0:T(8,128)S(1)} %convert_dynamic-update-slice_fusion) | copy-start | bytes 7864324
  (1 other events, 0.6 us)

commit v2 on v1

--- a/solution.py
+++ b/solution.py
@@ -8,7 +8,7 @@
 from jax.sharding import PartitionSpec as P
 
 
-VMEM_LIMIT = 36 * 1024 * 1024
+VMEM_LIMIT = 60 * 1024 * 1024
 
 
 def receive(block, axis, ahead):
@@ -27,6 +27,11 @@
 def rotated(array, start, axis):
     twice = jnp.concatenate([array, array], axis=axis)
     return lax.dynamic_slice_in_dim(twice, start, array.shape[axis], axis=axis)
+
+
+def stacking_base():
+    matched = lax.axis_size("dp") == lax.axis_size("chan")
+    return lax.axis_index("dp") if matched else jnp.int32(0)
 
 
 def columns_moved(block, step):
@@ -43,88 +48,116 @@
     depth, width = block.shape
     lanes = pl.ds(pl.multiple_of(row * width, width), width)
     wide = block.astype(jnp.float32)
-    stacked[pl.ds(channel, depth), lanes] = columns_moved(wide, -1).astype(block.dtype)
-    stacked[pl.ds(channels + channel, depth), lanes] = block
-    stacked[pl.ds(2 * channels + channel, depth), lanes] = columns_moved(wide, 1).astype(block.dtype)
-
-
-def taps(kernels, stacked, first, rows, width):
+
+    def below(copies):
+        start = copies * channels + channel
+        return pl.ds(start if isinstance(channel, int) else pl.multiple_of(start, 16), depth)
+
+    stacked[below(0), lanes] = columns_moved(wide, -1).astype(block.dtype)
+    stacked[below(1), lanes] = block
+    stacked[below(2), lanes] = columns_moved(wide, 1).astype(block.dtype)
+
+
+def window(stacked, tap_row, tap_col, channel, depth, first, rows, width, channels):
+    start = pl.multiple_of((first + tap_row) * width, width)
+    return stacked[tap_col * channels + channel : tap_col * channels + channel + depth, pl.ds(start, rows * width)]
+
+
+def forward_taps(halves, stacked, first, rows, width):
+    count = halves[0].shape[0]
+    depth = halves[0].shape[2] // 9
     total = None
-    for tap_row in range(3):
-        start = pl.multiple_of((first + tap_row) * width, width)
+    for block in range(count):
+        windows = [
+            window(stacked, a, b, block * depth, depth, first, rows, width, count * depth)
+            for a in range(3)
+            for b in range(3)
+        ]
         term = jnp.dot(
-            kernels[tap_row],
-            stacked[:, pl.ds(start, rows * width)],
+            jnp.concatenate([half[block] for half in halves]),
+            jnp.concatenate(windows),
             preferred_element_type=jnp.float32,
         )
         total = term if total is None else total + term
     return total
 
 
-def forward_body(count, rows, *refs):
-    pieces, rims, ends = (refs[k * count : (k + 1) * count] for k in range(3))
-    kernels = refs[3 * count]
-    outs = refs[3 * count + 1 : 4 * count + 1]
-    factor, stacked, first, last = refs[4 * count + 1 :]
+def forward_body(count, shares, rows, turns, *refs):
+    pieces, rims = refs[:count], refs[count : 2 * count]
+    halves = refs[2 * count : 2 * count + shares]
+    outs = refs[2 * count + shares : 3 * count + shares]
+    factor, stacked, first, last = refs[3 * count + shares :]
     height, depth, width = pieces[0].shape
     channels = count * depth
     step = pl.program_id(0)
 
     @pl.when(step == 0)
     def _():
+        slots = [lax.rem(turns[0] + j, count) * depth for j in range(count)]
         for j in range(count):
-            place(stacked, j * depth, 0, rims[j][0], channels)
-            place(stacked, j * depth, height + 1, rims[j][1], channels)
+            place(stacked, slots[j], 0, rims[j][0], channels)
+            place(stacked, slots[j], height + 1, rims[j][1], channels)
 
         def body(row, carry):
             for j in range(count):
-                place(stacked, j * depth, row + 1, pieces[j][row], channels)
+                place(stacked, slots[j], row + 1, pieces[j][row], channels)
             return carry
 
         lax.fori_loop(0, height, body, 0)
 
-    pre = taps(kernels, stacked, step * rows, rows, width)
-    sigma = jax.nn.sigmoid(pre)
-    activated = (pre * sigma).astype(jnp.bfloat16)
-    slope = sigma * (1.0 + pre * (1.0 - sigma))
-    for row in range(rows):
-        lanes = slice(row * width, (row + 1) * width)
-        factor[row] = slope[:, lanes]
-        for j in range(count):
-            outs[j][row] = activated[j * depth : (j + 1) * depth, lanes]
+    mixed = forward_taps(halves, stacked, step * rows, rows, width)
+    size = depth // shares
+    for j in range(count):
+        parts = []
+        for share in range(shares):
+            chosen = None
+            for at in range(shares):
+                start = at * count * size + j * size
+                value = mixed[start : start + size]
+                here = turns[1] == (share - at) % shares
+                chosen = value if chosen is None else jnp.where(here, value, chosen)
+            parts.append(chosen)
+        pre = jnp.concatenate(parts) if shares > 1 else parts[0]
+        sigma = jax.nn.sigmoid(pre)
+        activated = (pre * sigma).astype(jnp.bfloat16)
+        slope = sigma * (1.0 + pre * (1.0 - sigma))
+        for row in range(rows):
+            lanes = slice(row * width, (row + 1) * width)
+            factor[row, j * depth : (j + 1) * depth, :] = slope[:, lanes]
+            outs[j][row] = activated[:, lanes]
 
     def end(out, side, row):
         for j in range(count):
             part_of = slice(j * depth, (j + 1) * depth)
-            value = ends[j][side].astype(jnp.float32) * factor[row, part_of, :]
+            value = rims[j][side].astype(jnp.float32) * factor[row, part_of, :]
             out[0, part_of, :] = value.astype(jnp.bfloat16)
 
     @pl.when(step == 0)
     def _():
-        end(first, 0, 0)
+        end(first, 2, 0)
 
     @pl.when(step == pl.num_programs(0) - 1)
     def _():
-        end(last, 1, rows - 1)
+        end(last, 3, rows - 1)
 
 
 def whole(shape):
     return pl.BlockSpec(shape, lambda *_: (0,) * len(shape), pipeline_mode=pl.Buffered(1))
 
 
-def forward(pieces, rims, ends, kernels):
+def forward(turns, pieces, rims, halves):
     count = len(pieces)
     height, depth, width = pieces[0].shape
     channels = count * depth
     rows = 4 if height % 4 == 0 else 1
     flops = 2 * 9 * channels * channels * height * width
     call = pl.pallas_call(
-        functools.partial(forward_body, count, rows),
+        functools.partial(forward_body, count, len(halves), rows),
         grid=(height // rows,),
-        in_specs=[whole(pieces[0].shape)] * count
+        in_specs=[pl.BlockSpec(memory_space=pltpu.SMEM)]
+        + [whole(pieces[0].shape)] * count
         + [whole(rims[0].shape)] * count
-        + [whole(ends[0].shape)] * count
-        + [whole(kernels.shape)],
+        + [whole(halves[0].shape)] * len(halves),
         out_specs=[pl.BlockSpec((rows, depth, width), lambda g: (g, 0, 0))] * count
         + [
             pl.BlockSpec((rows, channels, width), lambda g: (g, 0, 0)),
@@ -145,7 +178,7 @@
         ),
         name="conv_forward",
     )
-    results = call(*pieces, *rims, *ends, kernels)
+    results = call(turns, *pieces, *rims, *halves)
     return results[:count], *results[count:]
 
 
@@ -169,9 +202,9 @@
             put(row + 1, [piece[row] for piece in pieces])
             return carry
 
-        put(0, [end[0] for end in ends])
+        put(0, [end[2] for end in ends])
         lax.fori_loop(0, height - 2, body, 0)
-        put(height - 1, [end[1] for end in ends])
+        put(height - 1, [end[3] for end in ends])
 
     source = stacked[
         pl.ds(pl.multiple_of(tap_col * channels, channels), channels),
@@ -188,7 +221,7 @@
             for j in range(rows):
                 for group in range(groups):
                     start = (group * rows + (own - j) % rows) * size
-                    shares[j][0, group] = grads[start : start + size]
+                    shares[j][group, 0] = grads[start : start + size]
 
 
 def correlate(stacked, factor, pieces, ends):
@@ -204,10 +237,10 @@
         + [whole(stacked.shape), whole(factor.shape)]
         + [whole(pieces[0].shape)] * count
         + [whole(ends[0].shape)] * count,
-        out_specs=[pl.BlockSpec((1, groups, size, channels), lambda a, b: (3 * a + b, 0, 0, 0))]
+        out_specs=[pl.BlockSpec((groups, 1, size, channels), lambda a, b: (0, 3 * a + b, 0, 0))]
         * rows
         + [whole((channels, height * width))],
-        out_shape=[jax.ShapeDtypeStruct((9, groups, size, channels), jnp.float32)] * rows
+        out_shape=[jax.ShapeDtypeStruct((groups, 9, size, channels), jnp.float32)] * rows
         + [jax.ShapeDtypeStruct((channels, height * width), jnp.bfloat16)],
         compiler_params=pltpu.CompilerParams(vmem_limit_bytes=VMEM_LIMIT),
         cost_estimate=pl.CostEstimate(
@@ -243,7 +276,14 @@
 
         lax.fori_loop(0, height, body, 0)
 
-    grad = taps(kernels, stacked, step * rows, rows, width)
+    windows = [
+        window(stacked, tap_row, 0, 0, 3 * channels, step * rows, rows, width, channels)
+        for tap_row in range(3)
+    ]
+    order = [kernels[lax.rem(turns[2] + j, count)] for j in range(count)]
+    grad = jnp.dot(
+        jnp.concatenate(order), jnp.concatenate(windows), preferred_element_type=jnp.float32
+    )
     for row in range(rows):
         lanes = slice(row * width, (row + 1) * width)
         for j in range(count):
@@ -282,35 +322,34 @@
 
 
 def gathered_kernel(kernel):
-    dp, chan, row = (lax.axis_index(a) for a in ("dp", "chan", "row"))
+    dp, row = lax.axis_index("dp"), lax.axis_index("row")
     dps, chans, rows = (lax.axis_size(a) for a in ("dp", "chan", "row"))
     _, inner, outer = kernel.shape
-    share = inner // rows
-    mine = part(kernel, row, share, 1)
-    mine = jnp.transpose(mine, (2, 0, 1)).reshape(outer, 9 * share)
+    size = outer // rows
+    mine = part(kernel, row, size, 2)
+    mine = jnp.transpose(mine, (2, 0, 1)).reshape(size, 9 * inner)
     over_chan = jnp.concatenate([mine] + [receive(mine, "chan", j) for j in range(1, chans)], axis=0)
     over_dp = jnp.stack([over_chan] + [receive(over_chan, "dp", j) for j in range(1, dps)])
-    over_row = jnp.stack([over_dp] + [receive(over_dp, "row", j) for j in range(1, rows)])
-    placed = rotated(over_row, (rows - row) % rows, 0)
-    placed = rotated(placed, (chan * (dps // chans) - dp) % dps, 1)
-    channels = chans * outer
-    taps_of = placed.reshape(rows, dps, channels, 3, 3, share)
-    return taps_of
-
-
-def ahead_order(taps_of):
-    channels = taps_of.shape[2]
-    return jnp.transpose(taps_of, (3, 2, 4, 1, 0, 5)).reshape(3, channels, 3 * channels)
-
-
-def back_order(taps_of):
-    channels = taps_of.shape[2]
-    flipped = taps_of[:, :, :, ::-1, ::-1]
-    return jnp.transpose(flipped, (3, 1, 0, 5, 4, 2)).reshape(3, channels, 3 * channels)
+    if dps != chans:
+        each = dps // chans
+        over_dp = rotated(over_dp, (dps - dp) % dps, 0)
+        over_dp = over_dp.reshape(chans, each, chans * size, 9, inner)
+        over_dp = jnp.transpose(over_dp, (0, 2, 3, 1, 4)).reshape(chans, chans * size, 9 * each * inner)
+    return [over_dp] + [receive(over_dp, "row", j) for j in range(1, rows)]
+
+
+def back_order(halves):
+    row, rows = lax.axis_index("row"), lax.axis_size("row")
+    chans = lax.axis_size("chan")
+    both = rotated(jnp.stack(halves), (rows - row) % rows, 0)
+    _, blocks, outs, depth = both.shape
+    inner = depth // 9
+    both = both.reshape(rows, blocks, chans, outs // chans, 9, inner)[:, :, :, :, ::-1]
+    return jnp.transpose(both, (1, 5, 4, 2, 0, 3)).reshape(blocks, inner, 9 * outs * rows)
 
 
 def summed_kernel_grad(shares, inner, outer):
-    dp, chan, row = (lax.axis_index(a) for a in ("dp", "chan", "row"))
+    dp, row = lax.axis_index("dp"), lax.axis_index("row")
     dps, chans, rows = (lax.axis_size(a) for a in ("dp", "chan", "row"))
     channels = shares[0].shape[3]
     share = inner // rows
@@ -318,13 +357,14 @@
     for j in range(1, rows):
         halves = halves + receive(shares[j], "row", j)
 
-    def of_dp(d):
-        at = (d - chan * (dps // chans)) % dps
-        return lax.dynamic_index_in_dim(halves, at, 1, keepdims=False)
-
-    total = of_dp(dp)
+    def of_dp(ahead):
+        if dps == chans:
+            return halves[ahead % dps]
+        return lax.dynamic_index_in_dim(halves, (dp + ahead) % dps, 0, keepdims=False)
+
+    total = of_dp(0)
     for j in range(1, dps):
-        total = total + receive(of_dp((dp - j) % dps), "dp", j)
+        total = total + receive(of_dp(-j), "dp", j)
     total = jnp.transpose(total, (2, 0, 1)).reshape(channels, 9 * share)
     own = total[:outer]
     for j in range(1, chans):
@@ -350,27 +390,50 @@
             receive(part(array, home(-j), size, 0), "chan", j) for j in range(1, chans)
         ]
 
-    taps_of = gathered_kernel(kernel)
+    halves = gathered_kernel(kernel)
     pieces = to_homes(images, height)
-    down = [(i, i + 1) for i in range(rows - 1)]
-    up = [(i + 1, i) for i in range(rows - 1)]
-    low = lax.ppermute(images[slab - 1 :], "row", down)
-    high = lax.ppermute(images[:1], "row", up)
-    tops = jnp.concatenate([low, images[height - 1 : slab - 1 : height]])
-    bottoms = jnp.concatenate([images[height::height], high])
-    rims = jnp.stack([tops, bottoms], axis=1).reshape(2 * chans, depth, width)
-    rims = to_homes(rims, 2)
-    firsts, lasts = cotangent[::height], cotangent[height - 1 :: height]
-    ends = jnp.stack([firsts, lasts], axis=1).reshape(2 * chans, depth, width)
-    ends = to_homes(ends, 2)
-    inside = cotangent.reshape(chans, height, depth, width)[:, 1:-1]
-    inside = inside.reshape(slab - 2 * chans, depth, width)
-    cotangents = to_homes(inside, height - 2)
-
-    results = forward(pieces, rims, ends, ahead_order(taps_of))
+    if rows == 2:
+        edge = jnp.where(row == 0, images[slab - 1 :], images[:1])
+        edge = receive(edge, "row", 1)
+        low = jnp.where(row == 0, jnp.zeros_like(edge), edge)
+        high = jnp.where(row == 0, edge, jnp.zeros_like(edge))
+    else:
+        low = lax.ppermute(images[slab - 1 :], "row", [(i, i + 1) for i in range(rows - 1)])
+        high = lax.ppermute(images[:1], "row", [(i + 1, i) for i in range(rows - 1)])
+
+    def rim_of(at):
+        begin = at * height
+        above = part(images, jnp.maximum(begin - 1, 0), 1, 0)
+        below = part(images, jnp.minimum(begin + height, slab - 1), 1, 0)
+        return jnp.concatenate(
+            [
+                jnp.where(at == 0, low, above),
+                jnp.where(at == chans - 1, high, below),
+                part(cotangent, begin, 1, 0),
+                part(cotangent, begin + height - 1, 1, 0),
+            ]
+        )
+
+    rims = [rim_of(home(0))]
+    rims += [receive(rim_of(home(-j)), "chan", j) for j in range(1, chans)]
+
+    def inside(ahead):
+        return lax.dynamic_slice_in_dim(cotangent, home(ahead) * height + 1, height - 2, 0)
+
+    cotangents = [inside(0)] + [receive(inside(-j), "chan", j) for j in range(1, chans)]
+
+    shift = (chan - stacking_base()) % chans
+    place_at = home(0)
+    forth = jnp.where(row % 2 == 0, 1, chans - 1)
+    above_turn = jnp.where(place_at == 0, 0, forth)
+    below_turn = jnp.where(place_at == chans - 1, 0, chans - forth)
+    turns = jnp.stack([shift, row]).astype(jnp.int32)
+    back_turns = jnp.stack([above_turn, below_turn, shift]).astype(jnp.int32)
+
+    results = forward(turns, pieces, rims, halves)
     activated, factor, stacked, first, last = results
-    taps_of, factor = lax.optimization_barrier((taps_of, factor))
-    back_kernel = back_order(taps_of)
+    halves, factor = lax.optimization_barrier((halves, factor))
+    back_kernel = back_order(halves)
 
     def snake(place_at):
         r, k = place_at // chans, place_at % chans
@@ -380,16 +443,8 @@
     above = lax.ppermute(last, ("chan", "row"), line)
     below = lax.ppermute(first, ("chan", "row"), [(b, a) for a, b in line])
 
-    place_at = home(0)
-    forth = jnp.where(row % 2 == 0, 1, chans - 1)
-    turns = jnp.stack(
-        [
-            jnp.where(place_at == 0, 0, forth),
-            jnp.where(place_at == chans - 1, 0, chans - forth),
-        ]
-    ).astype(jnp.int32)
-    grads, slope = correlate(stacked, factor, cotangents, ends)
-    input_grads = backward(turns, slope, above, below, back_kernel, chans)
+    grads, slope = correlate(stacked, factor, cotangents, rims)
+    input_grads = backward(back_turns, slope, above, below, back_kernel, chans)
     kernel_grad = summed_kernel_grad(grads, kernel.shape[1], kernel.shape[2])
 
     def to_owners(blocks, dtype):

time: 212 us -> 213 us (level)
  Pallas kernels: 25.2 us -> 35.5 us
  local copies, waits for them, and re-layouts: 48.2 us -> 40.8 us
  starting transfers between devices: 55.3 us -> 51 us
  waiting for transfers between devices: 69.3 us -> 72.1 us
    rev x0 -> x1, local copies, waits for them, and re-layouts: none -> 13.8 us  [back_order(): both.reshape(rows, blocks, chans, outs // chans, 9, inner)[:, :, :, :, ::-1]]
    unnamed x56 -> x40, local copies, waits for them, and re-layouts: 13.1 us -> 3.35 us
    pallas_call x1, Pallas kernels: 9.34 us -> 13.6 us  [correlate(): results = call(turn, stacked, factor, *pieces, *ends)]
    pallas_call x1, Pallas kernels: 8.45 us -> 12.3 us  [forward(): results = call(turns, *pieces, *rims, *halves)]
    transpose x3 -> x1, local copies, waits for them, and re-layouts: 6.52 us -> 3.29 us  [back_order(): jnp.transpose(both, (1, 5, 4, 2, 0, 3))]
    ppermute x2 -> x0, starting transfers between devices: 3.16 us -> none  [the longest x1 1.88 us: shards(): low = lax.ppermute(images[slab - 1:], 'row', down)]
    ppermute x33 -> x31, starting transfers between devices: 49.1 us -> 46 us  [receive(): lax.ppermute(block, axis, [(i, (i - ahead) % count) for i in range(count)])]
    ppermute x33 -> x31, waiting for transfers between devices: 69.2 us -> 72.1 us  [receive(): lax.ppermute(block, axis, [(i, (i - ahead) % count) for i in range(count)])]
  transfers between devices with their start and end apart: 37 -> 33, of which waited for: 11 -> 15; matrix products, arithmetic and copies ran while one was open for 22% -> 22% of each run, Pallas kernels for 8% -> 10%
where the time goes in v2:
time: 213 us; the launch traced here: 211 us
  waiting for transfers between devices  72.1 us (34%)
  starting transfers between devices  51 us (24%)
  local copies, waits for them, and re-layouts  40.8 us (19%)
  Pallas kernels  35.5 us (17%)
  other arithmetic  11 us (5%)
    ppermute x31, waiting for transfers between devices, receive(): lax.ppermute(block, axis, [(i, (i - ahead) % count) for i in range(count)])  72.1 us
    ppermute x31, starting transfers between devices, receive(): lax.ppermute(block, axis, [(i, (i - ahead) % count) for i in range(count)])  46 us
    rev x1, local copies, waits for them, and re-layouts, back_order(): both.reshape(rows, blocks, chans, outs // chans, 9, inner)[:, :, :, :, ::-1]  13.8 us
    pallas_call x1, Pallas kernels, correlate(): results = call(turn, stacked, factor, *pieces, *ends)  13.6 us
    pallas_call x1, Pallas kernels, forward(): results = call(turns, *pieces, *rims, *halves)  12.3 us
    pallas_call x1, Pallas kernels, backward(): pl.pallas_call(functools.partial(backward_body, count, rows), grid=(heigh...  9.64 us
    reshape x1, local copies, waits for them, and re-layouts, back_order(): both.reshape(rows, blocks, chans, outs // chans, 9, inner)[:, :, :, :, ::-1]  6.81 us
  transfers between devices with their start and end apart: 33, of which 15 were waited for; matrix products, arithmetic and copies ran while one was open for 22% of the time, Pallas kernels for 10%

profile of v2, /device:TPU:0, one launch (start us, length us, event | category | flops | bytes accessed | tf_op | source)
XLA Modules:
  0.0 211.4 jit_solution(10111288989920344991)
XLA Ops:
  0.7 0.9 copy-done
  1.8 5.1 %collective-permute-start.7 = (bf16[40,720]{1,0:T(8,128)(2,1)S(1)}, bf16[40,720]{1,0:T(8,128)(2,1)S(1)}, u32[]{:S(2)}, u32[]{:S(2)}) collective-permute-start(bf16[40,720]{1,0:T(8,128)(2,1)S(1)} %copy.14), channel_id=1, source_target_pairs={{0,6},{2,0},{4,2},{6,4},{1,7},{3,1},{5,3},{7,5},{8,14},{10,8},{12,... | collective-permute-start | bytes 172808 | tf_op jit(solution)/shard_map/ppermute | solution.py:16
  6.9 1.0 collective-permute-start.9
  7.9 1.4 collective-permute-done.7
  9.3 3.1 %collective-permute-done.8 = bf16[40,720]{1,0:T(8,128)(2,1)S(1)} collective-permute-done((bf16[40,720]{1,0:T(8,128)(2,1)S(1)}, bf16[40,720]{1,0:T(8,128)(2,1)S(1)}, u32[]{:S(2)}, u32[]{:S(2)}) %collective-permute-start.8) | collective-permute-done | bytes 57632 | tf_op jit(solution)/shard_map/ppermute | solution.py:16
  12.4 0.6 collective-permute-done.9
  13.1 2.5 %collective-permute-start.10 = (bf16[160,720]{1,0:T(8,128)(2,1)S(1)}, bf16[160,720]{1,0:T(8,128)(2,1)S(1)}, u32[]{:S(2)}, u32[]{:S(2)}) collective-permute-start(bf16[160,720]{1,0:T(8,128)(2,1)S(1)} %get-tuple-element.71), channel_id=1, source_target_pairs={{0,24},{8,0},{16,8},{24,16},{1,25},{9,1},{17,9},{25,17},{2,26},{10... | collective-permute-start | bytes 691208 | tf_op jit(solution)/shard_map/ppermute | solution.py:16
  15.6 0.5 collective-permute-start.11
  16.1 0.6 collective-permute-start.12
  16.7 1.4 select_bitcast_fusion
  18.0 0.9 dynamic-slice_bitcast_fusion
  19.0 2.0 collective-permute-start
  21.0 1.0 collective-permute-done.10
  21.9 1.9 collective-permute-start.1
  23.8 3.6 %collective-permute-done.11 = bf16[160,720]{1,0:T(8,128)(2,1)S(1)} collective-permute-done((bf16[160,720]{1,0:T(8,128)(2,1)S(1)}, bf16[160,720]{1,0:T(8,128)(2,1)S(1)}, u32[]{:S(2)}, u32[]{:S(2)}) %collective-permute-start.11) | collective-permute-done | bytes 230432 | tf_op jit(solution)/shard_map/ppermute | solution.py:16
  28.6 1.3 pad_maximum_fusion.refs_8_
  30.0 2.5 %dynamic-slice_bitcast_fusion.4 = (bf16[14,80,128]{2,1,0:T(8,128)(2,1)}, bf16[14,80,128]{2,1,0:T(8,128)(2,1)}, bf16[14,80,128]{2,1,0:T(8,128)(2,1)}, bf16[14,80,128]{2,1,0:T(8,128)(2,1)}) fusion(bf16[1,64,80,128]{3,2,1,0:T(8,128)(2,1)} %param.5, s32[]{:T(128)S(6)} %select_n.348, s32[]{:T(128)S(6)} %select_n.346, s32[]{:T(128)S(6)} %select_n.345, ...), kind=kLoop, calls=%fused_computation.35 | loop fusion | bytes 2293776 | tf_op jit(solution)/shard_map/dynamic_slice | solution.py:421
  32.5 0.9 dynamic-slice_bitcast_fusion.9
  33.3 0.6 pad_add_fusion.turns
  33.9 0.7 bitcast_select_fusion.1
  34.7 2.5 %collective-permute-start.6 = (bf16[4,80,128]{2,1,0:T(8,128)(2,1)S(1)}, bf16[4,80,128]{2,1,0:T(8,128)(2,1)S(1)}, u32[]{:S(2)}, u32[]{:S(2)}) collective-permute-start(bf16[4,80,128]{2,1,0:T(8,128)(2,1)S(1)} %pad_maximum_fusion.5), channel_id=1, source_target_pairs={{0,2},{2,4},{4,6},{6,0},{1,3},{3,5},{5,7},{7,1},{8,10},{10,12},{12... | collective-permute-start | bytes 245768 | tf_op jit(solution)/shard_map/ppermute | solution.py:16
  37.3 9.2 %collective-permute-done.6.refs_7_ = bf16[4,80,128]{2,1,0:T(8,128)(2,1)S(1)} collective-permute-done((bf16[4,80,128]{2,1,0:T(8,128)(2,1)S(1)}, bf16[4,80,128]{2,1,0:T(8,128)(2,1)S(1)}, u32[]{:S(2)}, u32[]{:S(2)}) %collective-permute-start.6) | collective-permute-done | bytes 81952 | tf_op jit(solution)/shard_map/ppermute | solution.py:16
  46.5 8.6 %collective-permute-start.5 = (bf16[4,80,128]{2,1,0:T(8,128)(2,1)S(1)}, bf16[4,80,128]{2,1,0:T(8,128)(2,1)S(1)}, u32[]{:S(2)}, u32[]{:S(2)}) collective-permute-start(bf16[4,80,128]{2,1,0:T(8,128)(2,1)S(1)} %pad_maximum_fusion.4), channel_id=1, source_target_pairs={{0,4},{2,6},{4,0},{6,2},{1,5},{3,7},{5,1},{7,3},{8,12},{10,14},{12... | collective-permute-start | bytes 245768 | tf_op jit(solution)/shard_map/ppermute | solution.py:16
  55.0 4.3 %collective-permute-done.5.refs_6_ = bf16[4,80,128]{2,1,0:T(8,128)(2,1)S(1)} collective-permute-done((bf16[4,80,128]{2,1,0:T(8,128)(2,1)S(1)}, bf16[4,80,128]{2,1,0:T(8,128)(2,1)S(1)}, u32[]{:S(2)}, u32[]{:S(2)}) %collective-permute-start.5) | collective-permute-done | bytes 81952 | tf_op jit(solution)/shard_map/ppermute | solution.py:16
  59.3 0.7 pad_maximum_fusion.2.refs_4_
  60.0 3.8 %collective-permute-done.4.refs_5_ = bf16[4,80,128]{2,1,0:T(8,128)(2,1)S(1)} collective-permute-done((bf16[4,80,128]{2,1,0:T(8,128)(2,1)S(1)}, bf16[4,80,128]{2,1,0:T(8,128)(2,1)S(1)}, u32[]{:S(2)}, u32[]{:S(2)}) %collective-permute-start.4) | collective-permute-done | bytes 81952 | tf_op jit(solution)/shard_map/ppermute | solution.py:16
  63.7 1.8 collective-permute-start.17
  65.6 1.2 collective-permute-start.19
  66.9 12.3 %conv_forward.1 = (bf16[16,80,128]{2,1,0:T(8,128)(2,1)}, bf16[16,80,128]{2,1,0:T(8,128)(2,1)}, bf16[16,80,128]{2,1,0:T(8,128)(2,1)}, bf16[16,80,128]{2,1,0:T(8,1...) custom-call(s32[2]{0:T(128)} %pad_add_fusion.turns, ...), custom_call_target="tpu_custom_call" | custom-call | flops 3774873600 | bytes 16777216 | tf_op jit(solution)/shard_map/conv_forward/pallas_call | solution.py:181
  79.2 10.0 %collective-permute-done.18.refs_2_ = bf16[14,80,128]{2,1,0:T(8,128)(2,1)S(1)} collective-permute-done((bf16[14,80,128]{2,1,0:T(8,128)(2,1)}, bf16[14,80,128]{2,1,0:T(8,128)(2,1)S(1)}, u32[]{:S(2)}, u32[]{:S(2)}) %collective-permute-start.18) | collective-permute-done | bytes 286752 | tf_op jit(solution)/shard_map/ppermute | solution.py:16
  89.2 0.7 copy-done.14
  90.0 13.6 %kernel_grad.1 = (f32[4,9,40,320]{3,2,1,0:T(8,128)}, f32[4,9,40,320]{3,2,1,0:T(8,128)}, bf16[320,2048]{1,0:T(8,128)(2,1)}) custom-call(s32[1]{0:T(128)} %bitcast.1.turn, bf16[960,2304]{1,0:T(8,128)(2,1)} %get-tuple-element.25.stacked, f32[16,320,128]{2,1,0:T(8,128)} %get-tuple-element.27.factor, bf16[14,80,128]{2,1,0:T(8,128)(2,1)} %get-tuple-element.52.refs_0_, ...), custom_call_target="tpu_custom_call" | custom-call | flops 3774873600 | bytes 14680064 | tf_op jit(solution)/shard_map/kernel_grad/pallas_call | solution.py:252
  103.7 0.7 pad_add_fusion.1.turns
  104.4 3.8 %collective-permute-start.20 = (bf16[1,320,128]{2,1,0:T(8,128)(2,1)}, bf16[1,320,128]{2,1,0:T(8,128)(2,1)}, u32[]{:S(2)}, u32[]{:S(2)}) collective-permute-start(bf16[1,320,128]{2,1,0:T(8,128)(2,1)} %get-tuple-element.29), channel_id=1, source_target_pairs={{0,2},{2,4},{4,6},{6,7},{7,5},{5,3},{3,1},{8,10},{10,12},{12,14},{... | collective-permute-start | bytes 245768 | tf_op jit(solution)/shard_map/ppermute | solution.py:443
  108.2 1.3 collective-permute-start.21
  109.5 2.7 %collective-permute-start.14 = (bf16[16,80,128]{2,1,0:T(8,128)(2,1)}, bf16[16,80,128]{2,1,0:T(8,128)(2,1)}, u32[]{:S(2)}, u32[]{:S(2)}) collective-permute-start(bf16[16,80,128]{2,1,0:T(8,128)(2,1)} %get-tuple-element.22), channel_id=1, source_target_pairs={{0,2},{2,4},{4,6},{6,0},{1,3},{3,5},{5,7},{7,1},{8,10},{10,12},{12... | collective-permute-start | bytes 983048 | tf_op jit(solution)/shard_map/ppermute | solution.py:16
  112.2 1.3 collective-permute-start.15
  113.4 3.1 %fusion.2 = bf16[2,4,160,720]{3,2,1,0:T(8,128)(2,1)S(1)} fusion(s32[]{:T(128)S(6)} %select_n.350, bf16[1,4,160,720]{3,2,1,0:T(8,128)(2,1)S(1)} %bitcast.122, bf16[1,4,160,720]{3,2,1,0:T(8,128)(2,1)} %bitcast.41), kind=kLoop, calls=%fused_computation.6 | loop fusion | flops 2764800 | bytes 3686404 | tf_op jit(solution)/shard_map/concatenate | solution.py:28
  116.5 1.2 broadcast_in_dim.31
  117.7 0.7 bitcast_dynamic-update-slice_fusion.4
  118.5 6.8 %reshape.94 = bf16[2,4,4,40,9,80]{5,4,3,2,1,0:T(8,128)(2,1)} reshape(bf16[2,4,160,720]{3,2,1,0:T(8,128)(2,1)S(1)} %fusion.2) | data formatting | bytes 3686400 | tf_op jit(solution)/shard_map/reshape | solution.py:347
  125.3 13.8 %rev.3 = bf16[2,4,4,40,9,80]{5,4,3,2,1,0:T(8,128)(2,1)} reverse(bf16[2,4,4,40,9,80]{5,4,3,2,1,0:T(8,128)(2,1)} %reshape.94), dimensions={4} | reverse | bytes 3686400 | tf_op jit(solution)/shard_map/rev | solution.py:347
  139.1 3.3 %copy.11 = bf16[4,80,9,4,2,40]{1,5,4,3,2,0:T(8,128)(2,1)S(1)} copy(bf16[4,80,9,4,2,40]{1,2,5,3,0,4:T(8,128)(2,1)} %bitcast.120) | data formatting | bytes 3686400 | tf_op jit(solution)/shard_map/transpose | solution.py:348
  142.4 2.5 %copy.12.kernels = bf16[4,80,2880]{2,1,0:T(8,128)(2,1)} copy(bf16[4,80,2880]{1,2,0:T(8,128)(2,1)S(1)} %bitcast.121) | data formatting | bytes 3686400 | tf_op jit(solution)/shard_map/reshape | solution.py:348
  144.9 2.8 %collective-permute-start.16 = (bf16[16,80,128]{2,1,0:T(8,128)(2,1)}, bf16[16,80,128]{2,1,0:T(8,128)(2,1)S(1)}, u32[]{:S(2)}, u32[]{:S(2)}) collective-permute-start(bf16[16,80,128]{2,1,0:T(8,128)(2,1)} %get-tuple-element.24), channel_id=1, source_target_pairs={{0,6},{2,0},{4,2},{6,4},{1,7},{3,1},{5,3},{7,5},{8,14},{10,8},{12,... | collective-permute-start | bytes 983048 | tf_op jit(solution)/shard_map/ppermute | solution.py:16
  147.8 9.6 %conv_backward.1 = (f32[16,80,128]{2,1,0:T(8,128)}, bf16[16,80,128]{2,1,0:T(8,128)(2,1)}, bf16[16,80,128]{2,1,0:T(8,128)(2,1)}, bf16[16,80,128]{2,1,0:T(8,128)(2,1)}) custom-call(s32[3]{0:T(128)} %pad_add_fusion.1.turns, bf16[320,2048]{1,0:T(8,128)(2,1)} %get-tuple-element.28.slope, bf16[1,320,128]{2,1,0:T(8,128)(2,1)} %collective-permute-done.20.above, ...), custom_call_target="tpu_custom_call" | custom-call | flops 3774873600 | bytes 8388608 | tf_op jit(solution)/shard_map/conv_backward/pallas_call | solution.py:300
  157.7 0.8 copy-done.6
  158.6 0.7 collective-permute-start.23
  159.3 1.7 bitcast_dynamic-update-slice_fusion.3
  161.0 0.7 bitcast_dynamic-update-slice_fusion.2
  161.7 2.0 add.270
  163.9 2.4 %collective-permute-start.26 = (f32[9,40,320]{2,1,0:T(8,128)S(1)}, f32[9,40,320]{2,1,0:T(8,128)S(1)}, u32[]{:S(2)}, u32[]{:S(2)}) collective-permute-start(f32[9,40,320]{2,1,0:T(8,128)S(1)} %get-tuple-element.39), channel_id=1, source_target_pairs={{0,24},{8,0},{16,8},{24,16},{1,25},{9,1},{17,9},{25,17},{2,26},{10... | collective-permute-start | bytes 1382408 | tf_op jit(solution)/shard_map/ppermute | solution.py:16
  166.2 1.5 collective-permute-start.27
  167.8 0.7 bitcast_dynamic-update-slice_fusion.1
  168.5 1.6 collective-permute-done.22
  170.1 1.4 collective-permute-start.24
  171.6 8.1 %collective-permute-done.26 = f32[9,40,320]{2,1,0:T(8,128)S(1)} collective-permute-done((f32[9,40,320]{2,1,0:T(8,128)S(1)}, f32[9,40,320]{2,1,0:T(8,128)S(1)}, u32[]{:S(2)}, u32[]{:S(2)}) %collective-permute-start.26) | collective-permute-done | bytes 460832 | tf_op jit(solution)/shard_map/ppermute | solution.py:16
  179.7 11.3 %collective-permute-done.27 = f32[9,40,320]{2,1,0:T(8,128)S(1)} collective-permute-done((f32[9,40,320]{2,1,0:T(8,128)S(1)}, f32[9,40,320]{2,1,0:T(8,128)S(1)}, u32[]{:S(2)}, u32[]{:S(2)}) %collective-permute-start.27) | collective-permute-done | bytes 460832 | tf_op jit(solution)/shard_map/ppermute | solution.py:16
  191.4 3.0 %collective-permute-start.29 = (f32[80,360]{0,1:T(8,128)S(1)}, f32[80,360]{0,1:T(8,128)S(1)}, u32[]{:S(2)}, u32[]{:S(2)}) collective-permute-start(f32[80,360]{0,1:T(8,128)S(1)} %bitcast.132), channel_id=1, source_target_pairs={{0,6},{2,0},{4,2},{6,4},{1,7},{3,1},{5,3},{7,5},{8,14},{10,8},{12,... | collective-permute-start | bytes 345608 | tf_op jit(solution)/shard_map/ppermute | solution.py:16
  194.5 1.7 collective-permute-start.30
  196.3 4.6 %collective-permute-done.29 = f32[80,360]{0,1:T(8,128)S(1)} collective-permute-done((f32[80,360]{0,1:T(8,128)S(1)}, f32[80,360]{0,1:T(8,128)S(1)}, u32[]{:S(2)}, u32[]{:S(2)}) %collective-permute-start.29) | collective-permute-done | bytes 115232 | tf_op jit(solution)/shard_map/ppermute | solution.py:16
  200.8 8.2 %collective-permute-done.30 = f32[80,360]{0,1:T(8,128)S(1)} collective-permute-done((f32[80,360]{0,1:T(8,128)S(1)}, f32[80,360]{0,1:T(8,128)S(1)}, u32[]{:S(2)}, u32[]{:S(2)}) %collective-permute-start.30) | collective-permute-done | bytes 115232 | tf_op jit(solution)/shard_map/ppermute | solution.py:16
  209.2 1.3 collective-permute-done.32
  210.7 0.8 copy.13
  (82 shorter events, 3.0 us)
Async XLA Ops:
  0.6 0.9 copy-start
  0.6 17.4 %copy-start.5 = (bf16[1,64,80,128]{3,2,1,0:T(8,128)(2,1)S(1)}, bf16[1,64,80,128]{3,2,1,0:T(8,128)(2,1)}, u32[]{:S(2)}) copy-start(bf16[1,64,80,128]{3,2,1,0:T(8,128)(2,1)} %param.3) | copy-start | bytes 3932164
  1.8 7.5 %collective-permute-start.7 = (bf16[40,720]{1,0:T(8,128)(2,1)S(1)}, bf16[40,720]{1,0:T(8,128)(2,1)S(1)}, u32[]{:S(2)}, u32[]{:S(2)}) collective-permute-start(bf16[40,720]{1,0:T(8,128)(2,1)S(1)} %copy.14), channel_id=1, source_target_pairs={{0,6},{2,0},{4,2},{6,4},{1,7},{3,1},{5,3},{7,5},{8,14},{10,8},{12,... | collective-permute-start | bytes 172808 | tf_op jit(solution)/shard_map/ppermute | solution.py:16
  6.9 5.5 %collective-permute-start.8 = (bf16[40,720]{1,0:T(8,128)(2,1)S(1)}, bf16[40,720]{1,0:T(8,128)(2,1)S(1)}, u32[]{:S(2)}, u32[]{:S(2)}) collective-permute-start(bf16[40,720]{1,0:T(8,128)(2,1)S(1)} %copy.14), channel_id=1, source_target_pairs={{0,4},{2,6},{4,0},{6,2},{1,5},{3,7},{5,1},{7,3},{8,12},{10,14},{12... | collective-permute-start | bytes 172808 | tf_op jit(solution)/shard_map/ppermute | solution.py:16
  6.9 6.1 %collective-permute-start.9 = (bf16[40,720]{1,0:T(8,128)(2,1)S(1)}, bf16[40,720]{1,0:T(8,128)(2,1)S(1)}, u32[]{:S(2)}, u32[]{:S(2)}) collective-permute-start(bf16[40,720]{1,0:T(8,128)(2,1)S(1)} %copy.14), channel_id=1, source_target_pairs={{0,2},{2,4},{4,6},{6,0},{1,3},{3,5},{5,7},{7,1},{8,10},{10,12},{12... | collective-permute-start | bytes 172808 | tf_op jit(solution)/shard_map/ppermute | solution.py:16
  13.1 8.8 %collective-permute-start.10 = (bf16[160,720]{1,0:T(8,128)(2,1)S(1)}, bf16[160,720]{1,0:T(8,128)(2,1)S(1)}, u32[]{:S(2)}, u32[]{:S(2)}) collective-permute-start(bf16[160,720]{1,0:T(8,128)(2,1)S(1)} %get-tuple-element.71), channel_id=1, source_target_pairs={{0,24},{8,0},{16,8},{24,16},{1,25},{9,1},{17,9},{25,17},{2,26},{10... | collective-permute-start | bytes 691208 | tf_op jit(solution)/shard_map/ppermute | solution.py:16
  15.6 11.8 %collective-permute-start.11 = (bf16[160,720]{1,0:T(8,128)(2,1)S(1)}, bf16[160,720]{1,0:T(8,128)(2,1)S(1)}, u32[]{:S(2)}, u32[]{:S(2)}) collective-permute-start(bf16[160,720]{1,0:T(8,128)(2,1)S(1)} %get-tuple-element.71), channel_id=1, source_target_pairs={{0,16},{8,24},{16,0},{24,8},{1,17},{9,25},{17,1},{25,9},{2,18},{10... | collective-permute-start | bytes 691208 | tf_op jit(solution)/shard_map/ppermute | solution.py:16
  16.1 11.8 %collective-permute-start.12 = (bf16[160,720]{1,0:T(8,128)(2,1)S(1)}, bf16[160,720]{1,0:T(8,128)(2,1)S(1)}, u32[]{:S(2)}, u32[]{:S(2)}) collective-permute-start(bf16[160,720]{1,0:T(8,128)(2,1)S(1)} %get-tuple-element.71), channel_id=1, source_target_pairs={{0,8},{8,16},{16,24},{24,0},{1,9},{9,17},{17,25},{25,1},{2,10},{10... | collective-permute-start | bytes 691208 | tf_op jit(solution)/shard_map/ppermute | solution.py:16
  18.0 15.9 %collective-permute-start.3 = (bf16[1,80,128]{2,1,0:T(8,128)(2,1)}, bf16[1,80,128]{2,1,0:T(8,128)(2,1)}, u32[]{:S(2)}, u32[]{:S(2)}) collective-permute-start(bf16[1,80,128]{2,1,0:T(8,128)(2,1)} %select_bitcast_fusion), channel_id=1, source_target_pairs={{0,1},{1,0},{2,3},{3,2},{4,5},{5,4},{6,7},{7,6},{8,9},{9,8},{10,11... | collective-permute-start | bytes 61448 | tf_op jit(solution)/shard_map/ppermute | solution.py:16
  19.0 46.6 %collective-permute-start = (bf16[16,80,128]{2,1,0:T(8,128)(2,1)}, bf16[16,80,128]{2,1,0:T(8,128)(2,1)}, u32[]{:S(2)}, u32[]{:S(2)}) collective-permute-start(bf16[16,80,128]{2,1,0:T(8,128)(2,1)} %get-tuple-element.64), channel_id=1, source_target_pairs={{0,6},{2,0},{4,2},{6,4},{1,7},{3,1},{5,3},{7,5},{8,14},{10,8},{12,... | collective-permute-start | bytes 983048 | tf_op jit(solution)/shard_map/ppermute | solution.py:16
  21.9 5.9 %copy-start.8 = (bf16[160,720]{1,0:T(8,128)(2,1)}, bf16[160,720]{1,0:T(8,128)(2,1)S(1)}, u32[]{:S(2)}) copy-start(bf16[160,720]{1,0:T(8,128)(2,1)S(1)} %collective-permute-done.10) | copy-start | bytes 691204
  21.9 43.7 %collective-permute-start.1 = (bf16[16,80,128]{2,1,0:T(8,128)(2,1)S(1)}, bf16[16,80,128]{2,1,0:T(8,128)(2,1)}, u32[]{:S(2)}, u32[]{:S(2)}) collective-permute-start(bf16[16,80,128]{2,1,0:T(8,128)(2,1)S(1)} %get-tuple-element.63), channel_id=1, source_target_pairs={{0,4},{2,6},{4,0},{6,2},{1,5},{3,7},{5,1},{7,3},{8,12},{10,14},{12... | collective-permute-start | bytes 983048 | tf_op jit(solution)/shard_map/ppermute | solution.py:16
  27.4 0.7 copy-start.9
  27.4 39.4 %collective-permute-start.2 = (bf16[16,80,128]{2,1,0:T(8,128)(2,1)S(1)}, bf16[16,80,128]{2,1,0:T(8,128)(2,1)}, u32[]{:S(2)}, u32[]{:S(2)}) collective-permute-start(bf16[16,80,128]{2,1,0:T(8,128)(2,1)S(1)} %get-tuple-element.62), channel_id=1, source_target_pairs={{0,2},{2,4},{4,6},{6,0},{1,3},{3,5},{5,7},{7,1},{8,10},{10,12},{12... | collective-permute-start | bytes 983048 | tf_op jit(solution)/shard_map/ppermute | solution.py:16
  27.9 0.7 copy-start.10
  29.9 37.0 %copy-start.1 = (bf16[4,160,720]{2,1,0:T(8,128)(2,1)}, bf16[4,160,720]{2,1,0:T(8,128)(2,1)S(1)}, u32[]{:S(2)}) copy-start(bf16[4,160,720]{2,1,0:T(8,128)(2,1)S(1)} %pad_maximum_fusion.refs_8_) | copy-start | bytes 2764804
  29.9 37.0 %collective-permute-start.13 = (bf16[4,160,720]{2,1,0:T(8,128)(2,1)S(1)}, bf16[4,160,720]{2,1,0:T(8,128)(2,1)}, u32[]{:S(2)}, u32[]{:S(2)}) collective-permute-start(bf16[4,160,720]{2,1,0:T(8,128)(2,1)S(1)} %pad_maximum_fusion.refs_8_), channel_id=1, source_target_pairs={{0,1},{1,0},{2,3},{3,2},{4,5},{5,4},{6,7},{7,6},{8,9},{9,8},{10,11... | collective-permute-start | bytes 2764808 | tf_op jit(solution)/shard_map/ppermute | solution.py:16
  34.7 11.7 %collective-permute-start.6 = (bf16[4,80,128]{2,1,0:T(8,128)(2,1)S(1)}, bf16[4,80,128]{2,1,0:T(8,128)(2,1)S(1)}, u32[]{:S(2)}, u32[]{:S(2)}) collective-permute-start(bf16[4,80,128]{2,1,0:T(8,128)(2,1)S(1)} %pad_maximum_fusion.5), channel_id=1, source_target_pairs={{0,2},{2,4},{4,6},{6,0},{1,3},{3,5},{5,7},{7,1},{8,10},{10,12},{12... | collective-permute-start | bytes 245768 | tf_op jit(solution)/shard_map/ppermute | solution.py:16
  46.5 20.4 %copy-start.17 = (bf16[4,80,128]{2,1,0:T(8,128)(2,1)}, bf16[4,80,128]{2,1,0:T(8,128)(2,1)S(1)}, u32[]{:S(2)}) copy-start(bf16[4,80,128]{2,1,0:T(8,128)(2,1)S(1)} %collective-permute-done.6.refs_7_) | copy-start | bytes 245764
  46.5 12.8 %collective-permute-start.5 = (bf16[4,80,128]{2,1,0:T(8,128)(2,1)S(1)}, bf16[4,80,128]{2,1,0:T(8,128)(2,1)S(1)}, u32[]{:S(2)}, u32[]{:S(2)}) collective-permute-start(bf16[4,80,128]{2,1,0:T(8,128)(2,1)S(1)} %pad_maximum_fusion.4), channel_id=1, source_target_pairs={{0,4},{2,6},{4,0},{6,2},{1,5},{3,7},{5,1},{7,3},{8,12},{10,14},{12... | collective-permute-start | bytes 245768 | tf_op jit(solution)/shard_map/ppermute | solution.py:16
  59.3 7.6 %copy-start.18 = (bf16[4,80,128]{2,1,0:T(8,128)(2,1)}, bf16[4,80,128]{2,1,0:T(8,128)(2,1)S(1)}, u32[]{:S(2)}) copy-start(bf16[4,80,128]{2,1,0:T(8,128)(2,1)S(1)} %collective-permute-done.5.refs_6_) | copy-start | bytes 245764
  59.3 4.4 %collective-permute-start.4 = (bf16[4,80,128]{2,1,0:T(8,128)(2,1)S(1)}, bf16[4,80,128]{2,1,0:T(8,128)(2,1)S(1)}, u32[]{:S(2)}, u32[]{:S(2)}) collective-permute-start(bf16[4,80,128]{2,1,0:T(8,128)(2,1)S(1)} %pad_maximum_fusion.3), channel_id=1, source_target_pairs={{0,6},{2,0},{4,2},{6,4},{1,7},{3,1},{5,3},{7,5},{8,14},{10,8},{12,... | collective-permute-start | bytes 245768 | tf_op jit(solution)/shard_map/ppermute | solution.py:16
  63.7 3.1 %copy-start.19 = (bf16[4,80,128]{2,1,0:T(8,128)(2,1)}, bf16[4,80,128]{2,1,0:T(8,128)(2,1)S(1)}, u32[]{:S(2)}) copy-start(bf16[4,80,128]{2,1,0:T(8,128)(2,1)S(1)} %collective-permute-done.4.refs_5_) | copy-start | bytes 245764
  63.7 15.4 %collective-permute-start.17 = (bf16[14,80,128]{2,1,0:T(8,128)(2,1)}, bf16[14,80,128]{2,1,0:T(8,128)(2,1)S(1)}, u32[]{:S(2)}, u32[]{:S(2)}) collective-permute-start(bf16[14,80,128]{2,1,0:T(8,128)(2,1)} %get-tuple-element.51), channel_id=1, source_target_pairs={{0,6},{2,0},{4,2},{6,4},{1,7},{3,1},{5,3},{7,5},{8,14},{10,8},{12,... | collective-permute-start | bytes 860168 | tf_op jit(solution)/shard_map/ppermute | solution.py:16
  65.6 23.6 %collective-permute-start.18 = (bf16[14,80,128]{2,1,0:T(8,128)(2,1)}, bf16[14,80,128]{2,1,0:T(8,128)(2,1)S(1)}, u32[]{:S(2)}, u32[]{:S(2)}) collective-permute-start(bf16[14,80,128]{2,1,0:T(8,128)(2,1)} %get-tuple-element.53), channel_id=1, source_target_pairs={{0,4},{2,6},{4,0},{6,2},{1,5},{3,7},{5,1},{7,3},{8,12},{10,14},{12... | collective-permute-start | bytes 860168 | tf_op jit(solution)/shard_map/ppermute | solution.py:16
  65.6 23.6 %collective-permute-start.19 = (bf16[14,80,128]{2,1,0:T(8,128)(2,1)}, bf16[14,80,128]{2,1,0:T(8,128)(2,1)S(1)}, u32[]{:S(2)}, u32[]{:S(2)}) collective-permute-start(bf16[14,80,128]{2,1,0:T(8,128)(2,1)} %get-tuple-element.50), channel_id=1, source_target_pairs={{0,2},{2,4},{4,6},{6,0},{1,3},{3,5},{5,7},{7,1},{8,10},{10,12},{12... | collective-permute-start | bytes 860168 | tf_op jit(solution)/shard_map/ppermute | solution.py:16
  79.2 10.0 %copy-start.13 = (bf16[14,80,128]{2,1,0:T(8,128)(2,1)}, bf16[14,80,128]{2,1,0:T(8,128)(2,1)S(1)}, u32[]{:S(2)}) copy-start(bf16[14,80,128]{2,1,0:T(8,128)(2,1)S(1)} %collective-permute-done.17.refs_1_) | copy-start | bytes 860164
  89.2 0.7 copy-start.14
  89.2 0.8 copy-start.15
  90.0 18.1 %copy-start.16 = (bf16[1,320,128]{2,1,0:T(8,128)(2,1)S(1)}, bf16[1,320,128]{2,1,0:T(8,128)(2,1)}, u32[]{:S(2)}) copy-start(bf16[1,320,128]{2,1,0:T(8,128)(2,1)} %get-tuple-element.30) | copy-start | bytes 245764
  90.0 23.4 %copy-start.2 = (bf16[4,160,720]{2,1,0:T(8,128)(2,1)S(1)}, bf16[4,160,720]{2,1,0:T(8,128)(2,1)}, u32[]{:S(2)}) copy-start(bf16[4,160,720]{2,1,0:T(8,128)(2,1)} %copy-done.1) | copy-start | bytes 2764804
  103.6 58.1 %collective-permute-start.25 = (f32[4,9,40,320]{3,2,1,0:T(8,128)}, f32[4,9,40,320]{3,2,1,0:T(8,128)}, u32[]{:S(2)}, u32[]{:S(2)}) collective-permute-start(f32[4,9,40,320]{3,2,1,0:T(8,128)} %get-tuple-element.38), channel_id=1, source_target_pairs={{0,1},{1,0},{2,3},{3,2},{4,5},{5,4},{6,7},{7,6},{8,9},{9,8},{10,11... | collective-permute-start | bytes 5529608 | tf_op jit(solution)/shard_map/ppermute | solution.py:16
  104.4 40.5 %collective-permute-start.20 = (bf16[1,320,128]{2,1,0:T(8,128)(2,1)}, bf16[1,320,128]{2,1,0:T(8,128)(2,1)}, u32[]{:S(2)}, u32[]{:S(2)}) collective-permute-start(bf16[1,320,128]{2,1,0:T(8,128)(2,1)} %get-tuple-element.29), channel_id=1, source_target_pairs={{0,2},{2,4},{4,6},{6,7},{7,5},{5,3},{3,1},{8,10},{10,12},{12,14},{... | collective-permute-start | bytes 245768 | tf_op jit(solution)/shard_map/ppermute | solution.py:443
  108.2 39.6 %collective-permute-start.21 = (bf16[1,320,128]{2,1,0:T(8,128)(2,1)S(1)}, bf16[1,320,128]{2,1,0:T(8,128)(2,1)}, u32[]{:S(2)}, u32[]{:S(2)}) collective-permute-start(bf16[1,320,128]{2,1,0:T(8,128)(2,1)S(1)} %copy-done.16), channel_id=1, source_target_pairs={{2,0},{4,2},{6,4},{7,6},{5,7},{3,5},{1,3},{10,8},{12,10},{14,12},{... | collective-permute-start | bytes 245768 | tf_op jit(solution)/shard_map/ppermute | solution.py:444
  109.5 49.1 %collective-permute-start.14 = (bf16[16,80,128]{2,1,0:T(8,128)(2,1)}, bf16[16,80,128]{2,1,0:T(8,128)(2,1)}, u32[]{:S(2)}, u32[]{:S(2)}) collective-permute-start(bf16[16,80,128]{2,1,0:T(8,128)(2,1)} %get-tuple-element.22), channel_id=1, source_target_pairs={{0,2},{2,4},{4,6},{6,0},{1,3},{3,5},{5,7},{7,1},{8,10},{10,12},{12... | collective-permute-start | bytes 983048 | tf_op jit(solution)/shard_map/ppermute | solution.py:16
  112.2 48.8 %collective-permute-start.15 = (bf16[16,80,128]{2,1,0:T(8,128)(2,1)}, bf16[16,80,128]{2,1,0:T(8,128)(2,1)S(1)}, u32[]{:S(2)}, u32[]{:S(2)}) collective-permute-start(bf16[16,80,128]{2,1,0:T(8,128)(2,1)} %get-tuple-element.23), channel_id=1, source_target_pairs={{0,4},{2,6},{4,0},{6,2},{1,5},{3,7},{5,1},{7,3},{8,12},{10,14},{12... | collective-permute-start | bytes 983048 | tf_op jit(solution)/shard_map/ppermute | solution.py:16
  113.4 4.3 %copy-start.7 = (bf16[16,80,128]{2,1,0:T(8,128)(2,1)S(1)}, bf16[16,80,128]{2,1,0:T(8,128)(2,1)}, u32[]{:S(2)}) copy-start(bf16[16,80,128]{2,1,0:T(8,128)(2,1)} %get-tuple-element.21) | copy-start | bytes 983044
  144.9 22.8 %collective-permute-start.16 = (bf16[16,80,128]{2,1,0:T(8,128)(2,1)}, bf16[16,80,128]{2,1,0:T(8,128)(2,1)S(1)}, u32[]{:S(2)}, u32[]{:S(2)}) collective-permute-start(bf16[16,80,128]{2,1,0:T(8,128)(2,1)} %get-tuple-element.24), channel_id=1, source_target_pairs={{0,6},{2,0},{4,2},{6,4},{1,7},{3,1},{5,3},{7,5},{8,14},{10,8},{12,... | collective-permute-start | bytes 983048 | tf_op jit(solution)/shard_map/ppermute | solution.py:16
  157.4 1.1 copy-start.6
  157.4 12.7 %collective-permute-start.22 = (bf16[16,80,128]{2,1,0:T(8,128)(2,1)}, bf16[16,80,128]{2,1,0:T(8,128)(2,1)S(1)}, u32[]{:S(2)}, u32[]{:S(2)}) collective-permute-start(bf16[16,80,128]{2,1,0:T(8,128)(2,1)} %get-tuple-element.34), channel_id=1, source_target_pairs={{0,2},{2,4},{4,6},{6,0},{1,3},{3,5},{5,7},{7,1},{8,10},{10,12},{12... | collective-permute-start | bytes 983048 | tf_op jit(solution)/shard_map/ppermute | solution.py:16
  157.5 1.1 copy-start.12
  158.5 3.2 %copy-start.4 = (f32[4,9,40,320]{3,2,1,0:T(8,128)S(1)}, f32[4,9,40,320]{3,2,1,0:T(8,128)}, u32[]{:S(2)}) copy-start(f32[4,9,40,320]{3,2,1,0:T(8,128)} %get-tuple-element.37) | copy-start | bytes 5529604
  158.6 37.6 %collective-permute-start.23 = (bf16[16,80,128]{2,1,0:T(8,128)(2,1)S(1)}, bf16[16,80,128]{2,1,0:T(8,128)(2,1)S(1)}, u32[]{:S(2)}, u32[]{:S(2)}) collective-permute-start(bf16[16,80,128]{2,1,0:T(8,128)(2,1)S(1)} %copy-done.12), channel_id=1, source_target_pairs={{0,4},{2,6},{4,0},{6,2},{1,5},{3,7},{5,1},{7,3},{8,12},{10,14},{12... | collective-permute-start | bytes 983048 | tf_op jit(solution)/shard_map/ppermute | solution.py:16
  163.7 6.4 %copy-start.11 = (bf16[16,80,128]{2,1,0:T(8,128)(2,1)S(1)}, bf16[16,80,128]{2,1,0:T(8,128)(2,1)}, u32[]{:S(2)}) copy-start(bf16[16,80,128]{2,1,0:T(8,128)(2,1)} %get-tuple-element.36) | copy-start | bytes 983044
  163.9 15.8 %collective-permute-start.26 = (f32[9,40,320]{2,1,0:T(8,128)S(1)}, f32[9,40,320]{2,1,0:T(8,128)S(1)}, u32[]{:S(2)}, u32[]{:S(2)}) collective-permute-start(f32[9,40,320]{2,1,0:T(8,128)S(1)} %get-tuple-element.39), channel_id=1, source_target_pairs={{0,24},{8,0},{16,8},{24,16},{1,25},{9,1},{17,9},{25,17},{2,26},{10... | collective-permute-start | bytes 1382408 | tf_op jit(solution)/shard_map/ppermute | solution.py:16
  166.2 24.8 %collective-permute-start.27 = (f32[9,40,320]{2,1,0:T(8,128)S(1)}, f32[9,40,320]{2,1,0:T(8,128)S(1)}, u32[]{:S(2)}, u32[]{:S(2)}) collective-permute-start(f32[9,40,320]{2,1,0:T(8,128)S(1)} %get-tuple-element.41), channel_id=1, source_target_pairs={{0,16},{8,24},{16,0},{24,8},{1,17},{9,25},{17,1},{25,9},{2,18},{10... | collective-permute-start | bytes 1382408 | tf_op jit(solution)/shard_map/ppermute | solution.py:16
  167.8 23.2 %collective-permute-start.28 = (f32[9,40,320]{2,1,0:T(8,128)S(1)}, f32[9,40,320]{2,1,0:T(8,128)S(1)}, u32[]{:S(2)}, u32[]{:S(2)}) collective-permute-start(f32[9,40,320]{2,1,0:T(8,128)S(1)} %get-tuple-element.40), channel_id=1, source_target_pairs={{0,8},{8,16},{16,24},{24,0},{1,9},{9,17},{17,25},{25,1},{2,10},{10... | collective-permute-start | bytes 1382408 | tf_op jit(solution)/shard_map/ppermute | solution.py:16
  170.1 39.0 %collective-permute-start.24 = (bf16[16,80,128]{2,1,0:T(8,128)(2,1)S(1)}, bf16[16,80,128]{2,1,0:T(8,128)(2,1)S(1)}, u32[]{:S(2)}, u32[]{:S(2)}) collective-permute-start(bf16[16,80,128]{2,1,0:T(8,128)(2,1)S(1)} %copy-done.11), channel_id=1, source_target_pairs={{0,6},{2,0},{4,2},{6,4},{1,7},{3,1},{5,3},{7,5},{8,14},{10,8},{12,... | collective-permute-start | bytes 983048 | tf_op jit(solution)/shard_map/ppermute | solution.py:16
  191.4 9.4 %collective-permute-start.29 = (f32[80,360]{0,1:T(8,128)S(1)}, f32[80,360]{0,1:T(8,128)S(1)}, u32[]{:S(2)}, u32[]{:S(2)}) collective-permute-start(f32[80,360]{0,1:T(8,128)S(1)} %bitcast.132), channel_id=1, source_target_pairs={{0,6},{2,0},{4,2},{6,4},{1,7},{3,1},{5,3},{7,5},{8,14},{10,8},{12,... | collective-permute-start | bytes 345608 | tf_op jit(solution)/shard_map/ppermute | solution.py:16
  194.5 14.5 %collective-permute-start.30 = (f32[80,360]{0,1:T(8,128)S(1)}, f32[80,360]{0,1:T(8,128)S(1)}, u32[]{:S(2)}, u32[]{:S(2)}) collective-permute-start(f32[80,360]{0,1:T(8,128)S(1)} %bitcast.131), channel_id=1, source_target_pairs={{0,4},{2,6},{4,0},{6,2},{1,5},{3,7},{5,1},{7,3},{8,12},{10,14},{12... | collective-permute-start | bytes 345608 | tf_op jit(solution)/shard_map/ppermute | solution.py:16
  196.2 12.8 %collective-permute-start.31 = (f32[80,360]{0,1:T(8,128)S(1)}, f32[80,360]{0,1:T(8,128)S(1)}, u32[]{:S(2)}, u32[]{:S(2)}) collective-permute-start(f32[80,360]{0,1:T(8,128)S(1)} %bitcast.130), channel_id=1, source_target_pairs={{0,2},{2,4},{4,6},{6,0},{1,3},{3,5},{5,7},{7,1},{8,10},{10,12},{12... | collective-permute-start | bytes 345608 | tf_op jit(solution)/shard_map/ppermute | solution.py:16
  209.0 1.5 collective-permute-start.32
  209.2 2.2 %copy-start.3 = (f32[1,64,80,128]{3,2,1,0:T(8,128)}, f32[1,64,80,128]{3,2,1,0:T(8,128)S(1)}, u32[]{:S(2)}) copy-start(f32[1,64,80,128]{3,2,1,0:T(8,128)S(1)} %convert_dynamic-update-slice_fusion) | copy-start | bytes 7864324

commit v3 on v2

--- a/solution.py
+++ b/solution.py
@@ -253,32 +253,117 @@
     return results[:-1], results[-1]
 
 
-def backward_body(count, rows, turns, slope, above, below, kernels, *refs):
+def padded_depth(depth):
+    return -(-depth // 128) * 128
+
+
+def turned_body(shares, *refs):
+    halves, out = refs[:shares], refs[shares]
+    _, depth, lanes = out.shape
+    stride = lanes // 9
+    total = halves[0].shape[2]
+    both = [jnp.concatenate([half[0] for half in halves])]
+    channels = both[0].shape[0]
+    rows = []
+    for start in range(0, total, 128):
+        size = min(128, total - start)
+        unit = (
+            lax.broadcasted_iota(jnp.int32, (size, size), 0)
+            == lax.broadcasted_iota(jnp.int32, (size, size), 1)
+        ).astype(jnp.bfloat16)
+        rows.append(
+            lax.dot_general(
+                unit,
+                both[0][:, start : start + size],
+                (((1,), (1,)), ((), ())),
+                preferred_element_type=jnp.float32,
+            )
+        )
+    turned = jnp.concatenate(rows)
+    for tap in range(9):
+        begin = (8 - tap) * depth
+        value = turned[begin : begin + depth].astype(jnp.bfloat16)
+        out[0, :, tap * stride : tap * stride + channels] = value
+        if stride > channels:
+            out[0, :, tap * stride + channels : (tap + 1) * stride] = jnp.zeros(
+                (depth, stride - channels), jnp.bfloat16
+            )
+
+
+def turned(halves):
+    shares = len(halves)
+    blocks, outs, lanes = halves[0].shape
+    depth = lanes // 9
+    stride = padded_depth(outs * shares)
+    return pl.pallas_call(
+        functools.partial(turned_body, shares),
+        grid=(blocks,),
+        in_specs=[pl.BlockSpec((1, outs, lanes), lambda g: (g, 0, 0))] * shares,
+        out_specs=pl.BlockSpec((1, depth, 9 * stride), lambda g: (g, 0, 0)),
+        out_shape=jax.ShapeDtypeStruct((blocks, depth, 9 * stride), jnp.bfloat16),
+        compiler_params=pltpu.CompilerParams(vmem_limit_bytes=VMEM_LIMIT),
+        cost_estimate=pl.CostEstimate(
+            flops=2 * 128 * blocks * outs * shares * lanes,
+            bytes_accessed=4 * 1024 * 1024,
+            transcendentals=0,
+        ),
+        name="turn_kernel",
+    )(*halves)
+
+
+def backward_body(count, shares, rows, turns, slope, above, below, kernels, *refs):
     outs, stacked = refs[:count], refs[count]
     channels = slope.shape[0]
     _, _, width = above.shape
     height = slope.shape[1] // width
     depth = channels // count
+    size = depth // shares
+    stride = stacked.shape[0] // 3
     step = pl.program_id(0)
+
+    def in_share_order(wide):
+        parts = []
+        for at in range(shares):
+            chosen = None
+            for share in range(shares):
+                value = jnp.concatenate(
+                    [wide[j * depth + share * size : j * depth + (share + 1) * size] for j in range(count)]
+                )
+                here = turns[3] == (share - at) % shares
+                chosen = value if chosen is None else jnp.where(here, value, chosen)
+            parts.append(chosen)
+        return jnp.concatenate(parts)
+
+    def put(row, block):
+        lanes = pl.ds(pl.multiple_of(row * width, width), width)
+        wide = in_share_order(block.astype(jnp.float32))
+        for copies, moved in enumerate((columns_moved(wide, -1), wide, columns_moved(wide, 1))):
+            stacked[copies * stride : copies * stride + channels, lanes] = moved.astype(slope.dtype)
 
     @pl.when(step == 0)
     def _():
-        for j in range(count):
-            for side, rim, row in ((0, above, 0), (1, below, height + 1)):
+        if stride > channels:
+            for copies in range(3):
+                stacked[copies * stride + channels : (copies + 1) * stride, :] = jnp.zeros(
+                    (stride - channels, stacked.shape[1]), stacked.dtype
+                )
+        for side, rim, row in ((0, above, 0), (1, below, height + 1)):
+            blocks = []
+            for j in range(count):
                 start = lax.rem(turns[side] + j, count) * depth
-                block = rim[0, pl.ds(pl.multiple_of(start, depth), depth), :]
-                place(stacked, j * depth, row, block, channels)
+                blocks.append(rim[0, pl.ds(pl.multiple_of(start, depth), depth), :])
+            put(row, jnp.concatenate(blocks))
 
         def body(row, carry):
             lanes = pl.ds(pl.multiple_of(row * width, width), width)
-            place(stacked, 0, row + 1, slope[:, lanes], channels)
+            put(row + 1, slope[:, lanes])
             return carry
 
         lax.fori_loop(0, height, body, 0)
 
     windows = [
-        window(stacked, tap_row, 0, 0, 3 * channels, step * rows, rows, width, channels)
-        for tap_row in range(3)
+        stacked[:, pl.ds(pl.multiple_of((step * rows + a) * width, width), rows * width)]
+        for a in range(3)
     ]
     order = [kernels[lax.rem(turns[2] + j, count)] for j in range(count)]
     grad = jnp.dot(
@@ -298,7 +383,7 @@
     rows = 4 if height % 4 == 0 else 1
     flops = 2 * 9 * channels * channels * height * width
     return pl.pallas_call(
-        functools.partial(backward_body, count, rows),
+        functools.partial(backward_body, count, lax.axis_size("row"), rows),
         grid=(height // rows,),
         in_specs=[
             pl.BlockSpec(memory_space=pltpu.SMEM),
@@ -312,7 +397,7 @@
             jax.ShapeDtypeStruct((height, depth, width), jnp.bfloat16 if j else jnp.float32)
             for j in range(count)
         ],
-        scratch_shapes=[pltpu.VMEM((3 * channels, (height + 2) * width), jnp.bfloat16)],
+        scratch_shapes=[pltpu.VMEM((kernels.shape[2] // 3, (height + 2) * width), jnp.bfloat16)],
         compiler_params=pltpu.CompilerParams(vmem_limit_bytes=VMEM_LIMIT),
         cost_estimate=pl.CostEstimate(
             flops=flops, bytes_accessed=8 * 1024 * 1024, transcendentals=0
@@ -338,16 +423,6 @@
     return [over_dp] + [receive(over_dp, "row", j) for j in range(1, rows)]
 
 
-def back_order(halves):
-    row, rows = lax.axis_index("row"), lax.axis_size("row")
-    chans = lax.axis_size("chan")
-    both = rotated(jnp.stack(halves), (rows - row) % rows, 0)
-    _, blocks, outs, depth = both.shape
-    inner = depth // 9
-    both = both.reshape(rows, blocks, chans, outs // chans, 9, inner)[:, :, :, :, ::-1]
-    return jnp.transpose(both, (1, 5, 4, 2, 0, 3)).reshape(blocks, inner, 9 * outs * rows)
-
-
 def summed_kernel_grad(shares, inner, outer):
     dp, row = lax.axis_index("dp"), lax.axis_index("row")
     dps, chans, rows = (lax.axis_size(a) for a in ("dp", "chan", "row"))
@@ -428,12 +503,11 @@
     above_turn = jnp.where(place_at == 0, 0, forth)
     below_turn = jnp.where(place_at == chans - 1, 0, chans - forth)
     turns = jnp.stack([shift, row]).astype(jnp.int32)
-    back_turns = jnp.stack([above_turn, below_turn, shift]).astype(jnp.int32)
+    back_turns = jnp.stack([above_turn, below_turn, shift, row]).astype(jnp.int32)
 
     results = forward(turns, pieces, rims, halves)
     activated, factor, stacked, first, last = results
-    halves, factor = lax.optimization_barrier((halves, factor))
-    back_kernel = back_order(halves)
+    back_kernel = turned(halves)
 
     def snake(place_at):
         r, k = place_at // chans, place_at % chans

time: 213 us -> 194 us (0.911)
  local copies, waits for them, and re-layouts: 40.8 us -> 14.2 us
  starting transfers between devices: 51 us -> 70.8 us
  waiting for transfers between devices: 72.1 us -> 59.5 us
  Pallas kernels: 35.5 us -> 40.9 us
  other arithmetic: 11 us -> 6.49 us
    ppermute x31, starting transfers between devices: 46 us -> 66.4 us  [receive(): lax.ppermute(block, axis, [(i, (i - ahead) % count) for i in range(count)])]
    rev x1 -> x0, local copies, waits for them, and re-layouts: 13.8 us -> none  [back_order(): both.reshape(rows, blocks, chans, outs // chans, 9, inner)[:, :, :, :, ::-1]]
    ppermute x31, waiting for transfers between devices: 72.1 us -> 59.5 us  [receive(): lax.ppermute(block, axis, [(i, (i - ahead) % count) for i in range(count)])]
    reshape x2 -> x0, local copies, waits for them, and re-layouts: 9.32 us -> none  [the longest x1 6.81 us: back_order(): both.reshape(rows, blocks, chans, outs // chans, 9, inner)[:, :, :, :, ::-1]]
    pallas_call x1 -> x2, Pallas kernels: 9.64 us -> 15.1 us  [the longest x1 10.6 us: backward(): pl.pallas_call(functools.partial(backward_body, count, lax.axis_size('row...]
    transpose x1 -> x0, local copies, waits for them, and re-layouts: 3.29 us -> none  [back_order(): jnp.transpose(both, (1, 5, 4, 2, 0, 3))]
    concatenate x2 -> x1, other arithmetic: 3.19 us -> 0.12 us  [rotated(): twice = jnp.concatenate([array, array], axis=axis)]
  transfers between devices with their start and end apart: 33 -> 33, of which waited for: 15 -> 14; matrix products, arithmetic and copies ran while one was open for 22% -> 8% of each run, Pallas kernels for 10% -> 14%
where the time goes in v3:
time: 194 us; the launch traced here: 193 us
  starting transfers between devices  70.8 us (36%)
  waiting for transfers between devices  59.5 us (31%)
  Pallas kernels  40.9 us (21%)
  local copies, waits for them, and re-layouts  14.2 us (7%)
  other arithmetic  6.49 us (3%)
    ppermute x31, starting transfers between devices, receive(): lax.ppermute(block, axis, [(i, (i - ahead) % count) for i in range(count)])  66.4 us
    ppermute x31, waiting for transfers between devices, receive(): lax.ppermute(block, axis, [(i, (i - ahead) % count) for i in range(count)])  59.5 us
    pallas_call x1, Pallas kernels, correlate(): results = call(turn, stacked, factor, *pieces, *ends)  13.6 us
    pallas_call x1, Pallas kernels, forward(): results = call(turns, *pieces, *rims, *halves)  12.3 us
    pallas_call x1, Pallas kernels, backward(): pl.pallas_call(functools.partial(backward_body, count, lax.axis_size('row...  10.6 us
    pallas_call x1, Pallas kernels, turned(): pl.pallas_call(functools.partial(turned_body, shares), grid=(blocks,), in...  4.48 us
  transfers between devices with their start and end apart: 33, of which 14 were waited for; matrix products, arithmetic and copies ran while one was open for 8% of the time, Pallas kernels for 14%

profile of v3, /device:TPU:0, one launch (start us, length us, event | category | flops | bytes accessed | tf_op | source)
XLA Modules:
  0.0 193.0 jit_solution(9644426947418886088)
XLA Ops:
  0.7 0.9 copy-done
  1.8 5.1 %collective-permute-start.7 = (bf16[40,720]{1,0:T(8,128)(2,1)S(1)}, bf16[40,720]{1,0:T(8,128)(2,1)S(1)}, u32[]{:S(2)}, u32[]{:S(2)}) collective-permute-start(bf16[40,720]{1,0:T(8,128)(2,1)S(1)} %copy.10), channel_id=1, source_target_pairs={{0,6},{2,0},{4,2},{6,4},{1,7},{3,1},{5,3},{7,5},{8,14},{10,8},{12,... | collective-permute-start | bytes 172808 | tf_op jit(solution)/shard_map/ppermute | solution.py:16
  6.9 1.0 collective-permute-start.9
  7.9 1.4 collective-permute-done.7
  9.3 3.1 %collective-permute-done.8 = bf16[40,720]{1,0:T(8,128)(2,1)S(1)} collective-permute-done((bf16[40,720]{1,0:T(8,128)(2,1)S(1)}, bf16[40,720]{1,0:T(8,128)(2,1)S(1)}, u32[]{:S(2)}, u32[]{:S(2)}) %collective-permute-start.8) | collective-permute-done | bytes 57632 | tf_op jit(solution)/shard_map/ppermute | solution.py:16
  12.4 0.6 collective-permute-done.9
  13.1 2.5 %collective-permute-start.10 = (bf16[160,720]{1,0:T(8,128)(2,1)S(1)}, bf16[160,720]{1,0:T(8,128)(2,1)S(1)}, u32[]{:S(2)}, u32[]{:S(2)}) collective-permute-start(bf16[160,720]{1,0:T(8,128)(2,1)S(1)} %get-tuple-element.65), channel_id=1, source_target_pairs={{0,24},{8,0},{16,8},{24,16},{1,25},{9,1},{17,9},{25,17},{2,26},{10... | collective-permute-start | bytes 691208 | tf_op jit(solution)/shard_map/ppermute | solution.py:16
  15.6 0.5 collective-permute-start.11
  16.1 0.6 collective-permute-start.12
  16.7 1.3 select_bitcast_fusion
  18.0 1.1 dynamic-slice_bitcast_fusion
  19.1 2.0 %collective-permute-start = (bf16[16,80,128]{2,1,0:T(8,128)(2,1)}, bf16[16,80,128]{2,1,0:T(8,128)(2,1)}, u32[]{:S(2)}, u32[]{:S(2)}) collective-permute-start(bf16[16,80,128]{2,1,0:T(8,128)(2,1)} %get-tuple-element.58), channel_id=1, source_target_pairs={{0,6},{2,0},{4,2},{6,4},{1,7},{3,1},{5,3},{7,5},{8,14},{10,8},{12,... | collective-permute-start | bytes 983048 | tf_op jit(solution)/shard_map/ppermute | solution.py:16
  21.1 0.8 collective-permute-done.10
  21.9 1.9 collective-permute-start.1
  23.8 3.6 %collective-permute-done.11 = bf16[160,720]{1,0:T(8,128)(2,1)S(1)} collective-permute-done((bf16[160,720]{1,0:T(8,128)(2,1)S(1)}, bf16[160,720]{1,0:T(8,128)(2,1)S(1)}, u32[]{:S(2)}, u32[]{:S(2)}) %collective-permute-start.11) | collective-permute-done | bytes 230432 | tf_op jit(solution)/shard_map/ppermute | solution.py:16
  27.4 0.4 collective-permute-start.2
  28.1 2.5 %dynamic-slice_bitcast_fusion.4 = (bf16[14,80,128]{2,1,0:T(8,128)(2,1)}, bf16[14,80,128]{2,1,0:T(8,128)(2,1)}, bf16[14,80,128]{2,1,0:T(8,128)(2,1)}, bf16[14,80,128]{2,1,0:T(8,128)(2,1)}) fusion(bf16[1,64,80,128]{3,2,1,0:T(8,128)(2,1)} %param.5, s32[]{:T(128)S(6)} %select_n.345, s32[]{:T(128)S(6)} %select_n.343, s32[]{:T(128)S(6)} %select_n.342, ...), kind=kLoop, calls=%fused_computation.28 | loop fusion | bytes 2293776 | tf_op jit(solution)/shard_map/dynamic_slice | solution.py:496
  30.6 1.5 dynamic-slice_bitcast_fusion.9
  32.1 0.6 pad_add_fusion.turns
  32.8 0.8 bitcast_select_fusion.1
  33.5 0.8 pad_maximum_fusion.5
  34.3 2.5 %collective-permute-start.6 = (bf16[4,80,128]{2,1,0:T(8,128)(2,1)S(1)}, bf16[4,80,128]{2,1,0:T(8,128)(2,1)S(1)}, u32[]{:S(2)}, u32[]{:S(2)}) collective-permute-start(bf16[4,80,128]{2,1,0:T(8,128)(2,1)S(1)} %pad_maximum_fusion.5), channel_id=1, source_target_pairs={{0,2},{2,4},{4,6},{6,0},{1,3},{3,5},{5,7},{7,1},{8,10},{10,12},{12... | collective-permute-start | bytes 245768 | tf_op jit(solution)/shard_map/ppermute | solution.py:16
  36.8 0.8 pad_maximum_fusion.4
  37.6 9.1 %collective-permute-done.6.refs_7_ = bf16[4,80,128]{2,1,0:T(8,128)(2,1)S(1)} collective-permute-done((bf16[4,80,128]{2,1,0:T(8,128)(2,1)S(1)}, bf16[4,80,128]{2,1,0:T(8,128)(2,1)S(1)}, u32[]{:S(2)}, u32[]{:S(2)}) %collective-permute-start.6) | collective-permute-done | bytes 81952 | tf_op jit(solution)/shard_map/ppermute | solution.py:16
  46.6 8.6 %collective-permute-start.5 = (bf16[4,80,128]{2,1,0:T(8,128)(2,1)S(1)}, bf16[4,80,128]{2,1,0:T(8,128)(2,1)S(1)}, u32[]{:S(2)}, u32[]{:S(2)}) collective-permute-start(bf16[4,80,128]{2,1,0:T(8,128)(2,1)S(1)} %pad_maximum_fusion.4), channel_id=1, source_target_pairs={{0,4},{2,6},{4,0},{6,2},{1,5},{3,7},{5,1},{7,3},{8,12},{10,14},{12... | collective-permute-start | bytes 245768 | tf_op jit(solution)/shard_map/ppermute | solution.py:16
  55.3 4.4 %collective-permute-done.5.refs_6_ = bf16[4,80,128]{2,1,0:T(8,128)(2,1)S(1)} collective-permute-done((bf16[4,80,128]{2,1,0:T(8,128)(2,1)S(1)}, bf16[4,80,128]{2,1,0:T(8,128)(2,1)S(1)}, u32[]{:S(2)}, u32[]{:S(2)}) %collective-permute-start.5) | collective-permute-done | bytes 81952 | tf_op jit(solution)/shard_map/ppermute | solution.py:16
  59.6 0.7 pad_maximum_fusion.2.refs_4_
  60.3 3.8 %collective-permute-done.4.refs_5_ = bf16[4,80,128]{2,1,0:T(8,128)(2,1)S(1)} collective-permute-done((bf16[4,80,128]{2,1,0:T(8,128)(2,1)S(1)}, bf16[4,80,128]{2,1,0:T(8,128)(2,1)S(1)}, u32[]{:S(2)}, u32[]{:S(2)}) %collective-permute-start.4) | collective-permute-done | bytes 81952 | tf_op jit(solution)/shard_map/ppermute | solution.py:16
  64.1 1.8 collective-permute-start.17
  65.9 1.1 collective-permute-start.19
  67.1 0.9 copy-done.5
  68.1 12.3 %conv_forward.1 = (bf16[16,80,128]{2,1,0:T(8,128)(2,1)}, bf16[16,80,128]{2,1,0:T(8,128)(2,1)}, bf16[16,80,128]{2,1,0:T(8,128)(2,1)}, bf16[16,80,128]{2,1,0:T(8,1...) custom-call(s32[2]{0:T(128)} %pad_add_fusion.turns, ...), custom_call_target="tpu_custom_call" | custom-call | flops 3774873600 | bytes 16777216 | tf_op jit(solution)/shard_map/conv_forward/pallas_call | solution.py:181
  80.4 9.2 %collective-permute-done.18.refs_2_ = bf16[14,80,128]{2,1,0:T(8,128)(2,1)S(1)} collective-permute-done((bf16[14,80,128]{2,1,0:T(8,128)(2,1)}, bf16[14,80,128]{2,1,0:T(8,128)(2,1)S(1)}, u32[]{:S(2)}, u32[]{:S(2)}) %collective-permute-start.18) | collective-permute-done | bytes 286752 | tf_op jit(solution)/shard_map/ppermute | solution.py:16
  89.6 0.7 copy-done.12
  90.4 13.6 %kernel_grad.1 = (f32[4,9,40,320]{3,2,1,0:T(8,128)}, f32[4,9,40,320]{3,2,1,0:T(8,128)}, bf16[320,2048]{1,0:T(8,128)(2,1)}) custom-call(s32[1]{0:T(128)} %bitcast.1.turn, bf16[960,2304]{1,0:T(8,128)(2,1)} %get-tuple-element.22.stacked, f32[16,320,128]{2,1,0:T(8,128)} %get-tuple-element.23.factor, bf16[14,80,128]{2,1,0:T(8,128)(2,1)} %get-tuple-element.46.refs_0_, ...), custom_call_target="tpu_custom_call" | custom-call | flops 3774873600 | bytes 14680064 | tf_op jit(solution)/shard_map/kernel_grad/pallas_call | solution.py:252
  104.0 0.7 pad_add_fusion.1.turns
  104.7 3.1 %collective-permute-start.20 = (bf16[1,320,128]{2,1,0:T(8,128)(2,1)S(1)}, bf16[1,320,128]{2,1,0:T(8,128)(2,1)S(1)}, u32[]{:S(2)}, u32[]{:S(2)}) collective-permute-start(bf16[1,320,128]{2,1,0:T(8,128)(2,1)S(1)} %copy-done.15), channel_id=1, source_target_pairs={{0,2},{2,4},{4,6},{6,7},{7,5},{5,3},{3,1},{8,10},{10,12},{12,14},{... | collective-permute-start | bytes 245768 | tf_op jit(solution)/shard_map/ppermute | solution.py:517
  107.9 1.3 collective-permute-start.21
  109.2 3.1 %collective-permute-start.14 = (bf16[16,80,128]{2,1,0:T(8,128)(2,1)}, bf16[16,80,128]{2,1,0:T(8,128)(2,1)S(1)}, u32[]{:S(2)}, u32[]{:S(2)}) collective-permute-start(bf16[16,80,128]{2,1,0:T(8,128)(2,1)} %get-tuple-element.19), channel_id=1, source_target_pairs={{0,2},{2,4},{4,6},{6,0},{1,3},{3,5},{5,7},{7,1},{8,10},{10,12},{12... | collective-permute-start | bytes 983048 | tf_op jit(solution)/shard_map/ppermute | solution.py:16
  112.2 1.5 collective-permute-start.15
  113.8 1.2 broadcast_in_dim.31
  115.0 0.7 bitcast_dynamic-update-slice_fusion.4
  115.7 4.5 %turn_kernel.1.kernels = bf16[4,80,3456]{2,1,0:T(8,128)(2,1)} custom-call(bf16[4,160,720]{2,1,0:T(8,128)(2,1)} %copy-done.1, bf16[4,160,720]{2,1,0:T(8,128)(2,1)} %copy-done.5), custom_call_target="tpu_custom_call" | custom-call | flops 235929600 | bytes 4194304 | tf_op jit(solution)/shard_map/turn_kernel/pallas_call | solution.py:298
  120.2 2.9 %collective-permute-start.16 = (bf16[16,80,128]{2,1,0:T(8,128)(2,1)S(1)}, bf16[16,80,128]{2,1,0:T(8,128)(2,1)S(1)}, u32[]{:S(2)}, u32[]{:S(2)}) collective-permute-start(bf16[16,80,128]{2,1,0:T(8,128)(2,1)S(1)} %copy-done.8), channel_id=1, source_target_pairs={{0,6},{2,0},{4,2},{6,4},{1,7},{3,1},{5,3},{7,5},{8,14},{10,8},{12,... | collective-permute-start | bytes 983048 | tf_op jit(solution)/shard_map/ppermute | solution.py:16
  123.1 0.6 copy-done.20
  123.8 10.6 %conv_backward.1 = (f32[16,80,128]{2,1,0:T(8,128)}, bf16[16,80,128]{2,1,0:T(8,128)(2,1)}, bf16[16,80,128]{2,1,0:T(8,128)(2,1)}, bf16[16,80,128]{2,1,0:T(8,128)(2,1)}) custom-call(s32[4]{0:T(128)} %pad_add_fusion.1.turns, bf16[320,2048]{1,0:T(8,128)(2,1)} %get-tuple-element.24.slope, bf16[1,320,128]{2,1,0:T(8,128)(2,1)} %copy-done.19, ...), custom_call_target="tpu_custom_call" | custom-call | flops 3774873600 | bytes 8388608 | tf_op jit(solution)/shard_map/conv_backward/pallas_call | solution.py:385
  134.4 8.1 %collective-permute-start.22 = (bf16[16,80,128]{2,1,0:T(8,128)(2,1)}, bf16[16,80,128]{2,1,0:T(8,128)(2,1)S(1)}, u32[]{:S(2)}, u32[]{:S(2)}) collective-permute-start(bf16[16,80,128]{2,1,0:T(8,128)(2,1)} %get-tuple-element.28), channel_id=1, source_target_pairs={{0,2},{2,4},{4,6},{6,0},{1,3},{3,5},{5,7},{7,1},{8,10},{10,12},{12... | collective-permute-start | bytes 983048 | tf_op jit(solution)/shard_map/ppermute | solution.py:16
  142.8 0.8 bitcast_dynamic-update-slice_fusion.3
  143.5 0.7 bitcast_dynamic-update-slice_fusion.2
  144.3 0.2 add.266
  144.6 2.4 %collective-permute-start.26 = (f32[9,40,320]{2,1,0:T(8,128)S(1)}, f32[9,40,320]{2,1,0:T(8,128)S(1)}, u32[]{:S(2)}, u32[]{:S(2)}) collective-permute-start(f32[9,40,320]{2,1,0:T(8,128)S(1)} %get-tuple-element.33), channel_id=1, source_target_pairs={{0,24},{8,0},{16,8},{24,16},{1,25},{9,1},{17,9},{25,17},{2,26},{10... | collective-permute-start | bytes 1382408 | tf_op jit(solution)/shard_map/ppermute | solution.py:16
  147.0 1.5 collective-permute-start.27
  148.5 0.7 bitcast_dynamic-update-slice_fusion.1
  149.3 6.5 %collective-permute-start.24 = (bf16[16,80,128]{2,1,0:T(8,128)(2,1)S(1)}, bf16[16,80,128]{2,1,0:T(8,128)(2,1)S(1)}, u32[]{:S(2)}, u32[]{:S(2)}) collective-permute-start(bf16[16,80,128]{2,1,0:T(8,128)(2,1)S(1)} %copy-done.9), channel_id=1, source_target_pairs={{0,6},{2,0},{4,2},{6,4},{1,7},{3,1},{5,3},{7,5},{8,14},{10,8},{12,... | collective-permute-start | bytes 983048 | tf_op jit(solution)/shard_map/ppermute | solution.py:16
  155.8 3.1 %collective-permute-done.26 = f32[9,40,320]{2,1,0:T(8,128)S(1)} collective-permute-done((f32[9,40,320]{2,1,0:T(8,128)S(1)}, f32[9,40,320]{2,1,0:T(8,128)S(1)}, u32[]{:S(2)}, u32[]{:S(2)}) %collective-permute-start.26) | collective-permute-done | bytes 460832 | tf_op jit(solution)/shard_map/ppermute | solution.py:16
  158.9 7.3 %collective-permute-done.27 = f32[9,40,320]{2,1,0:T(8,128)S(1)} collective-permute-done((f32[9,40,320]{2,1,0:T(8,128)S(1)}, f32[9,40,320]{2,1,0:T(8,128)S(1)}, u32[]{:S(2)}, u32[]{:S(2)}) %collective-permute-start.27) | collective-permute-done | bytes 460832 | tf_op jit(solution)/shard_map/ppermute | solution.py:16
  166.2 0.2 fusion.3
  166.4 0.2 fusion.10
  166.6 11.4 %collective-permute-start.29 = (f32[80,360]{0,1:T(8,128)S(1)}, f32[80,360]{0,1:T(8,128)S(1)}, u32[]{:S(2)}, u32[]{:S(2)}) collective-permute-start(f32[80,360]{0,1:T(8,128)S(1)} %bitcast.123), channel_id=1, source_target_pairs={{0,6},{2,0},{4,2},{6,4},{1,7},{3,1},{5,3},{7,5},{8,14},{10,8},{12,... | collective-permute-start | bytes 345608 | tf_op jit(solution)/shard_map/ppermute | solution.py:16
  177.9 0.6 collective-permute-start.31
  178.6 3.3 %collective-permute-done.29 = f32[80,360]{0,1:T(8,128)S(1)} collective-permute-done((f32[80,360]{0,1:T(8,128)S(1)}, f32[80,360]{0,1:T(8,128)S(1)}, u32[]{:S(2)}, u32[]{:S(2)}) %collective-permute-start.29) | collective-permute-done | bytes 115232 | tf_op jit(solution)/shard_map/ppermute | solution.py:16
  182.0 8.6 %collective-permute-done.30 = f32[80,360]{0,1:T(8,128)S(1)} collective-permute-done((f32[80,360]{0,1:T(8,128)S(1)}, f32[80,360]{0,1:T(8,128)S(1)}, u32[]{:S(2)}, u32[]{:S(2)}) %collective-permute-start.30) | collective-permute-done | bytes 115232 | tf_op jit(solution)/shard_map/ppermute | solution.py:16
  190.7 1.3 collective-permute-done.32
  192.2 0.8 copy.9
  (80 shorter events, 1.6 us)
Async XLA Ops:
  0.6 0.9 copy-start
  0.6 17.4 %copy-start.4 = (bf16[1,64,80,128]{3,2,1,0:T(8,128)(2,1)S(1)}, bf16[1,64,80,128]{3,2,1,0:T(8,128)(2,1)}, u32[]{:S(2)}) copy-start(bf16[1,64,80,128]{3,2,1,0:T(8,128)(2,1)} %param.3) | copy-start | bytes 3932164
  1.8 7.5 %collective-permute-start.7 = (bf16[40,720]{1,0:T(8,128)(2,1)S(1)}, bf16[40,720]{1,0:T(8,128)(2,1)S(1)}, u32[]{:S(2)}, u32[]{:S(2)}) collective-permute-start(bf16[40,720]{1,0:T(8,128)(2,1)S(1)} %copy.10), channel_id=1, source_target_pairs={{0,6},{2,0},{4,2},{6,4},{1,7},{3,1},{5,3},{7,5},{8,14},{10,8},{12,... | collective-permute-start | bytes 172808 | tf_op jit(solution)/shard_map/ppermute | solution.py:16
  6.9 5.5 %collective-permute-start.8 = (bf16[40,720]{1,0:T(8,128)(2,1)S(1)}, bf16[40,720]{1,0:T(8,128)(2,1)S(1)}, u32[]{:S(2)}, u32[]{:S(2)}) collective-permute-start(bf16[40,720]{1,0:T(8,128)(2,1)S(1)} %copy.10), channel_id=1, source_target_pairs={{0,4},{2,6},{4,0},{6,2},{1,5},{3,7},{5,1},{7,3},{8,12},{10,14},{12... | collective-permute-start | bytes 172808 | tf_op jit(solution)/shard_map/ppermute | solution.py:16
  6.9 6.1 %collective-permute-start.9 = (bf16[40,720]{1,0:T(8,128)(2,1)S(1)}, bf16[40,720]{1,0:T(8,128)(2,1)S(1)}, u32[]{:S(2)}, u32[]{:S(2)}) collective-permute-start(bf16[40,720]{1,0:T(8,128)(2,1)S(1)} %copy.10), channel_id=1, source_target_pairs={{0,2},{2,4},{4,6},{6,0},{1,3},{3,5},{5,7},{7,1},{8,10},{10,12},{12... | collective-permute-start | bytes 172808 | tf_op jit(solution)/shard_map/ppermute | solution.py:16
  13.1 8.8 %collective-permute-start.10 = (bf16[160,720]{1,0:T(8,128)(2,1)S(1)}, bf16[160,720]{1,0:T(8,128)(2,1)S(1)}, u32[]{:S(2)}, u32[]{:S(2)}) collective-permute-start(bf16[160,720]{1,0:T(8,128)(2,1)S(1)} %get-tuple-element.65), channel_id=1, source_target_pairs={{0,24},{8,0},{16,8},{24,16},{1,25},{9,1},{17,9},{25,17},{2,26},{10... | collective-permute-start | bytes 691208 | tf_op jit(solution)/shard_map/ppermute | solution.py:16
  15.6 11.8 %collective-permute-start.11 = (bf16[160,720]{1,0:T(8,128)(2,1)S(1)}, bf16[160,720]{1,0:T(8,128)(2,1)S(1)}, u32[]{:S(2)}, u32[]{:S(2)}) collective-permute-start(bf16[160,720]{1,0:T(8,128)(2,1)S(1)} %get-tuple-element.65), channel_id=1, source_target_pairs={{0,16},{8,24},{16,0},{24,8},{1,17},{9,25},{17,1},{25,9},{2,18},{10... | collective-permute-start | bytes 691208 | tf_op jit(solution)/shard_map/ppermute | solution.py:16
  16.1 11.8 %collective-permute-start.12 = (bf16[160,720]{1,0:T(8,128)(2,1)S(1)}, bf16[160,720]{1,0:T(8,128)(2,1)S(1)}, u32[]{:S(2)}, u32[]{:S(2)}) collective-permute-start(bf16[160,720]{1,0:T(8,128)(2,1)S(1)} %get-tuple-element.65), channel_id=1, source_target_pairs={{0,8},{8,16},{16,24},{24,0},{1,9},{9,17},{17,25},{25,1},{2,10},{10... | collective-permute-start | bytes 691208 | tf_op jit(solution)/shard_map/ppermute | solution.py:16
  18.0 14.7 %collective-permute-start.3 = (bf16[1,80,128]{2,1,0:T(8,128)(2,1)}, bf16[1,80,128]{2,1,0:T(8,128)(2,1)}, u32[]{:S(2)}, u32[]{:S(2)}) collective-permute-start(bf16[1,80,128]{2,1,0:T(8,128)(2,1)} %select_bitcast_fusion), channel_id=1, source_target_pairs={{0,1},{1,0},{2,3},{3,2},{4,5},{5,4},{6,7},{7,6},{8,9},{9,8},{10,11... | collective-permute-start | bytes 61448 | tf_op jit(solution)/shard_map/ppermute | solution.py:16
  19.1 46.8 %collective-permute-start = (bf16[16,80,128]{2,1,0:T(8,128)(2,1)}, bf16[16,80,128]{2,1,0:T(8,128)(2,1)}, u32[]{:S(2)}, u32[]{:S(2)}) collective-permute-start(bf16[16,80,128]{2,1,0:T(8,128)(2,1)} %get-tuple-element.58), channel_id=1, source_target_pairs={{0,6},{2,0},{4,2},{6,4},{1,7},{3,1},{5,3},{7,5},{8,14},{10,8},{12,... | collective-permute-start | bytes 983048 | tf_op jit(solution)/shard_map/ppermute | solution.py:16
  21.9 44.0 %collective-permute-start.1 = (bf16[16,80,128]{2,1,0:T(8,128)(2,1)}, bf16[16,80,128]{2,1,0:T(8,128)(2,1)}, u32[]{:S(2)}, u32[]{:S(2)}) collective-permute-start(bf16[16,80,128]{2,1,0:T(8,128)(2,1)} %get-tuple-element.57), channel_id=1, source_target_pairs={{0,4},{2,6},{4,0},{6,2},{1,5},{3,7},{5,1},{7,3},{8,12},{10,14},{12... | collective-permute-start | bytes 983048 | tf_op jit(solution)/shard_map/ppermute | solution.py:16
  27.4 39.7 %collective-permute-start.2 = (bf16[16,80,128]{2,1,0:T(8,128)(2,1)}, bf16[16,80,128]{2,1,0:T(8,128)(2,1)}, u32[]{:S(2)}, u32[]{:S(2)}) collective-permute-start(bf16[16,80,128]{2,1,0:T(8,128)(2,1)} %get-tuple-element.56), channel_id=1, source_target_pairs={{0,2},{2,4},{4,6},{6,0},{1,3},{3,5},{5,7},{7,1},{8,10},{10,12},{12... | collective-permute-start | bytes 983048 | tf_op jit(solution)/shard_map/ppermute | solution.py:16
  28.0 39.1 %copy-start.1 = (bf16[4,160,720]{2,1,0:T(8,128)(2,1)}, bf16[4,160,720]{2,1,0:T(8,128)(2,1)S(1)}, u32[]{:S(2)}) copy-start(bf16[4,160,720]{2,1,0:T(8,128)(2,1)S(1)} %pad_maximum_fusion.refs_8_.refs_0_) | copy-start | bytes 2764804
  28.0 39.1 %collective-permute-start.13 = (bf16[4,160,720]{2,1,0:T(8,128)(2,1)S(1)}, bf16[4,160,720]{2,1,0:T(8,128)(2,1)S(1)}, u32[]{:S(2)}, u32[]{:S(2)}) collective-permute-start(bf16[4,160,720]{2,1,0:T(8,128)(2,1)S(1)} %pad_maximum_fusion.refs_8_.refs_0_), channel_id=1, source_target_pairs={{0,1},{1,0},{2,3},{3,2},{4,5},{5,4},{6,7},{7,6},{8,9},{9,8},{10,11... | collective-permute-start | bytes 2764808 | tf_op jit(solution)/shard_map/ppermute | solution.py:16
  34.3 12.3 %collective-permute-start.6 = (bf16[4,80,128]{2,1,0:T(8,128)(2,1)S(1)}, bf16[4,80,128]{2,1,0:T(8,128)(2,1)S(1)}, u32[]{:S(2)}, u32[]{:S(2)}) collective-permute-start(bf16[4,80,128]{2,1,0:T(8,128)(2,1)S(1)} %pad_maximum_fusion.5), channel_id=1, source_target_pairs={{0,2},{2,4},{4,6},{6,0},{1,3},{3,5},{5,7},{7,1},{8,10},{10,12},{12... | collective-permute-start | bytes 245768 | tf_op jit(solution)/shard_map/ppermute | solution.py:16
  46.6 20.5 %copy-start.16 = (bf16[4,80,128]{2,1,0:T(8,128)(2,1)}, bf16[4,80,128]{2,1,0:T(8,128)(2,1)S(1)}, u32[]{:S(2)}) copy-start(bf16[4,80,128]{2,1,0:T(8,128)(2,1)S(1)} %collective-permute-done.6.refs_7_) | copy-start | bytes 245764
  46.6 13.0 %collective-permute-start.5 = (bf16[4,80,128]{2,1,0:T(8,128)(2,1)S(1)}, bf16[4,80,128]{2,1,0:T(8,128)(2,1)S(1)}, u32[]{:S(2)}, u32[]{:S(2)}) collective-permute-start(bf16[4,80,128]{2,1,0:T(8,128)(2,1)S(1)} %pad_maximum_fusion.4), channel_id=1, source_target_pairs={{0,4},{2,6},{4,0},{6,2},{1,5},{3,7},{5,1},{7,3},{8,12},{10,14},{12... | collective-permute-start | bytes 245768 | tf_op jit(solution)/shard_map/ppermute | solution.py:16
  59.6 7.5 %copy-start.17 = (bf16[4,80,128]{2,1,0:T(8,128)(2,1)}, bf16[4,80,128]{2,1,0:T(8,128)(2,1)S(1)}, u32[]{:S(2)}) copy-start(bf16[4,80,128]{2,1,0:T(8,128)(2,1)S(1)} %collective-permute-done.5.refs_6_) | copy-start | bytes 245764
  59.6 4.4 %collective-permute-start.4 = (bf16[4,80,128]{2,1,0:T(8,128)(2,1)S(1)}, bf16[4,80,128]{2,1,0:T(8,128)(2,1)S(1)}, u32[]{:S(2)}, u32[]{:S(2)}) collective-permute-start(bf16[4,80,128]{2,1,0:T(8,128)(2,1)S(1)} %pad_maximum_fusion.3), channel_id=1, source_target_pairs={{0,6},{2,0},{4,2},{6,4},{1,7},{3,1},{5,3},{7,5},{8,14},{10,8},{12,... | collective-permute-start | bytes 245768 | tf_op jit(solution)/shard_map/ppermute | solution.py:16
  64.1 3.0 %copy-start.18 = (bf16[4,80,128]{2,1,0:T(8,128)(2,1)}, bf16[4,80,128]{2,1,0:T(8,128)(2,1)S(1)}, u32[]{:S(2)}) copy-start(bf16[4,80,128]{2,1,0:T(8,128)(2,1)S(1)} %collective-permute-done.4.refs_5_) | copy-start | bytes 245764
  64.1 16.3 %collective-permute-start.17 = (bf16[14,80,128]{2,1,0:T(8,128)(2,1)}, bf16[14,80,128]{2,1,0:T(8,128)(2,1)S(1)}, u32[]{:S(2)}, u32[]{:S(2)}) collective-permute-start(bf16[14,80,128]{2,1,0:T(8,128)(2,1)} %get-tuple-element.45), channel_id=1, source_target_pairs={{0,6},{2,0},{4,2},{6,4},{1,7},{3,1},{5,3},{7,5},{8,14},{10,8},{12,... | collective-permute-start | bytes 860168 | tf_op jit(solution)/shard_map/ppermute | solution.py:16
  65.9 23.6 %collective-permute-start.18 = (bf16[14,80,128]{2,1,0:T(8,128)(2,1)}, bf16[14,80,128]{2,1,0:T(8,128)(2,1)S(1)}, u32[]{:S(2)}, u32[]{:S(2)}) collective-permute-start(bf16[14,80,128]{2,1,0:T(8,128)(2,1)} %get-tuple-element.47), channel_id=1, source_target_pairs={{0,4},{2,6},{4,0},{6,2},{1,5},{3,7},{5,1},{7,3},{8,12},{10,14},{12... | collective-permute-start | bytes 860168 | tf_op jit(solution)/shard_map/ppermute | solution.py:16
  65.9 23.6 %collective-permute-start.19 = (bf16[14,80,128]{2,1,0:T(8,128)(2,1)}, bf16[14,80,128]{2,1,0:T(8,128)(2,1)S(1)}, u32[]{:S(2)}, u32[]{:S(2)}) collective-permute-start(bf16[14,80,128]{2,1,0:T(8,128)(2,1)} %get-tuple-element.44), channel_id=1, source_target_pairs={{0,2},{2,4},{4,6},{6,0},{1,3},{3,5},{5,7},{7,1},{8,10},{10,12},{12... | collective-permute-start | bytes 860168 | tf_op jit(solution)/shard_map/ppermute | solution.py:16
  67.1 1.0 copy-start.5
  80.4 9.2 %copy-start.11 = (bf16[14,80,128]{2,1,0:T(8,128)(2,1)}, bf16[14,80,128]{2,1,0:T(8,128)(2,1)S(1)}, u32[]{:S(2)}) copy-start(bf16[14,80,128]{2,1,0:T(8,128)(2,1)S(1)} %collective-permute-done.17.refs_1_) | copy-start | bytes 860164
  89.5 0.7 copy-start.12
  89.6 0.8 copy-start.13
  90.4 14.3 %copy-start.15 = (bf16[1,320,128]{2,1,0:T(8,128)(2,1)S(1)}, bf16[1,320,128]{2,1,0:T(8,128)(2,1)}, u32[]{:S(2)}) copy-start(bf16[1,320,128]{2,1,0:T(8,128)(2,1)} %get-tuple-element.25) | copy-start | bytes 245764
  90.4 17.5 %copy-start.14 = (bf16[1,320,128]{2,1,0:T(8,128)(2,1)S(1)}, bf16[1,320,128]{2,1,0:T(8,128)(2,1)}, u32[]{:S(2)}) copy-start(bf16[1,320,128]{2,1,0:T(8,128)(2,1)} %get-tuple-element.26) | copy-start | bytes 245764
  90.4 24.6 %copy-start.7 = (bf16[16,80,128]{2,1,0:T(8,128)(2,1)S(1)}, bf16[16,80,128]{2,1,0:T(8,128)(2,1)}, u32[]{:S(2)}) copy-start(bf16[16,80,128]{2,1,0:T(8,128)(2,1)} %get-tuple-element.18) | copy-start | bytes 983044
  103.9 40.3 %collective-permute-start.25 = (f32[4,9,40,320]{3,2,1,0:T(8,128)}, f32[4,9,40,320]{3,2,1,0:T(8,128)S(1)}, u32[]{:S(2)}, u32[]{:S(2)}) collective-permute-start(f32[4,9,40,320]{3,2,1,0:T(8,128)} %get-tuple-element.32), channel_id=1, source_target_pairs={{0,1},{1,0},{2,3},{3,2},{4,5},{5,4},{6,7},{7,6},{8,9},{9,8},{10,11... | collective-permute-start | bytes 5529608 | tf_op jit(solution)/shard_map/ppermute | solution.py:16
  104.7 15.5 %collective-permute-start.20 = (bf16[1,320,128]{2,1,0:T(8,128)(2,1)S(1)}, bf16[1,320,128]{2,1,0:T(8,128)(2,1)S(1)}, u32[]{:S(2)}, u32[]{:S(2)}) collective-permute-start(bf16[1,320,128]{2,1,0:T(8,128)(2,1)S(1)} %copy-done.15), channel_id=1, source_target_pairs={{0,2},{2,4},{4,6},{6,7},{7,5},{5,3},{3,1},{8,10},{10,12},{12,14},{... | collective-permute-start | bytes 245768 | tf_op jit(solution)/shard_map/ppermute | solution.py:517
  107.9 15.3 %collective-permute-start.21 = (bf16[1,320,128]{2,1,0:T(8,128)(2,1)S(1)}, bf16[1,320,128]{2,1,0:T(8,128)(2,1)S(1)}, u32[]{:S(2)}, u32[]{:S(2)}) collective-permute-start(bf16[1,320,128]{2,1,0:T(8,128)(2,1)S(1)} %copy-done.14), channel_id=1, source_target_pairs={{2,0},{4,2},{6,4},{7,6},{5,7},{3,5},{1,3},{10,8},{12,10},{14,12},{... | collective-permute-start | bytes 245768 | tf_op jit(solution)/shard_map/ppermute | solution.py:518
  109.2 33.5 %collective-permute-start.14 = (bf16[16,80,128]{2,1,0:T(8,128)(2,1)}, bf16[16,80,128]{2,1,0:T(8,128)(2,1)S(1)}, u32[]{:S(2)}, u32[]{:S(2)}) collective-permute-start(bf16[16,80,128]{2,1,0:T(8,128)(2,1)} %get-tuple-element.19), channel_id=1, source_target_pairs={{0,2},{2,4},{4,6},{6,0},{1,3},{3,5},{5,7},{7,1},{8,10},{10,12},{12... | collective-permute-start | bytes 983048 | tf_op jit(solution)/shard_map/ppermute | solution.py:16
  112.2 31.3 %collective-permute-start.15 = (bf16[16,80,128]{2,1,0:T(8,128)(2,1)}, bf16[16,80,128]{2,1,0:T(8,128)(2,1)S(1)}, u32[]{:S(2)}, u32[]{:S(2)}) collective-permute-start(bf16[16,80,128]{2,1,0:T(8,128)(2,1)} %get-tuple-element.20), channel_id=1, source_target_pairs={{0,4},{2,6},{4,0},{6,2},{1,5},{3,7},{5,1},{7,3},{8,12},{10,14},{12... | collective-permute-start | bytes 983048 | tf_op jit(solution)/shard_map/ppermute | solution.py:16
  115.7 4.5 %copy-start.8 = (bf16[16,80,128]{2,1,0:T(8,128)(2,1)S(1)}, bf16[16,80,128]{2,1,0:T(8,128)(2,1)}, u32[]{:S(2)}) copy-start(bf16[16,80,128]{2,1,0:T(8,128)(2,1)} %get-tuple-element.21) | copy-start | bytes 983044
  120.2 2.9 %copy-start.19 = (bf16[1,320,128]{2,1,0:T(8,128)(2,1)}, bf16[1,320,128]{2,1,0:T(8,128)(2,1)S(1)}, u32[]{:S(2)}) copy-start(bf16[1,320,128]{2,1,0:T(8,128)(2,1)S(1)} %collective-permute-done.20.above) | copy-start | bytes 245764
  120.2 28.3 %collective-permute-start.16 = (bf16[16,80,128]{2,1,0:T(8,128)(2,1)S(1)}, bf16[16,80,128]{2,1,0:T(8,128)(2,1)S(1)}, u32[]{:S(2)}, u32[]{:S(2)}) collective-permute-start(bf16[16,80,128]{2,1,0:T(8,128)(2,1)S(1)} %copy-done.8), channel_id=1, source_target_pairs={{0,6},{2,0},{4,2},{6,4},{1,7},{3,1},{5,3},{7,5},{8,14},{10,8},{12,... | collective-permute-start | bytes 983048 | tf_op jit(solution)/shard_map/ppermute | solution.py:16
  123.1 0.6 copy-start.20
  134.3 8.2 %copy-start.6 = (f32[16,80,128]{2,1,0:T(8,128)S(1)}, f32[16,80,128]{2,1,0:T(8,128)}, u32[]{:S(2)}) copy-start(f32[16,80,128]{2,1,0:T(8,128)} %get-tuple-element.27) | copy-start | bytes 1966084
  134.4 8.3 %copy-start.10 = (bf16[16,80,128]{2,1,0:T(8,128)(2,1)S(1)}, bf16[16,80,128]{2,1,0:T(8,128)(2,1)}, u32[]{:S(2)}) copy-start(bf16[16,80,128]{2,1,0:T(8,128)(2,1)} %get-tuple-element.29) | copy-start | bytes 983044
  134.4 14.9 %collective-permute-start.22 = (bf16[16,80,128]{2,1,0:T(8,128)(2,1)}, bf16[16,80,128]{2,1,0:T(8,128)(2,1)S(1)}, u32[]{:S(2)}, u32[]{:S(2)}) collective-permute-start(bf16[16,80,128]{2,1,0:T(8,128)(2,1)} %get-tuple-element.28), channel_id=1, source_target_pairs={{0,2},{2,4},{4,6},{6,0},{1,3},{3,5},{5,7},{7,1},{8,10},{10,12},{12... | collective-permute-start | bytes 983048 | tf_op jit(solution)/shard_map/ppermute | solution.py:16
  142.4 1.9 copy-start.3
  142.7 35.9 %collective-permute-start.23 = (bf16[16,80,128]{2,1,0:T(8,128)(2,1)S(1)}, bf16[16,80,128]{2,1,0:T(8,128)(2,1)S(1)}, u32[]{:S(2)}, u32[]{:S(2)}) collective-permute-start(bf16[16,80,128]{2,1,0:T(8,128)(2,1)S(1)} %copy-done.10), channel_id=1, source_target_pairs={{0,4},{2,6},{4,0},{6,2},{1,5},{3,7},{5,1},{7,3},{8,12},{10,14},{12... | collective-permute-start | bytes 983048 | tf_op jit(solution)/shard_map/ppermute | solution.py:16
  144.5 4.8 %copy-start.9 = (bf16[16,80,128]{2,1,0:T(8,128)(2,1)S(1)}, bf16[16,80,128]{2,1,0:T(8,128)(2,1)}, u32[]{:S(2)}) copy-start(bf16[16,80,128]{2,1,0:T(8,128)(2,1)} %get-tuple-element.30) | copy-start | bytes 983044
  144.6 14.3 %collective-permute-start.26 = (f32[9,40,320]{2,1,0:T(8,128)S(1)}, f32[9,40,320]{2,1,0:T(8,128)S(1)}, u32[]{:S(2)}, u32[]{:S(2)}) collective-permute-start(f32[9,40,320]{2,1,0:T(8,128)S(1)} %get-tuple-element.33), channel_id=1, source_target_pairs={{0,24},{8,0},{16,8},{24,16},{1,25},{9,1},{17,9},{25,17},{2,26},{10... | collective-permute-start | bytes 1382408 | tf_op jit(solution)/shard_map/ppermute | solution.py:16
  147.0 19.2 %collective-permute-start.27 = (f32[9,40,320]{2,1,0:T(8,128)S(1)}, f32[9,40,320]{2,1,0:T(8,128)S(1)}, u32[]{:S(2)}, u32[]{:S(2)}) collective-permute-start(f32[9,40,320]{2,1,0:T(8,128)S(1)} %get-tuple-element.35), channel_id=1, source_target_pairs={{0,16},{8,24},{16,0},{24,8},{1,17},{9,25},{17,1},{25,9},{2,18},{10... | collective-permute-start | bytes 1382408 | tf_op jit(solution)/shard_map/ppermute | solution.py:16
  148.5 17.6 %collective-permute-start.28 = (f32[9,40,320]{2,1,0:T(8,128)S(1)}, f32[9,40,320]{2,1,0:T(8,128)S(1)}, u32[]{:S(2)}, u32[]{:S(2)}) collective-permute-start(f32[9,40,320]{2,1,0:T(8,128)S(1)} %get-tuple-element.34), channel_id=1, source_target_pairs={{0,8},{8,16},{16,24},{24,0},{1,9},{9,17},{17,25},{25,1},{2,10},{10... | collective-permute-start | bytes 1382408 | tf_op jit(solution)/shard_map/ppermute | solution.py:16
  149.3 41.4 %collective-permute-start.24 = (bf16[16,80,128]{2,1,0:T(8,128)(2,1)S(1)}, bf16[16,80,128]{2,1,0:T(8,128)(2,1)S(1)}, u32[]{:S(2)}, u32[]{:S(2)}) collective-permute-start(bf16[16,80,128]{2,1,0:T(8,128)(2,1)S(1)} %copy-done.9), channel_id=1, source_target_pairs={{0,6},{2,0},{4,2},{6,4},{1,7},{3,1},{5,3},{7,5},{8,14},{10,8},{12,... | collective-permute-start | bytes 983048 | tf_op jit(solution)/shard_map/ppermute | solution.py:16
  166.6 15.4 %collective-permute-start.29 = (f32[80,360]{0,1:T(8,128)S(1)}, f32[80,360]{0,1:T(8,128)S(1)}, u32[]{:S(2)}, u32[]{:S(2)}) collective-permute-start(f32[80,360]{0,1:T(8,128)S(1)} %bitcast.123), channel_id=1, source_target_pairs={{0,6},{2,0},{4,2},{6,4},{1,7},{3,1},{5,3},{7,5},{8,14},{10,8},{12,... | collective-permute-start | bytes 345608 | tf_op jit(solution)/shard_map/ppermute | solution.py:16
  177.9 12.6 %collective-permute-start.30 = (f32[80,360]{0,1:T(8,128)S(1)}, f32[80,360]{0,1:T(8,128)S(1)}, u32[]{:S(2)}, u32[]{:S(2)}) collective-permute-start(f32[80,360]{0,1:T(8,128)S(1)} %bitcast.122), channel_id=1, source_target_pairs={{0,4},{2,6},{4,0},{6,2},{1,5},{3,7},{5,1},{7,3},{8,12},{10,14},{12... | collective-permute-start | bytes 345608 | tf_op jit(solution)/shard_map/ppermute | solution.py:16
  177.9 12.6 %collective-permute-start.31 = (f32[80,360]{0,1:T(8,128)S(1)}, f32[80,360]{0,1:T(8,128)S(1)}, u32[]{:S(2)}, u32[]{:S(2)}) collective-permute-start(f32[80,360]{0,1:T(8,128)S(1)} %bitcast.121), channel_id=1, source_target_pairs={{0,2},{2,4},{4,6},{6,0},{1,3},{3,5},{5,7},{7,1},{8,10},{10,12},{12... | collective-permute-start | bytes 345608 | tf_op jit(solution)/shard_map/ppermute | solution.py:16
  190.6 1.5 collective-permute-start.32
  190.7 2.2 %copy-start.2 = (f32[1,64,80,128]{3,2,1,0:T(8,128)}, f32[1,64,80,128]{3,2,1,0:T(8,128)S(1)}, u32[]{:S(2)}) copy-start(f32[1,64,80,128]{3,2,1,0:T(8,128)S(1)} %convert_dynamic-update-slice_fusion) | copy-start | bytes 7864324

commit v4 on v3

--- a/solution.py
+++ b/solution.py
@@ -145,27 +145,34 @@
     return pl.BlockSpec(shape, lambda *_: (0,) * len(shape), pipeline_mode=pl.Buffered(1))
 
 
-def forward(turns, pieces, rims, halves):
+def forward(turns, pieces, rims, halves, slab):
     count = len(pieces)
     height, depth, width = pieces[0].shape
     channels = count * depth
     rows = 4 if height % 4 == 0 else 1
     flops = 2 * 9 * channels * channels * height * width
+    steps = height // rows
     call = pl.pallas_call(
         functools.partial(forward_body, count, len(halves), rows),
-        grid=(height // rows,),
-        in_specs=[pl.BlockSpec(memory_space=pltpu.SMEM)]
-        + [whole(pieces[0].shape)] * count
-        + [whole(rims[0].shape)] * count
-        + [whole(halves[0].shape)] * len(halves),
-        out_specs=[pl.BlockSpec((rows, depth, width), lambda g: (g, 0, 0))] * count
-        + [
-            pl.BlockSpec((rows, channels, width), lambda g: (g, 0, 0)),
-            whole((3 * channels, (height + 2) * width)),
-            whole((1, channels, width)),
-            whole((1, channels, width)),
-        ],
-        out_shape=[jax.ShapeDtypeStruct((height, depth, width), jnp.bfloat16)] * count
+        grid_spec=pltpu.PrefetchScalarGridSpec(
+            num_scalar_prefetch=1,
+            grid=(steps,),
+            in_specs=[whole(pieces[0].shape)] * count
+            + [whole(rims[0].shape)] * count
+            + [whole(halves[0].shape)] * len(halves),
+            out_specs=[pl.BlockSpec((rows, depth, width), lambda g, turns: (turns[2] * steps + g, 0, 0))]
+            + [pl.BlockSpec((rows, depth, width), lambda g, _: (g, 0, 0))] * (count - 1)
+            + [
+                pl.BlockSpec((rows, channels, width), lambda g, _: (g, 0, 0)),
+                whole((3 * channels, (height + 2) * width)),
+                whole((1, channels, width)),
+                whole((1, channels, width)),
+            ],
+        ),
+        out_shape=[
+            jax.ShapeDtypeStruct((height if j else slab, depth, width), jnp.bfloat16)
+            for j in range(count)
+        ]
         + [
             jax.ShapeDtypeStruct((height, channels, width), jnp.float32),
             jax.ShapeDtypeStruct((3 * channels, (height + 2) * width), jnp.bfloat16),
@@ -179,36 +186,50 @@
         name="conv_forward",
     )
     results = call(turns, *pieces, *rims, *halves)
-    return results[:count], *results[count:]
-
-
-def correlate_body(count, groups, rows, turn, stacked, factor, *refs):
-    pieces, ends = refs[:count], refs[count : 2 * count]
-    shares, slope = refs[2 * count : -1], refs[-1]
-    height, depth, width = factor.shape[0], pieces[0].shape[1], factor.shape[2]
-    channels = count * depth
-    tap_row, tap_col = pl.program_id(0), pl.program_id(1)
-
-    @pl.when((tap_row == 0) & (tap_col == 0))
-    def _():
-        def put(row, blocks):
-            lanes = pl.ds(pl.multiple_of(row * width, width), width)
-            for j in range(count):
-                part_of = pl.ds(j * depth, depth)
-                value = blocks[j].astype(jnp.float32) * factor[row, part_of, :]
-                slope[part_of, lanes] = value.astype(jnp.bfloat16)
-
-        def body(row, carry):
-            put(row + 1, [piece[row] for piece in pieces])
-            return carry
-
-        put(0, [end[2] for end in ends])
-        lax.fori_loop(0, height - 2, body, 0)
-        put(height - 1, [end[3] for end in ends])
+    return list(results[:count]), *results[count:]
+
+
+def slope_rows(factor, pieces, ends, slope):
+    count = len(pieces)
+    height, _, width = factor.shape
+    depth = pieces[0].shape[1]
+
+    def put(row, blocks):
+        lanes = pl.ds(pl.multiple_of(row * width, width), width)
+        for j in range(count):
+            part_of = pl.ds(j * depth, depth)
+            value = blocks[j].astype(jnp.float32) * factor[row, part_of, :]
+            slope[part_of, lanes] = value.astype(jnp.bfloat16)
+
+    def body(row, carry):
+        put(row + 1, [piece[row] for piece in pieces])
+        return carry
+
+    put(0, [end[2] for end in ends])
+    lax.fori_loop(0, height - 2, body, 0)
+    put(height - 1, [end[3] for end in ends])
+
+
+def correlate_body(first_tap, count, groups, rows, turn, stacked, *refs):
+    if count:
+        factor, pieces, ends = refs[0], refs[1 : 1 + count], refs[1 + count : 1 + 2 * count]
+        shares, slope = refs[1 + 2 * count : -1], refs[-1]
+    else:
+        slope, shares = refs[0], refs[1:]
+    channels, pixels = slope.shape
+    width = stacked.shape[1] - pixels
+    width = width // 2
+    tap = first_tap + pl.program_id(0)
+    tap_row, tap_col = tap // 3, lax.rem(tap, 3)
+    if count:
+
+        @pl.when(pl.program_id(0) == 0)
+        def _():
+            slope_rows(factor, pieces, ends, slope)
 
     source = stacked[
         pl.ds(pl.multiple_of(tap_col * channels, channels), channels),
-        pl.ds(pl.multiple_of(tap_row * width, width), height * width),
+        pl.ds(pl.multiple_of(tap_row * width, width), pixels),
     ]
     grads = lax.dot_general(
         source, slope[...], (((1,), (1,)), ((), ())), preferred_element_type=jnp.float32
@@ -224,33 +245,38 @@
                     shares[j][group, 0] = grads[start : start + size]
 
 
-def correlate(stacked, factor, pieces, ends):
-    count = len(pieces)
-    height, channels, width = factor.shape
+def correlate(taps, stacked, slope=None, factor=None, pieces=(), ends=()):
+    first_tap, tap_count = taps
+    channels = stacked.shape[0] // 3
     groups, rows = lax.axis_size("dp"), lax.axis_size("row")
     size = channels // (groups * rows)
-    flops = 2 * 9 * channels * channels * height * width
+    if slope is None:
+        height, _, width = factor.shape
+        pixels = height * width
+        operands = [factor, *pieces, *ends]
+        made = [jax.ShapeDtypeStruct((channels, pixels), jnp.bfloat16)]
+    else:
+        pixels = slope.shape[1]
+        operands, made = [slope], []
     call = pl.pallas_call(
-        functools.partial(correlate_body, count, groups, rows),
-        grid=(3, 3),
-        in_specs=[pl.BlockSpec(memory_space=pltpu.SMEM)]
-        + [whole(stacked.shape), whole(factor.shape)]
-        + [whole(pieces[0].shape)] * count
-        + [whole(ends[0].shape)] * count,
-        out_specs=[pl.BlockSpec((groups, 1, size, channels), lambda a, b: (0, 3 * a + b, 0, 0))]
-        * rows
-        + [whole((channels, height * width))],
-        out_shape=[jax.ShapeDtypeStruct((groups, 9, size, channels), jnp.float32)] * rows
-        + [jax.ShapeDtypeStruct((channels, height * width), jnp.bfloat16)],
+        functools.partial(correlate_body, first_tap, len(pieces), groups, rows),
+        grid=(tap_count,),
+        in_specs=[pl.BlockSpec(memory_space=pltpu.SMEM), whole(stacked.shape)]
+        + [whole(operand.shape) for operand in operands],
+        out_specs=[pl.BlockSpec((groups, 1, size, channels), lambda t: (0, t, 0, 0))] * rows
+        + [whole(each.shape) for each in made],
+        out_shape=[jax.ShapeDtypeStruct((groups, tap_count, size, channels), jnp.float32)] * rows
+        + made,
         compiler_params=pltpu.CompilerParams(vmem_limit_bytes=VMEM_LIMIT),
         cost_estimate=pl.CostEstimate(
-            flops=flops, bytes_accessed=14 * 1024 * 1024, transcendentals=0
-        ),
-        name="kernel_grad",
+            flops=2 * tap_count * channels * channels * pixels,
+            bytes_accessed=8 * 1024 * 1024,
+            transcendentals=0,
+        ),
     )
     turn = lax.axis_index("row").astype(jnp.int32)[None]
-    results = call(turn, stacked, factor, *pieces, *ends)
-    return results[:-1], results[-1]
+    results = call(turn, stacked, *operands)
+    return (results[:rows], *results[rows:])
 
 
 def padded_depth(depth):
@@ -375,29 +401,31 @@
             outs[j][row] = grad[j * depth : (j + 1) * depth, lanes].astype(outs[j].dtype)
 
 
-def backward(turns, slope, above, below, kernels, count):
+def backward(turns, slope, above, below, kernels, count, slab):
     channels = slope.shape[0]
     width = above.shape[2]
     height = slope.shape[1] // width
     depth = channels // count
     rows = 4 if height % 4 == 0 else 1
     flops = 2 * 9 * channels * channels * height * width
+    steps = height // rows
     return pl.pallas_call(
         functools.partial(backward_body, count, lax.axis_size("row"), rows),
-        grid=(height // rows,),
-        in_specs=[
-            pl.BlockSpec(memory_space=pltpu.SMEM),
-            whole(slope.shape),
-            whole(above.shape),
-            whole(below.shape),
-            whole(kernels.shape),
-        ],
-        out_specs=[pl.BlockSpec((rows, depth, width), lambda g: (g, 0, 0))] * count,
-        out_shape=[
-            jax.ShapeDtypeStruct((height, depth, width), jnp.bfloat16 if j else jnp.float32)
-            for j in range(count)
-        ],
-        scratch_shapes=[pltpu.VMEM((kernels.shape[2] // 3, (height + 2) * width), jnp.bfloat16)],
+        grid_spec=pltpu.PrefetchScalarGridSpec(
+            num_scalar_prefetch=1,
+            grid=(steps,),
+            in_specs=[
+                whole(slope.shape),
+                whole(above.shape),
+                whole(below.shape),
+                whole(kernels.shape),
+            ],
+            out_specs=[pl.BlockSpec((rows, depth, width), lambda g, turns: (turns[4] * steps + g, 0, 0))]
+            + [pl.BlockSpec((rows, depth, width), lambda g, _: (g, 0, 0))] * (count - 1),
+            scratch_shapes=[pltpu.VMEM((kernels.shape[2] // 3, (height + 2) * width), jnp.bfloat16)],
+        ),
+        out_shape=[jax.ShapeDtypeStruct((slab, depth, width), jnp.float32)]
+        + [jax.ShapeDtypeStruct((height, depth, width), jnp.bfloat16)] * (count - 1),
         compiler_params=pltpu.CompilerParams(vmem_limit_bytes=VMEM_LIMIT),
         cost_estimate=pl.CostEstimate(
             flops=flops, bytes_accessed=8 * 1024 * 1024, transcendentals=0
@@ -423,11 +451,9 @@
     return [over_dp] + [receive(over_dp, "row", j) for j in range(1, rows)]
 
 
-def summed_kernel_grad(shares, inner, outer):
-    dp, row = lax.axis_index("dp"), lax.axis_index("row")
+def summed_over_images(shares):
+    dp = lax.axis_index("dp")
     dps, chans, rows = (lax.axis_size(a) for a in ("dp", "chan", "row"))
-    channels = shares[0].shape[3]
-    share = inner // rows
     halves = shares[0]
     for j in range(1, rows):
         halves = halves + receive(shares[j], "row", j)
@@ -440,6 +466,15 @@
     total = of_dp(0)
     for j in range(1, dps):
         total = total + receive(of_dp(-j), "dp", j)
+    return total
+
+
+def summed_kernel_grad(terms, inner, outer):
+    row = lax.axis_index("row")
+    chans, rows = lax.axis_size("chan"), lax.axis_size("row")
+    share = inner // rows
+    channels = terms[0].shape[2]
+    total = jnp.concatenate(terms)
     total = jnp.transpose(total, (2, 0, 1)).reshape(channels, 9 * share)
     own = total[:outer]
     for j in range(1, chans):
@@ -453,7 +488,7 @@
 def shards(images, kernel, cotangent):
     row, chan = lax.axis_index("row"), lax.axis_index("chan")
     rows, chans = lax.axis_size("row"), lax.axis_size("chan")
-    _, slab, depth, width = images.shape
+    _, slab, _, _ = images.shape
     height = slab // chans
     images, cotangent = images[0], cotangent[0]
 
@@ -502,10 +537,10 @@
     forth = jnp.where(row % 2 == 0, 1, chans - 1)
     above_turn = jnp.where(place_at == 0, 0, forth)
     below_turn = jnp.where(place_at == chans - 1, 0, chans - forth)
-    turns = jnp.stack([shift, row]).astype(jnp.int32)
-    back_turns = jnp.stack([above_turn, below_turn, shift, row]).astype(jnp.int32)
-
-    results = forward(turns, pieces, rims, halves)
+    turns = jnp.stack([shift, row, place_at]).astype(jnp.int32)
+    back_turns = jnp.stack([above_turn, below_turn, shift, row, place_at]).astype(jnp.int32)
+
+    results = forward(turns, pieces, rims, halves, slab)
     activated, factor, stacked, first, last = results
     back_kernel = turned(halves)
 
@@ -517,18 +552,22 @@
     above = lax.ppermute(last, ("chan", "row"), line)
     below = lax.ppermute(first, ("chan", "row"), [(b, a) for a, b in line])
 
-    grads, slope = correlate(stacked, factor, cotangents, rims)
-    input_grads = backward(back_turns, slope, above, below, back_kernel, chans)
-    kernel_grad = summed_kernel_grad(grads, kernel.shape[1], kernel.shape[2])
-
-    def to_owners(blocks, dtype):
-        out = jnp.zeros((slab, depth, width), dtype)
-        for j in range(chans):
-            arrived = receive(blocks[j], "chan", chans - j) if j else blocks[0]
-            out = lax.dynamic_update_slice_in_dim(out, arrived.astype(dtype), home(-j) * height, 0)
+    lead, slope = correlate((0, 4), stacked, None, factor, cotangents, rims)
+    lead = summed_over_images(lead)
+    input_grads = list(backward(back_turns, slope, above, below, back_kernel, chans, slab))
+    slope, input_grads[1] = lax.optimization_barrier((slope, input_grads[1]))
+    (rest,) = correlate((4, 5), stacked, slope)
+    rest = summed_over_images(rest)
+    kernel_grad = summed_kernel_grad([lead, rest], kernel.shape[1], kernel.shape[2])
+
+    def to_owners(blocks):
+        out = blocks[0]
+        for j in range(1, chans):
+            arrived = receive(blocks[j], "chan", chans - j).astype(out.dtype)
+            out = lax.dynamic_update_slice_in_dim(out, arrived, home(-j) * height, 0)
         return out[None]
 
-    return to_owners(activated, jnp.bfloat16), to_owners(input_grads, jnp.float32), kernel_grad
+    return to_owners(activated), to_owners(input_grads), kernel_grad
 
 
 def solution(mesh):

time: 194 us -> 210 us (1.082)
  waiting for transfers between devices: 59.5 us -> 75 us
  starting transfers between devices: 70.8 us -> 66.2 us
  Pallas kernels: 40.9 us -> 45.4 us
    ppermute x31 -> x35, starting transfers between devices: 66.4 us -> 48 us  [receive(): lax.ppermute(block, axis, [(i, (i - ahead) % count) for i in range(count)])]
    ppermute x31 -> x35, waiting for transfers between devices: 59.5 us -> 75 us  [receive(): lax.ppermute(block, axis, [(i, (i - ahead) % count) for i in range(count)])]
    ppermute x1, starting transfers between devices: 3.14 us -> 16.9 us  [shards(): above = lax.ppermute(last, ('chan', 'row'), line)]
    pallas_call x1 -> x2, Pallas kernels: 13.6 us -> 16.7 us  [correlate(): results = call(turn, stacked, *operands)]
  transfers between devices with their start and end apart: 33 -> 37, of which waited for: 14 -> 18; matrix products, arithmetic and copies ran while one was open for 8% -> 8% of each run, Pallas kernels for 14% -> 22%
where the time goes in v4:
time: 210 us; the launch traced here: 209 us
  waiting for transfers between devices  75 us (36%)
  starting transfers between devices  66.2 us (32%)
  Pallas kernels  45.4 us (22%)
  local copies, waits for them, and re-layouts  15 us (7%)
  other arithmetic  6.06 us (3%)
    ppermute x35, waiting for transfers between devices, receive(): lax.ppermute(block, axis, [(i, (i - ahead) % count) for i in range(count)])  75 us
    ppermute x35, starting transfers between devices, receive(): lax.ppermute(block, axis, [(i, (i - ahead) % count) for i in range(count)])  48 us
    ppermute x1, starting transfers between devices, shards(): above = lax.ppermute(last, ('chan', 'row'), line)  16.9 us
    pallas_call x2, Pallas kernels, correlate(): results = call(turn, stacked, *operands)  16.7 us
    pallas_call x1, Pallas kernels, forward(): results = call(turns, *pieces, *rims, *halves)  12.9 us
    pallas_call x1, Pallas kernels, backward(): pl.pallas_call(functools.partial(backward_body, count, lax.axis_size('row...  11.3 us
    pallas_call x1, Pallas kernels, turned(): pl.pallas_call(functools.partial(turned_body, shares), grid=(blocks,), in...  4.49 us
  transfers between devices with their start and end apart: 37, of which 18 were waited for; matrix products, arithmetic and copies ran while one was open for 8% of the time, Pallas kernels for 22%

profile of v4, /device:TPU:0, one launch (start us, length us, event | category | flops | bytes accessed | tf_op | source)
XLA Modules:
  0.0 208.7 jit_solution(12694528252103134822)
XLA Ops:
  0.7 0.9 copy-done
  1.8 3.1 %collective-permute-start.9 = (bf16[40,720]{1,0:T(8,128)(2,1)S(1)}, bf16[40,720]{1,0:T(8,128)(2,1)S(1)}, u32[]{:S(2)}, u32[]{:S(2)}) collective-permute-start(bf16[40,720]{1,0:T(8,128)(2,1)S(1)} %copy.10), channel_id=1, source_target_pairs={{0,2},{2,4},{4,6},{6,0},{1,3},{3,5},{5,7},{7,1},{8,10},{10,12},{12... | collective-permute-start | bytes 172808 | tf_op jit(solution)/shard_map/ppermute | solution.py:16
  4.9 2.6 %collective-permute-start.8 = (bf16[40,720]{1,0:T(8,128)(2,1)S(1)}, bf16[40,720]{1,0:T(8,128)(2,1)S(1)}, u32[]{:S(2)}, u32[]{:S(2)}) collective-permute-start(bf16[40,720]{1,0:T(8,128)(2,1)S(1)} %copy.10), channel_id=1, source_target_pairs={{0,4},{2,6},{4,0},{6,2},{1,5},{3,7},{5,1},{7,3},{8,12},{10,14},{12... | collective-permute-start | bytes 172808 | tf_op jit(solution)/shard_map/ppermute | solution.py:16
  7.5 1.3 collective-permute-start.7
  9.3 2.5 %collective-permute-done.8 = bf16[40,720]{1,0:T(8,128)(2,1)S(1)} collective-permute-done((bf16[40,720]{1,0:T(8,128)(2,1)S(1)}, bf16[40,720]{1,0:T(8,128)(2,1)S(1)}, u32[]{:S(2)}, u32[]{:S(2)}) %collective-permute-start.8) | collective-permute-done | bytes 57632 | tf_op jit(solution)/shard_map/ppermute | solution.py:16
  12.1 1.5 collective-permute-start.12
  13.6 1.5 collective-permute-start.11
  15.1 1.4 collective-permute-start.10
  16.6 1.1 dynamic-slice_bitcast_fusion
  17.6 2.9 %collective-permute-start = (bf16[16,80,128]{2,1,0:T(8,128)(2,1)}, bf16[16,80,128]{2,1,0:T(8,128)(2,1)}, u32[]{:S(2)}, u32[]{:S(2)}) collective-permute-start(bf16[16,80,128]{2,1,0:T(8,128)(2,1)} %get-tuple-element.63), channel_id=1, source_target_pairs={{0,6},{2,0},{4,2},{6,4},{1,7},{3,1},{5,3},{7,5},{8,14},{10,8},{12,... | collective-permute-start | bytes 983048 | tf_op jit(solution)/shard_map/ppermute | solution.py:16
  21.2 0.7 collective-permute-done.12
  21.9 1.4 collective-permute-start.2
  23.3 2.0 collective-permute-done.11
  25.3 0.7 copy-done.9
  26.0 1.1 pad_maximum_fusion.refs_8_.refs_0_
  27.6 2.3 %dynamic-slice_bitcast_fusion.4 = (bf16[14,80,128]{2,1,0:T(8,128)(2,1)}, bf16[14,80,128]{2,1,0:T(8,128)(2,1)}, bf16[14,80,128]{2,1,0:T(8,128)(2,1)}, bf16[14,80,128]{2,1,0:T(8,128)(2,1)}) fusion(bf16[1,64,80,128]{3,2,1,0:T(8,128)(2,1)} %param.5, s32[]{:T(128)S(6)} %select_n.333, s32[]{:T(128)S(6)} %select_n.331, s32[]{:T(128)S(6)} %select_n.330, ...), kind=kLoop, calls=%fused_computation.26 | loop fusion | bytes 2293776 | tf_op jit(solution)/shard_map/dynamic_slice | solution.py:531
  29.9 1.5 dynamic-slice_bitcast_fusion.9
  31.4 0.7 pad_add_fusion.turns
  32.1 0.7 stack.57.turns
  32.8 0.7 bitcast_select_fusion.1
  33.5 0.8 pad_maximum_fusion.3
  34.3 2.2 %collective-permute-start.4 = (bf16[4,80,128]{2,1,0:T(8,128)(2,1)S(1)}, bf16[4,80,128]{2,1,0:T(8,128)(2,1)S(1)}, u32[]{:S(2)}, u32[]{:S(2)}) collective-permute-start(bf16[4,80,128]{2,1,0:T(8,128)(2,1)S(1)} %pad_maximum_fusion.3), channel_id=1, source_target_pairs={{0,6},{2,0},{4,2},{6,4},{1,7},{3,1},{5,3},{7,5},{8,14},{10,8},{12,... | collective-permute-start | bytes 245768 | tf_op jit(solution)/shard_map/ppermute | solution.py:16
  36.5 0.8 pad_maximum_fusion.4
  37.3 9.3 %collective-permute-done.4.refs_5_.refs_6_ = bf16[4,80,128]{2,1,0:T(8,128)(2,1)S(1)} collective-permute-done((bf16[4,80,128]{2,1,0:T(8,128)(2,1)S(1)}, bf16[4,80,128]{2,1,0:T(8,128)(2,1)S(1)}, u32[]{:S(2)}, u32[]{:S(2)}) %collective-permute-start.4) | collective-permute-done | bytes 81952 | tf_op jit(solution)/shard_map/ppermute | solution.py:16
  46.6 2.9 %collective-permute-start.5 = (bf16[4,80,128]{2,1,0:T(8,128)(2,1)S(1)}, bf16[4,80,128]{2,1,0:T(8,128)(2,1)S(1)}, u32[]{:S(2)}, u32[]{:S(2)}) collective-permute-start(bf16[4,80,128]{2,1,0:T(8,128)(2,1)S(1)} %pad_maximum_fusion.4), channel_id=1, source_target_pairs={{0,4},{2,6},{4,0},{6,2},{1,5},{3,7},{5,1},{7,3},{8,12},{10,14},{12... | collective-permute-start | bytes 245768 | tf_op jit(solution)/shard_map/ppermute | solution.py:16
  49.6 3.3 %collective-permute-done.5.refs_6_.refs_7_ = bf16[4,80,128]{2,1,0:T(8,128)(2,1)S(1)} collective-permute-done((bf16[4,80,128]{2,1,0:T(8,128)(2,1)S(1)}, bf16[4,80,128]{2,1,0:T(8,128)(2,1)S(1)}, u32[]{:S(2)}, u32[]{:S(2)}) %collective-permute-start.5) | collective-permute-done | bytes 81952 | tf_op jit(solution)/shard_map/ppermute | solution.py:16
  52.9 3.0 %collective-permute-start.6 = (bf16[4,80,128]{2,1,0:T(8,128)(2,1)S(1)}, bf16[4,80,128]{2,1,0:T(8,128)(2,1)S(1)}, u32[]{:S(2)}, u32[]{:S(2)}) collective-permute-start(bf16[4,80,128]{2,1,0:T(8,128)(2,1)S(1)} %pad_maximum_fusion.5), channel_id=1, source_target_pairs={{0,2},{2,4},{4,6},{6,0},{1,3},{3,5},{5,7},{7,1},{8,10},{10,12},{12... | collective-permute-start | bytes 245768 | tf_op jit(solution)/shard_map/ppermute | solution.py:16
  55.9 0.6 pad_maximum_fusion.2.refs_4_.refs_5_
  56.6 3.4 %collective-permute-done.6.refs_7_.refs_8_ = bf16[4,80,128]{2,1,0:T(8,128)(2,1)S(1)} collective-permute-done((bf16[4,80,128]{2,1,0:T(8,128)(2,1)S(1)}, bf16[4,80,128]{2,1,0:T(8,128)(2,1)S(1)}, u32[]{:S(2)}, u32[]{:S(2)}) %collective-permute-start.6) | collective-permute-done | bytes 81952 | tf_op jit(solution)/shard_map/ppermute | solution.py:16
  60.0 1.0 collective-permute-start.17
  61.0 1.5 collective-permute-start.18
  62.5 1.0 copy-done.5
  63.5 12.9 %conv_forward.1 = (bf16[64,80,128]{2,1,0:T(8,128)(2,1)}, bf16[16,80,128]{2,1,0:T(8,128)(2,1)}, bf16[16,80,128]{2,1,0:T(8,128)(2,1)}, bf16[16,80,128]{2,1,0:T(8,1...) custom-call(s32[3]{0:T(128)} %pad_add_fusion.turns, ...), custom_call_target="tpu_custom_call" | custom-call | flops 3774873600 | bytes 16777216 | tf_op jit(solution)/shard_map/conv_forward/pallas_call | solution.py:188
  76.4 2.1 collective-permute-start.14
  78.5 2.4 %collective-permute-start.15 = (bf16[16,80,128]{2,1,0:T(8,128)(2,1)}, bf16[16,80,128]{2,1,0:T(8,128)(2,1)}, u32[]{:S(2)}, u32[]{:S(2)}) collective-permute-start(bf16[16,80,128]{2,1,0:T(8,128)(2,1)} %get-tuple-element.24), channel_id=1, source_target_pairs={{0,4},{2,6},{4,0},{6,2},{1,5},{3,7},{5,1},{7,3},{8,12},{10,14},{12... | collective-permute-start | bytes 983048 | tf_op jit(solution)/shard_map/ppermute | solution.py:16
  80.9 16.9 %collective-permute-start.20 = (bf16[1,320,128]{2,1,0:T(8,128)(2,1)}, bf16[1,320,128]{2,1,0:T(8,128)(2,1)S(1)}, u32[]{:S(2)}, u32[]{:S(2)}) collective-permute-start(bf16[1,320,128]{2,1,0:T(8,128)(2,1)} %get-tuple-element.29), channel_id=1, source_target_pairs={{0,2},{2,4},{4,6},{6,7},{7,5},{5,3},{3,1},{8,10},{10,12},{12,14},{... | collective-permute-start | bytes 245768 | tf_op jit(solution)/shard_map/ppermute | solution.py:552
  97.8 3.7 %collective-permute-done.18.refs_3_ = bf16[14,80,128]{2,1,0:T(8,128)(2,1)S(1)} collective-permute-done((bf16[14,80,128]{2,1,0:T(8,128)(2,1)}, bf16[14,80,128]{2,1,0:T(8,128)(2,1)S(1)}, u32[]{:S(2)}, u32[]{:S(2)}) %collective-permute-start.18) | collective-permute-done | bytes 286752 | tf_op jit(solution)/shard_map/ppermute | solution.py:16
  101.5 1.3 collective-permute-start.21
  102.8 0.7 copy-done.8
  103.5 8.8 %shard_map.58 = (f32[4,4,40,320]{3,2,1,0:T(8,128)}, f32[4,4,40,320]{3,2,1,0:T(8,128)}, bf16[320,2048]{1,0:T(8,128)(2,1)}) custom-call(s32[1]{0:T(128)} %bitcast.1.turn, bf16[960,2304]{1,0:T(8,128)(2,1)} %get-tuple-element.26.stacked, f32[16,320,128]{2,1,0:T(8,128)} %get-tuple-element.27.refs_0_, bf16[14,80,128]{2,1,0:T(8,128)(2,1)} %get-tuple-element.51.refs_1_, ...), custom_call_target="tpu_custom_call" | custom-call | flops 1677721600 | bytes 8388608 | tf_op jit(solution)/shard_map/pallas_call | solution.py:278
  112.3 4.5 %turn_kernel.1.kernels = bf16[4,80,3456]{2,1,0:T(8,128)(2,1)} custom-call(bf16[4,160,720]{2,1,0:T(8,128)(2,1)} %copy-done.1, bf16[4,160,720]{2,1,0:T(8,128)(2,1)} %copy-done.5), custom_call_target="tpu_custom_call" | custom-call | flops 235929600 | bytes 4194304 | tf_op jit(solution)/shard_map/turn_kernel/pallas_call | solution.py:324
  117.5 11.3 %conv_backward.1 = (f32[64,80,128]{2,1,0:T(8,128)}, bf16[16,80,128]{2,1,0:T(8,128)(2,1)}, bf16[16,80,128]{2,1,0:T(8,128)(2,1)}, bf16[16,80,128]{2,1,0:T(8,128)(2,1)}) custom-call(s32[5]{0:T(128)} %stack.57.turns, bf16[320,2048]{1,0:T(8,128)(2,1)} %get-tuple-element.38.slope.refs_0_, bf16[1,320,128]{2,1,0:T(8,128)(2,1)} %copy-done.17, ...), custom_call_target="tpu_custom_call" | custom-call | flops 3774873600 | bytes 8388608 | tf_op jit(solution)/shard_map/conv_backward/pallas_call | solution.py:412
  128.8 8.0 %shard_map.59 = (f32[4,5,40,320]{3,2,1,0:T(8,128)}, f32[4,5,40,320]{3,2,1,0:T(8,128)}) custom-call(s32[1]{0:T(128)} %bitcast.1.turn, bf16[960,2304]{1,0:T(8,128)(2,1)} %get-tuple-element.26.stacked, bf16[320,2048]{1,0:T(8,128)(2,1)} %get-tuple-element.38.slope.refs_0_), custom_call_target="tpu_custom_call" | custom-call | flops 2097152000 | bytes 8388608 | tf_op jit(solution)/shard_map/pallas_call | solution.py:278
  137.3 1.7 collective-permute-start.16
  139.1 0.9 collective-permute-start.22
  140.0 1.7 bitcast_dynamic-update-slice_fusion.2
  141.7 1.7 bitcast_dynamic-update-slice_fusion.1
  143.4 11.7 %collective-permute-done.16 = bf16[16,80,128]{2,1,0:T(8,128)(2,1)S(1)} collective-permute-done((bf16[16,80,128]{2,1,0:T(8,128)(2,1)}, bf16[16,80,128]{2,1,0:T(8,128)(2,1)S(1)}, u32[]{:S(2)}, u32[]{:S(2)}) %collective-permute-start.16) | collective-permute-done | bytes 327712 | tf_op jit(solution)/shard_map/ppermute | solution.py:16
  155.2 0.7 bitcast_dynamic-update-slice_fusion
  157.2 2.6 %collective-permute-start.26 = (f32[4,40,320]{2,1,0:T(8,128)S(1)}, f32[4,40,320]{2,1,0:T(8,128)S(1)}, u32[]{:S(2)}, u32[]{:S(2)}) collective-permute-start(f32[4,40,320]{2,1,0:T(8,128)S(1)} %get-tuple-element.68), channel_id=1, source_target_pairs={{0,24},{8,0},{16,8},{24,16},{1,25},{9,1},{17,9},{25,17},{2,26},{10... | collective-permute-start | bytes 614408 | tf_op jit(solution)/shard_map/ppermute | solution.py:16
  160.2 1.3 collective-permute-start.31
  161.5 4.4 %collective-permute-done.28 = f32[4,40,320]{2,1,0:T(8,128)S(1)} collective-permute-done((f32[4,40,320]{2,1,0:T(8,128)S(1)}, f32[4,40,320]{2,1,0:T(8,128)S(1)}, u32[]{:S(2)}, u32[]{:S(2)}) %collective-permute-start.28) | collective-permute-done | bytes 204832 | tf_op jit(solution)/shard_map/ppermute | solution.py:16
  165.9 5.3 %collective-permute-done.27 = f32[4,40,320]{2,1,0:T(8,128)S(1)} collective-permute-done((f32[4,40,320]{2,1,0:T(8,128)S(1)}, f32[4,40,320]{2,1,0:T(8,128)S(1)}, u32[]{:S(2)}, u32[]{:S(2)}) %collective-permute-start.27) | collective-permute-done | bytes 204832 | tf_op jit(solution)/shard_map/ppermute | solution.py:16
  171.2 0.8 collective-permute-start.23
  172.0 3.3 %collective-permute-start.24 = (bf16[16,80,128]{2,1,0:T(8,128)(2,1)S(1)}, bf16[16,80,128]{2,1,0:T(8,128)(2,1)S(1)}, u32[]{:S(2)}, u32[]{:S(2)}) collective-permute-start(bf16[16,80,128]{2,1,0:T(8,128)(2,1)S(1)} %copy-done.15), channel_id=1, source_target_pairs={{0,6},{2,0},{4,2},{6,4},{1,7},{3,1},{5,3},{7,5},{8,14},{10,8},{12,... | collective-permute-start | bytes 983048 | tf_op jit(solution)/shard_map/ppermute | solution.py:16
  175.3 2.4 %collective-permute-done.32 = f32[5,40,320]{2,1,0:T(8,128)S(1)} collective-permute-done((f32[5,40,320]{2,1,0:T(8,128)S(1)}, f32[5,40,320]{2,1,0:T(8,128)S(1)}, u32[]{:S(2)}, u32[]{:S(2)}) %collective-permute-start.32) | collective-permute-done | bytes 256032 | tf_op jit(solution)/shard_map/ppermute | solution.py:16
  177.7 4.4 %collective-permute-done.31 = f32[5,40,320]{2,1,0:T(8,128)S(1)} collective-permute-done((f32[5,40,320]{2,1,0:T(8,128)S(1)}, f32[5,40,320]{2,1,0:T(8,128)S(1)}, u32[]{:S(2)}, u32[]{:S(2)}) %collective-permute-start.31) | collective-permute-done | bytes 256032 | tf_op jit(solution)/shard_map/ppermute | solution.py:16
  182.6 1.5 collective-permute-start.35
  184.1 2.4 %collective-permute-start.33 = (f32[80,360]{0,1:T(8,128)S(1)}, f32[80,360]{0,1:T(8,128)S(1)}, u32[]{:S(2)}, u32[]{:S(2)}) collective-permute-start(f32[80,360]{0,1:T(8,128)S(1)} %bitcast.132), channel_id=1, source_target_pairs={{0,6},{2,0},{4,2},{6,4},{1,7},{3,1},{5,3},{7,5},{8,14},{10,8},{12,... | collective-permute-start | bytes 345608 | tf_op jit(solution)/shard_map/ppermute | solution.py:16
  186.5 1.8 collective-permute-done.23
  188.4 3.9 %collective-permute-done.35 = f32[80,360]{0,1:T(8,128)S(1)} collective-permute-done((f32[80,360]{0,1:T(8,128)S(1)}, f32[80,360]{0,1:T(8,128)S(1)}, u32[]{:S(2)}, u32[]{:S(2)}) %collective-permute-start.35) | collective-permute-done | bytes 115232 | tf_op jit(solution)/shard_map/ppermute | solution.py:16
  192.3 14.0 %collective-permute-done.34 = f32[80,360]{0,1:T(8,128)S(1)} collective-permute-done((f32[80,360]{0,1:T(8,128)S(1)}, f32[80,360]{0,1:T(8,128)S(1)}, u32[]{:S(2)}, u32[]{:S(2)}) %collective-permute-start.34) | collective-permute-done | bytes 115232 | tf_op jit(solution)/shard_map/ppermute | solution.py:16
  206.5 1.3 collective-permute-done.36
  207.9 0.8 copy.9
  (85 shorter events, 6.0 us)
Async XLA Ops:
  0.6 0.9 copy-start
  0.6 15.9 %copy-start.2 = (bf16[1,64,80,128]{3,2,1,0:T(8,128)(2,1)S(1)}, bf16[1,64,80,128]{3,2,1,0:T(8,128)(2,1)}, u32[]{:S(2)}) copy-start(bf16[1,64,80,128]{3,2,1,0:T(8,128)(2,1)} %param.3) | copy-start | bytes 3932164
  1.8 7.5 %collective-permute-start.9 = (bf16[40,720]{1,0:T(8,128)(2,1)S(1)}, bf16[40,720]{1,0:T(8,128)(2,1)S(1)}, u32[]{:S(2)}, u32[]{:S(2)}) collective-permute-start(bf16[40,720]{1,0:T(8,128)(2,1)S(1)} %copy.10), channel_id=1, source_target_pairs={{0,2},{2,4},{4,6},{6,0},{1,3},{3,5},{5,7},{7,1},{8,10},{10,12},{12... | collective-permute-start | bytes 172808 | tf_op jit(solution)/shard_map/ppermute | solution.py:16
  4.9 6.9 %collective-permute-start.8 = (bf16[40,720]{1,0:T(8,128)(2,1)S(1)}, bf16[40,720]{1,0:T(8,128)(2,1)S(1)}, u32[]{:S(2)}, u32[]{:S(2)}) collective-permute-start(bf16[40,720]{1,0:T(8,128)(2,1)S(1)} %copy.10), channel_id=1, source_target_pairs={{0,4},{2,6},{4,0},{6,2},{1,5},{3,7},{5,1},{7,3},{8,12},{10,14},{12... | collective-permute-start | bytes 172808 | tf_op jit(solution)/shard_map/ppermute | solution.py:16
  7.5 4.6 %collective-permute-start.7 = (bf16[40,720]{1,0:T(8,128)(2,1)S(1)}, bf16[40,720]{1,0:T(8,128)(2,1)S(1)}, u32[]{:S(2)}, u32[]{:S(2)}) collective-permute-start(bf16[40,720]{1,0:T(8,128)(2,1)S(1)} %copy.10), channel_id=1, source_target_pairs={{0,6},{2,0},{4,2},{6,4},{1,7},{3,1},{5,3},{7,5},{8,14},{10,8},{12,... | collective-permute-start | bytes 172808 | tf_op jit(solution)/shard_map/ppermute | solution.py:16
  12.1 9.8 %collective-permute-start.12 = (bf16[160,720]{1,0:T(8,128)(2,1)S(1)}, bf16[160,720]{1,0:T(8,128)(2,1)S(1)}, u32[]{:S(2)}, u32[]{:S(2)}) collective-permute-start(bf16[160,720]{1,0:T(8,128)(2,1)S(1)} %get-tuple-element.76), channel_id=1, source_target_pairs={{0,8},{8,16},{16,24},{24,0},{1,9},{9,17},{17,25},{25,1},{2,10},{10... | collective-permute-start | bytes 691208 | tf_op jit(solution)/shard_map/ppermute | solution.py:16
  13.6 11.6 %collective-permute-start.11 = (bf16[160,720]{1,0:T(8,128)(2,1)S(1)}, bf16[160,720]{1,0:T(8,128)(2,1)S(1)}, u32[]{:S(2)}, u32[]{:S(2)}) collective-permute-start(bf16[160,720]{1,0:T(8,128)(2,1)S(1)} %get-tuple-element.76), channel_id=1, source_target_pairs={{0,16},{8,24},{16,0},{24,8},{1,17},{9,25},{17,1},{25,9},{2,18},{10... | collective-permute-start | bytes 691208 | tf_op jit(solution)/shard_map/ppermute | solution.py:16
  15.1 10.1 %collective-permute-start.10 = (bf16[160,720]{1,0:T(8,128)(2,1)S(1)}, bf16[160,720]{1,0:T(8,128)(2,1)S(1)}, u32[]{:S(2)}, u32[]{:S(2)}) collective-permute-start(bf16[160,720]{1,0:T(8,128)(2,1)S(1)} %get-tuple-element.76), channel_id=1, source_target_pairs={{0,24},{8,0},{16,8},{24,16},{1,25},{9,1},{17,9},{25,17},{2,26},{10... | collective-permute-start | bytes 691208 | tf_op jit(solution)/shard_map/ppermute | solution.py:16
  17.6 43.4 %collective-permute-start = (bf16[16,80,128]{2,1,0:T(8,128)(2,1)}, bf16[16,80,128]{2,1,0:T(8,128)(2,1)}, u32[]{:S(2)}, u32[]{:S(2)}) collective-permute-start(bf16[16,80,128]{2,1,0:T(8,128)(2,1)} %get-tuple-element.63), channel_id=1, source_target_pairs={{0,6},{2,0},{4,2},{6,4},{1,7},{3,1},{5,3},{7,5},{8,14},{10,8},{12,... | collective-permute-start | bytes 983048 | tf_op jit(solution)/shard_map/ppermute | solution.py:16
  20.6 41.9 %collective-permute-start.1 = (bf16[16,80,128]{2,1,0:T(8,128)(2,1)}, bf16[16,80,128]{2,1,0:T(8,128)(2,1)}, u32[]{:S(2)}, u32[]{:S(2)}) collective-permute-start(bf16[16,80,128]{2,1,0:T(8,128)(2,1)} %get-tuple-element.62), channel_id=1, source_target_pairs={{0,4},{2,6},{4,0},{6,2},{1,5},{3,7},{5,1},{7,3},{8,12},{10,14},{12... | collective-permute-start | bytes 983048 | tf_op jit(solution)/shard_map/ppermute | solution.py:16
  21.9 40.6 %collective-permute-start.2 = (bf16[16,80,128]{2,1,0:T(8,128)(2,1)}, bf16[16,80,128]{2,1,0:T(8,128)(2,1)}, u32[]{:S(2)}, u32[]{:S(2)}) collective-permute-start(bf16[16,80,128]{2,1,0:T(8,128)(2,1)} %get-tuple-element.61), channel_id=1, source_target_pairs={{0,2},{2,4},{4,6},{6,0},{1,3},{3,5},{5,7},{7,1},{8,10},{10,12},{12... | collective-permute-start | bytes 983048 | tf_op jit(solution)/shard_map/ppermute | solution.py:16
  25.3 7.5 %collective-permute-start.3 = (bf16[1,80,128]{2,1,0:T(8,128)(2,1)}, bf16[1,80,128]{2,1,0:T(8,128)(2,1)}, u32[]{:S(2)}, u32[]{:S(2)}) collective-permute-start(bf16[1,80,128]{2,1,0:T(8,128)(2,1)} %select_bitcast_fusion), channel_id=1, source_target_pairs={{0,1},{1,0},{2,3},{3,2},{4,5},{5,4},{6,7},{7,6},{8,9},{9,8},{10,11... | collective-permute-start | bytes 61448 | tf_op jit(solution)/shard_map/ppermute | solution.py:16
  25.3 0.7 copy-start.9
  27.1 4.4 %copy-start.1 = (bf16[4,160,720]{2,1,0:T(8,128)(2,1)}, bf16[4,160,720]{2,1,0:T(8,128)(2,1)S(1)}, u32[]{:S(2)}) copy-start(bf16[4,160,720]{2,1,0:T(8,128)(2,1)S(1)} %pad_maximum_fusion.refs_8_.refs_0_) | copy-start | bytes 2764804
  27.1 35.4 %collective-permute-start.13 = (bf16[4,160,720]{2,1,0:T(8,128)(2,1)S(1)}, bf16[4,160,720]{2,1,0:T(8,128)(2,1)S(1)}, u32[]{:S(2)}, u32[]{:S(2)}) collective-permute-start(bf16[4,160,720]{2,1,0:T(8,128)(2,1)S(1)} %pad_maximum_fusion.refs_8_.refs_0_), channel_id=1, source_target_pairs={{0,1},{1,0},{2,3},{3,2},{4,5},{5,4},{6,7},{7,6},{8,9},{9,8},{10,11... | collective-permute-start | bytes 2764808 | tf_op jit(solution)/shard_map/ppermute | solution.py:16
  34.3 12.3 %collective-permute-start.4 = (bf16[4,80,128]{2,1,0:T(8,128)(2,1)S(1)}, bf16[4,80,128]{2,1,0:T(8,128)(2,1)S(1)}, u32[]{:S(2)}, u32[]{:S(2)}) collective-permute-start(bf16[4,80,128]{2,1,0:T(8,128)(2,1)S(1)} %pad_maximum_fusion.3), channel_id=1, source_target_pairs={{0,6},{2,0},{4,2},{6,4},{1,7},{3,1},{5,3},{7,5},{8,14},{10,8},{12,... | collective-permute-start | bytes 245768 | tf_op jit(solution)/shard_map/ppermute | solution.py:16
  46.6 15.9 %copy-start.10 = (bf16[4,80,128]{2,1,0:T(8,128)(2,1)}, bf16[4,80,128]{2,1,0:T(8,128)(2,1)S(1)}, u32[]{:S(2)}) copy-start(bf16[4,80,128]{2,1,0:T(8,128)(2,1)S(1)} %collective-permute-done.4.refs_5_.refs_6_) | copy-start | bytes 245764
  46.6 6.3 %collective-permute-start.5 = (bf16[4,80,128]{2,1,0:T(8,128)(2,1)S(1)}, bf16[4,80,128]{2,1,0:T(8,128)(2,1)S(1)}, u32[]{:S(2)}, u32[]{:S(2)}) collective-permute-start(bf16[4,80,128]{2,1,0:T(8,128)(2,1)S(1)} %pad_maximum_fusion.4), channel_id=1, source_target_pairs={{0,4},{2,6},{4,0},{6,2},{1,5},{3,7},{5,1},{7,3},{8,12},{10,14},{12... | collective-permute-start | bytes 245768 | tf_op jit(solution)/shard_map/ppermute | solution.py:16
  52.9 9.6 %copy-start.11 = (bf16[4,80,128]{2,1,0:T(8,128)(2,1)}, bf16[4,80,128]{2,1,0:T(8,128)(2,1)S(1)}, u32[]{:S(2)}) copy-start(bf16[4,80,128]{2,1,0:T(8,128)(2,1)S(1)} %collective-permute-done.5.refs_6_.refs_7_) | copy-start | bytes 245764
  52.9 7.1 %collective-permute-start.6 = (bf16[4,80,128]{2,1,0:T(8,128)(2,1)S(1)}, bf16[4,80,128]{2,1,0:T(8,128)(2,1)S(1)}, u32[]{:S(2)}, u32[]{:S(2)}) collective-permute-start(bf16[4,80,128]{2,1,0:T(8,128)(2,1)S(1)} %pad_maximum_fusion.5), channel_id=1, source_target_pairs={{0,2},{2,4},{4,6},{6,0},{1,3},{3,5},{5,7},{7,1},{8,10},{10,12},{12... | collective-permute-start | bytes 245768 | tf_op jit(solution)/shard_map/ppermute | solution.py:16
  60.0 2.5 %copy-start.12 = (bf16[4,80,128]{2,1,0:T(8,128)(2,1)}, bf16[4,80,128]{2,1,0:T(8,128)(2,1)S(1)}, u32[]{:S(2)}) copy-start(bf16[4,80,128]{2,1,0:T(8,128)(2,1)S(1)} %collective-permute-done.6.refs_7_.refs_8_) | copy-start | bytes 245764
  60.0 20.9 %collective-permute-start.17 = (bf16[14,80,128]{2,1,0:T(8,128)(2,1)}, bf16[14,80,128]{2,1,0:T(8,128)(2,1)S(1)}, u32[]{:S(2)}, u32[]{:S(2)}) collective-permute-start(bf16[14,80,128]{2,1,0:T(8,128)(2,1)} %get-tuple-element.50), channel_id=1, source_target_pairs={{0,6},{2,0},{4,2},{6,4},{1,7},{3,1},{5,3},{7,5},{8,14},{10,8},{12,... | collective-permute-start | bytes 860168 | tf_op jit(solution)/shard_map/ppermute | solution.py:16
  61.0 40.5 %collective-permute-start.18 = (bf16[14,80,128]{2,1,0:T(8,128)(2,1)}, bf16[14,80,128]{2,1,0:T(8,128)(2,1)S(1)}, u32[]{:S(2)}, u32[]{:S(2)}) collective-permute-start(bf16[14,80,128]{2,1,0:T(8,128)(2,1)} %get-tuple-element.52), channel_id=1, source_target_pairs={{0,4},{2,6},{4,0},{6,2},{1,5},{3,7},{5,1},{7,3},{8,12},{10,14},{12... | collective-permute-start | bytes 860168 | tf_op jit(solution)/shard_map/ppermute | solution.py:16
  62.5 40.3 %collective-permute-start.19 = (bf16[14,80,128]{2,1,0:T(8,128)(2,1)}, bf16[14,80,128]{2,1,0:T(8,128)(2,1)S(1)}, u32[]{:S(2)}, u32[]{:S(2)}) collective-permute-start(bf16[14,80,128]{2,1,0:T(8,128)(2,1)} %get-tuple-element.49), channel_id=1, source_target_pairs={{0,2},{2,4},{4,6},{6,0},{1,3},{3,5},{5,7},{7,1},{8,10},{10,12},{12... | collective-permute-start | bytes 860168 | tf_op jit(solution)/shard_map/ppermute | solution.py:16
  62.5 1.0 copy-start.5
  76.4 62.6 %collective-permute-start.14 = (bf16[16,80,128]{2,1,0:T(8,128)(2,1)}, bf16[16,80,128]{2,1,0:T(8,128)(2,1)}, u32[]{:S(2)}, u32[]{:S(2)}) collective-permute-start(bf16[16,80,128]{2,1,0:T(8,128)(2,1)} %get-tuple-element.23), channel_id=1, source_target_pairs={{0,2},{2,4},{4,6},{6,0},{1,3},{3,5},{5,7},{7,1},{8,10},{10,12},{12... | collective-permute-start | bytes 983048 | tf_op jit(solution)/shard_map/ppermute | solution.py:16
  78.5 63.2 %collective-permute-start.15 = (bf16[16,80,128]{2,1,0:T(8,128)(2,1)}, bf16[16,80,128]{2,1,0:T(8,128)(2,1)}, u32[]{:S(2)}, u32[]{:S(2)}) collective-permute-start(bf16[16,80,128]{2,1,0:T(8,128)(2,1)} %get-tuple-element.24), channel_id=1, source_target_pairs={{0,4},{2,6},{4,0},{6,2},{1,5},{3,7},{5,1},{7,3},{8,12},{10,14},{12... | collective-permute-start | bytes 983048 | tf_op jit(solution)/shard_map/ppermute | solution.py:16
  80.9 21.9 %copy-start.6 = (bf16[14,80,128]{2,1,0:T(8,128)(2,1)}, bf16[14,80,128]{2,1,0:T(8,128)(2,1)S(1)}, u32[]{:S(2)}) copy-start(bf16[14,80,128]{2,1,0:T(8,128)(2,1)S(1)} %collective-permute-done.17.refs_2_) | copy-start | bytes 860164
  80.9 35.9 %collective-permute-start.20 = (bf16[1,320,128]{2,1,0:T(8,128)(2,1)}, bf16[1,320,128]{2,1,0:T(8,128)(2,1)S(1)}, u32[]{:S(2)}, u32[]{:S(2)}) collective-permute-start(bf16[1,320,128]{2,1,0:T(8,128)(2,1)} %get-tuple-element.29), channel_id=1, source_target_pairs={{0,2},{2,4},{4,6},{6,7},{7,5},{5,3},{3,1},{8,10},{10,12},{12,14},{... | collective-permute-start | bytes 245768 | tf_op jit(solution)/shard_map/ppermute | solution.py:552
  101.5 1.3 copy-start.7
  101.5 15.3 %collective-permute-start.21 = (bf16[1,320,128]{2,1,0:T(8,128)(2,1)}, bf16[1,320,128]{2,1,0:T(8,128)(2,1)S(1)}, u32[]{:S(2)}, u32[]{:S(2)}) collective-permute-start(bf16[1,320,128]{2,1,0:T(8,128)(2,1)} %get-tuple-element.30), channel_id=1, source_target_pairs={{2,0},{4,2},{6,4},{7,6},{5,7},{3,5},{1,3},{10,8},{12,10},{14,12},{... | collective-permute-start | bytes 245768 | tf_op jit(solution)/shard_map/ppermute | solution.py:553
  102.8 0.7 copy-start.8
  112.2 43.7 %collective-permute-start.25 = (f32[4,4,40,320]{3,2,1,0:T(8,128)}, f32[4,4,40,320]{3,2,1,0:T(8,128)S(1)}, u32[]{:S(2)}, u32[]{:S(2)}) collective-permute-start(f32[4,4,40,320]{3,2,1,0:T(8,128)} %get-tuple-element.37), channel_id=1, source_target_pairs={{0,1},{1,0},{2,3},{3,2},{4,5},{5,4},{6,7},{7,6},{8,9},{9,8},{10,11... | collective-permute-start | bytes 2457608 | tf_op jit(solution)/shard_map/ppermute | solution.py:16
  116.8 0.6 copy-start.17
  116.8 0.7 copy-start.18
  136.8 19.1 %copy-start.4 = (f32[4,4,40,320]{3,2,1,0:T(8,128)S(1)}, f32[4,4,40,320]{3,2,1,0:T(8,128)}, u32[]{:S(2)}) copy-start(f32[4,4,40,320]{3,2,1,0:T(8,128)} %get-tuple-element.36) | copy-start | bytes 2457604
  136.8 23.1 %collective-permute-start.29 = (f32[4,5,40,320]{3,2,1,0:T(8,128)}, f32[4,5,40,320]{3,2,1,0:T(8,128)S(1)}, u32[]{:S(2)}, u32[]{:S(2)}) collective-permute-start(f32[4,5,40,320]{3,2,1,0:T(8,128)} %get-tuple-element.40), channel_id=1, source_target_pairs={{0,1},{1,0},{2,3},{3,2},{4,5},{5,4},{6,7},{7,6},{8,9},{9,8},{10,11... | collective-permute-start | bytes 3072008 | tf_op jit(solution)/shard_map/ppermute | solution.py:16
  137.3 17.8 %collective-permute-start.16 = (bf16[16,80,128]{2,1,0:T(8,128)(2,1)}, bf16[16,80,128]{2,1,0:T(8,128)(2,1)S(1)}, u32[]{:S(2)}, u32[]{:S(2)}) collective-permute-start(bf16[16,80,128]{2,1,0:T(8,128)(2,1)} %get-tuple-element.25), channel_id=1, source_target_pairs={{0,6},{2,0},{4,2},{6,4},{1,7},{3,1},{5,3},{7,5},{8,14},{10,8},{12,... | collective-permute-start | bytes 983048 | tf_op jit(solution)/shard_map/ppermute | solution.py:16
  139.1 21.1 %collective-permute-start.22 = (bf16[16,80,128]{2,1,0:T(8,128)(2,1)}, bf16[16,80,128]{2,1,0:T(8,128)(2,1)S(1)}, u32[]{:S(2)}, u32[]{:S(2)}) collective-permute-start(bf16[16,80,128]{2,1,0:T(8,128)(2,1)} %get-tuple-element.33), channel_id=1, source_target_pairs={{0,2},{2,4},{4,6},{6,0},{1,3},{3,5},{5,7},{7,1},{8,10},{10,12},{12... | collective-permute-start | bytes 983048 | tf_op jit(solution)/shard_map/ppermute | solution.py:16
  156.0 3.8 %copy-start.3 = (f32[4,5,40,320]{3,2,1,0:T(8,128)S(1)}, f32[4,5,40,320]{3,2,1,0:T(8,128)}, u32[]{:S(2)}) copy-start(f32[4,5,40,320]{3,2,1,0:T(8,128)} %get-tuple-element.39) | copy-start | bytes 3072004
  156.1 9.8 %collective-permute-start.28 = (f32[4,40,320]{2,1,0:T(8,128)S(1)}, f32[4,40,320]{2,1,0:T(8,128)S(1)}, u32[]{:S(2)}, u32[]{:S(2)}) collective-permute-start(f32[4,40,320]{2,1,0:T(8,128)S(1)} %get-tuple-element.69), channel_id=1, source_target_pairs={{0,8},{8,16},{16,24},{24,0},{1,9},{9,17},{17,25},{25,1},{2,10},{10... | collective-permute-start | bytes 614408 | tf_op jit(solution)/shard_map/ppermute | solution.py:16
  156.7 14.5 %collective-permute-start.27 = (f32[4,40,320]{2,1,0:T(8,128)S(1)}, f32[4,40,320]{2,1,0:T(8,128)S(1)}, u32[]{:S(2)}, u32[]{:S(2)}) collective-permute-start(f32[4,40,320]{2,1,0:T(8,128)S(1)} %get-tuple-element.70), channel_id=1, source_target_pairs={{0,16},{8,24},{16,0},{24,8},{1,17},{9,25},{17,1},{25,9},{2,18},{10... | collective-permute-start | bytes 614408 | tf_op jit(solution)/shard_map/ppermute | solution.py:16
  157.2 14.8 %collective-permute-start.26 = (f32[4,40,320]{2,1,0:T(8,128)S(1)}, f32[4,40,320]{2,1,0:T(8,128)S(1)}, u32[]{:S(2)}, u32[]{:S(2)}) collective-permute-start(f32[4,40,320]{2,1,0:T(8,128)S(1)} %get-tuple-element.68), channel_id=1, source_target_pairs={{0,24},{8,0},{16,8},{24,16},{1,25},{9,1},{17,9},{25,17},{2,26},{10... | collective-permute-start | bytes 614408 | tf_op jit(solution)/shard_map/ppermute | solution.py:16
  159.8 6.0 %copy-start.13 = (f32[64,80,128]{2,1,0:T(8,128)S(1)}, f32[64,80,128]{2,1,0:T(8,128)}, u32[]{:S(2)}) copy-start(f32[64,80,128]{2,1,0:T(8,128)} %get-tuple-element.31) | copy-start | bytes 7864324
  160.0 11.2 %copy-start.16 = (bf16[16,80,128]{2,1,0:T(8,128)(2,1)S(1)}, bf16[16,80,128]{2,1,0:T(8,128)(2,1)}, u32[]{:S(2)}) copy-start(bf16[16,80,128]{2,1,0:T(8,128)(2,1)} %get-tuple-element.34) | copy-start | bytes 983044
  160.0 12.0 %copy-start.15 = (bf16[16,80,128]{2,1,0:T(8,128)(2,1)S(1)}, bf16[16,80,128]{2,1,0:T(8,128)(2,1)}, u32[]{:S(2)}) copy-start(bf16[16,80,128]{2,1,0:T(8,128)(2,1)} %get-tuple-element.35) | copy-start | bytes 983044
  160.1 17.7 %collective-permute-start.32 = (f32[5,40,320]{2,1,0:T(8,128)S(1)}, f32[5,40,320]{2,1,0:T(8,128)S(1)}, u32[]{:S(2)}, u32[]{:S(2)}) collective-permute-start(f32[5,40,320]{2,1,0:T(8,128)S(1)} %get-tuple-element.66), channel_id=1, source_target_pairs={{0,8},{8,16},{16,24},{24,0},{1,9},{9,17},{17,25},{25,1},{2,10},{10... | collective-permute-start | bytes 768008 | tf_op jit(solution)/shard_map/ppermute | solution.py:16
  160.2 22.0 %collective-permute-start.31 = (f32[5,40,320]{2,1,0:T(8,128)S(1)}, f32[5,40,320]{2,1,0:T(8,128)S(1)}, u32[]{:S(2)}, u32[]{:S(2)}) collective-permute-start(f32[5,40,320]{2,1,0:T(8,128)S(1)} %get-tuple-element.67), channel_id=1, source_target_pairs={{0,16},{8,24},{16,0},{24,8},{1,17},{9,25},{17,1},{25,9},{2,18},{10... | collective-permute-start | bytes 768008 | tf_op jit(solution)/shard_map/ppermute | solution.py:16
  165.9 16.4 %collective-permute-start.30 = (f32[5,40,320]{2,1,0:T(8,128)S(1)}, f32[5,40,320]{2,1,0:T(8,128)S(1)}, u32[]{:S(2)}, u32[]{:S(2)}) collective-permute-start(f32[5,40,320]{2,1,0:T(8,128)S(1)} %get-tuple-element.65), channel_id=1, source_target_pairs={{0,24},{8,0},{16,8},{24,16},{1,25},{9,1},{17,9},{25,17},{2,26},{10... | collective-permute-start | bytes 768008 | tf_op jit(solution)/shard_map/ppermute | solution.py:16
  171.2 17.1 %collective-permute-start.23 = (bf16[16,80,128]{2,1,0:T(8,128)(2,1)S(1)}, bf16[16,80,128]{2,1,0:T(8,128)(2,1)S(1)}, u32[]{:S(2)}, u32[]{:S(2)}) collective-permute-start(bf16[16,80,128]{2,1,0:T(8,128)(2,1)S(1)} %copy-done.16), channel_id=1, source_target_pairs={{0,4},{2,6},{4,0},{6,2},{1,5},{3,7},{5,1},{7,3},{8,12},{10,14},{12... | collective-permute-start | bytes 983048 | tf_op jit(solution)/shard_map/ppermute | solution.py:16
  172.0 34.4 %collective-permute-start.24 = (bf16[16,80,128]{2,1,0:T(8,128)(2,1)S(1)}, bf16[16,80,128]{2,1,0:T(8,128)(2,1)S(1)}, u32[]{:S(2)}, u32[]{:S(2)}) collective-permute-start(bf16[16,80,128]{2,1,0:T(8,128)(2,1)S(1)} %copy-done.15), channel_id=1, source_target_pairs={{0,6},{2,0},{4,2},{6,4},{1,7},{3,1},{5,3},{7,5},{8,14},{10,8},{12,... | collective-permute-start | bytes 983048 | tf_op jit(solution)/shard_map/ppermute | solution.py:16
  182.6 9.7 %collective-permute-start.35 = (f32[80,360]{0,1:T(8,128)S(1)}, f32[80,360]{0,1:T(8,128)S(1)}, u32[]{:S(2)}, u32[]{:S(2)}) collective-permute-start(f32[80,360]{0,1:T(8,128)S(1)} %bitcast.134), channel_id=1, source_target_pairs={{0,2},{2,4},{4,6},{6,0},{1,3},{3,5},{5,7},{7,1},{8,10},{10,12},{12... | collective-permute-start | bytes 345608 | tf_op jit(solution)/shard_map/ppermute | solution.py:16
  184.1 22.2 %collective-permute-start.34 = (f32[80,360]{0,1:T(8,128)S(1)}, f32[80,360]{0,1:T(8,128)S(1)}, u32[]{:S(2)}, u32[]{:S(2)}) collective-permute-start(f32[80,360]{0,1:T(8,128)S(1)} %bitcast.133), channel_id=1, source_target_pairs={{0,4},{2,6},{4,0},{6,2},{1,5},{3,7},{5,1},{7,3},{8,12},{10,14},{12... | collective-permute-start | bytes 345608 | tf_op jit(solution)/shard_map/ppermute | solution.py:16
  184.1 22.2 %collective-permute-start.33 = (f32[80,360]{0,1:T(8,128)S(1)}, f32[80,360]{0,1:T(8,128)S(1)}, u32[]{:S(2)}, u32[]{:S(2)}) collective-permute-start(f32[80,360]{0,1:T(8,128)S(1)} %bitcast.132), channel_id=1, source_target_pairs={{0,6},{2,0},{4,2},{6,4},{1,7},{3,1},{5,3},{7,5},{8,14},{10,8},{12,... | collective-permute-start | bytes 345608 | tf_op jit(solution)/shard_map/ppermute | solution.py:16
  206.3 1.5 collective-permute-start.36
  206.5 2.2 %copy-start.14 = (f32[1,64,80,128]{3,2,1,0:T(8,128)}, f32[1,64,80,128]{3,2,1,0:T(8,128)S(1)}, u32[]{:S(2)}) copy-start(f32[1,64,80,128]{3,2,1,0:T(8,128)S(1)} %convert_dynamic-update-slice_fusion) | copy-start | bytes 7864324

commit v5 on v4

--- a/solution.py
+++ b/solution.py
@@ -469,20 +469,18 @@
     return total
 
 
-def summed_kernel_grad(terms, inner, outer):
+def kernel_grad_of(total, inner, outer):
     row = lax.axis_index("row")
     chans, rows = lax.axis_size("chan"), lax.axis_size("row")
-    share = inner // rows
-    channels = terms[0].shape[2]
-    total = jnp.concatenate(terms)
-    total = jnp.transpose(total, (2, 0, 1)).reshape(channels, 9 * share)
+    taps, share, channels = total.shape
+    total = jnp.transpose(total, (2, 0, 1)).reshape(channels, taps * share)
     own = total[:outer]
     for j in range(1, chans):
         start = (chans - j) * outer
         own = own + receive(total[start : start + outer], "chan", j)
     both = jnp.stack([own] + [receive(own, "row", j) for j in range(1, rows)])
-    both = rotated(both, (rows - row) % rows, 0).reshape(rows, outer, 9, share)
-    return jnp.transpose(both, (2, 0, 3, 1)).reshape(9, inner, outer)
+    both = rotated(both, (rows - row) % rows, 0).reshape(rows, outer, taps, share)
+    return jnp.transpose(both, (2, 0, 3, 1)).reshape(taps, inner, outer)
 
 
 def shards(images, kernel, cotangent):
@@ -552,13 +550,14 @@
     above = lax.ppermute(last, ("chan", "row"), line)
     below = lax.ppermute(first, ("chan", "row"), [(b, a) for a, b in line])
 
-    lead, slope = correlate((0, 4), stacked, None, factor, cotangents, rims)
+    lead, slope = correlate((0, 6), stacked, None, factor, cotangents, rims)
     lead = summed_over_images(lead)
     input_grads = list(backward(back_turns, slope, above, below, back_kernel, chans, slab))
     slope, input_grads[1] = lax.optimization_barrier((slope, input_grads[1]))
-    (rest,) = correlate((4, 5), stacked, slope)
+    (rest,) = correlate((6, 3), stacked, slope)
     rest = summed_over_images(rest)
-    kernel_grad = summed_kernel_grad([lead, rest], kernel.shape[1], kernel.shape[2])
+    inner, outer = kernel.shape[1:]
+    kernel_grad = jnp.concatenate([kernel_grad_of(lead, inner, outer), kernel_grad_of(rest, inner, outer)])
 
     def to_owners(blocks):
         out = blocks[0]

time: 210 us -> 207 us (0.986)
  waiting for transfers between devices: 75 us -> 69.6 us
  local copies, waits for them, and re-layouts: 15 us -> 11.6 us
  other arithmetic: 6.06 us -> 9.28 us
  starting transfers between devices: 66.2 us -> 68.9 us
    ppermute x35 -> x39, starting transfers between devices: 48 us -> 66.4 us  [receive(): lax.ppermute(block, axis, [(i, (i - ahead) % count) for i in range(count)])]
    ppermute x1, starting transfers between devices: 16.9 us -> 1.28 us  [shards(): above = lax.ppermute(last, ('chan', 'row'), line)]
    ppermute x35 -> x39, waiting for transfers between devices: 75 us -> 69.6 us  [receive(): lax.ppermute(block, axis, [(i, (i - ahead) % count) for i in range(count)])]
    dynamic_update_slice x3, other arithmetic: 0.14 us -> 2.64 us  [to_owners(): out = lax.dynamic_update_slice_in_dim(out, arrived, home(-j) * height, 0)]
  transfers between devices with their start and end apart: 37 -> 41, of which waited for: 18 -> 15; matrix products, arithmetic and copies ran while one was open for 8% -> 8% of each run, Pallas kernels for 22% -> 22%
where the time goes in v5:
time: 207 us; the launch traced here: 206 us
  waiting for transfers between devices  69.6 us (34%)
  starting transfers between devices  68.9 us (33%)
  Pallas kernels  45.6 us (22%)
  local copies, waits for them, and re-layouts  11.6 us (6%)
  other arithmetic  9.28 us (4%)
    ppermute x39, waiting for transfers between devices, receive(): lax.ppermute(block, axis, [(i, (i - ahead) % count) for i in range(count)])  69.6 us
    ppermute x39, starting transfers between devices, receive(): lax.ppermute(block, axis, [(i, (i - ahead) % count) for i in range(count)])  66.4 us
    pallas_call x2, Pallas kernels, correlate(): results = call(turn, stacked, *operands)  16.8 us
    pallas_call x1, Pallas kernels, forward(): results = call(turns, *pieces, *rims, *halves)  12.9 us
    pallas_call x1, Pallas kernels, backward(): pl.pallas_call(functools.partial(backward_body, count, lax.axis_size('row...  11.3 us
    pallas_call x1, Pallas kernels, turned(): pl.pallas_call(functools.partial(turned_body, shares), grid=(blocks,), in...  4.53 us
  transfers between devices with their start and end apart: 41, of which 15 were waited for; matrix products, arithmetic and copies ran while one was open for 8% of the time, Pallas kernels for 22%

profile of v5, /device:TPU:0, one launch (start us, length us, event | category | flops | bytes accessed | tf_op | source)
XLA Modules:
  0.0 205.9 jit_solution(14834323194140267689)
XLA Ops:
  0.7 0.9 copy-done
  1.8 3.1 %collective-permute-start.9 = (bf16[40,720]{1,0:T(8,128)(2,1)S(1)}, bf16[40,720]{1,0:T(8,128)(2,1)S(1)}, u32[]{:S(2)}, u32[]{:S(2)}) collective-permute-start(bf16[40,720]{1,0:T(8,128)(2,1)S(1)} %copy.11), channel_id=1, source_target_pairs={{0,2},{2,4},{4,6},{6,0},{1,3},{3,5},{5,7},{7,1},{8,10},{10,12},{12... | collective-permute-start | bytes 172808 | tf_op jit(solution)/shard_map/ppermute | solution.py:16
  4.9 2.6 %collective-permute-start.8 = (bf16[40,720]{1,0:T(8,128)(2,1)S(1)}, bf16[40,720]{1,0:T(8,128)(2,1)S(1)}, u32[]{:S(2)}, u32[]{:S(2)}) collective-permute-start(bf16[40,720]{1,0:T(8,128)(2,1)S(1)} %copy.11), channel_id=1, source_target_pairs={{0,4},{2,6},{4,0},{6,2},{1,5},{3,7},{5,1},{7,3},{8,12},{10,14},{12... | collective-permute-start | bytes 172808 | tf_op jit(solution)/shard_map/ppermute | solution.py:16
  7.5 1.3 collective-permute-start.7
  9.3 2.5 %collective-permute-done.8 = bf16[40,720]{1,0:T(8,128)(2,1)S(1)} collective-permute-done((bf16[40,720]{1,0:T(8,128)(2,1)S(1)}, bf16[40,720]{1,0:T(8,128)(2,1)S(1)}, u32[]{:S(2)}, u32[]{:S(2)}) %collective-permute-start.8) | collective-permute-done | bytes 57632 | tf_op jit(solution)/shard_map/ppermute | solution.py:16
  12.1 1.5 collective-permute-start.12
  13.6 1.5 collective-permute-start.11
  15.1 1.4 collective-permute-start.10
  16.6 1.1 dynamic-slice_bitcast_fusion
  17.6 2.9 %collective-permute-start = (bf16[16,80,128]{2,1,0:T(8,128)(2,1)}, bf16[16,80,128]{2,1,0:T(8,128)(2,1)}, u32[]{:S(2)}, u32[]{:S(2)}) collective-permute-start(bf16[16,80,128]{2,1,0:T(8,128)(2,1)} %get-tuple-element.66), channel_id=1, source_target_pairs={{0,6},{2,0},{4,2},{6,4},{1,7},{3,1},{5,3},{7,5},{8,14},{10,8},{12,... | collective-permute-start | bytes 983048 | tf_op jit(solution)/shard_map/ppermute | solution.py:16
  21.2 0.7 collective-permute-done.12
  21.9 1.4 collective-permute-start.2
  23.3 2.0 collective-permute-done.11
  25.3 0.7 copy-done.6
  26.0 1.1 pad_maximum_fusion.refs_8_.refs_0_
  27.6 2.3 %dynamic-slice_bitcast_fusion.4 = (bf16[14,80,128]{2,1,0:T(8,128)(2,1)}, bf16[14,80,128]{2,1,0:T(8,128)(2,1)}, bf16[14,80,128]{2,1,0:T(8,128)(2,1)}, bf16[14,80,128]{2,1,0:T(8,128)(2,1)}) fusion(bf16[1,64,80,128]{3,2,1,0:T(8,128)(2,1)} %param.5, s32[]{:T(128)S(6)} %select_n.336, s32[]{:T(128)S(6)} %select_n.334, s32[]{:T(128)S(6)} %select_n.333, ...), kind=kLoop, calls=%fused_computation.24 | loop fusion | bytes 2293776 | tf_op jit(solution)/shard_map/dynamic_slice | solution.py:529
  30.0 1.5 dynamic-slice_bitcast_fusion.9
  32.0 0.7 stack.64.turns
  32.7 0.7 bitcast_select_fusion.1
  33.5 0.8 pad_maximum_fusion.4
  34.2 2.2 %collective-permute-start.4 = (bf16[4,80,128]{2,1,0:T(8,128)(2,1)S(1)}, bf16[4,80,128]{2,1,0:T(8,128)(2,1)S(1)}, u32[]{:S(2)}, u32[]{:S(2)}) collective-permute-start(bf16[4,80,128]{2,1,0:T(8,128)(2,1)S(1)} %pad_maximum_fusion.4), channel_id=1, source_target_pairs={{0,6},{2,0},{4,2},{6,4},{1,7},{3,1},{5,3},{7,5},{8,14},{10,8},{12,... | collective-permute-start | bytes 245768 | tf_op jit(solution)/shard_map/ppermute | solution.py:16
  36.4 0.8 pad_maximum_fusion.5
  37.2 9.4 %collective-permute-done.4.refs_5_.refs_6_ = bf16[4,80,128]{2,1,0:T(8,128)(2,1)S(1)} collective-permute-done((bf16[4,80,128]{2,1,0:T(8,128)(2,1)S(1)}, bf16[4,80,128]{2,1,0:T(8,128)(2,1)S(1)}, u32[]{:S(2)}, u32[]{:S(2)}) %collective-permute-start.4) | collective-permute-done | bytes 81952 | tf_op jit(solution)/shard_map/ppermute | solution.py:16
  46.6 2.9 %collective-permute-start.5 = (bf16[4,80,128]{2,1,0:T(8,128)(2,1)S(1)}, bf16[4,80,128]{2,1,0:T(8,128)(2,1)S(1)}, u32[]{:S(2)}, u32[]{:S(2)}) collective-permute-start(bf16[4,80,128]{2,1,0:T(8,128)(2,1)S(1)} %pad_maximum_fusion.5), channel_id=1, source_target_pairs={{0,4},{2,6},{4,0},{6,2},{1,5},{3,7},{5,1},{7,3},{8,12},{10,14},{12... | collective-permute-start | bytes 245768 | tf_op jit(solution)/shard_map/ppermute | solution.py:16
  49.5 3.3 %collective-permute-done.5.refs_6_.refs_7_ = bf16[4,80,128]{2,1,0:T(8,128)(2,1)S(1)} collective-permute-done((bf16[4,80,128]{2,1,0:T(8,128)(2,1)S(1)}, bf16[4,80,128]{2,1,0:T(8,128)(2,1)S(1)}, u32[]{:S(2)}, u32[]{:S(2)}) %collective-permute-start.5) | collective-permute-done | bytes 81952 | tf_op jit(solution)/shard_map/ppermute | solution.py:16
  52.9 3.0 %collective-permute-start.6 = (bf16[4,80,128]{2,1,0:T(8,128)(2,1)S(1)}, bf16[4,80,128]{2,1,0:T(8,128)(2,1)S(1)}, u32[]{:S(2)}, u32[]{:S(2)}) collective-permute-start(bf16[4,80,128]{2,1,0:T(8,128)(2,1)S(1)} %pad_maximum_fusion.6), channel_id=1, source_target_pairs={{0,2},{2,4},{4,6},{6,0},{1,3},{3,5},{5,7},{7,1},{8,10},{10,12},{12... | collective-permute-start | bytes 245768 | tf_op jit(solution)/shard_map/ppermute | solution.py:16
  55.9 0.7 pad_maximum_fusion.3.refs_4_.refs_5_
  56.5 3.4 %collective-permute-done.6.refs_7_.refs_8_ = bf16[4,80,128]{2,1,0:T(8,128)(2,1)S(1)} collective-permute-done((bf16[4,80,128]{2,1,0:T(8,128)(2,1)S(1)}, bf16[4,80,128]{2,1,0:T(8,128)(2,1)S(1)}, u32[]{:S(2)}, u32[]{:S(2)}) %collective-permute-start.6) | collective-permute-done | bytes 81952 | tf_op jit(solution)/shard_map/ppermute | solution.py:16
  60.0 1.0 collective-permute-start.17
  61.0 1.5 collective-permute-start.18
  62.5 0.9 copy-done.4
  63.4 12.9 %conv_forward.1 = (bf16[64,80,128]{2,1,0:T(8,128)(2,1)}, bf16[16,80,128]{2,1,0:T(8,128)(2,1)}, bf16[16,80,128]{2,1,0:T(8,128)(2,1)}, bf16[16,80,128]{2,1,0:T(8,1...) custom-call(s32[3]{0:T(128)} %pad_add_fusion.turns, ...), custom_call_target="tpu_custom_call" | custom-call | flops 3774873600 | bytes 16777216 | tf_op jit(solution)/shard_map/conv_forward/pallas_call | solution.py:188
  76.4 2.1 %collective-permute-start.14 = (bf16[16,80,128]{2,1,0:T(8,128)(2,1)}, bf16[16,80,128]{2,1,0:T(8,128)(2,1)S(1)}, u32[]{:S(2)}, u32[]{:S(2)}) collective-permute-start(bf16[16,80,128]{2,1,0:T(8,128)(2,1)} %get-tuple-element.23), channel_id=1, source_target_pairs={{0,2},{2,4},{4,6},{6,0},{1,3},{3,5},{5,7},{7,1},{8,10},{10,12},{12... | collective-permute-start | bytes 983048 | tf_op jit(solution)/shard_map/ppermute | solution.py:16
  78.4 2.4 %collective-permute-start.15 = (bf16[16,80,128]{2,1,0:T(8,128)(2,1)}, bf16[16,80,128]{2,1,0:T(8,128)(2,1)S(1)}, u32[]{:S(2)}, u32[]{:S(2)}) collective-permute-start(bf16[16,80,128]{2,1,0:T(8,128)(2,1)} %get-tuple-element.24), channel_id=1, source_target_pairs={{0,4},{2,6},{4,0},{6,2},{1,5},{3,7},{5,1},{7,3},{8,12},{10,14},{12... | collective-permute-start | bytes 983048 | tf_op jit(solution)/shard_map/ppermute | solution.py:16
  80.8 1.0 collective-permute-start.16
  81.8 19.7 %collective-permute-done.18.refs_3_ = bf16[14,80,128]{2,1,0:T(8,128)(2,1)S(1)} collective-permute-done((bf16[14,80,128]{2,1,0:T(8,128)(2,1)}, bf16[14,80,128]{2,1,0:T(8,128)(2,1)S(1)}, u32[]{:S(2)}, u32[]{:S(2)}) %collective-permute-start.18) | collective-permute-done | bytes 286752 | tf_op jit(solution)/shard_map/ppermute | solution.py:16
  101.5 1.3 collective-permute-start.20
  102.8 1.3 collective-permute-start.21
  104.1 10.7 %shard_map.58 = (f32[4,6,40,320]{3,2,1,0:T(8,128)}, f32[4,6,40,320]{3,2,1,0:T(8,128)}, bf16[320,2048]{1,0:T(8,128)(2,1)}) custom-call(s32[1]{0:T(128)} %bitcast.1.turn, bf16[960,2304]{1,0:T(8,128)(2,1)} %get-tuple-element.26.stacked, f32[16,320,128]{2,1,0:T(8,128)} %get-tuple-element.27.refs_0_, bf16[14,80,128]{2,1,0:T(8,128)(2,1)} %get-tuple-element.54.refs_1_, ...), custom_call_target="tpu_custom_call" | custom-call | flops 2516582400 | bytes 8388608 | tf_op jit(solution)/shard_map/pallas_call | solution.py:278
  114.8 4.5 %turn_kernel.1.kernels = bf16[4,80,3456]{2,1,0:T(8,128)(2,1)} custom-call(bf16[4,160,720]{2,1,0:T(8,128)(2,1)} %copy-done.1, bf16[4,160,720]{2,1,0:T(8,128)(2,1)} %copy-done.4), custom_call_target="tpu_custom_call" | custom-call | flops 235929600 | bytes 4194304 | tf_op jit(solution)/shard_map/turn_kernel/pallas_call | solution.py:324
  120.1 11.3 %conv_backward.1 = (f32[64,80,128]{2,1,0:T(8,128)}, bf16[16,80,128]{2,1,0:T(8,128)(2,1)}, bf16[16,80,128]{2,1,0:T(8,128)(2,1)}, bf16[16,80,128]{2,1,0:T(8,128)(2,1)}) custom-call(s32[5]{0:T(128)} %stack.64.turns, bf16[320,2048]{1,0:T(8,128)(2,1)} %get-tuple-element.38.slope.refs_0_, bf16[1,320,128]{2,1,0:T(8,128)(2,1)} %copy-done.15, ...), custom_call_target="tpu_custom_call" | custom-call | flops 3774873600 | bytes 8388608 | tf_op jit(solution)/shard_map/conv_backward/pallas_call | solution.py:412
  131.4 2.7 %collective-permute-start.22 = (bf16[16,80,128]{2,1,0:T(8,128)(2,1)}, bf16[16,80,128]{2,1,0:T(8,128)(2,1)S(1)}, u32[]{:S(2)}, u32[]{:S(2)}) collective-permute-start(bf16[16,80,128]{2,1,0:T(8,128)(2,1)} %get-tuple-element.33), channel_id=1, source_target_pairs={{0,2},{2,4},{4,6},{6,0},{1,3},{3,5},{5,7},{7,1},{8,10},{10,12},{12... | collective-permute-start | bytes 983048 | tf_op jit(solution)/shard_map/ppermute | solution.py:16
  134.1 6.1 %shard_map.59 = (f32[4,3,40,320]{3,2,1,0:T(8,128)}, f32[4,3,40,320]{3,2,1,0:T(8,128)}) custom-call(s32[1]{0:T(128)} %bitcast.1.turn, bf16[960,2304]{1,0:T(8,128)(2,1)} %get-tuple-element.26.stacked, bf16[320,2048]{1,0:T(8,128)(2,1)} %get-tuple-element.38.slope.refs_0_), custom_call_target="tpu_custom_call" | custom-call | flops 1258291200 | bytes 8388608 | tf_op jit(solution)/shard_map/pallas_call | solution.py:278
  140.6 0.7 bitcast_dynamic-update-slice_fusion.2
  141.4 2.8 %collective-permute-start.24 = (bf16[16,80,128]{2,1,0:T(8,128)(2,1)S(1)}, bf16[16,80,128]{2,1,0:T(8,128)(2,1)S(1)}, u32[]{:S(2)}, u32[]{:S(2)}) collective-permute-start(bf16[16,80,128]{2,1,0:T(8,128)(2,1)S(1)} %copy-done.7), channel_id=1, source_target_pairs={{0,6},{2,0},{4,2},{6,4},{1,7},{3,1},{5,3},{7,5},{8,14},{10,8},{12,... | collective-permute-start | bytes 983048 | tf_op jit(solution)/shard_map/ppermute | solution.py:16
  144.2 0.7 bitcast_dynamic-update-slice_fusion.1
  145.0 0.7 bitcast_dynamic-update-slice_fusion
  145.7 0.9 convert_dynamic-update-slice_fusion.2
  146.6 11.8 %collective-permute-done.23 = bf16[16,80,128]{2,1,0:T(8,128)(2,1)S(1)} collective-permute-done((bf16[16,80,128]{2,1,0:T(8,128)(2,1)S(1)}, bf16[16,80,128]{2,1,0:T(8,128)(2,1)S(1)}, u32[]{:S(2)}, u32[]{:S(2)}) %collective-permute-start.23) | collective-permute-done | bytes 327712 | tf_op jit(solution)/shard_map/ppermute | solution.py:16
  158.4 0.9 convert_dynamic-update-slice_fusion.1
  159.3 0.9 convert_dynamic-update-slice_fusion
  161.5 2.6 %collective-permute-start.34 = (f32[3,40,320]{2,1,0:T(8,128)S(1)}, f32[3,40,320]{2,1,0:T(8,128)S(1)}, u32[]{:S(2)}, u32[]{:S(2)}) collective-permute-start(f32[3,40,320]{2,1,0:T(8,128)S(1)} %get-tuple-element.68), channel_id=1, source_target_pairs={{0,24},{8,0},{16,8},{24,16},{1,25},{9,1},{17,9},{25,17},{2,26},{10... | collective-permute-start | bytes 460808 | tf_op jit(solution)/shard_map/ppermute | solution.py:16
  164.5 1.3 collective-permute-start.27
  165.8 3.0 %collective-permute-done.36 = f32[3,40,320]{2,1,0:T(8,128)S(1)} collective-permute-done((f32[3,40,320]{2,1,0:T(8,128)S(1)}, f32[3,40,320]{2,1,0:T(8,128)S(1)}, u32[]{:S(2)}, u32[]{:S(2)}) %collective-permute-start.36) | collective-permute-done | bytes 153632 | tf_op jit(solution)/shard_map/ppermute | solution.py:16
  168.8 4.0 %collective-permute-done.35 = f32[3,40,320]{2,1,0:T(8,128)S(1)} collective-permute-done((f32[3,40,320]{2,1,0:T(8,128)S(1)}, f32[3,40,320]{2,1,0:T(8,128)S(1)}, u32[]{:S(2)}, u32[]{:S(2)}) %collective-permute-start.35) | collective-permute-done | bytes 153632 | tf_op jit(solution)/shard_map/ppermute | solution.py:16
  173.0 6.4 %collective-permute-start.39 = (f32[80,120]{0,1:T(8,128)S(1)}, f32[80,120]{0,1:T(8,128)S(1)}, u32[]{:S(2)}, u32[]{:S(2)}) collective-permute-start(f32[80,120]{0,1:T(8,128)S(1)} %bitcast.162), channel_id=1, source_target_pairs={{0,2},{2,4},{4,6},{6,0},{1,3},{3,5},{5,7},{7,1},{8,10},{10,12},{12... | collective-permute-start | bytes 115208 | tf_op jit(solution)/shard_map/ppermute | solution.py:16
  179.4 2.4 %collective-permute-start.38 = (f32[80,120]{0,1:T(8,128)S(1)}, f32[80,120]{0,1:T(8,128)S(1)}, u32[]{:S(2)}, u32[]{:S(2)}) collective-permute-start(f32[80,120]{0,1:T(8,128)S(1)} %bitcast.161), channel_id=1, source_target_pairs={{0,4},{2,6},{4,0},{6,2},{1,5},{3,7},{5,1},{7,3},{8,12},{10,14},{12... | collective-permute-start | bytes 115208 | tf_op jit(solution)/shard_map/ppermute | solution.py:16
  181.8 7.1 %collective-permute-start.37 = (f32[80,120]{0,1:T(8,128)S(1)}, f32[80,120]{0,1:T(8,128)S(1)}, u32[]{:S(2)}, u32[]{:S(2)}) collective-permute-start(f32[80,120]{0,1:T(8,128)S(1)} %bitcast.160), channel_id=1, source_target_pairs={{0,6},{2,0},{4,2},{6,4},{1,7},{3,1},{5,3},{7,5},{8,14},{10,8},{12,... | collective-permute-start | bytes 115208 | tf_op jit(solution)/shard_map/ppermute | solution.py:16
  189.1 4.3 %collective-permute-start.31 = (f32[80,240]{0,1:T(8,128)S(1)}, f32[80,240]{0,1:T(8,128)S(1)}, u32[]{:S(2)}, u32[]{:S(2)}) collective-permute-start(f32[80,240]{0,1:T(8,128)S(1)} %bitcast.158), channel_id=1, source_target_pairs={{0,2},{2,4},{4,6},{6,0},{1,3},{3,5},{5,7},{7,1},{8,10},{10,12},{12... | collective-permute-start | bytes 230408 | tf_op jit(solution)/shard_map/ppermute | solution.py:16
  193.4 2.4 %collective-permute-start.30 = (f32[80,240]{0,1:T(8,128)S(1)}, f32[80,240]{0,1:T(8,128)S(1)}, u32[]{:S(2)}, u32[]{:S(2)}) collective-permute-start(f32[80,240]{0,1:T(8,128)S(1)} %bitcast.157), channel_id=1, source_target_pairs={{0,4},{2,6},{4,0},{6,2},{1,5},{3,7},{5,1},{7,3},{8,12},{10,14},{12... | collective-permute-start | bytes 230408 | tf_op jit(solution)/shard_map/ppermute | solution.py:16
  196.0 3.6 %collective-permute-done.31 = f32[80,240]{0,1:T(8,128)S(1)} collective-permute-done((f32[80,240]{0,1:T(8,128)S(1)}, f32[80,240]{0,1:T(8,128)S(1)}, u32[]{:S(2)}, u32[]{:S(2)}) %collective-permute-start.31) | collective-permute-done | bytes 76832 | tf_op jit(solution)/shard_map/ppermute | solution.py:16
  199.5 4.1 %collective-permute-done.30 = f32[80,240]{0,1:T(8,128)S(1)} collective-permute-done((f32[80,240]{0,1:T(8,128)S(1)}, f32[80,240]{0,1:T(8,128)S(1)}, u32[]{:S(2)}, u32[]{:S(2)}) %collective-permute-start.30) | collective-permute-done | bytes 76832 | tf_op jit(solution)/shard_map/ppermute | solution.py:16
  203.8 1.2 collective-permute-done.32
  205.2 0.8 pad_maximum_fusion.1
  (93 shorter events, 6.5 us)
Async XLA Ops:
  0.6 0.9 copy-start
  0.6 15.9 %copy-start.2 = (bf16[1,64,80,128]{3,2,1,0:T(8,128)(2,1)S(1)}, bf16[1,64,80,128]{3,2,1,0:T(8,128)(2,1)}, u32[]{:S(2)}) copy-start(bf16[1,64,80,128]{3,2,1,0:T(8,128)(2,1)} %param.3) | copy-start | bytes 3932164
  1.8 7.5 %collective-permute-start.9 = (bf16[40,720]{1,0:T(8,128)(2,1)S(1)}, bf16[40,720]{1,0:T(8,128)(2,1)S(1)}, u32[]{:S(2)}, u32[]{:S(2)}) collective-permute-start(bf16[40,720]{1,0:T(8,128)(2,1)S(1)} %copy.11), channel_id=1, source_target_pairs={{0,2},{2,4},{4,6},{6,0},{1,3},{3,5},{5,7},{7,1},{8,10},{10,12},{12... | collective-permute-start | bytes 172808 | tf_op jit(solution)/shard_map/ppermute | solution.py:16
  4.9 6.9 %collective-permute-start.8 = (bf16[40,720]{1,0:T(8,128)(2,1)S(1)}, bf16[40,720]{1,0:T(8,128)(2,1)S(1)}, u32[]{:S(2)}, u32[]{:S(2)}) collective-permute-start(bf16[40,720]{1,0:T(8,128)(2,1)S(1)} %copy.11), channel_id=1, source_target_pairs={{0,4},{2,6},{4,0},{6,2},{1,5},{3,7},{5,1},{7,3},{8,12},{10,14},{12... | collective-permute-start | bytes 172808 | tf_op jit(solution)/shard_map/ppermute | solution.py:16
  7.5 4.6 %collective-permute-start.7 = (bf16[40,720]{1,0:T(8,128)(2,1)S(1)}, bf16[40,720]{1,0:T(8,128)(2,1)S(1)}, u32[]{:S(2)}, u32[]{:S(2)}) collective-permute-start(bf16[40,720]{1,0:T(8,128)(2,1)S(1)} %copy.11), channel_id=1, source_target_pairs={{0,6},{2,0},{4,2},{6,4},{1,7},{3,1},{5,3},{7,5},{8,14},{10,8},{12,... | collective-permute-start | bytes 172808 | tf_op jit(solution)/shard_map/ppermute | solution.py:16
  12.1 9.8 %collective-permute-start.12 = (bf16[160,720]{1,0:T(8,128)(2,1)S(1)}, bf16[160,720]{1,0:T(8,128)(2,1)S(1)}, u32[]{:S(2)}, u32[]{:S(2)}) collective-permute-start(bf16[160,720]{1,0:T(8,128)(2,1)S(1)} %get-tuple-element.76), channel_id=1, source_target_pairs={{0,8},{8,16},{16,24},{24,0},{1,9},{9,17},{17,25},{25,1},{2,10},{10... | collective-permute-start | bytes 691208 | tf_op jit(solution)/shard_map/ppermute | solution.py:16
  13.6 11.6 %collective-permute-start.11 = (bf16[160,720]{1,0:T(8,128)(2,1)S(1)}, bf16[160,720]{1,0:T(8,128)(2,1)S(1)}, u32[]{:S(2)}, u32[]{:S(2)}) collective-permute-start(bf16[160,720]{1,0:T(8,128)(2,1)S(1)} %get-tuple-element.76), channel_id=1, source_target_pairs={{0,16},{8,24},{16,0},{24,8},{1,17},{9,25},{17,1},{25,9},{2,18},{10... | collective-permute-start | bytes 691208 | tf_op jit(solution)/shard_map/ppermute | solution.py:16
  15.1 10.1 %collective-permute-start.10 = (bf16[160,720]{1,0:T(8,128)(2,1)S(1)}, bf16[160,720]{1,0:T(8,128)(2,1)S(1)}, u32[]{:S(2)}, u32[]{:S(2)}) collective-permute-start(bf16[160,720]{1,0:T(8,128)(2,1)S(1)} %get-tuple-element.76), channel_id=1, source_target_pairs={{0,24},{8,0},{16,8},{24,16},{1,25},{9,1},{17,9},{25,17},{2,26},{10... | collective-permute-start | bytes 691208 | tf_op jit(solution)/shard_map/ppermute | solution.py:16
  17.6 43.4 %collective-permute-start = (bf16[16,80,128]{2,1,0:T(8,128)(2,1)}, bf16[16,80,128]{2,1,0:T(8,128)(2,1)}, u32[]{:S(2)}, u32[]{:S(2)}) collective-permute-start(bf16[16,80,128]{2,1,0:T(8,128)(2,1)} %get-tuple-element.66), channel_id=1, source_target_pairs={{0,6},{2,0},{4,2},{6,4},{1,7},{3,1},{5,3},{7,5},{8,14},{10,8},{12,... | collective-permute-start | bytes 983048 | tf_op jit(solution)/shard_map/ppermute | solution.py:16
  20.5 41.9 %collective-permute-start.1 = (bf16[16,80,128]{2,1,0:T(8,128)(2,1)}, bf16[16,80,128]{2,1,0:T(8,128)(2,1)}, u32[]{:S(2)}, u32[]{:S(2)}) collective-permute-start(bf16[16,80,128]{2,1,0:T(8,128)(2,1)} %get-tuple-element.65), channel_id=1, source_target_pairs={{0,4},{2,6},{4,0},{6,2},{1,5},{3,7},{5,1},{7,3},{8,12},{10,14},{12... | collective-permute-start | bytes 983048 | tf_op jit(solution)/shard_map/ppermute | solution.py:16
  21.9 40.6 %collective-permute-start.2 = (bf16[16,80,128]{2,1,0:T(8,128)(2,1)}, bf16[16,80,128]{2,1,0:T(8,128)(2,1)}, u32[]{:S(2)}, u32[]{:S(2)}) collective-permute-start(bf16[16,80,128]{2,1,0:T(8,128)(2,1)} %get-tuple-element.64), channel_id=1, source_target_pairs={{0,2},{2,4},{4,6},{6,0},{1,3},{3,5},{5,7},{7,1},{8,10},{10,12},{12... | collective-permute-start | bytes 983048 | tf_op jit(solution)/shard_map/ppermute | solution.py:16
  25.3 7.4 %collective-permute-start.3 = (bf16[1,80,128]{2,1,0:T(8,128)(2,1)}, bf16[1,80,128]{2,1,0:T(8,128)(2,1)}, u32[]{:S(2)}, u32[]{:S(2)}) collective-permute-start(bf16[1,80,128]{2,1,0:T(8,128)(2,1)} %select_bitcast_fusion), channel_id=1, source_target_pairs={{0,1},{1,0},{2,3},{3,2},{4,5},{5,4},{6,7},{7,6},{8,9},{9,8},{10,11... | collective-permute-start | bytes 61448 | tf_op jit(solution)/shard_map/ppermute | solution.py:16
  25.3 0.7 copy-start.6
  27.1 6.4 %copy-start.1 = (bf16[4,160,720]{2,1,0:T(8,128)(2,1)}, bf16[4,160,720]{2,1,0:T(8,128)(2,1)S(1)}, u32[]{:S(2)}) copy-start(bf16[4,160,720]{2,1,0:T(8,128)(2,1)S(1)} %pad_maximum_fusion.refs_8_.refs_0_) | copy-start | bytes 2764804
  27.1 35.4 %collective-permute-start.13 = (bf16[4,160,720]{2,1,0:T(8,128)(2,1)S(1)}, bf16[4,160,720]{2,1,0:T(8,128)(2,1)S(1)}, u32[]{:S(2)}, u32[]{:S(2)}) collective-permute-start(bf16[4,160,720]{2,1,0:T(8,128)(2,1)S(1)} %pad_maximum_fusion.refs_8_.refs_0_), channel_id=1, source_target_pairs={{0,1},{1,0},{2,3},{3,2},{4,5},{5,4},{6,7},{7,6},{8,9},{9,8},{10,11... | collective-permute-start | bytes 2764808 | tf_op jit(solution)/shard_map/ppermute | solution.py:16
  34.2 12.4 %collective-permute-start.4 = (bf16[4,80,128]{2,1,0:T(8,128)(2,1)S(1)}, bf16[4,80,128]{2,1,0:T(8,128)(2,1)S(1)}, u32[]{:S(2)}, u32[]{:S(2)}) collective-permute-start(bf16[4,80,128]{2,1,0:T(8,128)(2,1)S(1)} %pad_maximum_fusion.4), channel_id=1, source_target_pairs={{0,6},{2,0},{4,2},{6,4},{1,7},{3,1},{5,3},{7,5},{8,14},{10,8},{12,... | collective-permute-start | bytes 245768 | tf_op jit(solution)/shard_map/ppermute | solution.py:16
  46.6 15.9 %copy-start.12 = (bf16[4,80,128]{2,1,0:T(8,128)(2,1)}, bf16[4,80,128]{2,1,0:T(8,128)(2,1)S(1)}, u32[]{:S(2)}) copy-start(bf16[4,80,128]{2,1,0:T(8,128)(2,1)S(1)} %collective-permute-done.4.refs_5_.refs_6_) | copy-start | bytes 245764
  46.6 6.3 %collective-permute-start.5 = (bf16[4,80,128]{2,1,0:T(8,128)(2,1)S(1)}, bf16[4,80,128]{2,1,0:T(8,128)(2,1)S(1)}, u32[]{:S(2)}, u32[]{:S(2)}) collective-permute-start(bf16[4,80,128]{2,1,0:T(8,128)(2,1)S(1)} %pad_maximum_fusion.5), channel_id=1, source_target_pairs={{0,4},{2,6},{4,0},{6,2},{1,5},{3,7},{5,1},{7,3},{8,12},{10,14},{12... | collective-permute-start | bytes 245768 | tf_op jit(solution)/shard_map/ppermute | solution.py:16
  52.9 9.6 %copy-start.13 = (bf16[4,80,128]{2,1,0:T(8,128)(2,1)}, bf16[4,80,128]{2,1,0:T(8,128)(2,1)S(1)}, u32[]{:S(2)}) copy-start(bf16[4,80,128]{2,1,0:T(8,128)(2,1)S(1)} %collective-permute-done.5.refs_6_.refs_7_) | copy-start | bytes 245764
  52.9 7.1 %collective-permute-start.6 = (bf16[4,80,128]{2,1,0:T(8,128)(2,1)S(1)}, bf16[4,80,128]{2,1,0:T(8,128)(2,1)S(1)}, u32[]{:S(2)}, u32[]{:S(2)}) collective-permute-start(bf16[4,80,128]{2,1,0:T(8,128)(2,1)S(1)} %pad_maximum_fusion.6), channel_id=1, source_target_pairs={{0,2},{2,4},{4,6},{6,0},{1,3},{3,5},{5,7},{7,1},{8,10},{10,12},{12... | collective-permute-start | bytes 245768 | tf_op jit(solution)/shard_map/ppermute | solution.py:16
  60.0 2.5 %copy-start.14 = (bf16[4,80,128]{2,1,0:T(8,128)(2,1)}, bf16[4,80,128]{2,1,0:T(8,128)(2,1)S(1)}, u32[]{:S(2)}) copy-start(bf16[4,80,128]{2,1,0:T(8,128)(2,1)S(1)} %collective-permute-done.6.refs_7_.refs_8_) | copy-start | bytes 245764
  60.0 20.8 %collective-permute-start.17 = (bf16[14,80,128]{2,1,0:T(8,128)(2,1)}, bf16[14,80,128]{2,1,0:T(8,128)(2,1)S(1)}, u32[]{:S(2)}, u32[]{:S(2)}) collective-permute-start(bf16[14,80,128]{2,1,0:T(8,128)(2,1)} %get-tuple-element.53), channel_id=1, source_target_pairs={{0,6},{2,0},{4,2},{6,4},{1,7},{3,1},{5,3},{7,5},{8,14},{10,8},{12,... | collective-permute-start | bytes 860168 | tf_op jit(solution)/shard_map/ppermute | solution.py:16
  61.0 40.5 %collective-permute-start.18 = (bf16[14,80,128]{2,1,0:T(8,128)(2,1)}, bf16[14,80,128]{2,1,0:T(8,128)(2,1)S(1)}, u32[]{:S(2)}, u32[]{:S(2)}) collective-permute-start(bf16[14,80,128]{2,1,0:T(8,128)(2,1)} %get-tuple-element.55), channel_id=1, source_target_pairs={{0,4},{2,6},{4,0},{6,2},{1,5},{3,7},{5,1},{7,3},{8,12},{10,14},{12... | collective-permute-start | bytes 860168 | tf_op jit(solution)/shard_map/ppermute | solution.py:16
  62.5 40.3 %collective-permute-start.19 = (bf16[14,80,128]{2,1,0:T(8,128)(2,1)}, bf16[14,80,128]{2,1,0:T(8,128)(2,1)S(1)}, u32[]{:S(2)}, u32[]{:S(2)}) collective-permute-start(bf16[14,80,128]{2,1,0:T(8,128)(2,1)} %get-tuple-element.52), channel_id=1, source_target_pairs={{0,2},{2,4},{4,6},{6,0},{1,3},{3,5},{5,7},{7,1},{8,10},{10,12},{12... | collective-permute-start | bytes 860168 | tf_op jit(solution)/shard_map/ppermute | solution.py:16
  62.5 1.0 copy-start.4
  76.4 63.8 %collective-permute-start.14 = (bf16[16,80,128]{2,1,0:T(8,128)(2,1)}, bf16[16,80,128]{2,1,0:T(8,128)(2,1)S(1)}, u32[]{:S(2)}, u32[]{:S(2)}) collective-permute-start(bf16[16,80,128]{2,1,0:T(8,128)(2,1)} %get-tuple-element.23), channel_id=1, source_target_pairs={{0,2},{2,4},{4,6},{6,0},{1,3},{3,5},{5,7},{7,1},{8,10},{10,12},{12... | collective-permute-start | bytes 983048 | tf_op jit(solution)/shard_map/ppermute | solution.py:16
  78.4 62.9 %collective-permute-start.15 = (bf16[16,80,128]{2,1,0:T(8,128)(2,1)}, bf16[16,80,128]{2,1,0:T(8,128)(2,1)S(1)}, u32[]{:S(2)}, u32[]{:S(2)}) collective-permute-start(bf16[16,80,128]{2,1,0:T(8,128)(2,1)} %get-tuple-element.24), channel_id=1, source_target_pairs={{0,4},{2,6},{4,0},{6,2},{1,5},{3,7},{5,1},{7,3},{8,12},{10,14},{12... | collective-permute-start | bytes 983048 | tf_op jit(solution)/shard_map/ppermute | solution.py:16
  80.8 23.3 %copy-start.9 = (bf16[14,80,128]{2,1,0:T(8,128)(2,1)}, bf16[14,80,128]{2,1,0:T(8,128)(2,1)S(1)}, u32[]{:S(2)}) copy-start(bf16[14,80,128]{2,1,0:T(8,128)(2,1)S(1)} %collective-permute-done.17.refs_2_) | copy-start | bytes 860164
  80.8 64.1 %collective-permute-start.16 = (bf16[16,80,128]{2,1,0:T(8,128)(2,1)}, bf16[16,80,128]{2,1,0:T(8,128)(2,1)S(1)}, u32[]{:S(2)}, u32[]{:S(2)}) collective-permute-start(bf16[16,80,128]{2,1,0:T(8,128)(2,1)} %get-tuple-element.25), channel_id=1, source_target_pairs={{0,6},{2,0},{4,2},{6,4},{1,7},{3,1},{5,3},{7,5},{8,14},{10,8},{12,... | collective-permute-start | bytes 983048 | tf_op jit(solution)/shard_map/ppermute | solution.py:16
  101.5 2.6 %copy-start.10 = (bf16[14,80,128]{2,1,0:T(8,128)(2,1)}, bf16[14,80,128]{2,1,0:T(8,128)(2,1)S(1)}, u32[]{:S(2)}) copy-start(bf16[14,80,128]{2,1,0:T(8,128)(2,1)S(1)} %collective-permute-done.18.refs_3_) | copy-start | bytes 860164
  101.5 17.8 %collective-permute-start.20 = (bf16[1,320,128]{2,1,0:T(8,128)(2,1)}, bf16[1,320,128]{2,1,0:T(8,128)(2,1)S(1)}, u32[]{:S(2)}, u32[]{:S(2)}) collective-permute-start(bf16[1,320,128]{2,1,0:T(8,128)(2,1)} %get-tuple-element.29), channel_id=1, source_target_pairs={{0,2},{2,4},{4,6},{6,7},{7,5},{5,3},{3,1},{8,10},{10,12},{12,14},{... | collective-permute-start | bytes 245768 | tf_op jit(solution)/shard_map/ppermute | solution.py:550
  102.8 1.3 copy-start.11
  102.8 16.6 %collective-permute-start.21 = (bf16[1,320,128]{2,1,0:T(8,128)(2,1)}, bf16[1,320,128]{2,1,0:T(8,128)(2,1)S(1)}, u32[]{:S(2)}, u32[]{:S(2)}) collective-permute-start(bf16[1,320,128]{2,1,0:T(8,128)(2,1)} %get-tuple-element.30), channel_id=1, source_target_pairs={{2,0},{4,2},{6,4},{7,6},{5,7},{3,5},{1,3},{10,8},{12,10},{14,12},{... | collective-permute-start | bytes 245768 | tf_op jit(solution)/shard_map/ppermute | solution.py:551
  119.3 0.6 copy-start.15
  119.3 44.8 %collective-permute-start.25 = (f32[4,6,40,320]{3,2,1,0:T(8,128)}, f32[4,6,40,320]{3,2,1,0:T(8,128)S(1)}, u32[]{:S(2)}, u32[]{:S(2)}) collective-permute-start(f32[4,6,40,320]{3,2,1,0:T(8,128)} %get-tuple-element.37), channel_id=1, source_target_pairs={{0,1},{1,0},{2,3},{3,2},{4,5},{5,4},{6,7},{7,6},{8,9},{9,8},{10,11... | collective-permute-start | bytes 3686408 | tf_op jit(solution)/shard_map/ppermute | solution.py:16
  119.4 0.6 copy-start.16
  131.3 8.9 %copy-start.8 = (bf16[16,80,128]{2,1,0:T(8,128)(2,1)S(1)}, bf16[16,80,128]{2,1,0:T(8,128)(2,1)}, u32[]{:S(2)}) copy-start(bf16[16,80,128]{2,1,0:T(8,128)(2,1)} %get-tuple-element.34) | copy-start | bytes 983044
  131.3 10.0 %copy-start.7 = (bf16[16,80,128]{2,1,0:T(8,128)(2,1)S(1)}, bf16[16,80,128]{2,1,0:T(8,128)(2,1)}, u32[]{:S(2)}) copy-start(bf16[16,80,128]{2,1,0:T(8,128)(2,1)} %get-tuple-element.35) | copy-start | bytes 983044
  131.4 14.4 %collective-permute-start.22 = (bf16[16,80,128]{2,1,0:T(8,128)(2,1)}, bf16[16,80,128]{2,1,0:T(8,128)(2,1)S(1)}, u32[]{:S(2)}, u32[]{:S(2)}) collective-permute-start(bf16[16,80,128]{2,1,0:T(8,128)(2,1)} %get-tuple-element.33), channel_id=1, source_target_pairs={{0,2},{2,4},{4,6},{6,0},{1,3},{3,5},{5,7},{7,1},{8,10},{10,12},{12... | collective-permute-start | bytes 983048 | tf_op jit(solution)/shard_map/ppermute | solution.py:16
  140.2 18.2 %collective-permute-start.23 = (bf16[16,80,128]{2,1,0:T(8,128)(2,1)S(1)}, bf16[16,80,128]{2,1,0:T(8,128)(2,1)S(1)}, u32[]{:S(2)}, u32[]{:S(2)}) collective-permute-start(bf16[16,80,128]{2,1,0:T(8,128)(2,1)S(1)} %copy-done.8), channel_id=1, source_target_pairs={{0,4},{2,6},{4,0},{6,2},{1,5},{3,7},{5,1},{7,3},{8,12},{10,14},{12... | collective-permute-start | bytes 983048 | tf_op jit(solution)/shard_map/ppermute | solution.py:16
  141.4 17.9 %collective-permute-start.24 = (bf16[16,80,128]{2,1,0:T(8,128)(2,1)S(1)}, bf16[16,80,128]{2,1,0:T(8,128)(2,1)S(1)}, u32[]{:S(2)}, u32[]{:S(2)}) collective-permute-start(bf16[16,80,128]{2,1,0:T(8,128)(2,1)S(1)} %copy-done.7), channel_id=1, source_target_pairs={{0,6},{2,0},{4,2},{6,4},{1,7},{3,1},{5,3},{7,5},{8,14},{10,8},{12,... | collective-permute-start | bytes 983048 | tf_op jit(solution)/shard_map/ppermute | solution.py:16
  145.0 15.2 %collective-permute-start.33 = (f32[4,3,40,320]{3,2,1,0:T(8,128)}, f32[4,3,40,320]{3,2,1,0:T(8,128)S(1)}, u32[]{:S(2)}, u32[]{:S(2)}) collective-permute-start(f32[4,3,40,320]{3,2,1,0:T(8,128)} %get-tuple-element.40), channel_id=1, source_target_pairs={{0,1},{1,0},{2,3},{3,2},{4,5},{5,4},{6,7},{7,6},{8,9},{9,8},{10,11... | collective-permute-start | bytes 1843208 | tf_op jit(solution)/shard_map/ppermute | solution.py:16
  145.7 14.5 %copy-start.5 = (f32[4,3,40,320]{3,2,1,0:T(8,128)S(1)}, f32[4,3,40,320]{3,2,1,0:T(8,128)}, u32[]{:S(2)}) copy-start(f32[4,3,40,320]{3,2,1,0:T(8,128)} %get-tuple-element.39) | copy-start | bytes 1843204
  160.2 3.9 %copy-start.3 = (f32[4,6,40,320]{3,2,1,0:T(8,128)S(1)}, f32[4,6,40,320]{3,2,1,0:T(8,128)}, u32[]{:S(2)}) copy-start(f32[4,6,40,320]{3,2,1,0:T(8,128)} %get-tuple-element.36) | copy-start | bytes 3686404
  160.3 8.5 %collective-permute-start.36 = (f32[3,40,320]{2,1,0:T(8,128)S(1)}, f32[3,40,320]{2,1,0:T(8,128)S(1)}, u32[]{:S(2)}, u32[]{:S(2)}) collective-permute-start(f32[3,40,320]{2,1,0:T(8,128)S(1)} %get-tuple-element.69), channel_id=1, source_target_pairs={{0,8},{8,16},{16,24},{24,0},{1,9},{9,17},{17,25},{25,1},{2,10},{10... | collective-permute-start | bytes 460808 | tf_op jit(solution)/shard_map/ppermute | solution.py:16
  161.0 11.8 %collective-permute-start.35 = (f32[3,40,320]{2,1,0:T(8,128)S(1)}, f32[3,40,320]{2,1,0:T(8,128)S(1)}, u32[]{:S(2)}, u32[]{:S(2)}) collective-permute-start(f32[3,40,320]{2,1,0:T(8,128)S(1)} %get-tuple-element.70), channel_id=1, source_target_pairs={{0,16},{8,24},{16,0},{24,8},{1,17},{9,25},{17,1},{25,9},{2,18},{10... | collective-permute-start | bytes 460808 | tf_op jit(solution)/shard_map/ppermute | solution.py:16
  161.5 11.3 %collective-permute-start.34 = (f32[3,40,320]{2,1,0:T(8,128)S(1)}, f32[3,40,320]{2,1,0:T(8,128)S(1)}, u32[]{:S(2)}, u32[]{:S(2)}) collective-permute-start(f32[3,40,320]{2,1,0:T(8,128)S(1)} %get-tuple-element.68), channel_id=1, source_target_pairs={{0,24},{8,0},{16,8},{24,16},{1,25},{9,1},{17,9},{25,17},{2,26},{10... | collective-permute-start | bytes 460808 | tf_op jit(solution)/shard_map/ppermute | solution.py:16
  164.4 17.4 %collective-permute-start.28 = (f32[6,40,320]{2,1,0:T(8,128)S(1)}, f32[6,40,320]{2,1,0:T(8,128)S(1)}, u32[]{:S(2)}, u32[]{:S(2)}) collective-permute-start(f32[6,40,320]{2,1,0:T(8,128)S(1)} %get-tuple-element.42), channel_id=1, source_target_pairs={{0,8},{8,16},{16,24},{24,0},{1,9},{9,17},{17,25},{25,1},{2,10},{10... | collective-permute-start | bytes 921608 | tf_op jit(solution)/shard_map/ppermute | solution.py:16
  164.5 24.4 %collective-permute-start.27 = (f32[6,40,320]{2,1,0:T(8,128)S(1)}, f32[6,40,320]{2,1,0:T(8,128)S(1)}, u32[]{:S(2)}, u32[]{:S(2)}) collective-permute-start(f32[6,40,320]{2,1,0:T(8,128)S(1)} %get-tuple-element.43), channel_id=1, source_target_pairs={{0,16},{8,24},{16,0},{24,8},{1,17},{9,25},{17,1},{25,9},{2,18},{10... | collective-permute-start | bytes 921608 | tf_op jit(solution)/shard_map/ppermute | solution.py:16
  168.8 20.1 %collective-permute-start.26 = (f32[6,40,320]{2,1,0:T(8,128)S(1)}, f32[6,40,320]{2,1,0:T(8,128)S(1)}, u32[]{:S(2)}, u32[]{:S(2)}) collective-permute-start(f32[6,40,320]{2,1,0:T(8,128)S(1)} %get-tuple-element.41), channel_id=1, source_target_pairs={{0,24},{8,0},{16,8},{24,16},{1,25},{9,1},{17,9},{25,17},{2,26},{10... | collective-permute-start | bytes 921608 | tf_op jit(solution)/shard_map/ppermute | solution.py:16
  173.0 22.9 %collective-permute-start.39 = (f32[80,120]{0,1:T(8,128)S(1)}, f32[80,120]{0,1:T(8,128)S(1)}, u32[]{:S(2)}, u32[]{:S(2)}) collective-permute-start(f32[80,120]{0,1:T(8,128)S(1)} %bitcast.162), channel_id=1, source_target_pairs={{0,2},{2,4},{4,6},{6,0},{1,3},{3,5},{5,7},{7,1},{8,10},{10,12},{12... | collective-permute-start | bytes 115208 | tf_op jit(solution)/shard_map/ppermute | solution.py:16
  179.4 16.5 %collective-permute-start.38 = (f32[80,120]{0,1:T(8,128)S(1)}, f32[80,120]{0,1:T(8,128)S(1)}, u32[]{:S(2)}, u32[]{:S(2)}) collective-permute-start(f32[80,120]{0,1:T(8,128)S(1)} %bitcast.161), channel_id=1, source_target_pairs={{0,4},{2,6},{4,0},{6,2},{1,5},{3,7},{5,1},{7,3},{8,12},{10,14},{12... | collective-permute-start | bytes 115208 | tf_op jit(solution)/shard_map/ppermute | solution.py:16
  181.8 14.1 %collective-permute-start.37 = (f32[80,120]{0,1:T(8,128)S(1)}, f32[80,120]{0,1:T(8,128)S(1)}, u32[]{:S(2)}, u32[]{:S(2)}) collective-permute-start(f32[80,120]{0,1:T(8,128)S(1)} %bitcast.160), channel_id=1, source_target_pairs={{0,6},{2,0},{4,2},{6,4},{1,7},{3,1},{5,3},{7,5},{8,14},{10,8},{12,... | collective-permute-start | bytes 115208 | tf_op jit(solution)/shard_map/ppermute | solution.py:16
  189.1 10.4 %collective-permute-start.31 = (f32[80,240]{0,1:T(8,128)S(1)}, f32[80,240]{0,1:T(8,128)S(1)}, u32[]{:S(2)}, u32[]{:S(2)}) collective-permute-start(f32[80,240]{0,1:T(8,128)S(1)} %bitcast.158), channel_id=1, source_target_pairs={{0,2},{2,4},{4,6},{6,0},{1,3},{3,5},{5,7},{7,1},{8,10},{10,12},{12... | collective-permute-start | bytes 230408 | tf_op jit(solution)/shard_map/ppermute | solution.py:16
  193.4 10.2 %collective-permute-start.30 = (f32[80,240]{0,1:T(8,128)S(1)}, f32[80,240]{0,1:T(8,128)S(1)}, u32[]{:S(2)}, u32[]{:S(2)}) collective-permute-start(f32[80,240]{0,1:T(8,128)S(1)} %bitcast.157), channel_id=1, source_target_pairs={{0,4},{2,6},{4,0},{6,2},{1,5},{3,7},{5,1},{7,3},{8,12},{10,14},{12... | collective-permute-start | bytes 230408 | tf_op jit(solution)/shard_map/ppermute | solution.py:16
  195.8 7.8 %collective-permute-start.29 = (f32[80,240]{0,1:T(8,128)S(1)}, f32[80,240]{0,1:T(8,128)S(1)}, u32[]{:S(2)}, u32[]{:S(2)}) collective-permute-start(f32[80,240]{0,1:T(8,128)S(1)} %bitcast.156), channel_id=1, source_target_pairs={{0,6},{2,0},{4,2},{6,4},{1,7},{3,1},{5,3},{7,5},{8,14},{10,8},{12,... | collective-permute-start | bytes 230408 | tf_op jit(solution)/shard_map/ppermute | solution.py:16
  195.9 7.8 %collective-permute-start.40 = (f32[80,120]{0,1:T(8,128)S(1)}, f32[80,120]{0,1:T(8,128)S(1)}, u32[]{:S(2)}, u32[]{:S(2)}) collective-permute-start(f32[80,120]{0,1:T(8,128)S(1)} %fusion.17), channel_id=1, source_target_pairs={{0,1},{1,0},{2,3},{3,2},{4,5},{5,4},{6,7},{7,6},{8,9},{9,8},{10,11... | collective-permute-start | bytes 115208 | tf_op jit(solution)/shard_map/ppermute | solution.py:16
  203.6 1.4 collective-permute-start.32

commit v6 on v5

--- a/solution.py
+++ b/solution.py
@@ -14,6 +14,37 @@
 def receive(block, axis, ahead):
     count = lax.axis_size(axis)
     return lax.ppermute(block, axis, [(i, (i - ahead) % count) for i in range(count)])
+
+
+def swapped(block, axis, bit):
+    return lax.ppermute(block, axis, [(i, i ^ bit) for i in range(lax.axis_size(axis))])
+
+
+def gathered_over_chan(mine):
+    chans = lax.axis_size("chan")
+    if chans != 4:
+        return jnp.concatenate([mine] + [receive(mine, "chan", j) for j in range(1, chans)])
+    size = mine.shape[0]
+    even = lax.axis_index("chan") % 2 == 0
+    opposite = swapped(mine, "chan", 2)
+    beside = swapped(jnp.concatenate([mine, opposite]), "chan", 1)
+    near, far = beside[:size], beside[size:]
+    return jnp.concatenate([mine, jnp.where(even, near, far), opposite, jnp.where(even, far, near)])
+
+
+def summed_over_chan(total, outer, in_steps):
+    chans = lax.axis_size("chan")
+    blocks = [total[j * outer : (j + 1) * outer] for j in range(chans)]
+    if chans != 4 or not in_steps:
+        own = blocks[0]
+        for j in range(1, chans):
+            own = own + receive(blocks[chans - j], "chan", j)
+        return own
+    odd = lax.axis_index("chan") % 2 == 1
+    beside = swapped(jnp.concatenate([blocks[1], blocks[3]]), "chan", 1)
+    first, second = beside[:outer], beside[outer:]
+    other = blocks[2] + jnp.where(odd, second, first)
+    return blocks[0] + jnp.where(odd, first, second) + swapped(other, "chan", 2)
 
 
 def home_of(row, chan, chans):
@@ -441,7 +472,7 @@
     size = outer // rows
     mine = part(kernel, row, size, 2)
     mine = jnp.transpose(mine, (2, 0, 1)).reshape(size, 9 * inner)
-    over_chan = jnp.concatenate([mine] + [receive(mine, "chan", j) for j in range(1, chans)], axis=0)
+    over_chan = gathered_over_chan(mine)
     over_dp = jnp.stack([over_chan] + [receive(over_chan, "dp", j) for j in range(1, dps)])
     if dps != chans:
         each = dps // chans
@@ -469,15 +500,11 @@
     return total
 
 
-def kernel_grad_of(total, inner, outer):
-    row = lax.axis_index("row")
-    chans, rows = lax.axis_size("chan"), lax.axis_size("row")
+def kernel_grad_of(total, inner, outer, in_steps):
+    row, rows = lax.axis_index("row"), lax.axis_size("row")
     taps, share, channels = total.shape
     total = jnp.transpose(total, (2, 0, 1)).reshape(channels, taps * share)
-    own = total[:outer]
-    for j in range(1, chans):
-        start = (chans - j) * outer
-        own = own + receive(total[start : start + outer], "chan", j)
+    own = summed_over_chan(total, outer, in_steps)
     both = jnp.stack([own] + [receive(own, "row", j) for j in range(1, rows)])
     both = rotated(both, (rows - row) % rows, 0).reshape(rows, outer, taps, share)
     return jnp.transpose(both, (2, 0, 3, 1)).reshape(taps, inner, outer)
@@ -557,7 +584,7 @@
     (rest,) = correlate((6, 3), stacked, slope)
     rest = summed_over_images(rest)
     inner, outer = kernel.shape[1:]
-    kernel_grad = jnp.concatenate([kernel_grad_of(lead, inner, outer), kernel_grad_of(rest, inner, outer)])
+    kernel_grad = jnp.concatenate([kernel_grad_of(lead, inner, outer, True), kernel_grad_of(rest, inner, outer, False)])
 
     def to_owners(blocks):
         out = blocks[0]

time: 207 us -> 211 us (1.019)
  waiting for transfers between devices: 69.6 us -> 78.1 us
  starting transfers between devices: 68.9 us -> 64.8 us
    ppermute x39 -> x33, starting transfers between devices: 66.4 us -> 48.3 us  [receive(): lax.ppermute(block, axis, [(i, (i - ahead) % count) for i in range(count)])]
    ppermute x0 -> x4, starting transfers between devices: none -> 14 us  [swapped(): lax.ppermute(block, axis, [(i, i ^ bit) for i in range(lax.axis_size(axis...]
    ppermute x0 -> x4, waiting for transfers between devices: none -> 11.2 us  [swapped(): lax.ppermute(block, axis, [(i, i ^ bit) for i in range(lax.axis_size(axis...]
    ppermute x39 -> x33, waiting for transfers between devices: 69.6 us -> 66.9 us  [receive(): lax.ppermute(block, axis, [(i, (i - ahead) % count) for i in range(count)])]
  transfers between devices with their start and end apart: 41 -> 39, of which waited for: 15 -> 17; matrix products, arithmetic and copies ran while one was open for 8% -> 8% of each run, Pallas kernels for 22% -> 22%
where the time goes in v6:
time: 211 us
  waiting for transfers between devices  78.1 us (37%)
  starting transfers between devices  64.8 us (31%)
  Pallas kernels  45.5 us (22%)
  local copies, waits for them, and re-layouts  11.6 us (5%)
  other arithmetic  9.78 us (5%)
    ppermute x33, waiting for transfers between devices, receive(): lax.ppermute(block, axis, [(i, (i - ahead) % count) for i in range(count)])  66.9 us
    ppermute x33, starting transfers between devices, receive(): lax.ppermute(block, axis, [(i, (i - ahead) % count) for i in range(count)])  48.3 us
    pallas_call x2, Pallas kernels, correlate(): results = call(turn, stacked, *operands)  16.8 us
    ppermute x4, starting transfers between devices, swapped(): lax.ppermute(block, axis, [(i, i ^ bit) for i in range(lax.axis_size(axis...  14 us
    pallas_call x1, Pallas kernels, forward(): results = call(turns, *pieces, *rims, *halves)  12.9 us
    pallas_call x1, Pallas kernels, backward(): pl.pallas_call(functools.partial(backward_body, count, lax.axis_size('row...  11.3 us
    ppermute x4, waiting for transfers between devices, swapped(): lax.ppermute(block, axis, [(i, i ^ bit) for i in range(lax.axis_size(axis...  11.2 us
    pallas_call x1, Pallas kernels, turned(): pl.pallas_call(functools.partial(turned_body, shares), grid=(blocks,), in...  4.47 us
  transfers between devices with their start and end apart: 39, of which 17 were waited for; matrix products, arithmetic and copies ran while one was open for 8% of the time, Pallas kernels for 22%

profile of v6, /device:TPU:0, one launch (start us, length us, event | category | flops | bytes accessed | tf_op | source)
XLA Modules:
  0.0 210.8 jit_solution(12780016317660809239)
XLA Ops:
  0.7 0.9 copy-done
  1.8 4.1 %collective-permute-start.7 = (bf16[40,720]{1,0:T(8,128)(2,1)S(1)}, bf16[40,720]{1,0:T(8,128)(2,1)S(1)}, u32[]{:S(2)}, u32[]{:S(2)}) collective-permute-start(bf16[40,720]{1,0:T(8,128)(2,1)S(1)} %copy.11), channel_id=1, source_target_pairs={{0,4},{2,6},{4,0},{6,2},{1,5},{3,7},{5,1},{7,3},{8,12},{10,14},{12... | collective-permute-start | bytes 172808 | tf_op jit(solution)/shard_map/ppermute | solution.py:20
  5.9 2.9 %collective-permute-done.7 = bf16[40,720]{1,0:T(8,128)(2,1)S(1)} collective-permute-done((bf16[40,720]{1,0:T(8,128)(2,1)S(1)}, bf16[40,720]{1,0:T(8,128)(2,1)S(1)}, u32[]{:S(2)}, u32[]{:S(2)}) %collective-permute-start.7) | collective-permute-done | bytes 57632 | tf_op jit(solution)/shard_map/ppermute | solution.py:20
  8.8 1.3 collective-permute-start.8
  10.1 3.6 %collective-permute-done.8 = bf16[80,720]{1,0:T(8,128)(2,1)S(1)} collective-permute-done((bf16[80,720]{1,0:T(8,128)(2,1)S(1)}, bf16[80,720]{1,0:T(8,128)(2,1)S(1)}, u32[]{:S(2)}, u32[]{:S(2)}) %collective-permute-start.8) | collective-permute-done | bytes 115232 | tf_op jit(solution)/shard_map/ppermute | solution.py:20
  13.8 2.4 %collective-permute-start.11 = (bf16[160,720]{1,0:T(8,128)(2,1)S(1)}, bf16[160,720]{1,0:T(8,128)(2,1)S(1)}, u32[]{:S(2)}, u32[]{:S(2)}) collective-permute-start(bf16[160,720]{1,0:T(8,128)(2,1)S(1)} %get-tuple-element.76), channel_id=1, source_target_pairs={{0,8},{8,16},{16,24},{24,0},{1,9},{9,17},{17,25},{25,1},{2,10},{10... | collective-permute-start | bytes 691208 | tf_op jit(solution)/shard_map/ppermute | solution.py:16
  16.2 1.5 collective-permute-start.10
  17.7 1.4 collective-permute-start.9
  19.2 1.1 dynamic-slice_bitcast_fusion
  20.3 3.1 %collective-permute-start = (bf16[16,80,128]{2,1,0:T(8,128)(2,1)}, bf16[16,80,128]{2,1,0:T(8,128)(2,1)}, u32[]{:S(2)}, u32[]{:S(2)}) collective-permute-start(bf16[16,80,128]{2,1,0:T(8,128)(2,1)} %get-tuple-element.66), channel_id=1, source_target_pairs={{0,6},{2,0},{4,2},{6,4},{1,7},{3,1},{5,3},{7,5},{8,14},{10,8},{12,... | collective-permute-start | bytes 983048 | tf_op jit(solution)/shard_map/ppermute | solution.py:16
  24.0 0.8 collective-permute-start.2
  25.9 1.2 pad_maximum_fusion.refs_8_.refs_0_
  27.5 2.3 %dynamic-slice_bitcast_fusion.4 = (bf16[14,80,128]{2,1,0:T(8,128)(2,1)}, bf16[14,80,128]{2,1,0:T(8,128)(2,1)}, bf16[14,80,128]{2,1,0:T(8,128)(2,1)}, bf16[14,80,128]{2,1,0:T(8,128)(2,1)}) fusion(bf16[1,64,80,128]{3,2,1,0:T(8,128)(2,1)} %param.5, s32[]{:T(128)S(6)} %select_n.370, s32[]{:T(128)S(6)} %select_n.368, s32[]{:T(128)S(6)} %select_n.367, ...), kind=kLoop, calls=%fused_computation.24 | loop fusion | bytes 2293776 | tf_op jit(solution)/shard_map/dynamic_slice | solution.py:556
  29.8 1.5 dynamic-slice_bitcast_fusion.9
  31.3 0.7 pad_add_fusion.turns
  32.0 0.6 stack.64.turns
  32.6 0.7 bitcast_select_fusion.1
  33.3 0.8 pad_maximum_fusion.6
  34.1 5.4 %collective-permute-start.4 = (bf16[4,80,128]{2,1,0:T(8,128)(2,1)S(1)}, bf16[4,80,128]{2,1,0:T(8,128)(2,1)S(1)}, u32[]{:S(2)}, u32[]{:S(2)}) collective-permute-start(bf16[4,80,128]{2,1,0:T(8,128)(2,1)S(1)} %pad_maximum_fusion.6), channel_id=1, source_target_pairs={{0,6},{2,0},{4,2},{6,4},{1,7},{3,1},{5,3},{7,5},{8,14},{10,8},{12,... | collective-permute-start | bytes 245768 | tf_op jit(solution)/shard_map/ppermute | solution.py:16
  39.5 0.8 pad_maximum_fusion.7
  40.3 7.3 %collective-permute-done.4.refs_5_.refs_6_ = bf16[4,80,128]{2,1,0:T(8,128)(2,1)S(1)} collective-permute-done((bf16[4,80,128]{2,1,0:T(8,128)(2,1)S(1)}, bf16[4,80,128]{2,1,0:T(8,128)(2,1)S(1)}, u32[]{:S(2)}, u32[]{:S(2)}) %collective-permute-start.4) | collective-permute-done | bytes 81952 | tf_op jit(solution)/shard_map/ppermute | solution.py:16
  47.6 3.8 %collective-permute-start.5 = (bf16[4,80,128]{2,1,0:T(8,128)(2,1)S(1)}, bf16[4,80,128]{2,1,0:T(8,128)(2,1)S(1)}, u32[]{:S(2)}, u32[]{:S(2)}) collective-permute-start(bf16[4,80,128]{2,1,0:T(8,128)(2,1)S(1)} %pad_maximum_fusion.7), channel_id=1, source_target_pairs={{0,4},{2,6},{4,0},{6,2},{1,5},{3,7},{5,1},{7,3},{8,12},{10,14},{12... | collective-permute-start | bytes 245768 | tf_op jit(solution)/shard_map/ppermute | solution.py:16
  51.4 2.6 %collective-permute-done.5.refs_6_.refs_7_ = bf16[4,80,128]{2,1,0:T(8,128)(2,1)S(1)} collective-permute-done((bf16[4,80,128]{2,1,0:T(8,128)(2,1)S(1)}, bf16[4,80,128]{2,1,0:T(8,128)(2,1)S(1)}, u32[]{:S(2)}, u32[]{:S(2)}) %collective-permute-start.5) | collective-permute-done | bytes 81952 | tf_op jit(solution)/shard_map/ppermute | solution.py:16
  54.0 3.7 %collective-permute-start.6 = (bf16[4,80,128]{2,1,0:T(8,128)(2,1)S(1)}, bf16[4,80,128]{2,1,0:T(8,128)(2,1)S(1)}, u32[]{:S(2)}, u32[]{:S(2)}) collective-permute-start(bf16[4,80,128]{2,1,0:T(8,128)(2,1)S(1)} %pad_maximum_fusion.8), channel_id=1, source_target_pairs={{0,2},{2,4},{4,6},{6,0},{1,3},{3,5},{5,7},{7,1},{8,10},{10,12},{12... | collective-permute-start | bytes 245768 | tf_op jit(solution)/shard_map/ppermute | solution.py:16
  57.8 0.6 pad_maximum_fusion.5.refs_4_.refs_5_
  58.4 2.8 %collective-permute-done.6.refs_7_.refs_8_ = bf16[4,80,128]{2,1,0:T(8,128)(2,1)S(1)} collective-permute-done((bf16[4,80,128]{2,1,0:T(8,128)(2,1)S(1)}, bf16[4,80,128]{2,1,0:T(8,128)(2,1)S(1)}, u32[]{:S(2)}, u32[]{:S(2)}) %collective-permute-start.6) | collective-permute-done | bytes 81952 | tf_op jit(solution)/shard_map/ppermute | solution.py:16
  61.2 2.0 collective-permute-start.16
  63.9 1.0 copy-done.4
  64.9 12.9 %conv_forward.1 = (bf16[64,80,128]{2,1,0:T(8,128)(2,1)}, bf16[16,80,128]{2,1,0:T(8,128)(2,1)}, bf16[16,80,128]{2,1,0:T(8,128)(2,1)}, bf16[16,80,128]{2,1,0:T(8,1...) custom-call(s32[3]{0:T(128)} %pad_add_fusion.turns, ...), custom_call_target="tpu_custom_call" | custom-call | flops 3774873600 | bytes 16777216 | tf_op jit(solution)/shard_map/conv_forward/pallas_call | solution.py:219
  77.8 2.9 %collective-permute-start.13 = (bf16[16,80,128]{2,1,0:T(8,128)(2,1)}, bf16[16,80,128]{2,1,0:T(8,128)(2,1)S(1)}, u32[]{:S(2)}, u32[]{:S(2)}) collective-permute-start(bf16[16,80,128]{2,1,0:T(8,128)(2,1)} %get-tuple-element.23), channel_id=1, source_target_pairs={{0,2},{2,4},{4,6},{6,0},{1,3},{3,5},{5,7},{7,1},{8,10},{10,12},{12... | collective-permute-start | bytes 983048 | tf_op jit(solution)/shard_map/ppermute | solution.py:16
  80.7 1.3 collective-permute-start.14
  82.1 1.1 collective-permute-start.15
  83.2 21.0 %collective-permute-done.17.refs_3_ = bf16[14,80,128]{2,1,0:T(8,128)(2,1)S(1)} collective-permute-done((bf16[14,80,128]{2,1,0:T(8,128)(2,1)}, bf16[14,80,128]{2,1,0:T(8,128)(2,1)S(1)}, u32[]{:S(2)}, u32[]{:S(2)}) %collective-permute-start.17) | collective-permute-done | bytes 286752 | tf_op jit(solution)/shard_map/ppermute | solution.py:16
  104.2 1.3 collective-permute-start.19
  105.5 1.3 collective-permute-start.20
  106.8 10.7 %shard_map.58 = (f32[4,6,40,320]{3,2,1,0:T(8,128)}, f32[4,6,40,320]{3,2,1,0:T(8,128)}, bf16[320,2048]{1,0:T(8,128)(2,1)}) custom-call(s32[1]{0:T(128)} %bitcast.1.turn, bf16[960,2304]{1,0:T(8,128)(2,1)} %get-tuple-element.26.stacked, f32[16,320,128]{2,1,0:T(8,128)} %get-tuple-element.27.refs_0_, bf16[14,80,128]{2,1,0:T(8,128)(2,1)} %get-tuple-element.54.refs_1_, ...), custom_call_target="tpu_custom_call" | custom-call | flops 2516582400 | bytes 8388608 | tf_op jit(solution)/shard_map/pallas_call | solution.py:309
  117.5 4.5 %turn_kernel.1.kernels = bf16[4,80,3456]{2,1,0:T(8,128)(2,1)} custom-call(bf16[4,160,720]{2,1,0:T(8,128)(2,1)} %copy-done.1, bf16[4,160,720]{2,1,0:T(8,128)(2,1)} %copy-done.4), custom_call_target="tpu_custom_call" | custom-call | flops 235929600 | bytes 4194304 | tf_op jit(solution)/shard_map/turn_kernel/pallas_call | solution.py:355
  122.7 11.3 %conv_backward.1 = (f32[64,80,128]{2,1,0:T(8,128)}, bf16[16,80,128]{2,1,0:T(8,128)(2,1)}, bf16[16,80,128]{2,1,0:T(8,128)(2,1)}, bf16[16,80,128]{2,1,0:T(8,128)(2,1)}) custom-call(s32[5]{0:T(128)} %stack.64.turns, bf16[320,2048]{1,0:T(8,128)(2,1)} %get-tuple-element.38.slope.refs_0_, bf16[1,320,128]{2,1,0:T(8,128)(2,1)} %copy-done.16, ...), custom_call_target="tpu_custom_call" | custom-call | flops 3774873600 | bytes 8388608 | tf_op jit(solution)/shard_map/conv_backward/pallas_call | solution.py:443
  134.0 2.7 %collective-permute-start.21 = (bf16[16,80,128]{2,1,0:T(8,128)(2,1)}, bf16[16,80,128]{2,1,0:T(8,128)(2,1)S(1)}, u32[]{:S(2)}, u32[]{:S(2)}) collective-permute-start(bf16[16,80,128]{2,1,0:T(8,128)(2,1)} %get-tuple-element.33), channel_id=1, source_target_pairs={{0,2},{2,4},{4,6},{6,0},{1,3},{3,5},{5,7},{7,1},{8,10},{10,12},{12... | collective-permute-start | bytes 983048 | tf_op jit(solution)/shard_map/ppermute | solution.py:16
  136.7 6.1 %shard_map.59 = (f32[4,3,40,320]{3,2,1,0:T(8,128)}, f32[4,3,40,320]{3,2,1,0:T(8,128)}) custom-call(s32[1]{0:T(128)} %bitcast.1.turn, bf16[960,2304]{1,0:T(8,128)(2,1)} %get-tuple-element.26.stacked, bf16[320,2048]{1,0:T(8,128)(2,1)} %get-tuple-element.38.slope.refs_0_), custom_call_target="tpu_custom_call" | custom-call | flops 1258291200 | bytes 8388608 | tf_op jit(solution)/shard_map/pallas_call | solution.py:309
  143.2 0.7 bitcast_dynamic-update-slice_fusion.2
  143.9 2.8 %collective-permute-start.23 = (bf16[16,80,128]{2,1,0:T(8,128)(2,1)S(1)}, bf16[16,80,128]{2,1,0:T(8,128)(2,1)S(1)}, u32[]{:S(2)}, u32[]{:S(2)}) collective-permute-start(bf16[16,80,128]{2,1,0:T(8,128)(2,1)S(1)} %copy-done.8), channel_id=1, source_target_pairs={{0,6},{2,0},{4,2},{6,4},{1,7},{3,1},{5,3},{7,5},{8,14},{10,8},{12,... | collective-permute-start | bytes 983048 | tf_op jit(solution)/shard_map/ppermute | solution.py:16
  146.8 0.7 bitcast_dynamic-update-slice_fusion.1
  147.5 0.8 bitcast_dynamic-update-slice_fusion
  148.3 0.9 convert_dynamic-update-slice_fusion.2
  149.2 11.8 %collective-permute-done.22 = bf16[16,80,128]{2,1,0:T(8,128)(2,1)S(1)} collective-permute-done((bf16[16,80,128]{2,1,0:T(8,128)(2,1)S(1)}, bf16[16,80,128]{2,1,0:T(8,128)(2,1)S(1)}, u32[]{:S(2)}, u32[]{:S(2)}) %collective-permute-start.22) | collective-permute-done | bytes 327712 | tf_op jit(solution)/shard_map/ppermute | solution.py:16
  161.0 0.9 convert_dynamic-update-slice_fusion.1
  162.3 0.6 collective-permute-start.33
  162.9 2.1 collective-permute-start.32
  165.3 0.6 collective-permute-start.27
  165.9 1.5 collective-permute-start.26
  167.4 3.0 %collective-permute-done.34 = f32[3,40,320]{2,1,0:T(8,128)S(1)} collective-permute-done((f32[3,40,320]{2,1,0:T(8,128)S(1)}, f32[3,40,320]{2,1,0:T(8,128)S(1)}, u32[]{:S(2)}, u32[]{:S(2)}) %collective-permute-start.34) | collective-permute-done | bytes 153632 | tf_op jit(solution)/shard_map/ppermute | solution.py:16
  170.5 0.9 convert_dynamic-update-slice_fusion
  171.4 3.1 %collective-permute-done.33 = f32[3,40,320]{2,1,0:T(8,128)S(1)} collective-permute-done((f32[3,40,320]{2,1,0:T(8,128)S(1)}, f32[3,40,320]{2,1,0:T(8,128)S(1)}, u32[]{:S(2)}, u32[]{:S(2)}) %collective-permute-start.33) | collective-permute-done | bytes 153632 | tf_op jit(solution)/shard_map/ppermute | solution.py:16
  174.5 7.8 %collective-permute-done.27 = f32[6,40,320]{2,1,0:T(8,128)S(1)} collective-permute-done((f32[6,40,320]{2,1,0:T(8,128)S(1)}, f32[6,40,320]{2,1,0:T(8,128)S(1)}, u32[]{:S(2)}, u32[]{:S(2)}) %collective-permute-start.27) | collective-permute-done | bytes 307232 | tf_op jit(solution)/shard_map/ppermute | solution.py:16
  182.4 5.6 %collective-permute-done.26 = f32[6,40,320]{2,1,0:T(8,128)S(1)} collective-permute-done((f32[6,40,320]{2,1,0:T(8,128)S(1)}, f32[6,40,320]{2,1,0:T(8,128)S(1)}, u32[]{:S(2)}, u32[]{:S(2)}) %collective-permute-start.26) | collective-permute-done | bytes 307232 | tf_op jit(solution)/shard_map/ppermute | solution.py:16
  188.3 5.7 %collective-permute-start.28 = (f32[160,240]{0,1:T(8,128)S(1)}, f32[160,240]{0,1:T(8,128)S(1)}, u32[]{:S(2)}, u32[]{:S(2)}) collective-permute-start(f32[160,240]{0,1:T(8,128)S(1)} %pad_maximum_fusion.3), channel_id=1, source_target_pairs={{0,2},{2,0},{4,6},{6,4},{1,3},{3,1},{5,7},{7,5},{8,10},{10,8},{12,... | collective-permute-start | bytes 460808 | tf_op jit(solution)/shard_map/ppermute | solution.py:20
  194.2 3.4 %collective-permute-start.36 = (f32[80,120]{0,1:T(8,128)S(1)}, f32[80,120]{0,1:T(8,128)S(1)}, u32[]{:S(2)}, u32[]{:S(2)}) collective-permute-start(f32[80,120]{0,1:T(8,128)S(1)} %bitcast.159), channel_id=1, source_target_pairs={{0,4},{2,6},{4,0},{6,2},{1,5},{3,7},{5,1},{7,3},{8,12},{10,14},{12... | collective-permute-start | bytes 115208 | tf_op jit(solution)/shard_map/ppermute | solution.py:16
  197.7 2.8 %collective-permute-start.35 = (f32[80,120]{0,1:T(8,128)S(1)}, f32[80,120]{0,1:T(8,128)S(1)}, u32[]{:S(2)}, u32[]{:S(2)}) collective-permute-start(f32[80,120]{0,1:T(8,128)S(1)} %bitcast.158), channel_id=1, source_target_pairs={{0,6},{2,0},{4,2},{6,4},{1,7},{3,1},{5,3},{7,5},{8,14},{10,8},{12,... | collective-permute-start | bytes 115208 | tf_op jit(solution)/shard_map/ppermute | solution.py:16
  200.5 1.5 collective-permute-done.28
  202.1 2.8 %collective-permute-start.29 = (f32[80,240]{0,1:T(8,128)S(1)}, f32[80,240]{0,1:T(8,128)S(1)}, u32[]{:S(2)}, u32[]{:S(2)}) collective-permute-start(f32[80,240]{0,1:T(8,128)S(1)} %bitcast_add_fusion), channel_id=1, source_target_pairs={{0,4},{2,6},{4,0},{6,2},{1,5},{3,7},{5,1},{7,3},{8,12},{10,14},{12... | collective-permute-start | bytes 230408 | tf_op jit(solution)/shard_map/ppermute | solution.py:20
  205.2 3.2 %collective-permute-done.29 = f32[80,240]{0,1:T(8,128)S(1)} collective-permute-done((f32[80,240]{0,1:T(8,128)S(1)}, f32[80,240]{0,1:T(8,128)S(1)}, u32[]{:S(2)}, u32[]{:S(2)}) %collective-permute-start.29) | collective-permute-done | bytes 76832 | tf_op jit(solution)/shard_map/ppermute | solution.py:20
  208.7 1.2 collective-permute-done.30
  210.0 0.8 pad_maximum_fusion.1
  (95 shorter events, 6.2 us)
Async XLA Ops:
  0.6 0.9 copy-start
  0.6 18.5 %copy-start.2 = (bf16[1,64,80,128]{3,2,1,0:T(8,128)(2,1)S(1)}, bf16[1,64,80,128]{3,2,1,0:T(8,128)(2,1)}, u32[]{:S(2)}) copy-start(bf16[1,64,80,128]{3,2,1,0:T(8,128)(2,1)} %param.3) | copy-start | bytes 3932164
  1.8 7.0 %collective-permute-start.7 = (bf16[40,720]{1,0:T(8,128)(2,1)S(1)}, bf16[40,720]{1,0:T(8,128)(2,1)S(1)}, u32[]{:S(2)}, u32[]{:S(2)}) collective-permute-start(bf16[40,720]{1,0:T(8,128)(2,1)S(1)} %copy.11), channel_id=1, source_target_pairs={{0,4},{2,6},{4,0},{6,2},{1,5},{3,7},{5,1},{7,3},{8,12},{10,14},{12... | collective-permute-start | bytes 172808 | tf_op jit(solution)/shard_map/ppermute | solution.py:20
  8.8 4.9 %collective-permute-start.8 = (bf16[80,720]{1,0:T(8,128)(2,1)S(1)}, bf16[80,720]{1,0:T(8,128)(2,1)S(1)}, u32[]{:S(2)}, u32[]{:S(2)}) collective-permute-start(bf16[80,720]{1,0:T(8,128)(2,1)S(1)} %pad_maximum_fusion.4), channel_id=1, source_target_pairs={{0,2},{2,0},{4,6},{6,4},{1,3},{3,1},{5,7},{7,5},{8,10},{10,8},{12,... | collective-permute-start | bytes 345608 | tf_op jit(solution)/shard_map/ppermute | solution.py:20
  13.8 10.2 %collective-permute-start.11 = (bf16[160,720]{1,0:T(8,128)(2,1)S(1)}, bf16[160,720]{1,0:T(8,128)(2,1)S(1)}, u32[]{:S(2)}, u32[]{:S(2)}) collective-permute-start(bf16[160,720]{1,0:T(8,128)(2,1)S(1)} %get-tuple-element.76), channel_id=1, source_target_pairs={{0,8},{8,16},{16,24},{24,0},{1,9},{9,17},{17,25},{25,1},{2,10},{10... | collective-permute-start | bytes 691208 | tf_op jit(solution)/shard_map/ppermute | solution.py:16
  16.2 8.8 %collective-permute-start.10 = (bf16[160,720]{1,0:T(8,128)(2,1)S(1)}, bf16[160,720]{1,0:T(8,128)(2,1)S(1)}, u32[]{:S(2)}, u32[]{:S(2)}) collective-permute-start(bf16[160,720]{1,0:T(8,128)(2,1)S(1)} %get-tuple-element.76), channel_id=1, source_target_pairs={{0,16},{8,24},{16,0},{24,8},{1,17},{9,25},{17,1},{25,9},{2,18},{10... | collective-permute-start | bytes 691208 | tf_op jit(solution)/shard_map/ppermute | solution.py:16
  17.7 7.5 %collective-permute-start.9 = (bf16[160,720]{1,0:T(8,128)(2,1)S(1)}, bf16[160,720]{1,0:T(8,128)(2,1)S(1)}, u32[]{:S(2)}, u32[]{:S(2)}) collective-permute-start(bf16[160,720]{1,0:T(8,128)(2,1)S(1)} %get-tuple-element.76), channel_id=1, source_target_pairs={{0,24},{8,0},{16,8},{24,16},{1,25},{9,1},{17,9},{25,17},{2,26},{10... | collective-permute-start | bytes 691208 | tf_op jit(solution)/shard_map/ppermute | solution.py:16
  20.3 43.0 %collective-permute-start = (bf16[16,80,128]{2,1,0:T(8,128)(2,1)}, bf16[16,80,128]{2,1,0:T(8,128)(2,1)}, u32[]{:S(2)}, u32[]{:S(2)}) collective-permute-start(bf16[16,80,128]{2,1,0:T(8,128)(2,1)} %get-tuple-element.66), channel_id=1, source_target_pairs={{0,6},{2,0},{4,2},{6,4},{1,7},{3,1},{5,3},{7,5},{8,14},{10,8},{12,... | collective-permute-start | bytes 983048 | tf_op jit(solution)/shard_map/ppermute | solution.py:16
  23.4 40.3 %collective-permute-start.1 = (bf16[16,80,128]{2,1,0:T(8,128)(2,1)}, bf16[16,80,128]{2,1,0:T(8,128)(2,1)}, u32[]{:S(2)}, u32[]{:S(2)}) collective-permute-start(bf16[16,80,128]{2,1,0:T(8,128)(2,1)} %get-tuple-element.65), channel_id=1, source_target_pairs={{0,4},{2,6},{4,0},{6,2},{1,5},{3,7},{5,1},{7,3},{8,12},{10,14},{12... | collective-permute-start | bytes 983048 | tf_op jit(solution)/shard_map/ppermute | solution.py:16
  24.0 39.9 %collective-permute-start.2 = (bf16[16,80,128]{2,1,0:T(8,128)(2,1)}, bf16[16,80,128]{2,1,0:T(8,128)(2,1)}, u32[]{:S(2)}, u32[]{:S(2)}) collective-permute-start(bf16[16,80,128]{2,1,0:T(8,128)(2,1)} %get-tuple-element.64), channel_id=1, source_target_pairs={{0,2},{2,4},{4,6},{6,0},{1,3},{3,5},{5,7},{7,1},{8,10},{10,12},{12... | collective-permute-start | bytes 983048 | tf_op jit(solution)/shard_map/ppermute | solution.py:16
  25.0 0.7 copy-start.6
  25.0 7.5 %collective-permute-start.3 = (bf16[1,80,128]{2,1,0:T(8,128)(2,1)}, bf16[1,80,128]{2,1,0:T(8,128)(2,1)}, u32[]{:S(2)}, u32[]{:S(2)}) collective-permute-start(bf16[1,80,128]{2,1,0:T(8,128)(2,1)} %select_bitcast_fusion), channel_id=1, source_target_pairs={{0,1},{1,0},{2,3},{3,2},{4,5},{5,4},{6,7},{7,6},{8,9},{9,8},{10,11... | collective-permute-start | bytes 61448 | tf_op jit(solution)/shard_map/ppermute | solution.py:16
  25.2 0.7 copy-start.7
  27.1 6.2 %copy-start.1 = (bf16[4,160,720]{2,1,0:T(8,128)(2,1)}, bf16[4,160,720]{2,1,0:T(8,128)(2,1)S(1)}, u32[]{:S(2)}) copy-start(bf16[4,160,720]{2,1,0:T(8,128)(2,1)S(1)} %pad_maximum_fusion.refs_8_.refs_0_) | copy-start | bytes 2764804
  27.1 36.7 %collective-permute-start.12 = (bf16[4,160,720]{2,1,0:T(8,128)(2,1)S(1)}, bf16[4,160,720]{2,1,0:T(8,128)(2,1)S(1)}, u32[]{:S(2)}, u32[]{:S(2)}) collective-permute-start(bf16[4,160,720]{2,1,0:T(8,128)(2,1)S(1)} %pad_maximum_fusion.refs_8_.refs_0_), channel_id=1, source_target_pairs={{0,1},{1,0},{2,3},{3,2},{4,5},{5,4},{6,7},{7,6},{8,9},{9,8},{10,11... | collective-permute-start | bytes 2764808 | tf_op jit(solution)/shard_map/ppermute | solution.py:16
  34.1 13.5 %collective-permute-start.4 = (bf16[4,80,128]{2,1,0:T(8,128)(2,1)S(1)}, bf16[4,80,128]{2,1,0:T(8,128)(2,1)S(1)}, u32[]{:S(2)}, u32[]{:S(2)}) collective-permute-start(bf16[4,80,128]{2,1,0:T(8,128)(2,1)S(1)} %pad_maximum_fusion.6), channel_id=1, source_target_pairs={{0,6},{2,0},{4,2},{6,4},{1,7},{3,1},{5,3},{7,5},{8,14},{10,8},{12,... | collective-permute-start | bytes 245768 | tf_op jit(solution)/shard_map/ppermute | solution.py:16
  47.6 16.3 %copy-start.13 = (bf16[4,80,128]{2,1,0:T(8,128)(2,1)}, bf16[4,80,128]{2,1,0:T(8,128)(2,1)S(1)}, u32[]{:S(2)}) copy-start(bf16[4,80,128]{2,1,0:T(8,128)(2,1)S(1)} %collective-permute-done.4.refs_5_.refs_6_) | copy-start | bytes 245764
  47.6 6.4 %collective-permute-start.5 = (bf16[4,80,128]{2,1,0:T(8,128)(2,1)S(1)}, bf16[4,80,128]{2,1,0:T(8,128)(2,1)S(1)}, u32[]{:S(2)}, u32[]{:S(2)}) collective-permute-start(bf16[4,80,128]{2,1,0:T(8,128)(2,1)S(1)} %pad_maximum_fusion.7), channel_id=1, source_target_pairs={{0,4},{2,6},{4,0},{6,2},{1,5},{3,7},{5,1},{7,3},{8,12},{10,14},{12... | collective-permute-start | bytes 245768 | tf_op jit(solution)/shard_map/ppermute | solution.py:16
  54.0 9.9 %copy-start.14 = (bf16[4,80,128]{2,1,0:T(8,128)(2,1)}, bf16[4,80,128]{2,1,0:T(8,128)(2,1)S(1)}, u32[]{:S(2)}) copy-start(bf16[4,80,128]{2,1,0:T(8,128)(2,1)S(1)} %collective-permute-done.5.refs_6_.refs_7_) | copy-start | bytes 245764
  54.0 7.2 %collective-permute-start.6 = (bf16[4,80,128]{2,1,0:T(8,128)(2,1)S(1)}, bf16[4,80,128]{2,1,0:T(8,128)(2,1)S(1)}, u32[]{:S(2)}, u32[]{:S(2)}) collective-permute-start(bf16[4,80,128]{2,1,0:T(8,128)(2,1)S(1)} %pad_maximum_fusion.8), channel_id=1, source_target_pairs={{0,2},{2,4},{4,6},{6,0},{1,3},{3,5},{5,7},{7,1},{8,10},{10,12},{12... | collective-permute-start | bytes 245768 | tf_op jit(solution)/shard_map/ppermute | solution.py:16
  61.2 2.7 %copy-start.15 = (bf16[4,80,128]{2,1,0:T(8,128)(2,1)}, bf16[4,80,128]{2,1,0:T(8,128)(2,1)S(1)}, u32[]{:S(2)}) copy-start(bf16[4,80,128]{2,1,0:T(8,128)(2,1)S(1)} %collective-permute-done.6.refs_7_.refs_8_) | copy-start | bytes 245764
  61.2 20.9 %collective-permute-start.16 = (bf16[14,80,128]{2,1,0:T(8,128)(2,1)}, bf16[14,80,128]{2,1,0:T(8,128)(2,1)S(1)}, u32[]{:S(2)}, u32[]{:S(2)}) collective-permute-start(bf16[14,80,128]{2,1,0:T(8,128)(2,1)} %get-tuple-element.53), channel_id=1, source_target_pairs={{0,6},{2,0},{4,2},{6,4},{1,7},{3,1},{5,3},{7,5},{8,14},{10,8},{12,... | collective-permute-start | bytes 860168 | tf_op jit(solution)/shard_map/ppermute | solution.py:16
  63.2 40.9 %collective-permute-start.17 = (bf16[14,80,128]{2,1,0:T(8,128)(2,1)}, bf16[14,80,128]{2,1,0:T(8,128)(2,1)S(1)}, u32[]{:S(2)}, u32[]{:S(2)}) collective-permute-start(bf16[14,80,128]{2,1,0:T(8,128)(2,1)} %get-tuple-element.55), channel_id=1, source_target_pairs={{0,4},{2,6},{4,0},{6,2},{1,5},{3,7},{5,1},{7,3},{8,12},{10,14},{12... | collective-permute-start | bytes 860168 | tf_op jit(solution)/shard_map/ppermute | solution.py:16
  63.7 41.8 %collective-permute-start.18 = (bf16[14,80,128]{2,1,0:T(8,128)(2,1)}, bf16[14,80,128]{2,1,0:T(8,128)(2,1)S(1)}, u32[]{:S(2)}, u32[]{:S(2)}) collective-permute-start(bf16[14,80,128]{2,1,0:T(8,128)(2,1)} %get-tuple-element.52), channel_id=1, source_target_pairs={{0,2},{2,4},{4,6},{6,0},{1,3},{3,5},{5,7},{7,1},{8,10},{10,12},{12... | collective-permute-start | bytes 860168 | tf_op jit(solution)/shard_map/ppermute | solution.py:16
  63.9 1.0 copy-start.4
  77.8 65.0 %collective-permute-start.13 = (bf16[16,80,128]{2,1,0:T(8,128)(2,1)}, bf16[16,80,128]{2,1,0:T(8,128)(2,1)S(1)}, u32[]{:S(2)}, u32[]{:S(2)}) collective-permute-start(bf16[16,80,128]{2,1,0:T(8,128)(2,1)} %get-tuple-element.23), channel_id=1, source_target_pairs={{0,2},{2,4},{4,6},{6,0},{1,3},{3,5},{5,7},{7,1},{8,10},{10,12},{12... | collective-permute-start | bytes 983048 | tf_op jit(solution)/shard_map/ppermute | solution.py:16
  80.7 63.2 %collective-permute-start.14 = (bf16[16,80,128]{2,1,0:T(8,128)(2,1)}, bf16[16,80,128]{2,1,0:T(8,128)(2,1)S(1)}, u32[]{:S(2)}, u32[]{:S(2)}) collective-permute-start(bf16[16,80,128]{2,1,0:T(8,128)(2,1)} %get-tuple-element.24), channel_id=1, source_target_pairs={{0,4},{2,6},{4,0},{6,2},{1,5},{3,7},{5,1},{7,3},{8,12},{10,14},{12... | collective-permute-start | bytes 983048 | tf_op jit(solution)/shard_map/ppermute | solution.py:16
  82.1 24.7 %copy-start.10 = (bf16[14,80,128]{2,1,0:T(8,128)(2,1)}, bf16[14,80,128]{2,1,0:T(8,128)(2,1)S(1)}, u32[]{:S(2)}) copy-start(bf16[14,80,128]{2,1,0:T(8,128)(2,1)S(1)} %collective-permute-done.16.refs_2_) | copy-start | bytes 860164
  82.1 65.4 %collective-permute-start.15 = (bf16[16,80,128]{2,1,0:T(8,128)(2,1)}, bf16[16,80,128]{2,1,0:T(8,128)(2,1)S(1)}, u32[]{:S(2)}, u32[]{:S(2)}) collective-permute-start(bf16[16,80,128]{2,1,0:T(8,128)(2,1)} %get-tuple-element.25), channel_id=1, source_target_pairs={{0,6},{2,0},{4,2},{6,4},{1,7},{3,1},{5,3},{7,5},{8,14},{10,8},{12,... | collective-permute-start | bytes 983048 | tf_op jit(solution)/shard_map/ppermute | solution.py:16
  104.2 2.6 %copy-start.11 = (bf16[14,80,128]{2,1,0:T(8,128)(2,1)}, bf16[14,80,128]{2,1,0:T(8,128)(2,1)S(1)}, u32[]{:S(2)}) copy-start(bf16[14,80,128]{2,1,0:T(8,128)(2,1)S(1)} %collective-permute-done.17.refs_3_) | copy-start | bytes 860164
  104.2 17.8 %collective-permute-start.19 = (bf16[1,320,128]{2,1,0:T(8,128)(2,1)}, bf16[1,320,128]{2,1,0:T(8,128)(2,1)S(1)}, u32[]{:S(2)}, u32[]{:S(2)}) collective-permute-start(bf16[1,320,128]{2,1,0:T(8,128)(2,1)} %get-tuple-element.29), channel_id=1, source_target_pairs={{0,2},{2,4},{4,6},{6,7},{7,5},{5,3},{3,1},{8,10},{10,12},{12,14},{... | collective-permute-start | bytes 245768 | tf_op jit(solution)/shard_map/ppermute | solution.py:577
  105.5 1.3 copy-start.12
  105.5 16.5 %collective-permute-start.20 = (bf16[1,320,128]{2,1,0:T(8,128)(2,1)}, bf16[1,320,128]{2,1,0:T(8,128)(2,1)S(1)}, u32[]{:S(2)}, u32[]{:S(2)}) collective-permute-start(bf16[1,320,128]{2,1,0:T(8,128)(2,1)} %get-tuple-element.30), channel_id=1, source_target_pairs={{2,0},{4,2},{6,4},{7,6},{5,7},{3,5},{1,3},{10,8},{12,10},{14,12},{... | collective-permute-start | bytes 245768 | tf_op jit(solution)/shard_map/ppermute | solution.py:578
  122.0 0.6 copy-start.16
  122.0 43.0 %collective-permute-start.24 = (f32[4,6,40,320]{3,2,1,0:T(8,128)}, f32[4,6,40,320]{3,2,1,0:T(8,128)S(1)}, u32[]{:S(2)}, u32[]{:S(2)}) collective-permute-start(f32[4,6,40,320]{3,2,1,0:T(8,128)} %get-tuple-element.37), channel_id=1, source_target_pairs={{0,1},{1,0},{2,3},{3,2},{4,5},{5,4},{6,7},{7,6},{8,9},{9,8},{10,11... | collective-permute-start | bytes 3686408 | tf_op jit(solution)/shard_map/ppermute | solution.py:16
  122.0 0.6 copy-start.17
  134.0 8.9 %copy-start.9 = (bf16[16,80,128]{2,1,0:T(8,128)(2,1)S(1)}, bf16[16,80,128]{2,1,0:T(8,128)(2,1)}, u32[]{:S(2)}) copy-start(bf16[16,80,128]{2,1,0:T(8,128)(2,1)} %get-tuple-element.34) | copy-start | bytes 983044
  134.0 10.0 %copy-start.8 = (bf16[16,80,128]{2,1,0:T(8,128)(2,1)S(1)}, bf16[16,80,128]{2,1,0:T(8,128)(2,1)}, u32[]{:S(2)}) copy-start(bf16[16,80,128]{2,1,0:T(8,128)(2,1)} %get-tuple-element.35) | copy-start | bytes 983044
  134.0 14.3 %collective-permute-start.21 = (bf16[16,80,128]{2,1,0:T(8,128)(2,1)}, bf16[16,80,128]{2,1,0:T(8,128)(2,1)S(1)}, u32[]{:S(2)}, u32[]{:S(2)}) collective-permute-start(bf16[16,80,128]{2,1,0:T(8,128)(2,1)} %get-tuple-element.33), channel_id=1, source_target_pairs={{0,2},{2,4},{4,6},{6,0},{1,3},{3,5},{5,7},{7,1},{8,10},{10,12},{12... | collective-permute-start | bytes 983048 | tf_op jit(solution)/shard_map/ppermute | solution.py:16
  142.8 18.2 %collective-permute-start.22 = (bf16[16,80,128]{2,1,0:T(8,128)(2,1)S(1)}, bf16[16,80,128]{2,1,0:T(8,128)(2,1)S(1)}, u32[]{:S(2)}, u32[]{:S(2)}) collective-permute-start(bf16[16,80,128]{2,1,0:T(8,128)(2,1)S(1)} %copy-done.9), channel_id=1, source_target_pairs={{0,4},{2,6},{4,0},{6,2},{1,5},{3,7},{5,1},{7,3},{8,12},{10,14},{12... | collective-permute-start | bytes 983048 | tf_op jit(solution)/shard_map/ppermute | solution.py:16
  143.9 22.0 %collective-permute-start.23 = (bf16[16,80,128]{2,1,0:T(8,128)(2,1)S(1)}, bf16[16,80,128]{2,1,0:T(8,128)(2,1)S(1)}, u32[]{:S(2)}, u32[]{:S(2)}) collective-permute-start(bf16[16,80,128]{2,1,0:T(8,128)(2,1)S(1)} %copy-done.8), channel_id=1, source_target_pairs={{0,6},{2,0},{4,2},{6,4},{1,7},{3,1},{5,3},{7,5},{8,14},{10,8},{12,... | collective-permute-start | bytes 983048 | tf_op jit(solution)/shard_map/ppermute | solution.py:16
  147.5 14.4 %copy-start.5 = (f32[4,3,40,320]{3,2,1,0:T(8,128)S(1)}, f32[4,3,40,320]{3,2,1,0:T(8,128)}, u32[]{:S(2)}) copy-start(f32[4,3,40,320]{3,2,1,0:T(8,128)} %get-tuple-element.39) | copy-start | bytes 1843204
  147.5 14.4 %collective-permute-start.31 = (f32[4,3,40,320]{3,2,1,0:T(8,128)}, f32[4,3,40,320]{3,2,1,0:T(8,128)S(1)}, u32[]{:S(2)}, u32[]{:S(2)}) collective-permute-start(f32[4,3,40,320]{3,2,1,0:T(8,128)} %get-tuple-element.40), channel_id=1, source_target_pairs={{0,1},{1,0},{2,3},{3,2},{4,5},{5,4},{6,7},{7,6},{8,9},{9,8},{10,11... | collective-permute-start | bytes 1843208 | tf_op jit(solution)/shard_map/ppermute | solution.py:16
  161.9 3.1 %copy-start.3 = (f32[4,6,40,320]{3,2,1,0:T(8,128)S(1)}, f32[4,6,40,320]{3,2,1,0:T(8,128)}, u32[]{:S(2)}) copy-start(f32[4,6,40,320]{3,2,1,0:T(8,128)} %get-tuple-element.36) | copy-start | bytes 3686404
  162.0 8.5 %collective-permute-start.34 = (f32[3,40,320]{2,1,0:T(8,128)S(1)}, f32[3,40,320]{2,1,0:T(8,128)S(1)}, u32[]{:S(2)}, u32[]{:S(2)}) collective-permute-start(f32[3,40,320]{2,1,0:T(8,128)S(1)} %get-tuple-element.69), channel_id=1, source_target_pairs={{0,8},{8,16},{16,24},{24,0},{1,9},{9,17},{17,25},{25,1},{2,10},{10... | collective-permute-start | bytes 460808 | tf_op jit(solution)/shard_map/ppermute | solution.py:16
  162.3 12.2 %collective-permute-start.33 = (f32[3,40,320]{2,1,0:T(8,128)S(1)}, f32[3,40,320]{2,1,0:T(8,128)S(1)}, u32[]{:S(2)}, u32[]{:S(2)}) collective-permute-start(f32[3,40,320]{2,1,0:T(8,128)S(1)} %get-tuple-element.70), channel_id=1, source_target_pairs={{0,16},{8,24},{16,0},{24,8},{1,17},{9,25},{17,1},{25,9},{2,18},{10... | collective-permute-start | bytes 460808 | tf_op jit(solution)/shard_map/ppermute | solution.py:16
  162.9 11.5 %collective-permute-start.32 = (f32[3,40,320]{2,1,0:T(8,128)S(1)}, f32[3,40,320]{2,1,0:T(8,128)S(1)}, u32[]{:S(2)}, u32[]{:S(2)}) collective-permute-start(f32[3,40,320]{2,1,0:T(8,128)S(1)} %get-tuple-element.68), channel_id=1, source_target_pairs={{0,24},{8,0},{16,8},{24,16},{1,25},{9,1},{17,9},{25,17},{2,26},{10... | collective-permute-start | bytes 460808 | tf_op jit(solution)/shard_map/ppermute | solution.py:16
  165.3 17.1 %collective-permute-start.27 = (f32[6,40,320]{2,1,0:T(8,128)S(1)}, f32[6,40,320]{2,1,0:T(8,128)S(1)}, u32[]{:S(2)}, u32[]{:S(2)}) collective-permute-start(f32[6,40,320]{2,1,0:T(8,128)S(1)} %get-tuple-element.42), channel_id=1, source_target_pairs={{0,8},{8,16},{16,24},{24,0},{1,9},{9,17},{17,25},{25,1},{2,10},{10... | collective-permute-start | bytes 921608 | tf_op jit(solution)/shard_map/ppermute | solution.py:16
  165.9 22.0 %collective-permute-start.26 = (f32[6,40,320]{2,1,0:T(8,128)S(1)}, f32[6,40,320]{2,1,0:T(8,128)S(1)}, u32[]{:S(2)}, u32[]{:S(2)}) collective-permute-start(f32[6,40,320]{2,1,0:T(8,128)S(1)} %get-tuple-element.43), channel_id=1, source_target_pairs={{0,16},{8,24},{16,0},{24,8},{1,17},{9,25},{17,1},{25,9},{2,18},{10... | collective-permute-start | bytes 921608 | tf_op jit(solution)/shard_map/ppermute | solution.py:16
  170.5 17.5 %collective-permute-start.25 = (f32[6,40,320]{2,1,0:T(8,128)S(1)}, f32[6,40,320]{2,1,0:T(8,128)S(1)}, u32[]{:S(2)}, u32[]{:S(2)}) collective-permute-start(f32[6,40,320]{2,1,0:T(8,128)S(1)} %get-tuple-element.41), channel_id=1, source_target_pairs={{0,24},{8,0},{16,8},{24,16},{1,25},{9,1},{17,9},{25,17},{2,26},{10... | collective-permute-start | bytes 921608 | tf_op jit(solution)/shard_map/ppermute | solution.py:16
  188.3 13.6 %collective-permute-start.28 = (f32[160,240]{0,1:T(8,128)S(1)}, f32[160,240]{0,1:T(8,128)S(1)}, u32[]{:S(2)}, u32[]{:S(2)}) collective-permute-start(f32[160,240]{0,1:T(8,128)S(1)} %pad_maximum_fusion.3), channel_id=1, source_target_pairs={{0,2},{2,0},{4,6},{6,4},{1,3},{3,1},{5,7},{7,5},{8,10},{10,8},{12,... | collective-permute-start | bytes 460808 | tf_op jit(solution)/shard_map/ppermute | solution.py:20
  194.2 10.9 %collective-permute-start.37 = (f32[80,120]{0,1:T(8,128)S(1)}, f32[80,120]{0,1:T(8,128)S(1)}, u32[]{:S(2)}, u32[]{:S(2)}) collective-permute-start(f32[80,120]{0,1:T(8,128)S(1)} %bitcast.160), channel_id=1, source_target_pairs={{0,2},{2,4},{4,6},{6,0},{1,3},{3,5},{5,7},{7,1},{8,10},{10,12},{12... | collective-permute-start | bytes 115208 | tf_op jit(solution)/shard_map/ppermute | solution.py:16
  194.2 10.9 %collective-permute-start.36 = (f32[80,120]{0,1:T(8,128)S(1)}, f32[80,120]{0,1:T(8,128)S(1)}, u32[]{:S(2)}, u32[]{:S(2)}) collective-permute-start(f32[80,120]{0,1:T(8,128)S(1)} %bitcast.159), channel_id=1, source_target_pairs={{0,4},{2,6},{4,0},{6,2},{1,5},{3,7},{5,1},{7,3},{8,12},{10,14},{12... | collective-permute-start | bytes 115208 | tf_op jit(solution)/shard_map/ppermute | solution.py:16
  197.7 7.4 %collective-permute-start.35 = (f32[80,120]{0,1:T(8,128)S(1)}, f32[80,120]{0,1:T(8,128)S(1)}, u32[]{:S(2)}, u32[]{:S(2)}) collective-permute-start(f32[80,120]{0,1:T(8,128)S(1)} %bitcast.158), channel_id=1, source_target_pairs={{0,6},{2,0},{4,2},{6,4},{1,7},{3,1},{5,3},{7,5},{8,14},{10,8},{12,... | collective-permute-start | bytes 115208 | tf_op jit(solution)/shard_map/ppermute | solution.py:16
  202.1 6.3 %collective-permute-start.29 = (f32[80,240]{0,1:T(8,128)S(1)}, f32[80,240]{0,1:T(8,128)S(1)}, u32[]{:S(2)}, u32[]{:S(2)}) collective-permute-start(f32[80,240]{0,1:T(8,128)S(1)} %bitcast_add_fusion), channel_id=1, source_target_pairs={{0,4},{2,6},{4,0},{6,2},{1,5},{3,7},{5,1},{7,3},{8,12},{10,14},{12... | collective-permute-start | bytes 230408 | tf_op jit(solution)/shard_map/ppermute | solution.py:20
  205.1 3.5 %collective-permute-start.38 = (f32[80,120]{0,1:T(8,128)S(1)}, f32[80,120]{0,1:T(8,128)S(1)}, u32[]{:S(2)}, u32[]{:S(2)}) collective-permute-start(f32[80,120]{0,1:T(8,128)S(1)} %fusion.16), channel_id=1, source_target_pairs={{0,1},{1,0},{2,3},{3,2},{4,5},{5,4},{6,7},{7,6},{8,9},{9,8},{10,11... | collective-permute-start | bytes 115208 | tf_op jit(solution)/shard_map/ppermute | solution.py:16
  208.5 1.4 collective-permute-start.30

commit v7 on v5

--- a/solution.py
+++ b/solution.py
@@ -219,18 +219,14 @@
     channels, pixels = slope.shape
     width = stacked.shape[1] - pixels
     width = width // 2
-    tap = first_tap + pl.program_id(0)
-    tap_row, tap_col = tap // 3, lax.rem(tap, 3)
+    tap_row = (first_tap + pl.program_id(0)) // 3
     if count:
 
         @pl.when(pl.program_id(0) == 0)
         def _():
             slope_rows(factor, pieces, ends, slope)
 
-    source = stacked[
-        pl.ds(pl.multiple_of(tap_col * channels, channels), channels),
-        pl.ds(pl.multiple_of(tap_row * width, width), pixels),
-    ]
+    source = stacked[:, pl.ds(pl.multiple_of(tap_row * width, width), pixels)]
     grads = lax.dot_general(
         source, slope[...], (((1,), (1,)), ((), ())), preferred_element_type=jnp.float32
     )
@@ -261,7 +257,10 @@
     call = pl.pallas_call(
         functools.partial(correlate_body, first_tap, len(pieces), groups, rows),
         grid=(tap_count,),
-        in_specs=[pl.BlockSpec(memory_space=pltpu.SMEM), whole(stacked.shape)]
+        in_specs=[
+            pl.BlockSpec(memory_space=pltpu.SMEM),
+            pl.BlockSpec((channels, stacked.shape[1]), lambda t: ((first_tap + t) % 3, 0)),
+        ]
         + [whole(operand.shape) for operand in operands],
         out_specs=[pl.BlockSpec((groups, 1, size, channels), lambda t: (0, t, 0, 0))] * rows
         + [whole(each.shape) for each in made],
@@ -338,7 +337,7 @@
 
 
 def backward_body(count, shares, rows, turns, slope, above, below, kernels, *refs):
-    outs, stacked = refs[:count], refs[count]
+    outs, (stacked, weights, arrived) = refs[:count], refs[count:]
     channels = slope.shape[0]
     _, _, width = above.shape
     height = slope.shape[1] // width
@@ -368,6 +367,8 @@
 
     @pl.when(step == 0)
     def _():
+        fetch = pltpu.make_async_copy(kernels, weights, arrived)
+        fetch.start()
         if stride > channels:
             for copies in range(3):
                 stacked[copies * stride + channels : (copies + 1) * stride, :] = jnp.zeros(
@@ -386,12 +387,13 @@
             return carry
 
         lax.fori_loop(0, height, body, 0)
+        fetch.wait()
 
     windows = [
         stacked[:, pl.ds(pl.multiple_of((step * rows + a) * width, width), rows * width)]
         for a in range(3)
     ]
-    order = [kernels[lax.rem(turns[2] + j, count)] for j in range(count)]
+    order = [weights[lax.rem(turns[2] + j, count)] for j in range(count)]
     grad = jnp.dot(
         jnp.concatenate(order), jnp.concatenate(windows), preferred_element_type=jnp.float32
     )
@@ -418,11 +420,15 @@
                 whole(slope.shape),
                 whole(above.shape),
                 whole(below.shape),
-                whole(kernels.shape),
+                pl.BlockSpec(memory_space=pl.ANY),
             ],
             out_specs=[pl.BlockSpec((rows, depth, width), lambda g, turns: (turns[4] * steps + g, 0, 0))]
             + [pl.BlockSpec((rows, depth, width), lambda g, _: (g, 0, 0))] * (count - 1),
-            scratch_shapes=[pltpu.VMEM((kernels.shape[2] // 3, (height + 2) * width), jnp.bfloat16)],
+            scratch_shapes=[
+                pltpu.VMEM((kernels.shape[2] // 3, (height + 2) * width), jnp.bfloat16),
+                pltpu.VMEM(kernels.shape, kernels.dtype),
+                pltpu.SemaphoreType.DMA,
+            ],
         ),
         out_shape=[jax.ShapeDtypeStruct((slab, depth, width), jnp.float32)]
         + [jax.ShapeDtypeStruct((height, depth, width), jnp.bfloat16)] * (count - 1),

time: 207 us -> 207 us (level)
  no operation moved by 1% of the time
where the time goes in v7:
time: 207 us; the launch traced here: 206 us
  waiting for transfers between devices  69.6 us (34%)
  starting transfers between devices  69 us (33%)
  Pallas kernels  45.2 us (22%)
  local copies, waits for them, and re-layouts  11.6 us (6%)
  other arithmetic  9.28 us (4%)
    ppermute x39, waiting for transfers between devices, receive(): lax.ppermute(block, axis, [(i, (i - ahead) % count) for i in range(count)])  69.5 us
    ppermute x39, starting transfers between devices, receive(): lax.ppermute(block, axis, [(i, (i - ahead) % count) for i in range(count)])  66.4 us
    pallas_call x2, Pallas kernels, correlate(): results = call(turn, stacked, *operands)  17.1 us
    pallas_call x1, Pallas kernels, forward(): results = call(turns, *pieces, *rims, *halves)  12.9 us
    pallas_call x1, Pallas kernels, backward(): pl.pallas_call(functools.partial(backward_body, count, lax.axis_size('row...  10.6 us
    pallas_call x1, Pallas kernels, turned(): pl.pallas_call(functools.partial(turned_body, shares), grid=(blocks,), in...  4.53 us
  transfers between devices with their start and end apart: 41, of which 15 were waited for; matrix products, arithmetic and copies ran while one was open for 8% of the time, Pallas kernels for 22%

profile of v7, /device:TPU:0, one launch (start us, length us, event | category | flops | bytes accessed | tf_op | source)
XLA Modules:
  0.0 205.6 jit_solution(4908627194841573767)
XLA Ops:
  0.7 0.9 copy-done
  1.8 3.1 %collective-permute-start.9 = (bf16[40,720]{1,0:T(8,128)(2,1)S(1)}, bf16[40,720]{1,0:T(8,128)(2,1)S(1)}, u32[]{:S(2)}, u32[]{:S(2)}) collective-permute-start(bf16[40,720]{1,0:T(8,128)(2,1)S(1)} %copy.11), channel_id=1, source_target_pairs={{0,2},{2,4},{4,6},{6,0},{1,3},{3,5},{5,7},{7,1},{8,10},{10,12},{12... | collective-permute-start | bytes 172808 | tf_op jit(solution)/shard_map/ppermute | solution.py:16
  4.9 2.6 %collective-permute-start.8 = (bf16[40,720]{1,0:T(8,128)(2,1)S(1)}, bf16[40,720]{1,0:T(8,128)(2,1)S(1)}, u32[]{:S(2)}, u32[]{:S(2)}) collective-permute-start(bf16[40,720]{1,0:T(8,128)(2,1)S(1)} %copy.11), channel_id=1, source_target_pairs={{0,4},{2,6},{4,0},{6,2},{1,5},{3,7},{5,1},{7,3},{8,12},{10,14},{12... | collective-permute-start | bytes 172808 | tf_op jit(solution)/shard_map/ppermute | solution.py:16
  7.5 1.3 collective-permute-start.7
  9.3 2.5 %collective-permute-done.8 = bf16[40,720]{1,0:T(8,128)(2,1)S(1)} collective-permute-done((bf16[40,720]{1,0:T(8,128)(2,1)S(1)}, bf16[40,720]{1,0:T(8,128)(2,1)S(1)}, u32[]{:S(2)}, u32[]{:S(2)}) %collective-permute-start.8) | collective-permute-done | bytes 57632 | tf_op jit(solution)/shard_map/ppermute | solution.py:16
  12.1 1.5 collective-permute-start.12
  13.6 1.5 collective-permute-start.11
  15.1 1.4 collective-permute-start.10
  16.6 1.1 dynamic-slice_bitcast_fusion
  17.6 2.9 %collective-permute-start = (bf16[16,80,128]{2,1,0:T(8,128)(2,1)}, bf16[16,80,128]{2,1,0:T(8,128)(2,1)}, u32[]{:S(2)}, u32[]{:S(2)}) collective-permute-start(bf16[16,80,128]{2,1,0:T(8,128)(2,1)} %get-tuple-element.66), channel_id=1, source_target_pairs={{0,6},{2,0},{4,2},{6,4},{1,7},{3,1},{5,3},{7,5},{8,14},{10,8},{12,... | collective-permute-start | bytes 983048 | tf_op jit(solution)/shard_map/ppermute | solution.py:16
  21.2 0.7 collective-permute-done.12
  21.9 1.4 collective-permute-start.2
  23.3 2.0 collective-permute-done.11
  25.3 0.7 copy-done.6
  26.0 1.1 pad_maximum_fusion.refs_8_.refs_0_
  27.6 2.3 %dynamic-slice_bitcast_fusion.4 = (bf16[14,80,128]{2,1,0:T(8,128)(2,1)}, bf16[14,80,128]{2,1,0:T(8,128)(2,1)}, bf16[14,80,128]{2,1,0:T(8,128)(2,1)}, bf16[14,80,128]{2,1,0:T(8,128)(2,1)}) fusion(bf16[1,64,80,128]{3,2,1,0:T(8,128)(2,1)} %param.5, s32[]{:T(128)S(6)} %select_n.336, s32[]{:T(128)S(6)} %select_n.334, s32[]{:T(128)S(6)} %select_n.333, ...), kind=kLoop, calls=%fused_computation.24 | loop fusion | bytes 2293776 | tf_op jit(solution)/shard_map/dynamic_slice | solution.py:535
  30.0 1.5 dynamic-slice_bitcast_fusion.9
  32.0 0.7 stack.64.turns
  32.7 0.7 bitcast_select_fusion.1
  33.5 0.8 pad_maximum_fusion.4
  34.2 2.2 %collective-permute-start.4 = (bf16[4,80,128]{2,1,0:T(8,128)(2,1)S(1)}, bf16[4,80,128]{2,1,0:T(8,128)(2,1)S(1)}, u32[]{:S(2)}, u32[]{:S(2)}) collective-permute-start(bf16[4,80,128]{2,1,0:T(8,128)(2,1)S(1)} %pad_maximum_fusion.4), channel_id=1, source_target_pairs={{0,6},{2,0},{4,2},{6,4},{1,7},{3,1},{5,3},{7,5},{8,14},{10,8},{12,... | collective-permute-start | bytes 245768 | tf_op jit(solution)/shard_map/ppermute | solution.py:16
  36.4 0.8 pad_maximum_fusion.5
  37.2 9.4 %collective-permute-done.4.refs_5_.refs_6_ = bf16[4,80,128]{2,1,0:T(8,128)(2,1)S(1)} collective-permute-done((bf16[4,80,128]{2,1,0:T(8,128)(2,1)S(1)}, bf16[4,80,128]{2,1,0:T(8,128)(2,1)S(1)}, u32[]{:S(2)}, u32[]{:S(2)}) %collective-permute-start.4) | collective-permute-done | bytes 81952 | tf_op jit(solution)/shard_map/ppermute | solution.py:16
  46.6 2.9 %collective-permute-start.5 = (bf16[4,80,128]{2,1,0:T(8,128)(2,1)S(1)}, bf16[4,80,128]{2,1,0:T(8,128)(2,1)S(1)}, u32[]{:S(2)}, u32[]{:S(2)}) collective-permute-start(bf16[4,80,128]{2,1,0:T(8,128)(2,1)S(1)} %pad_maximum_fusion.5), channel_id=1, source_target_pairs={{0,4},{2,6},{4,0},{6,2},{1,5},{3,7},{5,1},{7,3},{8,12},{10,14},{12... | collective-permute-start | bytes 245768 | tf_op jit(solution)/shard_map/ppermute | solution.py:16
  49.5 3.3 %collective-permute-done.5.refs_6_.refs_7_ = bf16[4,80,128]{2,1,0:T(8,128)(2,1)S(1)} collective-permute-done((bf16[4,80,128]{2,1,0:T(8,128)(2,1)S(1)}, bf16[4,80,128]{2,1,0:T(8,128)(2,1)S(1)}, u32[]{:S(2)}, u32[]{:S(2)}) %collective-permute-start.5) | collective-permute-done | bytes 81952 | tf_op jit(solution)/shard_map/ppermute | solution.py:16
  52.9 3.0 %collective-permute-start.6 = (bf16[4,80,128]{2,1,0:T(8,128)(2,1)S(1)}, bf16[4,80,128]{2,1,0:T(8,128)(2,1)S(1)}, u32[]{:S(2)}, u32[]{:S(2)}) collective-permute-start(bf16[4,80,128]{2,1,0:T(8,128)(2,1)S(1)} %pad_maximum_fusion.6), channel_id=1, source_target_pairs={{0,2},{2,4},{4,6},{6,0},{1,3},{3,5},{5,7},{7,1},{8,10},{10,12},{12... | collective-permute-start | bytes 245768 | tf_op jit(solution)/shard_map/ppermute | solution.py:16
  55.9 0.7 pad_maximum_fusion.3.refs_4_.refs_5_
  56.5 3.4 %collective-permute-done.6.refs_7_.refs_8_ = bf16[4,80,128]{2,1,0:T(8,128)(2,1)S(1)} collective-permute-done((bf16[4,80,128]{2,1,0:T(8,128)(2,1)S(1)}, bf16[4,80,128]{2,1,0:T(8,128)(2,1)S(1)}, u32[]{:S(2)}, u32[]{:S(2)}) %collective-permute-start.6) | collective-permute-done | bytes 81952 | tf_op jit(solution)/shard_map/ppermute | solution.py:16
  60.0 1.0 collective-permute-start.17
  61.0 1.5 collective-permute-start.18
  62.5 0.9 copy-done.4
  63.4 12.9 %conv_forward.1 = (bf16[64,80,128]{2,1,0:T(8,128)(2,1)}, bf16[16,80,128]{2,1,0:T(8,128)(2,1)}, bf16[16,80,128]{2,1,0:T(8,128)(2,1)}, bf16[16,80,128]{2,1,0:T(8,1...) custom-call(s32[3]{0:T(128)} %pad_add_fusion.turns, ...), custom_call_target="tpu_custom_call" | custom-call | flops 3774873600 | bytes 16777216 | tf_op jit(solution)/shard_map/conv_forward/pallas_call | solution.py:188
  76.4 2.1 %collective-permute-start.14 = (bf16[16,80,128]{2,1,0:T(8,128)(2,1)}, bf16[16,80,128]{2,1,0:T(8,128)(2,1)S(1)}, u32[]{:S(2)}, u32[]{:S(2)}) collective-permute-start(bf16[16,80,128]{2,1,0:T(8,128)(2,1)} %get-tuple-element.23), channel_id=1, source_target_pairs={{0,2},{2,4},{4,6},{6,0},{1,3},{3,5},{5,7},{7,1},{8,10},{10,12},{12... | collective-permute-start | bytes 983048 | tf_op jit(solution)/shard_map/ppermute | solution.py:16
  78.4 2.4 %collective-permute-start.15 = (bf16[16,80,128]{2,1,0:T(8,128)(2,1)}, bf16[16,80,128]{2,1,0:T(8,128)(2,1)S(1)}, u32[]{:S(2)}, u32[]{:S(2)}) collective-permute-start(bf16[16,80,128]{2,1,0:T(8,128)(2,1)} %get-tuple-element.24), channel_id=1, source_target_pairs={{0,4},{2,6},{4,0},{6,2},{1,5},{3,7},{5,1},{7,3},{8,12},{10,14},{12... | collective-permute-start | bytes 983048 | tf_op jit(solution)/shard_map/ppermute | solution.py:16
  80.8 1.0 collective-permute-start.16
  81.8 19.7 %collective-permute-done.18.refs_3_ = bf16[14,80,128]{2,1,0:T(8,128)(2,1)S(1)} collective-permute-done((bf16[14,80,128]{2,1,0:T(8,128)(2,1)}, bf16[14,80,128]{2,1,0:T(8,128)(2,1)S(1)}, u32[]{:S(2)}, u32[]{:S(2)}) %collective-permute-start.18) | collective-permute-done | bytes 286752 | tf_op jit(solution)/shard_map/ppermute | solution.py:16
  101.5 1.3 collective-permute-start.20
  102.8 1.3 collective-permute-start.21
  104.1 11.2 %shard_map.58 = (f32[4,6,40,320]{3,2,1,0:T(8,128)}, f32[4,6,40,320]{3,2,1,0:T(8,128)}, bf16[320,2048]{1,0:T(8,128)(2,1)}) custom-call(s32[1]{0:T(128)} %bitcast.1.turn, bf16[960,2304]{1,0:T(8,128)(2,1)} %get-tuple-element.26.stacked, f32[16,320,128]{2,1,0:T(8,128)} %get-tuple-element.27.refs_0_, bf16[14,80,128]{2,1,0:T(8,128)(2,1)} %get-tuple-element.54.refs_1_, ...), custom_call_target="tpu_custom_call" | custom-call | flops 2516582400 | bytes 8388608 | tf_op jit(solution)/shard_map/pallas_call | solution.py:277
  115.4 4.5 %turn_kernel.1.kernels = bf16[4,80,3456]{2,1,0:T(8,128)(2,1)} custom-call(bf16[4,160,720]{2,1,0:T(8,128)(2,1)} %copy-done.1, bf16[4,160,720]{2,1,0:T(8,128)(2,1)} %copy-done.4), custom_call_target="tpu_custom_call" | custom-call | flops 235929600 | bytes 4194304 | tf_op jit(solution)/shard_map/turn_kernel/pallas_call | solution.py:323
  120.6 10.6 %conv_backward.1 = (f32[64,80,128]{2,1,0:T(8,128)}, bf16[16,80,128]{2,1,0:T(8,128)(2,1)}, bf16[16,80,128]{2,1,0:T(8,128)(2,1)}, bf16[16,80,128]{2,1,0:T(8,128)(2,1)}) custom-call(s32[5]{0:T(128)} %stack.64.turns, bf16[320,2048]{1,0:T(8,128)(2,1)} %get-tuple-element.38.slope.refs_0_, bf16[1,320,128]{2,1,0:T(8,128)(2,1)} %copy-done.15, ...), custom_call_target="tpu_custom_call" | custom-call | flops 3774873600 | bytes 8388608 | tf_op jit(solution)/shard_map/conv_backward/pallas_call | solution.py:414
  131.2 2.7 %collective-permute-start.22 = (bf16[16,80,128]{2,1,0:T(8,128)(2,1)}, bf16[16,80,128]{2,1,0:T(8,128)(2,1)S(1)}, u32[]{:S(2)}, u32[]{:S(2)}) collective-permute-start(bf16[16,80,128]{2,1,0:T(8,128)(2,1)} %get-tuple-element.33), channel_id=1, source_target_pairs={{0,2},{2,4},{4,6},{6,0},{1,3},{3,5},{5,7},{7,1},{8,10},{10,12},{12... | collective-permute-start | bytes 983048 | tf_op jit(solution)/shard_map/ppermute | solution.py:16
  133.9 5.9 %shard_map.59 = (f32[4,3,40,320]{3,2,1,0:T(8,128)}, f32[4,3,40,320]{3,2,1,0:T(8,128)}) custom-call(s32[1]{0:T(128)} %bitcast.1.turn, bf16[960,2304]{1,0:T(8,128)(2,1)} %get-tuple-element.26.stacked, bf16[320,2048]{1,0:T(8,128)(2,1)} %get-tuple-element.38.slope.refs_0_), custom_call_target="tpu_custom_call" | custom-call | flops 1258291200 | bytes 8388608 | tf_op jit(solution)/shard_map/pallas_call | solution.py:277
  140.2 0.7 bitcast_dynamic-update-slice_fusion.2
  141.0 2.8 %collective-permute-start.24 = (bf16[16,80,128]{2,1,0:T(8,128)(2,1)S(1)}, bf16[16,80,128]{2,1,0:T(8,128)(2,1)S(1)}, u32[]{:S(2)}, u32[]{:S(2)}) collective-permute-start(bf16[16,80,128]{2,1,0:T(8,128)(2,1)S(1)} %copy-done.7), channel_id=1, source_target_pairs={{0,6},{2,0},{4,2},{6,4},{1,7},{3,1},{5,3},{7,5},{8,14},{10,8},{12,... | collective-permute-start | bytes 983048 | tf_op jit(solution)/shard_map/ppermute | solution.py:16
  143.8 0.7 bitcast_dynamic-update-slice_fusion.1
  144.6 0.7 bitcast_dynamic-update-slice_fusion
  145.3 0.9 convert_dynamic-update-slice_fusion.2
  146.2 11.8 %collective-permute-done.23 = bf16[16,80,128]{2,1,0:T(8,128)(2,1)S(1)} collective-permute-done((bf16[16,80,128]{2,1,0:T(8,128)(2,1)S(1)}, bf16[16,80,128]{2,1,0:T(8,128)(2,1)S(1)}, u32[]{:S(2)}, u32[]{:S(2)}) %collective-permute-start.23) | collective-permute-done | bytes 327712 | tf_op jit(solution)/shard_map/ppermute | solution.py:16
  158.0 0.9 convert_dynamic-update-slice_fusion.1
  158.9 0.9 convert_dynamic-update-slice_fusion
  161.1 2.6 %collective-permute-start.34 = (f32[3,40,320]{2,1,0:T(8,128)S(1)}, f32[3,40,320]{2,1,0:T(8,128)S(1)}, u32[]{:S(2)}, u32[]{:S(2)}) collective-permute-start(f32[3,40,320]{2,1,0:T(8,128)S(1)} %get-tuple-element.68), channel_id=1, source_target_pairs={{0,24},{8,0},{16,8},{24,16},{1,25},{9,1},{17,9},{25,17},{2,26},{10... | collective-permute-start | bytes 460808 | tf_op jit(solution)/shard_map/ppermute | solution.py:16
  164.0 1.3 collective-permute-start.27
  165.3 3.0 %collective-permute-done.36 = f32[3,40,320]{2,1,0:T(8,128)S(1)} collective-permute-done((f32[3,40,320]{2,1,0:T(8,128)S(1)}, f32[3,40,320]{2,1,0:T(8,128)S(1)}, u32[]{:S(2)}, u32[]{:S(2)}) %collective-permute-start.36) | collective-permute-done | bytes 153632 | tf_op jit(solution)/shard_map/ppermute | solution.py:16
  168.4 4.0 %collective-permute-done.35 = f32[3,40,320]{2,1,0:T(8,128)S(1)} collective-permute-done((f32[3,40,320]{2,1,0:T(8,128)S(1)}, f32[3,40,320]{2,1,0:T(8,128)S(1)}, u32[]{:S(2)}, u32[]{:S(2)}) %collective-permute-start.35) | collective-permute-done | bytes 153632 | tf_op jit(solution)/shard_map/ppermute | solution.py:16
  172.6 6.4 %collective-permute-start.39 = (f32[80,120]{0,1:T(8,128)S(1)}, f32[80,120]{0,1:T(8,128)S(1)}, u32[]{:S(2)}, u32[]{:S(2)}) collective-permute-start(f32[80,120]{0,1:T(8,128)S(1)} %bitcast.162), channel_id=1, source_target_pairs={{0,2},{2,4},{4,6},{6,0},{1,3},{3,5},{5,7},{7,1},{8,10},{10,12},{12... | collective-permute-start | bytes 115208 | tf_op jit(solution)/shard_map/ppermute | solution.py:16
  179.0 2.6 %collective-permute-start.38 = (f32[80,120]{0,1:T(8,128)S(1)}, f32[80,120]{0,1:T(8,128)S(1)}, u32[]{:S(2)}, u32[]{:S(2)}) collective-permute-start(f32[80,120]{0,1:T(8,128)S(1)} %bitcast.161), channel_id=1, source_target_pairs={{0,4},{2,6},{4,0},{6,2},{1,5},{3,7},{5,1},{7,3},{8,12},{10,14},{12... | collective-permute-start | bytes 115208 | tf_op jit(solution)/shard_map/ppermute | solution.py:16
  181.6 7.1 %collective-permute-start.37 = (f32[80,120]{0,1:T(8,128)S(1)}, f32[80,120]{0,1:T(8,128)S(1)}, u32[]{:S(2)}, u32[]{:S(2)}) collective-permute-start(f32[80,120]{0,1:T(8,128)S(1)} %bitcast.160), channel_id=1, source_target_pairs={{0,6},{2,0},{4,2},{6,4},{1,7},{3,1},{5,3},{7,5},{8,14},{10,8},{12,... | collective-permute-start | bytes 115208 | tf_op jit(solution)/shard_map/ppermute | solution.py:16
  189.0 4.0 %collective-permute-start.31 = (f32[80,240]{0,1:T(8,128)S(1)}, f32[80,240]{0,1:T(8,128)S(1)}, u32[]{:S(2)}, u32[]{:S(2)}) collective-permute-start(f32[80,240]{0,1:T(8,128)S(1)} %bitcast.158), channel_id=1, source_target_pairs={{0,2},{2,4},{4,6},{6,0},{1,3},{3,5},{5,7},{7,1},{8,10},{10,12},{12... | collective-permute-start | bytes 230408 | tf_op jit(solution)/shard_map/ppermute | solution.py:16
  193.0 2.5 %collective-permute-start.30 = (f32[80,240]{0,1:T(8,128)S(1)}, f32[80,240]{0,1:T(8,128)S(1)}, u32[]{:S(2)}, u32[]{:S(2)}) collective-permute-start(f32[80,240]{0,1:T(8,128)S(1)} %bitcast.157), channel_id=1, source_target_pairs={{0,4},{2,6},{4,0},{6,2},{1,5},{3,7},{5,1},{7,3},{8,12},{10,14},{12... | collective-permute-start | bytes 230408 | tf_op jit(solution)/shard_map/ppermute | solution.py:16
  195.6 3.6 %collective-permute-done.31 = f32[80,240]{0,1:T(8,128)S(1)} collective-permute-done((f32[80,240]{0,1:T(8,128)S(1)}, f32[80,240]{0,1:T(8,128)S(1)}, u32[]{:S(2)}, u32[]{:S(2)}) %collective-permute-start.31) | collective-permute-done | bytes 76832 | tf_op jit(solution)/shard_map/ppermute | solution.py:16
  199.2 4.0 %collective-permute-done.30 = f32[80,240]{0,1:T(8,128)S(1)} collective-permute-done((f32[80,240]{0,1:T(8,128)S(1)}, f32[80,240]{0,1:T(8,128)S(1)}, u32[]{:S(2)}, u32[]{:S(2)}) %collective-permute-start.30) | collective-permute-done | bytes 76832 | tf_op jit(solution)/shard_map/ppermute | solution.py:16
  203.5 1.2 collective-permute-done.32
  204.8 0.8 pad_maximum_fusion.1
  (93 shorter events, 6.4 us)
Async XLA Ops:
  0.6 0.9 copy-start
  0.6 15.9 %copy-start.2 = (bf16[1,64,80,128]{3,2,1,0:T(8,128)(2,1)S(1)}, bf16[1,64,80,128]{3,2,1,0:T(8,128)(2,1)}, u32[]{:S(2)}) copy-start(bf16[1,64,80,128]{3,2,1,0:T(8,128)(2,1)} %param.3) | copy-start | bytes 3932164
  1.8 7.5 %collective-permute-start.9 = (bf16[40,720]{1,0:T(8,128)(2,1)S(1)}, bf16[40,720]{1,0:T(8,128)(2,1)S(1)}, u32[]{:S(2)}, u32[]{:S(2)}) collective-permute-start(bf16[40,720]{1,0:T(8,128)(2,1)S(1)} %copy.11), channel_id=1, source_target_pairs={{0,2},{2,4},{4,6},{6,0},{1,3},{3,5},{5,7},{7,1},{8,10},{10,12},{12... | collective-permute-start | bytes 172808 | tf_op jit(solution)/shard_map/ppermute | solution.py:16
  4.9 6.9 %collective-permute-start.8 = (bf16[40,720]{1,0:T(8,128)(2,1)S(1)}, bf16[40,720]{1,0:T(8,128)(2,1)S(1)}, u32[]{:S(2)}, u32[]{:S(2)}) collective-permute-start(bf16[40,720]{1,0:T(8,128)(2,1)S(1)} %copy.11), channel_id=1, source_target_pairs={{0,4},{2,6},{4,0},{6,2},{1,5},{3,7},{5,1},{7,3},{8,12},{10,14},{12... | collective-permute-start | bytes 172808 | tf_op jit(solution)/shard_map/ppermute | solution.py:16
  7.5 4.6 %collective-permute-start.7 = (bf16[40,720]{1,0:T(8,128)(2,1)S(1)}, bf16[40,720]{1,0:T(8,128)(2,1)S(1)}, u32[]{:S(2)}, u32[]{:S(2)}) collective-permute-start(bf16[40,720]{1,0:T(8,128)(2,1)S(1)} %copy.11), channel_id=1, source_target_pairs={{0,6},{2,0},{4,2},{6,4},{1,7},{3,1},{5,3},{7,5},{8,14},{10,8},{12,... | collective-permute-start | bytes 172808 | tf_op jit(solution)/shard_map/ppermute | solution.py:16
  12.1 9.8 %collective-permute-start.12 = (bf16[160,720]{1,0:T(8,128)(2,1)S(1)}, bf16[160,720]{1,0:T(8,128)(2,1)S(1)}, u32[]{:S(2)}, u32[]{:S(2)}) collective-permute-start(bf16[160,720]{1,0:T(8,128)(2,1)S(1)} %get-tuple-element.76), channel_id=1, source_target_pairs={{0,8},{8,16},{16,24},{24,0},{1,9},{9,17},{17,25},{25,1},{2,10},{10... | collective-permute-start | bytes 691208 | tf_op jit(solution)/shard_map/ppermute | solution.py:16
  13.6 11.6 %collective-permute-start.11 = (bf16[160,720]{1,0:T(8,128)(2,1)S(1)}, bf16[160,720]{1,0:T(8,128)(2,1)S(1)}, u32[]{:S(2)}, u32[]{:S(2)}) collective-permute-start(bf16[160,720]{1,0:T(8,128)(2,1)S(1)} %get-tuple-element.76), channel_id=1, source_target_pairs={{0,16},{8,24},{16,0},{24,8},{1,17},{9,25},{17,1},{25,9},{2,18},{10... | collective-permute-start | bytes 691208 | tf_op jit(solution)/shard_map/ppermute | solution.py:16
  15.1 10.1 %collective-permute-start.10 = (bf16[160,720]{1,0:T(8,128)(2,1)S(1)}, bf16[160,720]{1,0:T(8,128)(2,1)S(1)}, u32[]{:S(2)}, u32[]{:S(2)}) collective-permute-start(bf16[160,720]{1,0:T(8,128)(2,1)S(1)} %get-tuple-element.76), channel_id=1, source_target_pairs={{0,24},{8,0},{16,8},{24,16},{1,25},{9,1},{17,9},{25,17},{2,26},{10... | collective-permute-start | bytes 691208 | tf_op jit(solution)/shard_map/ppermute | solution.py:16
  17.6 43.4 %collective-permute-start = (bf16[16,80,128]{2,1,0:T(8,128)(2,1)}, bf16[16,80,128]{2,1,0:T(8,128)(2,1)}, u32[]{:S(2)}, u32[]{:S(2)}) collective-permute-start(bf16[16,80,128]{2,1,0:T(8,128)(2,1)} %get-tuple-element.66), channel_id=1, source_target_pairs={{0,6},{2,0},{4,2},{6,4},{1,7},{3,1},{5,3},{7,5},{8,14},{10,8},{12,... | collective-permute-start | bytes 983048 | tf_op jit(solution)/shard_map/ppermute | solution.py:16
  20.5 41.9 %collective-permute-start.1 = (bf16[16,80,128]{2,1,0:T(8,128)(2,1)}, bf16[16,80,128]{2,1,0:T(8,128)(2,1)}, u32[]{:S(2)}, u32[]{:S(2)}) collective-permute-start(bf16[16,80,128]{2,1,0:T(8,128)(2,1)} %get-tuple-element.65), channel_id=1, source_target_pairs={{0,4},{2,6},{4,0},{6,2},{1,5},{3,7},{5,1},{7,3},{8,12},{10,14},{12... | collective-permute-start | bytes 983048 | tf_op jit(solution)/shard_map/ppermute | solution.py:16
  21.9 40.6 %collective-permute-start.2 = (bf16[16,80,128]{2,1,0:T(8,128)(2,1)}, bf16[16,80,128]{2,1,0:T(8,128)(2,1)}, u32[]{:S(2)}, u32[]{:S(2)}) collective-permute-start(bf16[16,80,128]{2,1,0:T(8,128)(2,1)} %get-tuple-element.64), channel_id=1, source_target_pairs={{0,2},{2,4},{4,6},{6,0},{1,3},{3,5},{5,7},{7,1},{8,10},{10,12},{12... | collective-permute-start | bytes 983048 | tf_op jit(solution)/shard_map/ppermute | solution.py:16
  25.3 7.4 %collective-permute-start.3 = (bf16[1,80,128]{2,1,0:T(8,128)(2,1)}, bf16[1,80,128]{2,1,0:T(8,128)(2,1)}, u32[]{:S(2)}, u32[]{:S(2)}) collective-permute-start(bf16[1,80,128]{2,1,0:T(8,128)(2,1)} %select_bitcast_fusion), channel_id=1, source_target_pairs={{0,1},{1,0},{2,3},{3,2},{4,5},{5,4},{6,7},{7,6},{8,9},{9,8},{10,11... | collective-permute-start | bytes 61448 | tf_op jit(solution)/shard_map/ppermute | solution.py:16
  25.3 0.7 copy-start.6
  27.1 6.4 %copy-start.1 = (bf16[4,160,720]{2,1,0:T(8,128)(2,1)}, bf16[4,160,720]{2,1,0:T(8,128)(2,1)S(1)}, u32[]{:S(2)}) copy-start(bf16[4,160,720]{2,1,0:T(8,128)(2,1)S(1)} %pad_maximum_fusion.refs_8_.refs_0_) | copy-start | bytes 2764804
  27.1 35.4 %collective-permute-start.13 = (bf16[4,160,720]{2,1,0:T(8,128)(2,1)S(1)}, bf16[4,160,720]{2,1,0:T(8,128)(2,1)S(1)}, u32[]{:S(2)}, u32[]{:S(2)}) collective-permute-start(bf16[4,160,720]{2,1,0:T(8,128)(2,1)S(1)} %pad_maximum_fusion.refs_8_.refs_0_), channel_id=1, source_target_pairs={{0,1},{1,0},{2,3},{3,2},{4,5},{5,4},{6,7},{7,6},{8,9},{9,8},{10,11... | collective-permute-start | bytes 2764808 | tf_op jit(solution)/shard_map/ppermute | solution.py:16
  34.2 12.4 %collective-permute-start.4 = (bf16[4,80,128]{2,1,0:T(8,128)(2,1)S(1)}, bf16[4,80,128]{2,1,0:T(8,128)(2,1)S(1)}, u32[]{:S(2)}, u32[]{:S(2)}) collective-permute-start(bf16[4,80,128]{2,1,0:T(8,128)(2,1)S(1)} %pad_maximum_fusion.4), channel_id=1, source_target_pairs={{0,6},{2,0},{4,2},{6,4},{1,7},{3,1},{5,3},{7,5},{8,14},{10,8},{12,... | collective-permute-start | bytes 245768 | tf_op jit(solution)/shard_map/ppermute | solution.py:16
  46.6 15.9 %copy-start.12 = (bf16[4,80,128]{2,1,0:T(8,128)(2,1)}, bf16[4,80,128]{2,1,0:T(8,128)(2,1)S(1)}, u32[]{:S(2)}) copy-start(bf16[4,80,128]{2,1,0:T(8,128)(2,1)S(1)} %collective-permute-done.4.refs_5_.refs_6_) | copy-start | bytes 245764
  46.6 6.3 %collective-permute-start.5 = (bf16[4,80,128]{2,1,0:T(8,128)(2,1)S(1)}, bf16[4,80,128]{2,1,0:T(8,128)(2,1)S(1)}, u32[]{:S(2)}, u32[]{:S(2)}) collective-permute-start(bf16[4,80,128]{2,1,0:T(8,128)(2,1)S(1)} %pad_maximum_fusion.5), channel_id=1, source_target_pairs={{0,4},{2,6},{4,0},{6,2},{1,5},{3,7},{5,1},{7,3},{8,12},{10,14},{12... | collective-permute-start | bytes 245768 | tf_op jit(solution)/shard_map/ppermute | solution.py:16
  52.9 9.6 %copy-start.13 = (bf16[4,80,128]{2,1,0:T(8,128)(2,1)}, bf16[4,80,128]{2,1,0:T(8,128)(2,1)S(1)}, u32[]{:S(2)}) copy-start(bf16[4,80,128]{2,1,0:T(8,128)(2,1)S(1)} %collective-permute-done.5.refs_6_.refs_7_) | copy-start | bytes 245764
  52.9 7.1 %collective-permute-start.6 = (bf16[4,80,128]{2,1,0:T(8,128)(2,1)S(1)}, bf16[4,80,128]{2,1,0:T(8,128)(2,1)S(1)}, u32[]{:S(2)}, u32[]{:S(2)}) collective-permute-start(bf16[4,80,128]{2,1,0:T(8,128)(2,1)S(1)} %pad_maximum_fusion.6), channel_id=1, source_target_pairs={{0,2},{2,4},{4,6},{6,0},{1,3},{3,5},{5,7},{7,1},{8,10},{10,12},{12... | collective-permute-start | bytes 245768 | tf_op jit(solution)/shard_map/ppermute | solution.py:16
  60.0 2.5 %copy-start.14 = (bf16[4,80,128]{2,1,0:T(8,128)(2,1)}, bf16[4,80,128]{2,1,0:T(8,128)(2,1)S(1)}, u32[]{:S(2)}) copy-start(bf16[4,80,128]{2,1,0:T(8,128)(2,1)S(1)} %collective-permute-done.6.refs_7_.refs_8_) | copy-start | bytes 245764
  60.0 20.8 %collective-permute-start.17 = (bf16[14,80,128]{2,1,0:T(8,128)(2,1)}, bf16[14,80,128]{2,1,0:T(8,128)(2,1)S(1)}, u32[]{:S(2)}, u32[]{:S(2)}) collective-permute-start(bf16[14,80,128]{2,1,0:T(8,128)(2,1)} %get-tuple-element.53), channel_id=1, source_target_pairs={{0,6},{2,0},{4,2},{6,4},{1,7},{3,1},{5,3},{7,5},{8,14},{10,8},{12,... | collective-permute-start | bytes 860168 | tf_op jit(solution)/shard_map/ppermute | solution.py:16
  61.0 40.5 %collective-permute-start.18 = (bf16[14,80,128]{2,1,0:T(8,128)(2,1)}, bf16[14,80,128]{2,1,0:T(8,128)(2,1)S(1)}, u32[]{:S(2)}, u32[]{:S(2)}) collective-permute-start(bf16[14,80,128]{2,1,0:T(8,128)(2,1)} %get-tuple-element.55), channel_id=1, source_target_pairs={{0,4},{2,6},{4,0},{6,2},{1,5},{3,7},{5,1},{7,3},{8,12},{10,14},{12... | collective-permute-start | bytes 860168 | tf_op jit(solution)/shard_map/ppermute | solution.py:16
  62.5 40.3 %collective-permute-start.19 = (bf16[14,80,128]{2,1,0:T(8,128)(2,1)}, bf16[14,80,128]{2,1,0:T(8,128)(2,1)S(1)}, u32[]{:S(2)}, u32[]{:S(2)}) collective-permute-start(bf16[14,80,128]{2,1,0:T(8,128)(2,1)} %get-tuple-element.52), channel_id=1, source_target_pairs={{0,2},{2,4},{4,6},{6,0},{1,3},{3,5},{5,7},{7,1},{8,10},{10,12},{12... | collective-permute-start | bytes 860168 | tf_op jit(solution)/shard_map/ppermute | solution.py:16
  62.5 1.0 copy-start.4
  76.4 63.4 %collective-permute-start.14 = (bf16[16,80,128]{2,1,0:T(8,128)(2,1)}, bf16[16,80,128]{2,1,0:T(8,128)(2,1)S(1)}, u32[]{:S(2)}, u32[]{:S(2)}) collective-permute-start(bf16[16,80,128]{2,1,0:T(8,128)(2,1)} %get-tuple-element.23), channel_id=1, source_target_pairs={{0,2},{2,4},{4,6},{6,0},{1,3},{3,5},{5,7},{7,1},{8,10},{10,12},{12... | collective-permute-start | bytes 983048 | tf_op jit(solution)/shard_map/ppermute | solution.py:16
  78.4 62.5 %collective-permute-start.15 = (bf16[16,80,128]{2,1,0:T(8,128)(2,1)}, bf16[16,80,128]{2,1,0:T(8,128)(2,1)S(1)}, u32[]{:S(2)}, u32[]{:S(2)}) collective-permute-start(bf16[16,80,128]{2,1,0:T(8,128)(2,1)} %get-tuple-element.24), channel_id=1, source_target_pairs={{0,4},{2,6},{4,0},{6,2},{1,5},{3,7},{5,1},{7,3},{8,12},{10,14},{12... | collective-permute-start | bytes 983048 | tf_op jit(solution)/shard_map/ppermute | solution.py:16
  80.8 23.3 %copy-start.9 = (bf16[14,80,128]{2,1,0:T(8,128)(2,1)}, bf16[14,80,128]{2,1,0:T(8,128)(2,1)S(1)}, u32[]{:S(2)}) copy-start(bf16[14,80,128]{2,1,0:T(8,128)(2,1)S(1)} %collective-permute-done.17.refs_2_) | copy-start | bytes 860164
  80.8 63.7 %collective-permute-start.16 = (bf16[16,80,128]{2,1,0:T(8,128)(2,1)}, bf16[16,80,128]{2,1,0:T(8,128)(2,1)S(1)}, u32[]{:S(2)}, u32[]{:S(2)}) collective-permute-start(bf16[16,80,128]{2,1,0:T(8,128)(2,1)} %get-tuple-element.25), channel_id=1, source_target_pairs={{0,6},{2,0},{4,2},{6,4},{1,7},{3,1},{5,3},{7,5},{8,14},{10,8},{12,... | collective-permute-start | bytes 983048 | tf_op jit(solution)/shard_map/ppermute | solution.py:16
  101.5 2.6 %copy-start.10 = (bf16[14,80,128]{2,1,0:T(8,128)(2,1)}, bf16[14,80,128]{2,1,0:T(8,128)(2,1)S(1)}, u32[]{:S(2)}) copy-start(bf16[14,80,128]{2,1,0:T(8,128)(2,1)S(1)} %collective-permute-done.18.refs_3_) | copy-start | bytes 860164
  101.5 18.4 %collective-permute-start.20 = (bf16[1,320,128]{2,1,0:T(8,128)(2,1)}, bf16[1,320,128]{2,1,0:T(8,128)(2,1)S(1)}, u32[]{:S(2)}, u32[]{:S(2)}) collective-permute-start(bf16[1,320,128]{2,1,0:T(8,128)(2,1)} %get-tuple-element.29), channel_id=1, source_target_pairs={{0,2},{2,4},{4,6},{6,7},{7,5},{5,3},{3,1},{8,10},{10,12},{12,14},{... | collective-permute-start | bytes 245768 | tf_op jit(solution)/shard_map/ppermute | solution.py:556
  102.8 1.3 copy-start.11
  102.8 17.2 %collective-permute-start.21 = (bf16[1,320,128]{2,1,0:T(8,128)(2,1)}, bf16[1,320,128]{2,1,0:T(8,128)(2,1)S(1)}, u32[]{:S(2)}, u32[]{:S(2)}) collective-permute-start(bf16[1,320,128]{2,1,0:T(8,128)(2,1)} %get-tuple-element.30), channel_id=1, source_target_pairs={{2,0},{4,2},{6,4},{7,6},{5,7},{3,5},{1,3},{10,8},{12,10},{14,12},{... | collective-permute-start | bytes 245768 | tf_op jit(solution)/shard_map/ppermute | solution.py:557
  119.9 0.6 copy-start.15
  119.9 43.8 %collective-permute-start.25 = (f32[4,6,40,320]{3,2,1,0:T(8,128)}, f32[4,6,40,320]{3,2,1,0:T(8,128)S(1)}, u32[]{:S(2)}, u32[]{:S(2)}) collective-permute-start(f32[4,6,40,320]{3,2,1,0:T(8,128)} %get-tuple-element.37), channel_id=1, source_target_pairs={{0,1},{1,0},{2,3},{3,2},{4,5},{5,4},{6,7},{7,6},{8,9},{9,8},{10,11... | collective-permute-start | bytes 3686408 | tf_op jit(solution)/shard_map/ppermute | solution.py:16
  120.0 0.6 copy-start.16
  131.2 8.6 %copy-start.8 = (bf16[16,80,128]{2,1,0:T(8,128)(2,1)S(1)}, bf16[16,80,128]{2,1,0:T(8,128)(2,1)}, u32[]{:S(2)}) copy-start(bf16[16,80,128]{2,1,0:T(8,128)(2,1)} %get-tuple-element.34) | copy-start | bytes 983044
  131.2 9.8 %copy-start.7 = (bf16[16,80,128]{2,1,0:T(8,128)(2,1)S(1)}, bf16[16,80,128]{2,1,0:T(8,128)(2,1)}, u32[]{:S(2)}) copy-start(bf16[16,80,128]{2,1,0:T(8,128)(2,1)} %get-tuple-element.35) | copy-start | bytes 983044
  131.2 14.1 %collective-permute-start.22 = (bf16[16,80,128]{2,1,0:T(8,128)(2,1)}, bf16[16,80,128]{2,1,0:T(8,128)(2,1)S(1)}, u32[]{:S(2)}, u32[]{:S(2)}) collective-permute-start(bf16[16,80,128]{2,1,0:T(8,128)(2,1)} %get-tuple-element.33), channel_id=1, source_target_pairs={{0,2},{2,4},{4,6},{6,0},{1,3},{3,5},{5,7},{7,1},{8,10},{10,12},{12... | collective-permute-start | bytes 983048 | tf_op jit(solution)/shard_map/ppermute | solution.py:16
  139.8 18.2 %collective-permute-start.23 = (bf16[16,80,128]{2,1,0:T(8,128)(2,1)S(1)}, bf16[16,80,128]{2,1,0:T(8,128)(2,1)S(1)}, u32[]{:S(2)}, u32[]{:S(2)}) collective-permute-start(bf16[16,80,128]{2,1,0:T(8,128)(2,1)S(1)} %copy-done.8), channel_id=1, source_target_pairs={{0,4},{2,6},{4,0},{6,2},{1,5},{3,7},{5,1},{7,3},{8,12},{10,14},{12... | collective-permute-start | bytes 983048 | tf_op jit(solution)/shard_map/ppermute | solution.py:16
  141.0 17.9 %collective-permute-start.24 = (bf16[16,80,128]{2,1,0:T(8,128)(2,1)S(1)}, bf16[16,80,128]{2,1,0:T(8,128)(2,1)S(1)}, u32[]{:S(2)}, u32[]{:S(2)}) collective-permute-start(bf16[16,80,128]{2,1,0:T(8,128)(2,1)S(1)} %copy-done.7), channel_id=1, source_target_pairs={{0,6},{2,0},{4,2},{6,4},{1,7},{3,1},{5,3},{7,5},{8,14},{10,8},{12,... | collective-permute-start | bytes 983048 | tf_op jit(solution)/shard_map/ppermute | solution.py:16
  144.6 15.2 %collective-permute-start.33 = (f32[4,3,40,320]{3,2,1,0:T(8,128)}, f32[4,3,40,320]{3,2,1,0:T(8,128)S(1)}, u32[]{:S(2)}, u32[]{:S(2)}) collective-permute-start(f32[4,3,40,320]{3,2,1,0:T(8,128)} %get-tuple-element.40), channel_id=1, source_target_pairs={{0,1},{1,0},{2,3},{3,2},{4,5},{5,4},{6,7},{7,6},{8,9},{9,8},{10,11... | collective-permute-start | bytes 1843208 | tf_op jit(solution)/shard_map/ppermute | solution.py:16
  145.3 14.5 %copy-start.5 = (f32[4,3,40,320]{3,2,1,0:T(8,128)S(1)}, f32[4,3,40,320]{3,2,1,0:T(8,128)}, u32[]{:S(2)}) copy-start(f32[4,3,40,320]{3,2,1,0:T(8,128)} %get-tuple-element.39) | copy-start | bytes 1843204
  159.8 3.9 %copy-start.3 = (f32[4,6,40,320]{3,2,1,0:T(8,128)S(1)}, f32[4,6,40,320]{3,2,1,0:T(8,128)}, u32[]{:S(2)}) copy-start(f32[4,6,40,320]{3,2,1,0:T(8,128)} %get-tuple-element.36) | copy-start | bytes 3686404
  159.9 8.5 %collective-permute-start.36 = (f32[3,40,320]{2,1,0:T(8,128)S(1)}, f32[3,40,320]{2,1,0:T(8,128)S(1)}, u32[]{:S(2)}, u32[]{:S(2)}) collective-permute-start(f32[3,40,320]{2,1,0:T(8,128)S(1)} %get-tuple-element.69), channel_id=1, source_target_pairs={{0,8},{8,16},{16,24},{24,0},{1,9},{9,17},{17,25},{25,1},{2,10},{10... | collective-permute-start | bytes 460808 | tf_op jit(solution)/shard_map/ppermute | solution.py:16
  160.6 11.8 %collective-permute-start.35 = (f32[3,40,320]{2,1,0:T(8,128)S(1)}, f32[3,40,320]{2,1,0:T(8,128)S(1)}, u32[]{:S(2)}, u32[]{:S(2)}) collective-permute-start(f32[3,40,320]{2,1,0:T(8,128)S(1)} %get-tuple-element.70), channel_id=1, source_target_pairs={{0,16},{8,24},{16,0},{24,8},{1,17},{9,25},{17,1},{25,9},{2,18},{10... | collective-permute-start | bytes 460808 | tf_op jit(solution)/shard_map/ppermute | solution.py:16
  161.1 11.3 %collective-permute-start.34 = (f32[3,40,320]{2,1,0:T(8,128)S(1)}, f32[3,40,320]{2,1,0:T(8,128)S(1)}, u32[]{:S(2)}, u32[]{:S(2)}) collective-permute-start(f32[3,40,320]{2,1,0:T(8,128)S(1)} %get-tuple-element.68), channel_id=1, source_target_pairs={{0,24},{8,0},{16,8},{24,16},{1,25},{9,1},{17,9},{25,17},{2,26},{10... | collective-permute-start | bytes 460808 | tf_op jit(solution)/shard_map/ppermute | solution.py:16
  164.0 17.6 %collective-permute-start.28 = (f32[6,40,320]{2,1,0:T(8,128)S(1)}, f32[6,40,320]{2,1,0:T(8,128)S(1)}, u32[]{:S(2)}, u32[]{:S(2)}) collective-permute-start(f32[6,40,320]{2,1,0:T(8,128)S(1)} %get-tuple-element.42), channel_id=1, source_target_pairs={{0,8},{8,16},{16,24},{24,0},{1,9},{9,17},{17,25},{25,1},{2,10},{10... | collective-permute-start | bytes 921608 | tf_op jit(solution)/shard_map/ppermute | solution.py:16
  164.0 24.7 %collective-permute-start.27 = (f32[6,40,320]{2,1,0:T(8,128)S(1)}, f32[6,40,320]{2,1,0:T(8,128)S(1)}, u32[]{:S(2)}, u32[]{:S(2)}) collective-permute-start(f32[6,40,320]{2,1,0:T(8,128)S(1)} %get-tuple-element.43), channel_id=1, source_target_pairs={{0,16},{8,24},{16,0},{24,8},{1,17},{9,25},{17,1},{25,9},{2,18},{10... | collective-permute-start | bytes 921608 | tf_op jit(solution)/shard_map/ppermute | solution.py:16
  168.4 20.3 %collective-permute-start.26 = (f32[6,40,320]{2,1,0:T(8,128)S(1)}, f32[6,40,320]{2,1,0:T(8,128)S(1)}, u32[]{:S(2)}, u32[]{:S(2)}) collective-permute-start(f32[6,40,320]{2,1,0:T(8,128)S(1)} %get-tuple-element.41), channel_id=1, source_target_pairs={{0,24},{8,0},{16,8},{24,16},{1,25},{9,1},{17,9},{25,17},{2,26},{10... | collective-permute-start | bytes 921608 | tf_op jit(solution)/shard_map/ppermute | solution.py:16
  172.6 23.0 %collective-permute-start.39 = (f32[80,120]{0,1:T(8,128)S(1)}, f32[80,120]{0,1:T(8,128)S(1)}, u32[]{:S(2)}, u32[]{:S(2)}) collective-permute-start(f32[80,120]{0,1:T(8,128)S(1)} %bitcast.162), channel_id=1, source_target_pairs={{0,2},{2,4},{4,6},{6,0},{1,3},{3,5},{5,7},{7,1},{8,10},{10,12},{12... | collective-permute-start | bytes 115208 | tf_op jit(solution)/shard_map/ppermute | solution.py:16
  179.0 16.6 %collective-permute-start.38 = (f32[80,120]{0,1:T(8,128)S(1)}, f32[80,120]{0,1:T(8,128)S(1)}, u32[]{:S(2)}, u32[]{:S(2)}) collective-permute-start(f32[80,120]{0,1:T(8,128)S(1)} %bitcast.161), channel_id=1, source_target_pairs={{0,4},{2,6},{4,0},{6,2},{1,5},{3,7},{5,1},{7,3},{8,12},{10,14},{12... | collective-permute-start | bytes 115208 | tf_op jit(solution)/shard_map/ppermute | solution.py:16
  181.6 13.9 %collective-permute-start.37 = (f32[80,120]{0,1:T(8,128)S(1)}, f32[80,120]{0,1:T(8,128)S(1)}, u32[]{:S(2)}, u32[]{:S(2)}) collective-permute-start(f32[80,120]{0,1:T(8,128)S(1)} %bitcast.160), channel_id=1, source_target_pairs={{0,6},{2,0},{4,2},{6,4},{1,7},{3,1},{5,3},{7,5},{8,14},{10,8},{12,... | collective-permute-start | bytes 115208 | tf_op jit(solution)/shard_map/ppermute | solution.py:16
  189.0 10.3 %collective-permute-start.31 = (f32[80,240]{0,1:T(8,128)S(1)}, f32[80,240]{0,1:T(8,128)S(1)}, u32[]{:S(2)}, u32[]{:S(2)}) collective-permute-start(f32[80,240]{0,1:T(8,128)S(1)} %bitcast.158), channel_id=1, source_target_pairs={{0,2},{2,4},{4,6},{6,0},{1,3},{3,5},{5,7},{7,1},{8,10},{10,12},{12... | collective-permute-start | bytes 230408 | tf_op jit(solution)/shard_map/ppermute | solution.py:16
  193.0 10.3 %collective-permute-start.30 = (f32[80,240]{0,1:T(8,128)S(1)}, f32[80,240]{0,1:T(8,128)S(1)}, u32[]{:S(2)}, u32[]{:S(2)}) collective-permute-start(f32[80,240]{0,1:T(8,128)S(1)} %bitcast.157), channel_id=1, source_target_pairs={{0,4},{2,6},{4,0},{6,2},{1,5},{3,7},{5,1},{7,3},{8,12},{10,14},{12... | collective-permute-start | bytes 230408 | tf_op jit(solution)/shard_map/ppermute | solution.py:16
  195.5 7.7 %collective-permute-start.29 = (f32[80,240]{0,1:T(8,128)S(1)}, f32[80,240]{0,1:T(8,128)S(1)}, u32[]{:S(2)}, u32[]{:S(2)}) collective-permute-start(f32[80,240]{0,1:T(8,128)S(1)} %bitcast.156), channel_id=1, source_target_pairs={{0,6},{2,0},{4,2},{6,4},{1,7},{3,1},{5,3},{7,5},{8,14},{10,8},{12,... | collective-permute-start | bytes 230408 | tf_op jit(solution)/shard_map/ppermute | solution.py:16
  195.6 7.8 %collective-permute-start.40 = (f32[80,120]{0,1:T(8,128)S(1)}, f32[80,120]{0,1:T(8,128)S(1)}, u32[]{:S(2)}, u32[]{:S(2)}) collective-permute-start(f32[80,120]{0,1:T(8,128)S(1)} %fusion.17), channel_id=1, source_target_pairs={{0,1},{1,0},{2,3},{3,2},{4,5},{5,4},{6,7},{7,6},{8,9},{9,8},{10,11... | collective-permute-start | bytes 115208 | tf_op jit(solution)/shard_map/ppermute | solution.py:16
  203.3 1.4 collective-permute-start.32

commit v8 on v6

--- a/solution.py
+++ b/solution.py
@@ -18,18 +18,6 @@
 
 def swapped(block, axis, bit):
     return lax.ppermute(block, axis, [(i, i ^ bit) for i in range(lax.axis_size(axis))])
-
-
-def gathered_over_chan(mine):
-    chans = lax.axis_size("chan")
-    if chans != 4:
-        return jnp.concatenate([mine] + [receive(mine, "chan", j) for j in range(1, chans)])
-    size = mine.shape[0]
-    even = lax.axis_index("chan") % 2 == 0
-    opposite = swapped(mine, "chan", 2)
-    beside = swapped(jnp.concatenate([mine, opposite]), "chan", 1)
-    near, far = beside[:size], beside[size:]
-    return jnp.concatenate([mine, jnp.where(even, near, far), opposite, jnp.where(even, far, near)])
 
 
 def summed_over_chan(total, outer, in_steps):
@@ -250,14 +238,14 @@
     channels, pixels = slope.shape
     width = stacked.shape[1] - pixels
     width = width // 2
-    tap = first_tap + pl.program_id(0)
-    tap_row, tap_col = tap // 3, lax.rem(tap, 3)
+    tap_row = (first_tap + pl.program_id(0)) // 3
     if count:
 
         @pl.when(pl.program_id(0) == 0)
         def _():
             slope_rows(factor, pieces, ends, slope)
 
+    tap_col = lax.rem(first_tap + pl.program_id(0), 3) if count else 0
     source = stacked[
         pl.ds(pl.multiple_of(tap_col * channels, channels), channels),
         pl.ds(pl.multiple_of(tap_row * width, width), pixels),
@@ -292,7 +280,12 @@
     call = pl.pallas_call(
         functools.partial(correlate_body, first_tap, len(pieces), groups, rows),
         grid=(tap_count,),
-        in_specs=[pl.BlockSpec(memory_space=pltpu.SMEM), whole(stacked.shape)]
+        in_specs=[
+            pl.BlockSpec(memory_space=pltpu.SMEM),
+            pl.BlockSpec((channels, stacked.shape[1]), lambda t: ((first_tap + t) % 3, 0))
+            if made == []
+            else whole(stacked.shape),
+        ]
         + [whole(operand.shape) for operand in operands],
         out_specs=[pl.BlockSpec((groups, 1, size, channels), lambda t: (0, t, 0, 0))] * rows
         + [whole(each.shape) for each in made],
@@ -369,7 +362,7 @@
 
 
 def backward_body(count, shares, rows, turns, slope, above, below, kernels, *refs):
-    outs, stacked = refs[:count], refs[count]
+    outs, (stacked, weights, arrived) = refs[:count], refs[count:]
     channels = slope.shape[0]
     _, _, width = above.shape
     height = slope.shape[1] // width
@@ -386,7 +379,7 @@
                 value = jnp.concatenate(
                     [wide[j * depth + share * size : j * depth + (share + 1) * size] for j in range(count)]
                 )
-                here = turns[3] == (share - at) % shares
+                here = turns[1] == (share - at) % shares
                 chosen = value if chosen is None else jnp.where(here, value, chosen)
             parts.append(chosen)
         return jnp.concatenate(parts)
@@ -399,12 +392,14 @@
 
     @pl.when(step == 0)
     def _():
+        fetch = pltpu.make_async_copy(kernels, weights, arrived)
+        fetch.start()
         if stride > channels:
             for copies in range(3):
                 stacked[copies * stride + channels : (copies + 1) * stride, :] = jnp.zeros(
                     (stride - channels, stacked.shape[1]), stacked.dtype
                 )
-        for side, rim, row in ((0, above, 0), (1, below, height + 1)):
+        for side, rim, row in ((3, above, 0), (4, below, height + 1)):
             blocks = []
             for j in range(count):
                 start = lax.rem(turns[side] + j, count) * depth
@@ -417,12 +412,13 @@
             return carry
 
         lax.fori_loop(0, height, body, 0)
+        fetch.wait()
 
     windows = [
         stacked[:, pl.ds(pl.multiple_of((step * rows + a) * width, width), rows * width)]
         for a in range(3)
     ]
-    order = [kernels[lax.rem(turns[2] + j, count)] for j in range(count)]
+    order = [weights[lax.rem(turns[0] + j, count)] for j in range(count)]
     grad = jnp.dot(
         jnp.concatenate(order), jnp.concatenate(windows), preferred_element_type=jnp.float32
     )
@@ -449,11 +445,15 @@
                 whole(slope.shape),
                 whole(above.shape),
                 whole(below.shape),
-                whole(kernels.shape),
+                pl.BlockSpec(memory_space=pl.ANY),
             ],
-            out_specs=[pl.BlockSpec((rows, depth, width), lambda g, turns: (turns[4] * steps + g, 0, 0))]
+            out_specs=[pl.BlockSpec((rows, depth, width), lambda g, turns: (turns[2] * steps + g, 0, 0))]
             + [pl.BlockSpec((rows, depth, width), lambda g, _: (g, 0, 0))] * (count - 1),
-            scratch_shapes=[pltpu.VMEM((kernels.shape[2] // 3, (height + 2) * width), jnp.bfloat16)],
+            scratch_shapes=[
+                pltpu.VMEM((kernels.shape[2] // 3, (height + 2) * width), jnp.bfloat16),
+                pltpu.VMEM(kernels.shape, kernels.dtype),
+                pltpu.SemaphoreType.DMA,
+            ],
         ),
         out_shape=[jax.ShapeDtypeStruct((slab, depth, width), jnp.float32)]
         + [jax.ShapeDtypeStruct((height, depth, width), jnp.bfloat16)] * (count - 1),
@@ -472,7 +472,7 @@
     size = outer // rows
     mine = part(kernel, row, size, 2)
     mine = jnp.transpose(mine, (2, 0, 1)).reshape(size, 9 * inner)
-    over_chan = gathered_over_chan(mine)
+    over_chan = jnp.concatenate([mine] + [receive(mine, "chan", j) for j in range(1, chans)], axis=0)
     over_dp = jnp.stack([over_chan] + [receive(over_chan, "dp", j) for j in range(1, dps)])
     if dps != chans:
         each = dps // chans
@@ -562,8 +562,7 @@
     forth = jnp.where(row % 2 == 0, 1, chans - 1)
     above_turn = jnp.where(place_at == 0, 0, forth)
     below_turn = jnp.where(place_at == chans - 1, 0, chans - forth)
-    turns = jnp.stack([shift, row, place_at]).astype(jnp.int32)
-    back_turns = jnp.stack([above_turn, below_turn, shift, row, place_at]).astype(jnp.int32)
+    turns = jnp.stack([shift, row, place_at, above_turn, below_turn]).astype(jnp.int32)
 
     results = forward(turns, pieces, rims, halves, slab)
     activated, factor, stacked, first, last = results
@@ -579,7 +578,7 @@
 
     lead, slope = correlate((0, 6), stacked, None, factor, cotangents, rims)
     lead = summed_over_images(lead)
-    input_grads = list(backward(back_turns, slope, above, below, back_kernel, chans, slab))
+    input_grads = list(backward(turns, slope, above, below, back_kernel, chans, slab))
     slope, input_grads[1] = lax.optimization_barrier((slope, input_grads[1]))
     (rest,) = correlate((6, 3), stacked, slope)
     rest = summed_over_images(rest)

time: 211 us -> 208 us (0.986)
  starting transfers between devices: 64.8 us -> 61.7 us
    ppermute x33 -> x36, waiting for transfers between devices: 66.9 us -> 75.2 us  [receive(): lax.ppermute(block, axis, [(i, (i - ahead) % count) for i in range(count)])]
    ppermute x4 -> x2, waiting for transfers between devices: 11.2 us -> 4.75 us  [swapped(): lax.ppermute(block, axis, [(i, i ^ bit) for i in range(lax.axis_size(axis...]
    ppermute x4 -> x2, starting transfers between devices: 14 us -> 9.07 us  [swapped(): lax.ppermute(block, axis, [(i, i ^ bit) for i in range(lax.axis_size(axis...]
    ppermute x33 -> x36, starting transfers between devices: 48.3 us -> 50.1 us  [receive(): lax.ppermute(block, axis, [(i, (i - ahead) % count) for i in range(count)])]
  transfers between devices with their start and end apart: 39 -> 40, of which waited for: 17 -> 17; matrix products, arithmetic and copies ran while one was open for 8% -> 8% of each run, Pallas kernels for 22% -> 21%
where the time goes in v8:
time: 208 us
  waiting for transfers between devices  80 us (38%)
  starting transfers between devices  61.7 us (30%)
  Pallas kernels  44.5 us (21%)
  local copies, waits for them, and re-layouts  11.5 us (6%)
  other arithmetic  8.97 us (4%)
    ppermute x36, waiting for transfers between devices, receive(): lax.ppermute(block, axis, [(i, (i - ahead) % count) for i in range(count)])  75.2 us
    ppermute x36, starting transfers between devices, receive(): lax.ppermute(block, axis, [(i, (i - ahead) % count) for i in range(count)])  50.1 us
    pallas_call x2, Pallas kernels, correlate(): results = call(turn, stacked, *operands)  16.5 us
    pallas_call x1, Pallas kernels, forward(): results = call(turns, *pieces, *rims, *halves)  12.9 us
    pallas_call x1, Pallas kernels, backward(): pl.pallas_call(functools.partial(backward_body, count, lax.axis_size('row...  10.6 us
    ppermute x2, starting transfers between devices, swapped(): lax.ppermute(block, axis, [(i, i ^ bit) for i in range(lax.axis_size(axis...  9.07 us
    ppermute x2, waiting for transfers between devices, swapped(): lax.ppermute(block, axis, [(i, i ^ bit) for i in range(lax.axis_size(axis...  4.75 us
    pallas_call x1, Pallas kernels, turned(): pl.pallas_call(functools.partial(turned_body, shares), grid=(blocks,), in...  4.54 us
  transfers between devices with their start and end apart: 40, of which 17 were waited for; matrix products, arithmetic and copies ran while one was open for 8% of the time, Pallas kernels for 21%

profile of v8, /device:TPU:0, one launch (start us, length us, event | category | flops | bytes accessed | tf_op | source)
XLA Modules:
  0.0 207.8 jit_solution(10050286603334794543)
XLA Ops:
  0.7 0.9 copy-done
  1.8 3.1 %collective-permute-start.9 = (bf16[40,720]{1,0:T(8,128)(2,1)S(1)}, bf16[40,720]{1,0:T(8,128)(2,1)S(1)}, u32[]{:S(2)}, u32[]{:S(2)}) collective-permute-start(bf16[40,720]{1,0:T(8,128)(2,1)S(1)} %copy.11), channel_id=1, source_target_pairs={{0,2},{2,4},{4,6},{6,0},{1,3},{3,5},{5,7},{7,1},{8,10},{10,12},{12... | collective-permute-start | bytes 172808 | tf_op jit(solution)/shard_map/ppermute | solution.py:16
  4.9 2.6 %collective-permute-start.8 = (bf16[40,720]{1,0:T(8,128)(2,1)S(1)}, bf16[40,720]{1,0:T(8,128)(2,1)S(1)}, u32[]{:S(2)}, u32[]{:S(2)}) collective-permute-start(bf16[40,720]{1,0:T(8,128)(2,1)S(1)} %copy.11), channel_id=1, source_target_pairs={{0,4},{2,6},{4,0},{6,2},{1,5},{3,7},{5,1},{7,3},{8,12},{10,14},{12... | collective-permute-start | bytes 172808 | tf_op jit(solution)/shard_map/ppermute | solution.py:16
  7.5 1.3 collective-permute-start.7
  9.3 2.5 %collective-permute-done.8 = bf16[40,720]{1,0:T(8,128)(2,1)S(1)} collective-permute-done((bf16[40,720]{1,0:T(8,128)(2,1)S(1)}, bf16[40,720]{1,0:T(8,128)(2,1)S(1)}, u32[]{:S(2)}, u32[]{:S(2)}) %collective-permute-start.8) | collective-permute-done | bytes 57632 | tf_op jit(solution)/shard_map/ppermute | solution.py:16
  12.1 1.5 collective-permute-start.12
  13.6 1.5 collective-permute-start.11
  15.1 1.4 collective-permute-start.10
  16.6 1.1 dynamic-slice_bitcast_fusion
  17.6 2.9 %collective-permute-start = (bf16[16,80,128]{2,1,0:T(8,128)(2,1)}, bf16[16,80,128]{2,1,0:T(8,128)(2,1)}, u32[]{:S(2)}, u32[]{:S(2)}) collective-permute-start(bf16[16,80,128]{2,1,0:T(8,128)(2,1)} %get-tuple-element.66), channel_id=1, source_target_pairs={{0,6},{2,0},{4,2},{6,4},{1,7},{3,1},{5,3},{7,5},{8,14},{10,8},{12,... | collective-permute-start | bytes 983048 | tf_op jit(solution)/shard_map/ppermute | solution.py:16
  21.2 0.7 collective-permute-done.12
  21.9 1.4 collective-permute-start.2
  23.3 2.0 collective-permute-done.11
  25.3 0.7 copy-done.6
  26.0 1.1 pad_maximum_fusion.refs_8_.refs_0_
  27.6 2.3 %dynamic-slice_bitcast_fusion.4 = (bf16[14,80,128]{2,1,0:T(8,128)(2,1)}, bf16[14,80,128]{2,1,0:T(8,128)(2,1)}, bf16[14,80,128]{2,1,0:T(8,128)(2,1)}, bf16[14,80,128]{2,1,0:T(8,128)(2,1)}) fusion(bf16[1,64,80,128]{3,2,1,0:T(8,128)(2,1)} %param.5, s32[]{:T(128)S(6)} %select_n.352, s32[]{:T(128)S(6)} %select_n.350, s32[]{:T(128)S(6)} %select_n.349, ...), kind=kLoop, calls=%fused_computation.24 | loop fusion | bytes 2293776 | tf_op jit(solution)/shard_map/dynamic_slice | solution.py:556
  29.9 1.5 dynamic-slice_bitcast_fusion.9
  32.0 0.7 bitcast_select_fusion.1
  32.8 0.8 pad_maximum_fusion.5
  33.5 2.2 %collective-permute-start.4 = (bf16[4,80,128]{2,1,0:T(8,128)(2,1)S(1)}, bf16[4,80,128]{2,1,0:T(8,128)(2,1)S(1)}, u32[]{:S(2)}, u32[]{:S(2)}) collective-permute-start(bf16[4,80,128]{2,1,0:T(8,128)(2,1)S(1)} %pad_maximum_fusion.5), channel_id=1, source_target_pairs={{0,6},{2,0},{4,2},{6,4},{1,7},{3,1},{5,3},{7,5},{8,14},{10,8},{12,... | collective-permute-start | bytes 245768 | tf_op jit(solution)/shard_map/ppermute | solution.py:16
  35.7 0.8 pad_maximum_fusion.6
  36.5 10.1 %collective-permute-done.4.refs_5_.refs_6_ = bf16[4,80,128]{2,1,0:T(8,128)(2,1)S(1)} collective-permute-done((bf16[4,80,128]{2,1,0:T(8,128)(2,1)S(1)}, bf16[4,80,128]{2,1,0:T(8,128)(2,1)S(1)}, u32[]{:S(2)}, u32[]{:S(2)}) %collective-permute-start.4) | collective-permute-done | bytes 81952 | tf_op jit(solution)/shard_map/ppermute | solution.py:16
  46.6 2.9 %collective-permute-start.5 = (bf16[4,80,128]{2,1,0:T(8,128)(2,1)S(1)}, bf16[4,80,128]{2,1,0:T(8,128)(2,1)S(1)}, u32[]{:S(2)}, u32[]{:S(2)}) collective-permute-start(bf16[4,80,128]{2,1,0:T(8,128)(2,1)S(1)} %pad_maximum_fusion.6), channel_id=1, source_target_pairs={{0,4},{2,6},{4,0},{6,2},{1,5},{3,7},{5,1},{7,3},{8,12},{10,14},{12... | collective-permute-start | bytes 245768 | tf_op jit(solution)/shard_map/ppermute | solution.py:16
  49.6 3.3 %collective-permute-done.5.refs_6_.refs_7_ = bf16[4,80,128]{2,1,0:T(8,128)(2,1)S(1)} collective-permute-done((bf16[4,80,128]{2,1,0:T(8,128)(2,1)S(1)}, bf16[4,80,128]{2,1,0:T(8,128)(2,1)S(1)}, u32[]{:S(2)}, u32[]{:S(2)}) %collective-permute-start.5) | collective-permute-done | bytes 81952 | tf_op jit(solution)/shard_map/ppermute | solution.py:16
  52.9 3.0 %collective-permute-start.6 = (bf16[4,80,128]{2,1,0:T(8,128)(2,1)S(1)}, bf16[4,80,128]{2,1,0:T(8,128)(2,1)S(1)}, u32[]{:S(2)}, u32[]{:S(2)}) collective-permute-start(bf16[4,80,128]{2,1,0:T(8,128)(2,1)S(1)} %pad_maximum_fusion.7), channel_id=1, source_target_pairs={{0,2},{2,4},{4,6},{6,0},{1,3},{3,5},{5,7},{7,1},{8,10},{10,12},{12... | collective-permute-start | bytes 245768 | tf_op jit(solution)/shard_map/ppermute | solution.py:16
  56.5 3.4 %collective-permute-done.6.refs_7_.refs_8_ = bf16[4,80,128]{2,1,0:T(8,128)(2,1)S(1)} collective-permute-done((bf16[4,80,128]{2,1,0:T(8,128)(2,1)S(1)}, bf16[4,80,128]{2,1,0:T(8,128)(2,1)S(1)}, u32[]{:S(2)}, u32[]{:S(2)}) %collective-permute-start.6) | collective-permute-done | bytes 81952 | tf_op jit(solution)/shard_map/ppermute | solution.py:16
  60.0 1.0 collective-permute-start.17
  61.0 1.5 collective-permute-start.18
  62.5 0.9 copy-done.4
  63.5 12.9 %conv_forward.1 = (bf16[64,80,128]{2,1,0:T(8,128)(2,1)}, bf16[16,80,128]{2,1,0:T(8,128)(2,1)}, bf16[16,80,128]{2,1,0:T(8,128)(2,1)}, bf16[16,80,128]{2,1,0:T(8,1...) custom-call(s32[5]{0:T(128)} %stack.52.turns, ...), custom_call_target="tpu_custom_call" | custom-call | flops 3774873600 | bytes 16777216 | tf_op jit(solution)/shard_map/conv_forward/pallas_call | solution.py:207
  76.4 2.1 collective-permute-start.14
  78.5 2.4 %collective-permute-start.15 = (bf16[16,80,128]{2,1,0:T(8,128)(2,1)}, bf16[16,80,128]{2,1,0:T(8,128)(2,1)S(1)}, u32[]{:S(2)}, u32[]{:S(2)}) collective-permute-start(bf16[16,80,128]{2,1,0:T(8,128)(2,1)} %get-tuple-element.24), channel_id=1, source_target_pairs={{0,4},{2,6},{4,0},{6,2},{1,5},{3,7},{5,1},{7,3},{8,12},{10,14},{12... | collective-permute-start | bytes 983048 | tf_op jit(solution)/shard_map/ppermute | solution.py:16
  80.9 1.0 collective-permute-start.16
  81.9 19.6 %collective-permute-done.18.refs_3_ = bf16[14,80,128]{2,1,0:T(8,128)(2,1)S(1)} collective-permute-done((bf16[14,80,128]{2,1,0:T(8,128)(2,1)}, bf16[14,80,128]{2,1,0:T(8,128)(2,1)S(1)}, u32[]{:S(2)}, u32[]{:S(2)}) %collective-permute-start.18) | collective-permute-done | bytes 286752 | tf_op jit(solution)/shard_map/ppermute | solution.py:16
  101.5 1.3 collective-permute-start.20
  102.8 1.3 collective-permute-start.21
  104.1 10.6 %shard_map.58 = (f32[4,6,40,320]{3,2,1,0:T(8,128)}, f32[4,6,40,320]{3,2,1,0:T(8,128)}, bf16[320,2048]{1,0:T(8,128)(2,1)}) custom-call(s32[1]{0:T(128)} %bitcast.1.turn, bf16[960,2304]{1,0:T(8,128)(2,1)} %get-tuple-element.26.stacked, f32[16,320,128]{2,1,0:T(8,128)} %get-tuple-element.27.refs_0_, bf16[14,80,128]{2,1,0:T(8,128)(2,1)} %get-tuple-element.54.refs_1_, ...), custom_call_target="tpu_custom_call" | custom-call | flops 2516582400 | bytes 8388608 | tf_op jit(solution)/shard_map/pallas_call | solution.py:302
  114.8 4.5 %turn_kernel.1.kernels = bf16[4,80,3456]{2,1,0:T(8,128)(2,1)} custom-call(bf16[4,160,720]{2,1,0:T(8,128)(2,1)} %copy-done.1, bf16[4,160,720]{2,1,0:T(8,128)(2,1)} %copy-done.4), custom_call_target="tpu_custom_call" | custom-call | flops 235929600 | bytes 4194304 | tf_op jit(solution)/shard_map/turn_kernel/pallas_call | solution.py:348
  120.0 10.6 %conv_backward.1 = (f32[64,80,128]{2,1,0:T(8,128)}, bf16[16,80,128]{2,1,0:T(8,128)(2,1)}, bf16[16,80,128]{2,1,0:T(8,128)(2,1)}, bf16[16,80,128]{2,1,0:T(8,128)(2,1)}) custom-call(s32[5]{0:T(128)} %stack.52.turns, bf16[320,2048]{1,0:T(8,128)(2,1)} %get-tuple-element.38.slope.refs_0_, bf16[1,320,128]{2,1,0:T(8,128)(2,1)} %copy-done.15, ...), custom_call_target="tpu_custom_call" | custom-call | flops 3774873600 | bytes 8388608 | tf_op jit(solution)/shard_map/conv_backward/pallas_call | solution.py:439
  130.6 2.7 %collective-permute-start.22 = (bf16[16,80,128]{2,1,0:T(8,128)(2,1)}, bf16[16,80,128]{2,1,0:T(8,128)(2,1)S(1)}, u32[]{:S(2)}, u32[]{:S(2)}) collective-permute-start(bf16[16,80,128]{2,1,0:T(8,128)(2,1)} %get-tuple-element.33), channel_id=1, source_target_pairs={{0,2},{2,4},{4,6},{6,0},{1,3},{3,5},{5,7},{7,1},{8,10},{10,12},{12... | collective-permute-start | bytes 983048 | tf_op jit(solution)/shard_map/ppermute | solution.py:16
  133.3 5.9 %shard_map.59 = (f32[4,3,40,320]{3,2,1,0:T(8,128)}, f32[4,3,40,320]{3,2,1,0:T(8,128)}) custom-call(s32[1]{0:T(128)} %bitcast.1.turn, bf16[960,2304]{1,0:T(8,128)(2,1)} %get-tuple-element.26.stacked, bf16[320,2048]{1,0:T(8,128)(2,1)} %get-tuple-element.38.slope.refs_0_), custom_call_target="tpu_custom_call" | custom-call | flops 1258291200 | bytes 8388608 | tf_op jit(solution)/shard_map/pallas_call | solution.py:302
  139.6 0.7 bitcast_dynamic-update-slice_fusion.2
  140.4 2.8 %collective-permute-start.24 = (bf16[16,80,128]{2,1,0:T(8,128)(2,1)S(1)}, bf16[16,80,128]{2,1,0:T(8,128)(2,1)S(1)}, u32[]{:S(2)}, u32[]{:S(2)}) collective-permute-start(bf16[16,80,128]{2,1,0:T(8,128)(2,1)S(1)} %copy-done.7), channel_id=1, source_target_pairs={{0,6},{2,0},{4,2},{6,4},{1,7},{3,1},{5,3},{7,5},{8,14},{10,8},{12,... | collective-permute-start | bytes 983048 | tf_op jit(solution)/shard_map/ppermute | solution.py:16
  143.2 0.7 bitcast_dynamic-update-slice_fusion.1
  143.9 0.8 bitcast_dynamic-update-slice_fusion
  144.7 0.9 convert_dynamic-update-slice_fusion.2
  145.6 11.8 %collective-permute-done.23 = bf16[16,80,128]{2,1,0:T(8,128)(2,1)S(1)} collective-permute-done((bf16[16,80,128]{2,1,0:T(8,128)(2,1)S(1)}, bf16[16,80,128]{2,1,0:T(8,128)(2,1)S(1)}, u32[]{:S(2)}, u32[]{:S(2)}) %collective-permute-start.23) | collective-permute-done | bytes 327712 | tf_op jit(solution)/shard_map/ppermute | solution.py:16
  157.4 0.9 convert_dynamic-update-slice_fusion.1
  158.4 0.6 collective-permute-start.35
  159.5 2.6 %collective-permute-start.33 = (f32[3,40,320]{2,1,0:T(8,128)S(1)}, f32[3,40,320]{2,1,0:T(8,128)S(1)}, u32[]{:S(2)}, u32[]{:S(2)}) collective-permute-start(f32[3,40,320]{2,1,0:T(8,128)S(1)} %get-tuple-element.68), channel_id=1, source_target_pairs={{0,24},{8,0},{16,8},{24,16},{1,25},{9,1},{17,9},{25,17},{2,26},{10... | collective-permute-start | bytes 460808 | tf_op jit(solution)/shard_map/ppermute | solution.py:16
  162.5 1.3 collective-permute-start.27
  163.8 3.0 %collective-permute-done.35 = f32[3,40,320]{2,1,0:T(8,128)S(1)} collective-permute-done((f32[3,40,320]{2,1,0:T(8,128)S(1)}, f32[3,40,320]{2,1,0:T(8,128)S(1)}, u32[]{:S(2)}, u32[]{:S(2)}) %collective-permute-start.35) | collective-permute-done | bytes 153632 | tf_op jit(solution)/shard_map/ppermute | solution.py:16
  166.9 0.9 convert_dynamic-update-slice_fusion
  167.7 3.1 %collective-permute-done.34 = f32[3,40,320]{2,1,0:T(8,128)S(1)} collective-permute-done((f32[3,40,320]{2,1,0:T(8,128)S(1)}, f32[3,40,320]{2,1,0:T(8,128)S(1)}, u32[]{:S(2)}, u32[]{:S(2)}) %collective-permute-start.34) | collective-permute-done | bytes 153632 | tf_op jit(solution)/shard_map/ppermute | solution.py:16
  170.9 7.8 %collective-permute-done.28 = f32[6,40,320]{2,1,0:T(8,128)S(1)} collective-permute-done((f32[6,40,320]{2,1,0:T(8,128)S(1)}, f32[6,40,320]{2,1,0:T(8,128)S(1)}, u32[]{:S(2)}, u32[]{:S(2)}) %collective-permute-start.28) | collective-permute-done | bytes 307232 | tf_op jit(solution)/shard_map/ppermute | solution.py:16
  178.8 5.7 %collective-permute-done.27 = f32[6,40,320]{2,1,0:T(8,128)S(1)} collective-permute-done((f32[6,40,320]{2,1,0:T(8,128)S(1)}, f32[6,40,320]{2,1,0:T(8,128)S(1)}, u32[]{:S(2)}, u32[]{:S(2)}) %collective-permute-start.27) | collective-permute-done | bytes 307232 | tf_op jit(solution)/shard_map/ppermute | solution.py:16
  184.9 5.9 %collective-permute-start.29 = (f32[160,240]{0,1:T(8,128)S(1)}, f32[160,240]{0,1:T(8,128)S(1)}, u32[]{:S(2)}, u32[]{:S(2)}) collective-permute-start(f32[160,240]{0,1:T(8,128)S(1)} %pad_maximum_fusion.3), channel_id=1, source_target_pairs={{0,2},{2,0},{4,6},{6,4},{1,3},{3,1},{5,7},{7,5},{8,10},{10,8},{12,... | collective-permute-start | bytes 460808 | tf_op jit(solution)/shard_map/ppermute | solution.py:20
  191.0 3.4 %collective-permute-start.37 = (f32[80,120]{0,1:T(8,128)S(1)}, f32[80,120]{0,1:T(8,128)S(1)}, u32[]{:S(2)}, u32[]{:S(2)}) collective-permute-start(f32[80,120]{0,1:T(8,128)S(1)} %bitcast.159), channel_id=1, source_target_pairs={{0,4},{2,6},{4,0},{6,2},{1,5},{3,7},{5,1},{7,3},{8,12},{10,14},{12... | collective-permute-start | bytes 115208 | tf_op jit(solution)/shard_map/ppermute | solution.py:16
  194.4 2.8 %collective-permute-start.36 = (f32[80,120]{0,1:T(8,128)S(1)}, f32[80,120]{0,1:T(8,128)S(1)}, u32[]{:S(2)}, u32[]{:S(2)}) collective-permute-start(f32[80,120]{0,1:T(8,128)S(1)} %bitcast.158), channel_id=1, source_target_pairs={{0,6},{2,0},{4,2},{6,4},{1,7},{3,1},{5,3},{7,5},{8,14},{10,8},{12,... | collective-permute-start | bytes 115208 | tf_op jit(solution)/shard_map/ppermute | solution.py:16
  197.3 1.5 collective-permute-done.29
  198.8 3.1 %collective-permute-start.30 = (f32[80,240]{0,1:T(8,128)S(1)}, f32[80,240]{0,1:T(8,128)S(1)}, u32[]{:S(2)}, u32[]{:S(2)}) collective-permute-start(f32[80,240]{0,1:T(8,128)S(1)} %bitcast_add_fusion), channel_id=1, source_target_pairs={{0,4},{2,6},{4,0},{6,2},{1,5},{3,7},{5,1},{7,3},{8,12},{10,14},{12... | collective-permute-start | bytes 230408 | tf_op jit(solution)/shard_map/ppermute | solution.py:20
  202.1 3.3 %collective-permute-done.30 = f32[80,240]{0,1:T(8,128)S(1)} collective-permute-done((f32[80,240]{0,1:T(8,128)S(1)}, f32[80,240]{0,1:T(8,128)S(1)}, u32[]{:S(2)}, u32[]{:S(2)}) %collective-permute-start.30) | collective-permute-done | bytes 76832 | tf_op jit(solution)/shard_map/ppermute | solution.py:20
  205.6 1.2 collective-permute-done.31
  207.0 0.8 pad_maximum_fusion.1
  (92 shorter events, 6.8 us)
Async XLA Ops:
  0.6 0.9 copy-start
  0.6 15.9 %copy-start.2 = (bf16[1,64,80,128]{3,2,1,0:T(8,128)(2,1)S(1)}, bf16[1,64,80,128]{3,2,1,0:T(8,128)(2,1)}, u32[]{:S(2)}) copy-start(bf16[1,64,80,128]{3,2,1,0:T(8,128)(2,1)} %param.3) | copy-start | bytes 3932164
  1.8 7.5 %collective-permute-start.9 = (bf16[40,720]{1,0:T(8,128)(2,1)S(1)}, bf16[40,720]{1,0:T(8,128)(2,1)S(1)}, u32[]{:S(2)}, u32[]{:S(2)}) collective-permute-start(bf16[40,720]{1,0:T(8,128)(2,1)S(1)} %copy.11), channel_id=1, source_target_pairs={{0,2},{2,4},{4,6},{6,0},{1,3},{3,5},{5,7},{7,1},{8,10},{10,12},{12... | collective-permute-start | bytes 172808 | tf_op jit(solution)/shard_map/ppermute | solution.py:16
  4.9 6.9 %collective-permute-start.8 = (bf16[40,720]{1,0:T(8,128)(2,1)S(1)}, bf16[40,720]{1,0:T(8,128)(2,1)S(1)}, u32[]{:S(2)}, u32[]{:S(2)}) collective-permute-start(bf16[40,720]{1,0:T(8,128)(2,1)S(1)} %copy.11), channel_id=1, source_target_pairs={{0,4},{2,6},{4,0},{6,2},{1,5},{3,7},{5,1},{7,3},{8,12},{10,14},{12... | collective-permute-start | bytes 172808 | tf_op jit(solution)/shard_map/ppermute | solution.py:16
  7.5 4.6 %collective-permute-start.7 = (bf16[40,720]{1,0:T(8,128)(2,1)S(1)}, bf16[40,720]{1,0:T(8,128)(2,1)S(1)}, u32[]{:S(2)}, u32[]{:S(2)}) collective-permute-start(bf16[40,720]{1,0:T(8,128)(2,1)S(1)} %copy.11), channel_id=1, source_target_pairs={{0,6},{2,0},{4,2},{6,4},{1,7},{3,1},{5,3},{7,5},{8,14},{10,8},{12,... | collective-permute-start | bytes 172808 | tf_op jit(solution)/shard_map/ppermute | solution.py:16
  12.1 9.8 %collective-permute-start.12 = (bf16[160,720]{1,0:T(8,128)(2,1)S(1)}, bf16[160,720]{1,0:T(8,128)(2,1)S(1)}, u32[]{:S(2)}, u32[]{:S(2)}) collective-permute-start(bf16[160,720]{1,0:T(8,128)(2,1)S(1)} %get-tuple-element.76), channel_id=1, source_target_pairs={{0,8},{8,16},{16,24},{24,0},{1,9},{9,17},{17,25},{25,1},{2,10},{10... | collective-permute-start | bytes 691208 | tf_op jit(solution)/shard_map/ppermute | solution.py:16
  13.6 11.6 %collective-permute-start.11 = (bf16[160,720]{1,0:T(8,128)(2,1)S(1)}, bf16[160,720]{1,0:T(8,128)(2,1)S(1)}, u32[]{:S(2)}, u32[]{:S(2)}) collective-permute-start(bf16[160,720]{1,0:T(8,128)(2,1)S(1)} %get-tuple-element.76), channel_id=1, source_target_pairs={{0,16},{8,24},{16,0},{24,8},{1,17},{9,25},{17,1},{25,9},{2,18},{10... | collective-permute-start | bytes 691208 | tf_op jit(solution)/shard_map/ppermute | solution.py:16
  15.1 10.1 %collective-permute-start.10 = (bf16[160,720]{1,0:T(8,128)(2,1)S(1)}, bf16[160,720]{1,0:T(8,128)(2,1)S(1)}, u32[]{:S(2)}, u32[]{:S(2)}) collective-permute-start(bf16[160,720]{1,0:T(8,128)(2,1)S(1)} %get-tuple-element.76), channel_id=1, source_target_pairs={{0,24},{8,0},{16,8},{24,16},{1,25},{9,1},{17,9},{25,17},{2,26},{10... | collective-permute-start | bytes 691208 | tf_op jit(solution)/shard_map/ppermute | solution.py:16
  17.6 43.4 %collective-permute-start = (bf16[16,80,128]{2,1,0:T(8,128)(2,1)}, bf16[16,80,128]{2,1,0:T(8,128)(2,1)}, u32[]{:S(2)}, u32[]{:S(2)}) collective-permute-start(bf16[16,80,128]{2,1,0:T(8,128)(2,1)} %get-tuple-element.66), channel_id=1, source_target_pairs={{0,6},{2,0},{4,2},{6,4},{1,7},{3,1},{5,3},{7,5},{8,14},{10,8},{12,... | collective-permute-start | bytes 983048 | tf_op jit(solution)/shard_map/ppermute | solution.py:16
  20.5 41.9 %collective-permute-start.1 = (bf16[16,80,128]{2,1,0:T(8,128)(2,1)}, bf16[16,80,128]{2,1,0:T(8,128)(2,1)}, u32[]{:S(2)}, u32[]{:S(2)}) collective-permute-start(bf16[16,80,128]{2,1,0:T(8,128)(2,1)} %get-tuple-element.65), channel_id=1, source_target_pairs={{0,4},{2,6},{4,0},{6,2},{1,5},{3,7},{5,1},{7,3},{8,12},{10,14},{12... | collective-permute-start | bytes 983048 | tf_op jit(solution)/shard_map/ppermute | solution.py:16
  21.9 40.6 %collective-permute-start.2 = (bf16[16,80,128]{2,1,0:T(8,128)(2,1)}, bf16[16,80,128]{2,1,0:T(8,128)(2,1)}, u32[]{:S(2)}, u32[]{:S(2)}) collective-permute-start(bf16[16,80,128]{2,1,0:T(8,128)(2,1)} %get-tuple-element.64), channel_id=1, source_target_pairs={{0,2},{2,4},{4,6},{6,0},{1,3},{3,5},{5,7},{7,1},{8,10},{10,12},{12... | collective-permute-start | bytes 983048 | tf_op jit(solution)/shard_map/ppermute | solution.py:16
  25.3 6.8 %collective-permute-start.3 = (bf16[1,80,128]{2,1,0:T(8,128)(2,1)}, bf16[1,80,128]{2,1,0:T(8,128)(2,1)}, u32[]{:S(2)}, u32[]{:S(2)}) collective-permute-start(bf16[1,80,128]{2,1,0:T(8,128)(2,1)} %select_bitcast_fusion), channel_id=1, source_target_pairs={{0,1},{1,0},{2,3},{3,2},{4,5},{5,4},{6,7},{7,6},{8,9},{9,8},{10,11... | collective-permute-start | bytes 61448 | tf_op jit(solution)/shard_map/ppermute | solution.py:16
  25.3 0.7 copy-start.6
  27.0 5.7 %copy-start.1 = (bf16[4,160,720]{2,1,0:T(8,128)(2,1)}, bf16[4,160,720]{2,1,0:T(8,128)(2,1)S(1)}, u32[]{:S(2)}) copy-start(bf16[4,160,720]{2,1,0:T(8,128)(2,1)S(1)} %pad_maximum_fusion.refs_8_.refs_0_) | copy-start | bytes 2764804
  27.1 35.4 %collective-permute-start.13 = (bf16[4,160,720]{2,1,0:T(8,128)(2,1)S(1)}, bf16[4,160,720]{2,1,0:T(8,128)(2,1)S(1)}, u32[]{:S(2)}, u32[]{:S(2)}) collective-permute-start(bf16[4,160,720]{2,1,0:T(8,128)(2,1)S(1)} %pad_maximum_fusion.refs_8_.refs_0_), channel_id=1, source_target_pairs={{0,1},{1,0},{2,3},{3,2},{4,5},{5,4},{6,7},{7,6},{8,9},{9,8},{10,11... | collective-permute-start | bytes 2764808 | tf_op jit(solution)/shard_map/ppermute | solution.py:16
  33.5 13.1 %collective-permute-start.4 = (bf16[4,80,128]{2,1,0:T(8,128)(2,1)S(1)}, bf16[4,80,128]{2,1,0:T(8,128)(2,1)S(1)}, u32[]{:S(2)}, u32[]{:S(2)}) collective-permute-start(bf16[4,80,128]{2,1,0:T(8,128)(2,1)S(1)} %pad_maximum_fusion.5), channel_id=1, source_target_pairs={{0,6},{2,0},{4,2},{6,4},{1,7},{3,1},{5,3},{7,5},{8,14},{10,8},{12,... | collective-permute-start | bytes 245768 | tf_op jit(solution)/shard_map/ppermute | solution.py:16
  46.6 15.9 %copy-start.12 = (bf16[4,80,128]{2,1,0:T(8,128)(2,1)}, bf16[4,80,128]{2,1,0:T(8,128)(2,1)S(1)}, u32[]{:S(2)}) copy-start(bf16[4,80,128]{2,1,0:T(8,128)(2,1)S(1)} %collective-permute-done.4.refs_5_.refs_6_) | copy-start | bytes 245764
  46.6 6.3 %collective-permute-start.5 = (bf16[4,80,128]{2,1,0:T(8,128)(2,1)S(1)}, bf16[4,80,128]{2,1,0:T(8,128)(2,1)S(1)}, u32[]{:S(2)}, u32[]{:S(2)}) collective-permute-start(bf16[4,80,128]{2,1,0:T(8,128)(2,1)S(1)} %pad_maximum_fusion.6), channel_id=1, source_target_pairs={{0,4},{2,6},{4,0},{6,2},{1,5},{3,7},{5,1},{7,3},{8,12},{10,14},{12... | collective-permute-start | bytes 245768 | tf_op jit(solution)/shard_map/ppermute | solution.py:16
  52.9 9.6 %copy-start.13 = (bf16[4,80,128]{2,1,0:T(8,128)(2,1)}, bf16[4,80,128]{2,1,0:T(8,128)(2,1)S(1)}, u32[]{:S(2)}) copy-start(bf16[4,80,128]{2,1,0:T(8,128)(2,1)S(1)} %collective-permute-done.5.refs_6_.refs_7_) | copy-start | bytes 245764
  52.9 7.1 %collective-permute-start.6 = (bf16[4,80,128]{2,1,0:T(8,128)(2,1)S(1)}, bf16[4,80,128]{2,1,0:T(8,128)(2,1)S(1)}, u32[]{:S(2)}, u32[]{:S(2)}) collective-permute-start(bf16[4,80,128]{2,1,0:T(8,128)(2,1)S(1)} %pad_maximum_fusion.7), channel_id=1, source_target_pairs={{0,2},{2,4},{4,6},{6,0},{1,3},{3,5},{5,7},{7,1},{8,10},{10,12},{12... | collective-permute-start | bytes 245768 | tf_op jit(solution)/shard_map/ppermute | solution.py:16
  60.0 2.5 %copy-start.14 = (bf16[4,80,128]{2,1,0:T(8,128)(2,1)}, bf16[4,80,128]{2,1,0:T(8,128)(2,1)S(1)}, u32[]{:S(2)}) copy-start(bf16[4,80,128]{2,1,0:T(8,128)(2,1)S(1)} %collective-permute-done.6.refs_7_.refs_8_) | copy-start | bytes 245764
  60.0 20.9 %collective-permute-start.17 = (bf16[14,80,128]{2,1,0:T(8,128)(2,1)}, bf16[14,80,128]{2,1,0:T(8,128)(2,1)S(1)}, u32[]{:S(2)}, u32[]{:S(2)}) collective-permute-start(bf16[14,80,128]{2,1,0:T(8,128)(2,1)} %get-tuple-element.53), channel_id=1, source_target_pairs={{0,6},{2,0},{4,2},{6,4},{1,7},{3,1},{5,3},{7,5},{8,14},{10,8},{12,... | collective-permute-start | bytes 860168 | tf_op jit(solution)/shard_map/ppermute | solution.py:16
  61.0 40.5 %collective-permute-start.18 = (bf16[14,80,128]{2,1,0:T(8,128)(2,1)}, bf16[14,80,128]{2,1,0:T(8,128)(2,1)S(1)}, u32[]{:S(2)}, u32[]{:S(2)}) collective-permute-start(bf16[14,80,128]{2,1,0:T(8,128)(2,1)} %get-tuple-element.55), channel_id=1, source_target_pairs={{0,4},{2,6},{4,0},{6,2},{1,5},{3,7},{5,1},{7,3},{8,12},{10,14},{12... | collective-permute-start | bytes 860168 | tf_op jit(solution)/shard_map/ppermute | solution.py:16
  62.5 40.3 %collective-permute-start.19 = (bf16[14,80,128]{2,1,0:T(8,128)(2,1)}, bf16[14,80,128]{2,1,0:T(8,128)(2,1)S(1)}, u32[]{:S(2)}, u32[]{:S(2)}) collective-permute-start(bf16[14,80,128]{2,1,0:T(8,128)(2,1)} %get-tuple-element.52), channel_id=1, source_target_pairs={{0,2},{2,4},{4,6},{6,0},{1,3},{3,5},{5,7},{7,1},{8,10},{10,12},{12... | collective-permute-start | bytes 860168 | tf_op jit(solution)/shard_map/ppermute | solution.py:16
  62.5 1.0 copy-start.4
  76.4 62.7 %collective-permute-start.14 = (bf16[16,80,128]{2,1,0:T(8,128)(2,1)}, bf16[16,80,128]{2,1,0:T(8,128)(2,1)S(1)}, u32[]{:S(2)}, u32[]{:S(2)}) collective-permute-start(bf16[16,80,128]{2,1,0:T(8,128)(2,1)} %get-tuple-element.23), channel_id=1, source_target_pairs={{0,2},{2,4},{4,6},{6,0},{1,3},{3,5},{5,7},{7,1},{8,10},{10,12},{12... | collective-permute-start | bytes 983048 | tf_op jit(solution)/shard_map/ppermute | solution.py:16
  78.5 61.9 %collective-permute-start.15 = (bf16[16,80,128]{2,1,0:T(8,128)(2,1)}, bf16[16,80,128]{2,1,0:T(8,128)(2,1)S(1)}, u32[]{:S(2)}, u32[]{:S(2)}) collective-permute-start(bf16[16,80,128]{2,1,0:T(8,128)(2,1)} %get-tuple-element.24), channel_id=1, source_target_pairs={{0,4},{2,6},{4,0},{6,2},{1,5},{3,7},{5,1},{7,3},{8,12},{10,14},{12... | collective-permute-start | bytes 983048 | tf_op jit(solution)/shard_map/ppermute | solution.py:16
  80.9 23.3 %copy-start.9 = (bf16[14,80,128]{2,1,0:T(8,128)(2,1)}, bf16[14,80,128]{2,1,0:T(8,128)(2,1)S(1)}, u32[]{:S(2)}) copy-start(bf16[14,80,128]{2,1,0:T(8,128)(2,1)S(1)} %collective-permute-done.17.refs_2_) | copy-start | bytes 860164
  80.9 63.1 %collective-permute-start.16 = (bf16[16,80,128]{2,1,0:T(8,128)(2,1)}, bf16[16,80,128]{2,1,0:T(8,128)(2,1)S(1)}, u32[]{:S(2)}, u32[]{:S(2)}) collective-permute-start(bf16[16,80,128]{2,1,0:T(8,128)(2,1)} %get-tuple-element.25), channel_id=1, source_target_pairs={{0,6},{2,0},{4,2},{6,4},{1,7},{3,1},{5,3},{7,5},{8,14},{10,8},{12,... | collective-permute-start | bytes 983048 | tf_op jit(solution)/shard_map/ppermute | solution.py:16
  101.5 2.6 %copy-start.10 = (bf16[14,80,128]{2,1,0:T(8,128)(2,1)}, bf16[14,80,128]{2,1,0:T(8,128)(2,1)S(1)}, u32[]{:S(2)}) copy-start(bf16[14,80,128]{2,1,0:T(8,128)(2,1)S(1)} %collective-permute-done.18.refs_3_) | copy-start | bytes 860164
  101.5 17.8 %collective-permute-start.20 = (bf16[1,320,128]{2,1,0:T(8,128)(2,1)}, bf16[1,320,128]{2,1,0:T(8,128)(2,1)S(1)}, u32[]{:S(2)}, u32[]{:S(2)}) collective-permute-start(bf16[1,320,128]{2,1,0:T(8,128)(2,1)} %get-tuple-element.29), channel_id=1, source_target_pairs={{0,2},{2,4},{4,6},{6,7},{7,5},{5,3},{3,1},{8,10},{10,12},{12,14},{... | collective-permute-start | bytes 245768 | tf_op jit(solution)/shard_map/ppermute | solution.py:576
  102.8 1.3 copy-start.11
  102.8 16.6 %collective-permute-start.21 = (bf16[1,320,128]{2,1,0:T(8,128)(2,1)}, bf16[1,320,128]{2,1,0:T(8,128)(2,1)S(1)}, u32[]{:S(2)}, u32[]{:S(2)}) collective-permute-start(bf16[1,320,128]{2,1,0:T(8,128)(2,1)} %get-tuple-element.30), channel_id=1, source_target_pairs={{2,0},{4,2},{6,4},{7,6},{5,7},{3,5},{1,3},{10,8},{12,10},{14,12},{... | collective-permute-start | bytes 245768 | tf_op jit(solution)/shard_map/ppermute | solution.py:577
  119.3 0.6 copy-start.15
  119.3 42.9 %collective-permute-start.25 = (f32[4,6,40,320]{3,2,1,0:T(8,128)}, f32[4,6,40,320]{3,2,1,0:T(8,128)S(1)}, u32[]{:S(2)}, u32[]{:S(2)}) collective-permute-start(f32[4,6,40,320]{3,2,1,0:T(8,128)} %get-tuple-element.37), channel_id=1, source_target_pairs={{0,1},{1,0},{2,3},{3,2},{4,5},{5,4},{6,7},{7,6},{8,9},{9,8},{10,11... | collective-permute-start | bytes 3686408 | tf_op jit(solution)/shard_map/ppermute | solution.py:16
  119.4 0.6 copy-start.16
  130.6 8.6 %copy-start.8 = (bf16[16,80,128]{2,1,0:T(8,128)(2,1)S(1)}, bf16[16,80,128]{2,1,0:T(8,128)(2,1)}, u32[]{:S(2)}) copy-start(bf16[16,80,128]{2,1,0:T(8,128)(2,1)} %get-tuple-element.34) | copy-start | bytes 983044
  130.6 9.8 %copy-start.7 = (bf16[16,80,128]{2,1,0:T(8,128)(2,1)S(1)}, bf16[16,80,128]{2,1,0:T(8,128)(2,1)}, u32[]{:S(2)}) copy-start(bf16[16,80,128]{2,1,0:T(8,128)(2,1)} %get-tuple-element.35) | copy-start | bytes 983044
  130.6 14.1 %collective-permute-start.22 = (bf16[16,80,128]{2,1,0:T(8,128)(2,1)}, bf16[16,80,128]{2,1,0:T(8,128)(2,1)S(1)}, u32[]{:S(2)}, u32[]{:S(2)}) collective-permute-start(bf16[16,80,128]{2,1,0:T(8,128)(2,1)} %get-tuple-element.33), channel_id=1, source_target_pairs={{0,2},{2,4},{4,6},{6,0},{1,3},{3,5},{5,7},{7,1},{8,10},{10,12},{12... | collective-permute-start | bytes 983048 | tf_op jit(solution)/shard_map/ppermute | solution.py:16
  139.2 18.2 %collective-permute-start.23 = (bf16[16,80,128]{2,1,0:T(8,128)(2,1)S(1)}, bf16[16,80,128]{2,1,0:T(8,128)(2,1)S(1)}, u32[]{:S(2)}, u32[]{:S(2)}) collective-permute-start(bf16[16,80,128]{2,1,0:T(8,128)(2,1)S(1)} %copy-done.8), channel_id=1, source_target_pairs={{0,4},{2,6},{4,0},{6,2},{1,5},{3,7},{5,1},{7,3},{8,12},{10,14},{12... | collective-permute-start | bytes 983048 | tf_op jit(solution)/shard_map/ppermute | solution.py:16
  140.4 22.2 %collective-permute-start.24 = (bf16[16,80,128]{2,1,0:T(8,128)(2,1)S(1)}, bf16[16,80,128]{2,1,0:T(8,128)(2,1)S(1)}, u32[]{:S(2)}, u32[]{:S(2)}) collective-permute-start(bf16[16,80,128]{2,1,0:T(8,128)(2,1)S(1)} %copy-done.7), channel_id=1, source_target_pairs={{0,6},{2,0},{4,2},{6,4},{1,7},{3,1},{5,3},{7,5},{8,14},{10,8},{12,... | collective-permute-start | bytes 983048 | tf_op jit(solution)/shard_map/ppermute | solution.py:16
  143.9 14.3 %copy-start.5 = (f32[4,3,40,320]{3,2,1,0:T(8,128)S(1)}, f32[4,3,40,320]{3,2,1,0:T(8,128)}, u32[]{:S(2)}) copy-start(f32[4,3,40,320]{3,2,1,0:T(8,128)} %get-tuple-element.39) | copy-start | bytes 1843204
  143.9 14.3 %collective-permute-start.32 = (f32[4,3,40,320]{3,2,1,0:T(8,128)}, f32[4,3,40,320]{3,2,1,0:T(8,128)S(1)}, u32[]{:S(2)}, u32[]{:S(2)}) collective-permute-start(f32[4,3,40,320]{3,2,1,0:T(8,128)} %get-tuple-element.40), channel_id=1, source_target_pairs={{0,1},{1,0},{2,3},{3,2},{4,5},{5,4},{6,7},{7,6},{8,9},{9,8},{10,11... | collective-permute-start | bytes 1843208 | tf_op jit(solution)/shard_map/ppermute | solution.py:16
  158.3 3.9 %copy-start.3 = (f32[4,6,40,320]{3,2,1,0:T(8,128)S(1)}, f32[4,6,40,320]{3,2,1,0:T(8,128)}, u32[]{:S(2)}) copy-start(f32[4,6,40,320]{3,2,1,0:T(8,128)} %get-tuple-element.36) | copy-start | bytes 3686404
  158.4 8.5 %collective-permute-start.35 = (f32[3,40,320]{2,1,0:T(8,128)S(1)}, f32[3,40,320]{2,1,0:T(8,128)S(1)}, u32[]{:S(2)}, u32[]{:S(2)}) collective-permute-start(f32[3,40,320]{2,1,0:T(8,128)S(1)} %get-tuple-element.69), channel_id=1, source_target_pairs={{0,8},{8,16},{16,24},{24,0},{1,9},{9,17},{17,25},{25,1},{2,10},{10... | collective-permute-start | bytes 460808 | tf_op jit(solution)/shard_map/ppermute | solution.py:16
  159.0 11.8 %collective-permute-start.34 = (f32[3,40,320]{2,1,0:T(8,128)S(1)}, f32[3,40,320]{2,1,0:T(8,128)S(1)}, u32[]{:S(2)}, u32[]{:S(2)}) collective-permute-start(f32[3,40,320]{2,1,0:T(8,128)S(1)} %get-tuple-element.70), channel_id=1, source_target_pairs={{0,16},{8,24},{16,0},{24,8},{1,17},{9,25},{17,1},{25,9},{2,18},{10... | collective-permute-start | bytes 460808 | tf_op jit(solution)/shard_map/ppermute | solution.py:16
  159.5 11.3 %collective-permute-start.33 = (f32[3,40,320]{2,1,0:T(8,128)S(1)}, f32[3,40,320]{2,1,0:T(8,128)S(1)}, u32[]{:S(2)}, u32[]{:S(2)}) collective-permute-start(f32[3,40,320]{2,1,0:T(8,128)S(1)} %get-tuple-element.68), channel_id=1, source_target_pairs={{0,24},{8,0},{16,8},{24,16},{1,25},{9,1},{17,9},{25,17},{2,26},{10... | collective-permute-start | bytes 460808 | tf_op jit(solution)/shard_map/ppermute | solution.py:16
  162.5 16.3 %collective-permute-start.28 = (f32[6,40,320]{2,1,0:T(8,128)S(1)}, f32[6,40,320]{2,1,0:T(8,128)S(1)}, u32[]{:S(2)}, u32[]{:S(2)}) collective-permute-start(f32[6,40,320]{2,1,0:T(8,128)S(1)} %get-tuple-element.42), channel_id=1, source_target_pairs={{0,8},{8,16},{16,24},{24,0},{1,9},{9,17},{17,25},{25,1},{2,10},{10... | collective-permute-start | bytes 921608 | tf_op jit(solution)/shard_map/ppermute | solution.py:16
  162.5 21.9 %collective-permute-start.27 = (f32[6,40,320]{2,1,0:T(8,128)S(1)}, f32[6,40,320]{2,1,0:T(8,128)S(1)}, u32[]{:S(2)}, u32[]{:S(2)}) collective-permute-start(f32[6,40,320]{2,1,0:T(8,128)S(1)} %get-tuple-element.43), channel_id=1, source_target_pairs={{0,16},{8,24},{16,0},{24,8},{1,17},{9,25},{17,1},{25,9},{2,18},{10... | collective-permute-start | bytes 921608 | tf_op jit(solution)/shard_map/ppermute | solution.py:16
  166.9 17.6 %collective-permute-start.26 = (f32[6,40,320]{2,1,0:T(8,128)S(1)}, f32[6,40,320]{2,1,0:T(8,128)S(1)}, u32[]{:S(2)}, u32[]{:S(2)}) collective-permute-start(f32[6,40,320]{2,1,0:T(8,128)S(1)} %get-tuple-element.41), channel_id=1, source_target_pairs={{0,24},{8,0},{16,8},{24,16},{1,25},{9,1},{17,9},{25,17},{2,26},{10... | collective-permute-start | bytes 921608 | tf_op jit(solution)/shard_map/ppermute | solution.py:16
  184.9 13.9 %collective-permute-start.29 = (f32[160,240]{0,1:T(8,128)S(1)}, f32[160,240]{0,1:T(8,128)S(1)}, u32[]{:S(2)}, u32[]{:S(2)}) collective-permute-start(f32[160,240]{0,1:T(8,128)S(1)} %pad_maximum_fusion.3), channel_id=1, source_target_pairs={{0,2},{2,0},{4,6},{6,4},{1,3},{3,1},{5,7},{7,5},{8,10},{10,8},{12,... | collective-permute-start | bytes 460808 | tf_op jit(solution)/shard_map/ppermute | solution.py:20
  190.9 11.1 %collective-permute-start.38 = (f32[80,120]{0,1:T(8,128)S(1)}, f32[80,120]{0,1:T(8,128)S(1)}, u32[]{:S(2)}, u32[]{:S(2)}) collective-permute-start(f32[80,120]{0,1:T(8,128)S(1)} %bitcast.160), channel_id=1, source_target_pairs={{0,2},{2,4},{4,6},{6,0},{1,3},{3,5},{5,7},{7,1},{8,10},{10,12},{12... | collective-permute-start | bytes 115208 | tf_op jit(solution)/shard_map/ppermute | solution.py:16
  191.0 11.0 %collective-permute-start.37 = (f32[80,120]{0,1:T(8,128)S(1)}, f32[80,120]{0,1:T(8,128)S(1)}, u32[]{:S(2)}, u32[]{:S(2)}) collective-permute-start(f32[80,120]{0,1:T(8,128)S(1)} %bitcast.159), channel_id=1, source_target_pairs={{0,4},{2,6},{4,0},{6,2},{1,5},{3,7},{5,1},{7,3},{8,12},{10,14},{12... | collective-permute-start | bytes 115208 | tf_op jit(solution)/shard_map/ppermute | solution.py:16
  194.4 7.6 %collective-permute-start.36 = (f32[80,120]{0,1:T(8,128)S(1)}, f32[80,120]{0,1:T(8,128)S(1)}, u32[]{:S(2)}, u32[]{:S(2)}) collective-permute-start(f32[80,120]{0,1:T(8,128)S(1)} %bitcast.158), channel_id=1, source_target_pairs={{0,6},{2,0},{4,2},{6,4},{1,7},{3,1},{5,3},{7,5},{8,14},{10,8},{12,... | collective-permute-start | bytes 115208 | tf_op jit(solution)/shard_map/ppermute | solution.py:16
  198.8 6.5 %collective-permute-start.30 = (f32[80,240]{0,1:T(8,128)S(1)}, f32[80,240]{0,1:T(8,128)S(1)}, u32[]{:S(2)}, u32[]{:S(2)}) collective-permute-start(f32[80,240]{0,1:T(8,128)S(1)} %bitcast_add_fusion), channel_id=1, source_target_pairs={{0,4},{2,6},{4,0},{6,2},{1,5},{3,7},{5,1},{7,3},{8,12},{10,14},{12... | collective-permute-start | bytes 230408 | tf_op jit(solution)/shard_map/ppermute | solution.py:20
  202.0 3.5 %collective-permute-start.39 = (f32[80,120]{0,1:T(8,128)S(1)}, f32[80,120]{0,1:T(8,128)S(1)}, u32[]{:S(2)}, u32[]{:S(2)}) collective-permute-start(f32[80,120]{0,1:T(8,128)S(1)} %fusion.16), channel_id=1, source_target_pairs={{0,1},{1,0},{2,3},{3,2},{4,5},{5,4},{6,7},{7,6},{8,9},{9,8},{10,11... | collective-permute-start | bytes 115208 | tf_op jit(solution)/shard_map/ppermute | solution.py:16
  205.5 1.4 collective-permute-start.31

commit v9 on v8

--- a/solution.py
+++ b/solution.py
@@ -465,6 +465,44 @@
     )(turns, slope, above, below, kernels)
 
 
+def put_body(count, places, *refs):
+    out = refs[count + 1]
+    for j in range(count):
+
+        @pl.when(pl.program_id(0) == j)
+        def _():
+            out[...] = refs[j][...].astype(out.dtype)
+
+
+def put(places, arrived, whole_array):
+    count = len(arrived)
+    height, depth, width = arrived[0].shape
+    rows = 8 if height % 8 == 0 else 1
+    steps = height // rows
+
+    def from_block(j):
+        def index(block, step, places):
+            return jnp.where(block == j, step, jnp.where(block < j, 0, steps - 1)), 0, 0
+
+        return pl.BlockSpec((rows, depth, width), index)
+
+    return pl.pallas_call(
+        functools.partial(put_body, count),
+        grid_spec=pltpu.PrefetchScalarGridSpec(
+            num_scalar_prefetch=1,
+            grid=(count, steps),
+            in_specs=[from_block(j) for j in range(count)] + [pl.BlockSpec(memory_space=pl.ANY)],
+            out_specs=pl.BlockSpec(
+                (rows, depth, width), lambda block, step, places: (places[block] * steps + step, 0, 0)
+            ),
+        ),
+        out_shape=jax.ShapeDtypeStruct(whole_array.shape, whole_array.dtype),
+        input_output_aliases={count + 1: 0},
+        cost_estimate=pl.CostEstimate(flops=0, bytes_accessed=4 * 1024 * 1024, transcendentals=0),
+        name="put_rows",
+    )(places, *arrived, whole_array)
+
+
 def gathered_kernel(kernel):
     dp, row = lax.axis_index("dp"), lax.axis_index("row")
     dps, chans, rows = (lax.axis_size(a) for a in ("dp", "chan", "row"))
@@ -583,14 +621,15 @@
     (rest,) = correlate((6, 3), stacked, slope)
     rest = summed_over_images(rest)
     inner, outer = kernel.shape[1:]
-    kernel_grad = jnp.concatenate([kernel_grad_of(lead, inner, outer, True), kernel_grad_of(rest, inner, outer, False)])
+    kernel_grad = jnp.concatenate(
+        [kernel_grad_of(lead, inner, outer, False), kernel_grad_of(rest, inner, outer, False)]
+    )
+
+    places = jnp.stack([home(-j) for j in range(1, chans)]).astype(jnp.int32)
 
     def to_owners(blocks):
-        out = blocks[0]
-        for j in range(1, chans):
-            arrived = receive(blocks[j], "chan", chans - j).astype(out.dtype)
-            out = lax.dynamic_update_slice_in_dim(out, arrived, home(-j) * height, 0)
-        return out[None]
+        arrived = [receive(blocks[j], "chan", chans - j) for j in range(1, chans)]
+        return put(places, arrived, blocks[0])[None]
 
     return to_owners(activated), to_owners(input_grads), kernel_grad
 

time: 208 us -> 218 us (1.048)
  Pallas kernels: 44.5 us -> 55.2 us
  waiting for transfers between devices: 80 us -> 71.2 us
  starting transfers between devices: 61.7 us -> 70.1 us
    ppermute x36 -> x39, starting transfers between devices: 50.1 us -> 67.5 us  [receive(): lax.ppermute(block, axis, [(i, (i - ahead) % count) for i in range(count)])]
    pallas_call x0 -> x2, Pallas kernels: none -> 10.7 us  [put(): pl.pallas_call(functools.partial(put_body, count), grid_spec=pltpu.Prefet...]
    ppermute x2 -> x0, starting transfers between devices: 9.07 us -> none  [swapped(): lax.ppermute(block, axis, [(i, i ^ bit) for i in range(lax.axis_size(axis...]
    ppermute x2 -> x0, waiting for transfers between devices: 4.75 us -> none  [swapped(): lax.ppermute(block, axis, [(i, i ^ bit) for i in range(lax.axis_size(axis...]
    ppermute x36 -> x39, waiting for transfers between devices: 75.2 us -> 71.2 us  [receive(): lax.ppermute(block, axis, [(i, (i - ahead) % count) for i in range(count)])]
    dynamic_update_slice x3 -> x0, other arithmetic: 2.64 us -> none  [to_owners(): out = lax.dynamic_update_slice_in_dim(out, arrived, home(-j) * height, 0)]
    unnamed x34 -> x36, local copies, waits for them, and re-layouts: 3.21 us -> 5.59 us
    dynamic_update_slice x3 -> x0, local copies, waits for them, and re-layouts: 2.24 us -> none  [to_owners(): out = lax.dynamic_update_slice_in_dim(out, arrived, home(-j) * height, 0)]
  transfers between devices with their start and end apart: 40 -> 41, of which waited for: 17 -> 17; matrix products, arithmetic and copies ran while one was open for 8% -> 6% of each run, Pallas kernels for 21% -> 25%
where the time goes in v9:
time: 218 us; the launch traced here: 217 us
  waiting for transfers between devices  71.2 us (33%)
  starting transfers between devices  70.1 us (32%)
  Pallas kernels  55.2 us (25%)
  local copies, waits for them, and re-layouts  11.6 us (5%)
  other arithmetic  8.15 us (4%)
    ppermute x39, waiting for transfers between devices, receive(): lax.ppermute(block, axis, [(i, (i - ahead) % count) for i in range(count)])  71.2 us
    ppermute x39, starting transfers between devices, receive(): lax.ppermute(block, axis, [(i, (i - ahead) % count) for i in range(count)])  67.5 us
    pallas_call x2, Pallas kernels, correlate(): results = call(turn, stacked, *operands)  16.5 us
    pallas_call x1, Pallas kernels, forward(): results = call(turns, *pieces, *rims, *halves)  12.9 us
    pallas_call x2, Pallas kernels, put(): pl.pallas_call(functools.partial(put_body, count), grid_spec=pltpu.Prefet...  10.7 us
    pallas_call x1, Pallas kernels, backward(): pl.pallas_call(functools.partial(backward_body, count, lax.axis_size('row...  10.6 us
    unnamed x36, local copies, waits for them, and re-layouts  5.59 us
    pallas_call x1, Pallas kernels, turned(): pl.pallas_call(functools.partial(turned_body, shares), grid=(blocks,), in...  4.47 us
  transfers between devices with their start and end apart: 41, of which 17 were waited for; matrix products, arithmetic and copies ran while one was open for 6% of the time, Pallas kernels for 25%

profile of v9, /device:TPU:0, one launch (start us, length us, event | category | flops | bytes accessed | tf_op | source)
XLA Modules:
  0.0 217.3 jit_solution(2964330196347774616)
XLA Ops:
  0.7 0.9 copy-done
  1.8 3.1 %collective-permute-start.9 = (bf16[40,720]{1,0:T(8,128)(2,1)S(1)}, bf16[40,720]{1,0:T(8,128)(2,1)S(1)}, u32[]{:S(2)}, u32[]{:S(2)}) collective-permute-start(bf16[40,720]{1,0:T(8,128)(2,1)S(1)} %copy.13), channel_id=1, source_target_pairs={{0,2},{2,4},{4,6},{6,0},{1,3},{3,5},{5,7},{7,1},{8,10},{10,12},{12... | collective-permute-start | bytes 172808 | tf_op jit(solution)/shard_map/ppermute | solution.py:16
  4.9 2.6 %collective-permute-start.8 = (bf16[40,720]{1,0:T(8,128)(2,1)S(1)}, bf16[40,720]{1,0:T(8,128)(2,1)S(1)}, u32[]{:S(2)}, u32[]{:S(2)}) collective-permute-start(bf16[40,720]{1,0:T(8,128)(2,1)S(1)} %copy.13), channel_id=1, source_target_pairs={{0,4},{2,6},{4,0},{6,2},{1,5},{3,7},{5,1},{7,3},{8,12},{10,14},{12... | collective-permute-start | bytes 172808 | tf_op jit(solution)/shard_map/ppermute | solution.py:16
  7.5 1.3 collective-permute-start.7
  9.3 2.5 %collective-permute-done.8 = bf16[40,720]{1,0:T(8,128)(2,1)S(1)} collective-permute-done((bf16[40,720]{1,0:T(8,128)(2,1)S(1)}, bf16[40,720]{1,0:T(8,128)(2,1)S(1)}, u32[]{:S(2)}, u32[]{:S(2)}) %collective-permute-start.8) | collective-permute-done | bytes 57632 | tf_op jit(solution)/shard_map/ppermute | solution.py:16
  12.1 1.5 collective-permute-start.12
  13.6 1.5 collective-permute-start.11
  15.1 1.4 collective-permute-start.10
  16.6 1.1 dynamic-slice_bitcast_fusion
  17.7 2.9 %collective-permute-start = (bf16[16,80,128]{2,1,0:T(8,128)(2,1)}, bf16[16,80,128]{2,1,0:T(8,128)(2,1)}, u32[]{:S(2)}, u32[]{:S(2)}) collective-permute-start(bf16[16,80,128]{2,1,0:T(8,128)(2,1)} %get-tuple-element.66), channel_id=1, source_target_pairs={{0,6},{2,0},{4,2},{6,4},{1,7},{3,1},{5,3},{7,5},{8,14},{10,8},{12,... | collective-permute-start | bytes 983048 | tf_op jit(solution)/shard_map/ppermute | solution.py:16
  21.2 0.7 collective-permute-done.12
  21.9 1.4 collective-permute-start.2
  23.3 2.0 collective-permute-done.11
  25.3 0.7 copy-done.9
  26.0 1.1 pad_maximum_fusion.refs_8_.refs_0_
  27.6 2.3 %dynamic-slice_bitcast_fusion.4 = (bf16[14,80,128]{2,1,0:T(8,128)(2,1)}, bf16[14,80,128]{2,1,0:T(8,128)(2,1)}, bf16[14,80,128]{2,1,0:T(8,128)(2,1)}, bf16[14,80,128]{2,1,0:T(8,128)(2,1)}) fusion(bf16[1,64,80,128]{3,2,1,0:T(8,128)(2,1)} %param.5, s32[]{:T(128)S(6)} %select_n.315, s32[]{:T(128)S(6)} %select_n.313, s32[]{:T(128)S(6)} %select_n.312, ...), kind=kLoop, calls=%fused_computation.18 | loop fusion | bytes 2293776 | tf_op jit(solution)/shard_map/dynamic_slice | solution.py:594
  29.9 1.5 dynamic-slice_bitcast_fusion.9
  32.0 0.7 bitcast_select_fusion.1
  32.7 0.8 pad_maximum_fusion.4
  33.5 2.2 %collective-permute-start.4 = (bf16[4,80,128]{2,1,0:T(8,128)(2,1)S(1)}, bf16[4,80,128]{2,1,0:T(8,128)(2,1)S(1)}, u32[]{:S(2)}, u32[]{:S(2)}) collective-permute-start(bf16[4,80,128]{2,1,0:T(8,128)(2,1)S(1)} %pad_maximum_fusion.4), channel_id=1, source_target_pairs={{0,6},{2,0},{4,2},{6,4},{1,7},{3,1},{5,3},{7,5},{8,14},{10,8},{12,... | collective-permute-start | bytes 245768 | tf_op jit(solution)/shard_map/ppermute | solution.py:16
  35.7 0.8 pad_maximum_fusion.5
  36.5 10.2 %collective-permute-done.4.refs_5_.refs_6_ = bf16[4,80,128]{2,1,0:T(8,128)(2,1)S(1)} collective-permute-done((bf16[4,80,128]{2,1,0:T(8,128)(2,1)S(1)}, bf16[4,80,128]{2,1,0:T(8,128)(2,1)S(1)}, u32[]{:S(2)}, u32[]{:S(2)}) %collective-permute-start.4) | collective-permute-done | bytes 81952 | tf_op jit(solution)/shard_map/ppermute | solution.py:16
  46.6 2.9 %collective-permute-start.5 = (bf16[4,80,128]{2,1,0:T(8,128)(2,1)S(1)}, bf16[4,80,128]{2,1,0:T(8,128)(2,1)S(1)}, u32[]{:S(2)}, u32[]{:S(2)}) collective-permute-start(bf16[4,80,128]{2,1,0:T(8,128)(2,1)S(1)} %pad_maximum_fusion.5), channel_id=1, source_target_pairs={{0,4},{2,6},{4,0},{6,2},{1,5},{3,7},{5,1},{7,3},{8,12},{10,14},{12... | collective-permute-start | bytes 245768 | tf_op jit(solution)/shard_map/ppermute | solution.py:16
  49.6 3.3 %collective-permute-done.5.refs_6_.refs_7_ = bf16[4,80,128]{2,1,0:T(8,128)(2,1)S(1)} collective-permute-done((bf16[4,80,128]{2,1,0:T(8,128)(2,1)S(1)}, bf16[4,80,128]{2,1,0:T(8,128)(2,1)S(1)}, u32[]{:S(2)}, u32[]{:S(2)}) %collective-permute-start.5) | collective-permute-done | bytes 81952 | tf_op jit(solution)/shard_map/ppermute | solution.py:16
  52.9 3.0 %collective-permute-start.6 = (bf16[4,80,128]{2,1,0:T(8,128)(2,1)S(1)}, bf16[4,80,128]{2,1,0:T(8,128)(2,1)S(1)}, u32[]{:S(2)}, u32[]{:S(2)}) collective-permute-start(bf16[4,80,128]{2,1,0:T(8,128)(2,1)S(1)} %pad_maximum_fusion.6), channel_id=1, source_target_pairs={{0,2},{2,4},{4,6},{6,0},{1,3},{3,5},{5,7},{7,1},{8,10},{10,12},{12... | collective-permute-start | bytes 245768 | tf_op jit(solution)/shard_map/ppermute | solution.py:16
  56.6 3.4 %collective-permute-done.6.refs_7_.refs_8_ = bf16[4,80,128]{2,1,0:T(8,128)(2,1)S(1)} collective-permute-done((bf16[4,80,128]{2,1,0:T(8,128)(2,1)S(1)}, bf16[4,80,128]{2,1,0:T(8,128)(2,1)S(1)}, u32[]{:S(2)}, u32[]{:S(2)}) %collective-permute-start.6) | collective-permute-done | bytes 81952 | tf_op jit(solution)/shard_map/ppermute | solution.py:16
  60.0 1.0 collective-permute-start.17
  61.0 1.5 collective-permute-start.18
  62.6 1.0 copy-done.4
  63.5 12.9 %conv_forward.1 = (bf16[64,80,128]{2,1,0:T(8,128)(2,1)}, bf16[16,80,128]{2,1,0:T(8,128)(2,1)}, bf16[16,80,128]{2,1,0:T(8,128)(2,1)}, bf16[16,80,128]{2,1,0:T(8,1...) custom-call(s32[5]{0:T(128)} %stack.68.turns, ...), custom_call_target="tpu_custom_call" | custom-call | flops 3774873600 | bytes 16777216 | tf_op jit(solution)/shard_map/conv_forward/pallas_call | solution.py:207
  76.5 2.1 collective-permute-start.14
  78.5 2.4 %collective-permute-start.15 = (bf16[16,80,128]{2,1,0:T(8,128)(2,1)}, bf16[16,80,128]{2,1,0:T(8,128)(2,1)S(1)}, u32[]{:S(2)}, u32[]{:S(2)}) collective-permute-start(bf16[16,80,128]{2,1,0:T(8,128)(2,1)} %get-tuple-element.23), channel_id=1, source_target_pairs={{0,4},{2,6},{4,0},{6,2},{1,5},{3,7},{5,1},{7,3},{8,12},{10,14},{12... | collective-permute-start | bytes 983048 | tf_op jit(solution)/shard_map/ppermute | solution.py:16
  80.9 1.0 collective-permute-start.16
  81.9 19.6 %collective-permute-done.18.refs_3_ = bf16[14,80,128]{2,1,0:T(8,128)(2,1)S(1)} collective-permute-done((bf16[14,80,128]{2,1,0:T(8,128)(2,1)}, bf16[14,80,128]{2,1,0:T(8,128)(2,1)S(1)}, u32[]{:S(2)}, u32[]{:S(2)}) %collective-permute-start.18) | collective-permute-done | bytes 286752 | tf_op jit(solution)/shard_map/ppermute | solution.py:16
  101.5 1.3 collective-permute-start.20
  102.8 1.3 collective-permute-start.21
  104.2 10.6 %shard_map.58 = (f32[4,6,40,320]{3,2,1,0:T(8,128)}, f32[4,6,40,320]{3,2,1,0:T(8,128)}, bf16[320,2048]{1,0:T(8,128)(2,1)}) custom-call(s32[1]{0:T(128)} %bitcast.4.turn, bf16[960,2304]{1,0:T(8,128)(2,1)} %get-tuple-element.26.stacked, f32[16,320,128]{2,1,0:T(8,128)} %get-tuple-element.27.refs_0_, bf16[14,80,128]{2,1,0:T(8,128)(2,1)} %get-tuple-element.54.refs_1_, ...), custom_call_target="tpu_custom_call" | custom-call | flops 2516582400 | bytes 8388608 | tf_op jit(solution)/shard_map/pallas_call | solution.py:302
  114.8 4.5 %turn_kernel.1.kernels = bf16[4,80,3456]{2,1,0:T(8,128)(2,1)} custom-call(bf16[4,160,720]{2,1,0:T(8,128)(2,1)} %copy-done.1, bf16[4,160,720]{2,1,0:T(8,128)(2,1)} %copy-done.4), custom_call_target="tpu_custom_call" | custom-call | flops 235929600 | bytes 4194304 | tf_op jit(solution)/shard_map/turn_kernel/pallas_call | solution.py:348
  120.0 10.6 %conv_backward.1 = (f32[64,80,128]{2,1,0:T(8,128)}, bf16[16,80,128]{2,1,0:T(8,128)(2,1)}, bf16[16,80,128]{2,1,0:T(8,128)(2,1)}, bf16[16,80,128]{2,1,0:T(8,128)(2,1)}) custom-call(s32[5]{0:T(128)} %stack.68.turns, bf16[320,2048]{1,0:T(8,128)(2,1)} %get-tuple-element.38.slope.refs_0_, bf16[1,320,128]{2,1,0:T(8,128)(2,1)} %copy-done.16, ...), custom_call_target="tpu_custom_call" | custom-call | flops 3774873600 | bytes 8388608 | tf_op jit(solution)/shard_map/conv_backward/pallas_call | solution.py:439
  130.6 5.9 %shard_map.59 = (f32[4,3,40,320]{3,2,1,0:T(8,128)}, f32[4,3,40,320]{3,2,1,0:T(8,128)}) custom-call(s32[1]{0:T(128)} %bitcast.4.turn, bf16[960,2304]{1,0:T(8,128)(2,1)} %get-tuple-element.26.stacked, bf16[320,2048]{1,0:T(8,128)(2,1)} %get-tuple-element.38.slope.refs_0_), custom_call_target="tpu_custom_call" | custom-call | flops 1258291200 | bytes 8388608 | tf_op jit(solution)/shard_map/pallas_call | solution.py:302
  137.0 2.6 %collective-permute-start.22 = (bf16[16,80,128]{2,1,0:T(8,128)(2,1)}, bf16[16,80,128]{2,1,0:T(8,128)(2,1)S(1)}, u32[]{:S(2)}, u32[]{:S(2)}) collective-permute-start(bf16[16,80,128]{2,1,0:T(8,128)(2,1)} %get-tuple-element.32), channel_id=1, source_target_pairs={{0,2},{2,4},{4,6},{6,0},{1,3},{3,5},{5,7},{7,1},{8,10},{10,12},{12... | collective-permute-start | bytes 983048 | tf_op jit(solution)/shard_map/ppermute | solution.py:16
  139.7 0.7 copy-done.8
  140.7 2.9 %collective-permute-start.24 = (bf16[16,80,128]{2,1,0:T(8,128)(2,1)}, bf16[16,80,128]{2,1,0:T(8,128)(2,1)}, u32[]{:S(2)}, u32[]{:S(2)}) collective-permute-start(bf16[16,80,128]{2,1,0:T(8,128)(2,1)} %get-tuple-element.34), channel_id=1, source_target_pairs={{0,6},{2,0},{4,2},{6,4},{1,7},{3,1},{5,3},{7,5},{8,14},{10,8},{12,... | collective-permute-start | bytes 983048 | tf_op jit(solution)/shard_map/ppermute | solution.py:16
  143.6 0.7 pad_add_fusion.places
  144.2 5.2 %put_rows.2 = bf16[64,80,128]{2,1,0:T(8,128)(2,1)} custom-call(s32[3]{0:T(128)} %pad_add_fusion.places, bf16[16,80,128]{2,1,0:T(8,128)(2,1)} %collective-permute-done.14.refs_0_, bf16[16,80,128]{2,1,0:T(8,128)(2,1)} %copy-done.8, bf16[16,80,128]{2,1,0:T(8,128)(2,1)} %collective-permute-done.16.refs_2_, ...), custom_call_target="tpu_custom_call", output_to_operand_aliasing={{}: (4, {})} | custom-call | bytes 4194304 | tf_op jit(solution)/shard_map/put_rows/pallas_call | solution.py:489
  149.7 13.1 %collective-permute-done.23.refs_1_ = bf16[16,80,128]{2,1,0:T(8,128)(2,1)S(1)} collective-permute-done((bf16[16,80,128]{2,1,0:T(8,128)(2,1)}, bf16[16,80,128]{2,1,0:T(8,128)(2,1)S(1)}, u32[]{:S(2)}, u32[]{:S(2)}) %collective-permute-start.23) | collective-permute-done | bytes 327712 | tf_op jit(solution)/shard_map/ppermute | solution.py:16
  162.9 0.7 copy-done.7
  163.6 5.5 %put_rows.3 = f32[64,80,128]{2,1,0:T(8,128)} custom-call(s32[3]{0:T(128)} %pad_add_fusion.places, bf16[16,80,128]{2,1,0:T(8,128)(2,1)} %copy-done.6, bf16[16,80,128]{2,1,0:T(8,128)(2,1)} %copy-done.7, bf16[16,80,128]{2,1,0:T(8,128)(2,1)} %collective-permute-done.24.refs_2_, f32[64,80,128]{2,1,0:T(8,128)} %get-tuple-element.35.refs_3_), custom_call_target="tpu_custom_call", output_to_operand_aliasing={{}: (4, {})} | custom-call | bytes 4194304 | tf_op jit(solution)/shard_map/put_rows/pallas_call | solution.py:489
  169.1 0.9 copy-done.5
  170.0 1.5 add.277
  172.7 2.6 %collective-permute-start.34 = (f32[3,40,320]{2,1,0:T(8,128)S(1)}, f32[3,40,320]{2,1,0:T(8,128)S(1)}, u32[]{:S(2)}, u32[]{:S(2)}) collective-permute-start(f32[3,40,320]{2,1,0:T(8,128)S(1)} %get-tuple-element.68), channel_id=1, source_target_pairs={{0,24},{8,0},{16,8},{24,16},{1,25},{9,1},{17,9},{25,17},{2,26},{10... | collective-permute-start | bytes 460808 | tf_op jit(solution)/shard_map/ppermute | solution.py:16
  175.7 1.3 collective-permute-start.27
  177.0 3.0 %collective-permute-done.36 = f32[3,40,320]{2,1,0:T(8,128)S(1)} collective-permute-done((f32[3,40,320]{2,1,0:T(8,128)S(1)}, f32[3,40,320]{2,1,0:T(8,128)S(1)}, u32[]{:S(2)}, u32[]{:S(2)}) %collective-permute-start.36) | collective-permute-done | bytes 153632 | tf_op jit(solution)/shard_map/ppermute | solution.py:16
  180.0 4.0 %collective-permute-done.35 = f32[3,40,320]{2,1,0:T(8,128)S(1)} collective-permute-done((f32[3,40,320]{2,1,0:T(8,128)S(1)}, f32[3,40,320]{2,1,0:T(8,128)S(1)}, u32[]{:S(2)}, u32[]{:S(2)}) %collective-permute-start.35) | collective-permute-done | bytes 153632 | tf_op jit(solution)/shard_map/ppermute | solution.py:16
  184.2 6.9 %collective-permute-start.39 = (f32[80,120]{0,1:T(8,128)S(1)}, f32[80,120]{0,1:T(8,128)S(1)}, u32[]{:S(2)}, u32[]{:S(2)}) collective-permute-start(f32[80,120]{0,1:T(8,128)S(1)} %bitcast.152), channel_id=1, source_target_pairs={{0,2},{2,4},{4,6},{6,0},{1,3},{3,5},{5,7},{7,1},{8,10},{10,12},{12... | collective-permute-start | bytes 115208 | tf_op jit(solution)/shard_map/ppermute | solution.py:16
  191.1 2.6 %collective-permute-start.38 = (f32[80,120]{0,1:T(8,128)S(1)}, f32[80,120]{0,1:T(8,128)S(1)}, u32[]{:S(2)}, u32[]{:S(2)}) collective-permute-start(f32[80,120]{0,1:T(8,128)S(1)} %bitcast.151), channel_id=1, source_target_pairs={{0,4},{2,6},{4,0},{6,2},{1,5},{3,7},{5,1},{7,3},{8,12},{10,14},{12... | collective-permute-start | bytes 115208 | tf_op jit(solution)/shard_map/ppermute | solution.py:16
  193.7 7.1 %collective-permute-start.37 = (f32[80,120]{0,1:T(8,128)S(1)}, f32[80,120]{0,1:T(8,128)S(1)}, u32[]{:S(2)}, u32[]{:S(2)}) collective-permute-start(f32[80,120]{0,1:T(8,128)S(1)} %bitcast.150), channel_id=1, source_target_pairs={{0,6},{2,0},{4,2},{6,4},{1,7},{3,1},{5,3},{7,5},{8,14},{10,8},{12,... | collective-permute-start | bytes 115208 | tf_op jit(solution)/shard_map/ppermute | solution.py:16
  201.1 4.3 %collective-permute-start.31 = (f32[80,240]{0,1:T(8,128)S(1)}, f32[80,240]{0,1:T(8,128)S(1)}, u32[]{:S(2)}, u32[]{:S(2)}) collective-permute-start(f32[80,240]{0,1:T(8,128)S(1)} %bitcast.148), channel_id=1, source_target_pairs={{0,2},{2,4},{4,6},{6,0},{1,3},{3,5},{5,7},{7,1},{8,10},{10,12},{12... | collective-permute-start | bytes 230408 | tf_op jit(solution)/shard_map/ppermute | solution.py:16
  205.4 1.8 collective-permute-start.30
  207.2 0.7 collective-permute-start.29
  207.9 2.9 %collective-permute-done.31 = f32[80,240]{0,1:T(8,128)S(1)} collective-permute-done((f32[80,240]{0,1:T(8,128)S(1)}, f32[80,240]{0,1:T(8,128)S(1)}, u32[]{:S(2)}, u32[]{:S(2)}) %collective-permute-start.31) | collective-permute-done | bytes 76832 | tf_op jit(solution)/shard_map/ppermute | solution.py:16
  210.9 4.0 %collective-permute-done.30 = f32[80,240]{0,1:T(8,128)S(1)} collective-permute-done((f32[80,240]{0,1:T(8,128)S(1)}, f32[80,240]{0,1:T(8,128)S(1)}, u32[]{:S(2)}, u32[]{:S(2)}) %collective-permute-start.30) | collective-permute-done | bytes 76832 | tf_op jit(solution)/shard_map/ppermute | solution.py:16
  215.2 1.2 collective-permute-done.32
  216.5 0.8 pad_maximum_fusion.1
  (91 shorter events, 7.7 us)
Async XLA Ops:
  0.6 0.9 copy-start
  0.6 15.9 %copy-start.2 = (bf16[1,64,80,128]{3,2,1,0:T(8,128)(2,1)S(1)}, bf16[1,64,80,128]{3,2,1,0:T(8,128)(2,1)}, u32[]{:S(2)}) copy-start(bf16[1,64,80,128]{3,2,1,0:T(8,128)(2,1)} %param.3) | copy-start | bytes 3932164
  1.8 7.5 %collective-permute-start.9 = (bf16[40,720]{1,0:T(8,128)(2,1)S(1)}, bf16[40,720]{1,0:T(8,128)(2,1)S(1)}, u32[]{:S(2)}, u32[]{:S(2)}) collective-permute-start(bf16[40,720]{1,0:T(8,128)(2,1)S(1)} %copy.13), channel_id=1, source_target_pairs={{0,2},{2,4},{4,6},{6,0},{1,3},{3,5},{5,7},{7,1},{8,10},{10,12},{12... | collective-permute-start | bytes 172808 | tf_op jit(solution)/shard_map/ppermute | solution.py:16
  4.9 6.9 %collective-permute-start.8 = (bf16[40,720]{1,0:T(8,128)(2,1)S(1)}, bf16[40,720]{1,0:T(8,128)(2,1)S(1)}, u32[]{:S(2)}, u32[]{:S(2)}) collective-permute-start(bf16[40,720]{1,0:T(8,128)(2,1)S(1)} %copy.13), channel_id=1, source_target_pairs={{0,4},{2,6},{4,0},{6,2},{1,5},{3,7},{5,1},{7,3},{8,12},{10,14},{12... | collective-permute-start | bytes 172808 | tf_op jit(solution)/shard_map/ppermute | solution.py:16
  7.5 4.6 %collective-permute-start.7 = (bf16[40,720]{1,0:T(8,128)(2,1)S(1)}, bf16[40,720]{1,0:T(8,128)(2,1)S(1)}, u32[]{:S(2)}, u32[]{:S(2)}) collective-permute-start(bf16[40,720]{1,0:T(8,128)(2,1)S(1)} %copy.13), channel_id=1, source_target_pairs={{0,6},{2,0},{4,2},{6,4},{1,7},{3,1},{5,3},{7,5},{8,14},{10,8},{12,... | collective-permute-start | bytes 172808 | tf_op jit(solution)/shard_map/ppermute | solution.py:16
  12.1 9.8 %collective-permute-start.12 = (bf16[160,720]{1,0:T(8,128)(2,1)S(1)}, bf16[160,720]{1,0:T(8,128)(2,1)S(1)}, u32[]{:S(2)}, u32[]{:S(2)}) collective-permute-start(bf16[160,720]{1,0:T(8,128)(2,1)S(1)} %get-tuple-element.76), channel_id=1, source_target_pairs={{0,8},{8,16},{16,24},{24,0},{1,9},{9,17},{17,25},{25,1},{2,10},{10... | collective-permute-start | bytes 691208 | tf_op jit(solution)/shard_map/ppermute | solution.py:16
  13.6 11.6 %collective-permute-start.11 = (bf16[160,720]{1,0:T(8,128)(2,1)S(1)}, bf16[160,720]{1,0:T(8,128)(2,1)S(1)}, u32[]{:S(2)}, u32[]{:S(2)}) collective-permute-start(bf16[160,720]{1,0:T(8,128)(2,1)S(1)} %get-tuple-element.76), channel_id=1, source_target_pairs={{0,16},{8,24},{16,0},{24,8},{1,17},{9,25},{17,1},{25,9},{2,18},{10... | collective-permute-start | bytes 691208 | tf_op jit(solution)/shard_map/ppermute | solution.py:16
  15.1 10.1 %collective-permute-start.10 = (bf16[160,720]{1,0:T(8,128)(2,1)S(1)}, bf16[160,720]{1,0:T(8,128)(2,1)S(1)}, u32[]{:S(2)}, u32[]{:S(2)}) collective-permute-start(bf16[160,720]{1,0:T(8,128)(2,1)S(1)} %get-tuple-element.76), channel_id=1, source_target_pairs={{0,24},{8,0},{16,8},{24,16},{1,25},{9,1},{17,9},{25,17},{2,26},{10... | collective-permute-start | bytes 691208 | tf_op jit(solution)/shard_map/ppermute | solution.py:16
  17.7 43.4 %collective-permute-start = (bf16[16,80,128]{2,1,0:T(8,128)(2,1)}, bf16[16,80,128]{2,1,0:T(8,128)(2,1)}, u32[]{:S(2)}, u32[]{:S(2)}) collective-permute-start(bf16[16,80,128]{2,1,0:T(8,128)(2,1)} %get-tuple-element.66), channel_id=1, source_target_pairs={{0,6},{2,0},{4,2},{6,4},{1,7},{3,1},{5,3},{7,5},{8,14},{10,8},{12,... | collective-permute-start | bytes 983048 | tf_op jit(solution)/shard_map/ppermute | solution.py:16
  20.6 41.9 %collective-permute-start.1 = (bf16[16,80,128]{2,1,0:T(8,128)(2,1)}, bf16[16,80,128]{2,1,0:T(8,128)(2,1)}, u32[]{:S(2)}, u32[]{:S(2)}) collective-permute-start(bf16[16,80,128]{2,1,0:T(8,128)(2,1)} %get-tuple-element.65), channel_id=1, source_target_pairs={{0,4},{2,6},{4,0},{6,2},{1,5},{3,7},{5,1},{7,3},{8,12},{10,14},{12... | collective-permute-start | bytes 983048 | tf_op jit(solution)/shard_map/ppermute | solution.py:16
  21.9 40.6 %collective-permute-start.2 = (bf16[16,80,128]{2,1,0:T(8,128)(2,1)}, bf16[16,80,128]{2,1,0:T(8,128)(2,1)}, u32[]{:S(2)}, u32[]{:S(2)}) collective-permute-start(bf16[16,80,128]{2,1,0:T(8,128)(2,1)} %get-tuple-element.64), channel_id=1, source_target_pairs={{0,2},{2,4},{4,6},{6,0},{1,3},{3,5},{5,7},{7,1},{8,10},{10,12},{12... | collective-permute-start | bytes 983048 | tf_op jit(solution)/shard_map/ppermute | solution.py:16
  25.3 6.7 %collective-permute-start.3 = (bf16[1,80,128]{2,1,0:T(8,128)(2,1)}, bf16[1,80,128]{2,1,0:T(8,128)(2,1)}, u32[]{:S(2)}, u32[]{:S(2)}) collective-permute-start(bf16[1,80,128]{2,1,0:T(8,128)(2,1)} %select_bitcast_fusion), channel_id=1, source_target_pairs={{0,1},{1,0},{2,3},{3,2},{4,5},{5,4},{6,7},{7,6},{8,9},{9,8},{10,11... | collective-permute-start | bytes 61448 | tf_op jit(solution)/shard_map/ppermute | solution.py:16
  25.3 0.7 copy-start.9
  27.1 5.7 %copy-start.1 = (bf16[4,160,720]{2,1,0:T(8,128)(2,1)}, bf16[4,160,720]{2,1,0:T(8,128)(2,1)S(1)}, u32[]{:S(2)}) copy-start(bf16[4,160,720]{2,1,0:T(8,128)(2,1)S(1)} %pad_maximum_fusion.refs_8_.refs_0_) | copy-start | bytes 2764804
  27.1 35.4 %collective-permute-start.13 = (bf16[4,160,720]{2,1,0:T(8,128)(2,1)S(1)}, bf16[4,160,720]{2,1,0:T(8,128)(2,1)S(1)}, u32[]{:S(2)}, u32[]{:S(2)}) collective-permute-start(bf16[4,160,720]{2,1,0:T(8,128)(2,1)S(1)} %pad_maximum_fusion.refs_8_.refs_0_), channel_id=1, source_target_pairs={{0,1},{1,0},{2,3},{3,2},{4,5},{5,4},{6,7},{7,6},{8,9},{9,8},{10,11... | collective-permute-start | bytes 2764808 | tf_op jit(solution)/shard_map/ppermute | solution.py:16
  33.5 13.1 %collective-permute-start.4 = (bf16[4,80,128]{2,1,0:T(8,128)(2,1)S(1)}, bf16[4,80,128]{2,1,0:T(8,128)(2,1)S(1)}, u32[]{:S(2)}, u32[]{:S(2)}) collective-permute-start(bf16[4,80,128]{2,1,0:T(8,128)(2,1)S(1)} %pad_maximum_fusion.4), channel_id=1, source_target_pairs={{0,6},{2,0},{4,2},{6,4},{1,7},{3,1},{5,3},{7,5},{8,14},{10,8},{12,... | collective-permute-start | bytes 245768 | tf_op jit(solution)/shard_map/ppermute | solution.py:16
  46.6 15.9 %copy-start.13 = (bf16[4,80,128]{2,1,0:T(8,128)(2,1)}, bf16[4,80,128]{2,1,0:T(8,128)(2,1)S(1)}, u32[]{:S(2)}) copy-start(bf16[4,80,128]{2,1,0:T(8,128)(2,1)S(1)} %collective-permute-done.4.refs_5_.refs_6_) | copy-start | bytes 245764
  46.6 6.3 %collective-permute-start.5 = (bf16[4,80,128]{2,1,0:T(8,128)(2,1)S(1)}, bf16[4,80,128]{2,1,0:T(8,128)(2,1)S(1)}, u32[]{:S(2)}, u32[]{:S(2)}) collective-permute-start(bf16[4,80,128]{2,1,0:T(8,128)(2,1)S(1)} %pad_maximum_fusion.5), channel_id=1, source_target_pairs={{0,4},{2,6},{4,0},{6,2},{1,5},{3,7},{5,1},{7,3},{8,12},{10,14},{12... | collective-permute-start | bytes 245768 | tf_op jit(solution)/shard_map/ppermute | solution.py:16
  52.9 9.6 %copy-start.14 = (bf16[4,80,128]{2,1,0:T(8,128)(2,1)}, bf16[4,80,128]{2,1,0:T(8,128)(2,1)S(1)}, u32[]{:S(2)}) copy-start(bf16[4,80,128]{2,1,0:T(8,128)(2,1)S(1)} %collective-permute-done.5.refs_6_.refs_7_) | copy-start | bytes 245764
  52.9 7.1 %collective-permute-start.6 = (bf16[4,80,128]{2,1,0:T(8,128)(2,1)S(1)}, bf16[4,80,128]{2,1,0:T(8,128)(2,1)S(1)}, u32[]{:S(2)}, u32[]{:S(2)}) collective-permute-start(bf16[4,80,128]{2,1,0:T(8,128)(2,1)S(1)} %pad_maximum_fusion.6), channel_id=1, source_target_pairs={{0,2},{2,4},{4,6},{6,0},{1,3},{3,5},{5,7},{7,1},{8,10},{10,12},{12... | collective-permute-start | bytes 245768 | tf_op jit(solution)/shard_map/ppermute | solution.py:16
  60.0 2.5 %copy-start.15 = (bf16[4,80,128]{2,1,0:T(8,128)(2,1)}, bf16[4,80,128]{2,1,0:T(8,128)(2,1)S(1)}, u32[]{:S(2)}) copy-start(bf16[4,80,128]{2,1,0:T(8,128)(2,1)S(1)} %collective-permute-done.6.refs_7_.refs_8_) | copy-start | bytes 245764
  60.0 20.9 %collective-permute-start.17 = (bf16[14,80,128]{2,1,0:T(8,128)(2,1)}, bf16[14,80,128]{2,1,0:T(8,128)(2,1)S(1)}, u32[]{:S(2)}, u32[]{:S(2)}) collective-permute-start(bf16[14,80,128]{2,1,0:T(8,128)(2,1)} %get-tuple-element.53), channel_id=1, source_target_pairs={{0,6},{2,0},{4,2},{6,4},{1,7},{3,1},{5,3},{7,5},{8,14},{10,8},{12,... | collective-permute-start | bytes 860168 | tf_op jit(solution)/shard_map/ppermute | solution.py:16
  61.0 40.5 %collective-permute-start.18 = (bf16[14,80,128]{2,1,0:T(8,128)(2,1)}, bf16[14,80,128]{2,1,0:T(8,128)(2,1)S(1)}, u32[]{:S(2)}, u32[]{:S(2)}) collective-permute-start(bf16[14,80,128]{2,1,0:T(8,128)(2,1)} %get-tuple-element.55), channel_id=1, source_target_pairs={{0,4},{2,6},{4,0},{6,2},{1,5},{3,7},{5,1},{7,3},{8,12},{10,14},{12... | collective-permute-start | bytes 860168 | tf_op jit(solution)/shard_map/ppermute | solution.py:16
  62.5 40.3 %collective-permute-start.19 = (bf16[14,80,128]{2,1,0:T(8,128)(2,1)}, bf16[14,80,128]{2,1,0:T(8,128)(2,1)S(1)}, u32[]{:S(2)}, u32[]{:S(2)}) collective-permute-start(bf16[14,80,128]{2,1,0:T(8,128)(2,1)} %get-tuple-element.52), channel_id=1, source_target_pairs={{0,2},{2,4},{4,6},{6,0},{1,3},{3,5},{5,7},{7,1},{8,10},{10,12},{12... | collective-permute-start | bytes 860168 | tf_op jit(solution)/shard_map/ppermute | solution.py:16
  62.5 1.0 copy-start.4
  76.5 60.5 %collective-permute-start.14 = (bf16[16,80,128]{2,1,0:T(8,128)(2,1)}, bf16[16,80,128]{2,1,0:T(8,128)(2,1)}, u32[]{:S(2)}, u32[]{:S(2)}) collective-permute-start(bf16[16,80,128]{2,1,0:T(8,128)(2,1)} %get-tuple-element.22), channel_id=1, source_target_pairs={{0,2},{2,4},{4,6},{6,0},{1,3},{3,5},{5,7},{7,1},{8,10},{10,12},{12... | collective-permute-start | bytes 983048 | tf_op jit(solution)/shard_map/ppermute | solution.py:16
  78.5 61.1 %collective-permute-start.15 = (bf16[16,80,128]{2,1,0:T(8,128)(2,1)}, bf16[16,80,128]{2,1,0:T(8,128)(2,1)S(1)}, u32[]{:S(2)}, u32[]{:S(2)}) collective-permute-start(bf16[16,80,128]{2,1,0:T(8,128)(2,1)} %get-tuple-element.23), channel_id=1, source_target_pairs={{0,4},{2,6},{4,0},{6,2},{1,5},{3,7},{5,1},{7,3},{8,12},{10,14},{12... | collective-permute-start | bytes 983048 | tf_op jit(solution)/shard_map/ppermute | solution.py:16
  80.9 23.2 %copy-start.10 = (bf16[14,80,128]{2,1,0:T(8,128)(2,1)}, bf16[14,80,128]{2,1,0:T(8,128)(2,1)S(1)}, u32[]{:S(2)}) copy-start(bf16[14,80,128]{2,1,0:T(8,128)(2,1)S(1)} %collective-permute-done.17.refs_2_) | copy-start | bytes 860164
  80.9 59.8 %collective-permute-start.16 = (bf16[16,80,128]{2,1,0:T(8,128)(2,1)}, bf16[16,80,128]{2,1,0:T(8,128)(2,1)}, u32[]{:S(2)}, u32[]{:S(2)}) collective-permute-start(bf16[16,80,128]{2,1,0:T(8,128)(2,1)} %get-tuple-element.24), channel_id=1, source_target_pairs={{0,6},{2,0},{4,2},{6,4},{1,7},{3,1},{5,3},{7,5},{8,14},{10,8},{12,... | collective-permute-start | bytes 983048 | tf_op jit(solution)/shard_map/ppermute | solution.py:16
  101.5 2.6 %copy-start.11 = (bf16[14,80,128]{2,1,0:T(8,128)(2,1)}, bf16[14,80,128]{2,1,0:T(8,128)(2,1)S(1)}, u32[]{:S(2)}) copy-start(bf16[14,80,128]{2,1,0:T(8,128)(2,1)S(1)} %collective-permute-done.18.refs_3_) | copy-start | bytes 860164
  101.5 17.8 %collective-permute-start.20 = (bf16[1,320,128]{2,1,0:T(8,128)(2,1)}, bf16[1,320,128]{2,1,0:T(8,128)(2,1)S(1)}, u32[]{:S(2)}, u32[]{:S(2)}) collective-permute-start(bf16[1,320,128]{2,1,0:T(8,128)(2,1)} %get-tuple-element.29), channel_id=1, source_target_pairs={{0,2},{2,4},{4,6},{6,7},{7,5},{5,3},{3,1},{8,10},{10,12},{12,14},{... | collective-permute-start | bytes 245768 | tf_op jit(solution)/shard_map/ppermute | solution.py:614
  102.8 1.3 copy-start.12
  102.8 16.5 %collective-permute-start.21 = (bf16[1,320,128]{2,1,0:T(8,128)(2,1)}, bf16[1,320,128]{2,1,0:T(8,128)(2,1)S(1)}, u32[]{:S(2)}, u32[]{:S(2)}) collective-permute-start(bf16[1,320,128]{2,1,0:T(8,128)(2,1)} %get-tuple-element.30), channel_id=1, source_target_pairs={{2,0},{4,2},{6,4},{7,6},{5,7},{3,5},{1,3},{10,8},{12,10},{14,12},{... | collective-permute-start | bytes 245768 | tf_op jit(solution)/shard_map/ppermute | solution.py:615
  119.3 0.6 copy-start.16
  119.3 56.0 %collective-permute-start.25 = (f32[4,6,40,320]{3,2,1,0:T(8,128)}, f32[4,6,40,320]{3,2,1,0:T(8,128)S(1)}, u32[]{:S(2)}, u32[]{:S(2)}) collective-permute-start(f32[4,6,40,320]{3,2,1,0:T(8,128)} %get-tuple-element.37), channel_id=1, source_target_pairs={{0,1},{1,0},{2,3},{3,2},{4,5},{5,4},{6,7},{7,6},{8,9},{9,8},{10,11... | collective-permute-start | bytes 3686408 | tf_op jit(solution)/shard_map/ppermute | solution.py:16
  119.4 0.6 copy-start.17
  136.5 32.6 %collective-permute-start.33 = (f32[4,3,40,320]{3,2,1,0:T(8,128)}, f32[4,3,40,320]{3,2,1,0:T(8,128)S(1)}, u32[]{:S(2)}, u32[]{:S(2)}) collective-permute-start(f32[4,3,40,320]{3,2,1,0:T(8,128)} %get-tuple-element.40), channel_id=1, source_target_pairs={{0,1},{1,0},{2,3},{3,2},{4,5},{5,4},{6,7},{7,6},{8,9},{9,8},{10,11... | collective-permute-start | bytes 1843208 | tf_op jit(solution)/shard_map/ppermute | solution.py:16
  137.0 12.7 %collective-permute-start.22 = (bf16[16,80,128]{2,1,0:T(8,128)(2,1)}, bf16[16,80,128]{2,1,0:T(8,128)(2,1)S(1)}, u32[]{:S(2)}, u32[]{:S(2)}) collective-permute-start(bf16[16,80,128]{2,1,0:T(8,128)(2,1)} %get-tuple-element.32), channel_id=1, source_target_pairs={{0,2},{2,4},{4,6},{6,0},{1,3},{3,5},{5,7},{7,1},{8,10},{10,12},{12... | collective-permute-start | bytes 983048 | tf_op jit(solution)/shard_map/ppermute | solution.py:16
  139.6 0.7 copy-start.8
  140.4 22.5 %collective-permute-start.23 = (bf16[16,80,128]{2,1,0:T(8,128)(2,1)}, bf16[16,80,128]{2,1,0:T(8,128)(2,1)S(1)}, u32[]{:S(2)}, u32[]{:S(2)}) collective-permute-start(bf16[16,80,128]{2,1,0:T(8,128)(2,1)} %get-tuple-element.33), channel_id=1, source_target_pairs={{0,4},{2,6},{4,0},{6,2},{1,5},{3,7},{5,1},{7,3},{8,12},{10,14},{12... | collective-permute-start | bytes 983048 | tf_op jit(solution)/shard_map/ppermute | solution.py:16
  140.7 22.2 %collective-permute-start.24 = (bf16[16,80,128]{2,1,0:T(8,128)(2,1)}, bf16[16,80,128]{2,1,0:T(8,128)(2,1)}, u32[]{:S(2)}, u32[]{:S(2)}) collective-permute-start(bf16[16,80,128]{2,1,0:T(8,128)(2,1)} %get-tuple-element.34), channel_id=1, source_target_pairs={{0,6},{2,0},{4,2},{6,4},{1,7},{3,1},{5,3},{7,5},{8,14},{10,8},{12,... | collective-permute-start | bytes 983048 | tf_op jit(solution)/shard_map/ppermute | solution.py:16
  149.7 13.1 %copy-start.6 = (bf16[16,80,128]{2,1,0:T(8,128)(2,1)}, bf16[16,80,128]{2,1,0:T(8,128)(2,1)S(1)}, u32[]{:S(2)}) copy-start(bf16[16,80,128]{2,1,0:T(8,128)(2,1)S(1)} %collective-permute-done.22.refs_0_) | copy-start | bytes 983044
  162.9 0.8 copy-start.7
  169.1 0.9 copy-start.5
  170.0 5.4 %copy-start.3 = (f32[4,6,40,320]{3,2,1,0:T(8,128)S(1)}, f32[4,6,40,320]{3,2,1,0:T(8,128)}, u32[]{:S(2)}) copy-start(f32[4,6,40,320]{3,2,1,0:T(8,128)} %get-tuple-element.36) | copy-start | bytes 3686404
  171.5 8.5 %collective-permute-start.36 = (f32[3,40,320]{2,1,0:T(8,128)S(1)}, f32[3,40,320]{2,1,0:T(8,128)S(1)}, u32[]{:S(2)}, u32[]{:S(2)}) collective-permute-start(f32[3,40,320]{2,1,0:T(8,128)S(1)} %get-tuple-element.69), channel_id=1, source_target_pairs={{0,8},{8,16},{16,24},{24,0},{1,9},{9,17},{17,25},{25,1},{2,10},{10... | collective-permute-start | bytes 460808 | tf_op jit(solution)/shard_map/ppermute | solution.py:16
  172.2 11.8 %collective-permute-start.35 = (f32[3,40,320]{2,1,0:T(8,128)S(1)}, f32[3,40,320]{2,1,0:T(8,128)S(1)}, u32[]{:S(2)}, u32[]{:S(2)}) collective-permute-start(f32[3,40,320]{2,1,0:T(8,128)S(1)} %get-tuple-element.70), channel_id=1, source_target_pairs={{0,16},{8,24},{16,0},{24,8},{1,17},{9,25},{17,1},{25,9},{2,18},{10... | collective-permute-start | bytes 460808 | tf_op jit(solution)/shard_map/ppermute | solution.py:16
  172.7 11.3 %collective-permute-start.34 = (f32[3,40,320]{2,1,0:T(8,128)S(1)}, f32[3,40,320]{2,1,0:T(8,128)S(1)}, u32[]{:S(2)}, u32[]{:S(2)}) collective-permute-start(f32[3,40,320]{2,1,0:T(8,128)S(1)} %get-tuple-element.68), channel_id=1, source_target_pairs={{0,24},{8,0},{16,8},{24,16},{1,25},{9,1},{17,9},{25,17},{2,26},{10... | collective-permute-start | bytes 460808 | tf_op jit(solution)/shard_map/ppermute | solution.py:16
  175.6 18.1 %collective-permute-start.28 = (f32[6,40,320]{2,1,0:T(8,128)S(1)}, f32[6,40,320]{2,1,0:T(8,128)S(1)}, u32[]{:S(2)}, u32[]{:S(2)}) collective-permute-start(f32[6,40,320]{2,1,0:T(8,128)S(1)} %get-tuple-element.42), channel_id=1, source_target_pairs={{0,8},{8,16},{16,24},{24,0},{1,9},{9,17},{17,25},{25,1},{2,10},{10... | collective-permute-start | bytes 921608 | tf_op jit(solution)/shard_map/ppermute | solution.py:16
  175.7 25.1 %collective-permute-start.27 = (f32[6,40,320]{2,1,0:T(8,128)S(1)}, f32[6,40,320]{2,1,0:T(8,128)S(1)}, u32[]{:S(2)}, u32[]{:S(2)}) collective-permute-start(f32[6,40,320]{2,1,0:T(8,128)S(1)} %get-tuple-element.43), channel_id=1, source_target_pairs={{0,16},{8,24},{16,0},{24,8},{1,17},{9,25},{17,1},{25,9},{2,18},{10... | collective-permute-start | bytes 921608 | tf_op jit(solution)/shard_map/ppermute | solution.py:16
  180.0 20.8 %collective-permute-start.26 = (f32[6,40,320]{2,1,0:T(8,128)S(1)}, f32[6,40,320]{2,1,0:T(8,128)S(1)}, u32[]{:S(2)}, u32[]{:S(2)}) collective-permute-start(f32[6,40,320]{2,1,0:T(8,128)S(1)} %get-tuple-element.41), channel_id=1, source_target_pairs={{0,24},{8,0},{16,8},{24,16},{1,25},{9,1},{17,9},{25,17},{2,26},{10... | collective-permute-start | bytes 921608 | tf_op jit(solution)/shard_map/ppermute | solution.py:16
  184.2 23.0 %collective-permute-start.39 = (f32[80,120]{0,1:T(8,128)S(1)}, f32[80,120]{0,1:T(8,128)S(1)}, u32[]{:S(2)}, u32[]{:S(2)}) collective-permute-start(f32[80,120]{0,1:T(8,128)S(1)} %bitcast.152), channel_id=1, source_target_pairs={{0,2},{2,4},{4,6},{6,0},{1,3},{3,5},{5,7},{7,1},{8,10},{10,12},{12... | collective-permute-start | bytes 115208 | tf_op jit(solution)/shard_map/ppermute | solution.py:16
  191.1 16.7 %collective-permute-start.38 = (f32[80,120]{0,1:T(8,128)S(1)}, f32[80,120]{0,1:T(8,128)S(1)}, u32[]{:S(2)}, u32[]{:S(2)}) collective-permute-start(f32[80,120]{0,1:T(8,128)S(1)} %bitcast.151), channel_id=1, source_target_pairs={{0,4},{2,6},{4,0},{6,2},{1,5},{3,7},{5,1},{7,3},{8,12},{10,14},{12... | collective-permute-start | bytes 115208 | tf_op jit(solution)/shard_map/ppermute | solution.py:16
  193.7 14.1 %collective-permute-start.37 = (f32[80,120]{0,1:T(8,128)S(1)}, f32[80,120]{0,1:T(8,128)S(1)}, u32[]{:S(2)}, u32[]{:S(2)}) collective-permute-start(f32[80,120]{0,1:T(8,128)S(1)} %bitcast.150), channel_id=1, source_target_pairs={{0,6},{2,0},{4,2},{6,4},{1,7},{3,1},{5,3},{7,5},{8,14},{10,8},{12,... | collective-permute-start | bytes 115208 | tf_op jit(solution)/shard_map/ppermute | solution.py:16
  201.1 9.8 %collective-permute-start.31 = (f32[80,240]{0,1:T(8,128)S(1)}, f32[80,240]{0,1:T(8,128)S(1)}, u32[]{:S(2)}, u32[]{:S(2)}) collective-permute-start(f32[80,240]{0,1:T(8,128)S(1)} %bitcast.148), channel_id=1, source_target_pairs={{0,2},{2,4},{4,6},{6,0},{1,3},{3,5},{5,7},{7,1},{8,10},{10,12},{12... | collective-permute-start | bytes 230408 | tf_op jit(solution)/shard_map/ppermute | solution.py:16
  205.4 9.5 %collective-permute-start.30 = (f32[80,240]{0,1:T(8,128)S(1)}, f32[80,240]{0,1:T(8,128)S(1)}, u32[]{:S(2)}, u32[]{:S(2)}) collective-permute-start(f32[80,240]{0,1:T(8,128)S(1)} %bitcast.147), channel_id=1, source_target_pairs={{0,4},{2,6},{4,0},{6,2},{1,5},{3,7},{5,1},{7,3},{8,12},{10,14},{12... | collective-permute-start | bytes 230408 | tf_op jit(solution)/shard_map/ppermute | solution.py:16
  207.2 7.8 %collective-permute-start.29 = (f32[80,240]{0,1:T(8,128)S(1)}, f32[80,240]{0,1:T(8,128)S(1)}, u32[]{:S(2)}, u32[]{:S(2)}) collective-permute-start(f32[80,240]{0,1:T(8,128)S(1)} %bitcast.146), channel_id=1, source_target_pairs={{0,6},{2,0},{4,2},{6,4},{1,7},{3,1},{5,3},{7,5},{8,14},{10,8},{12,... | collective-permute-start | bytes 230408 | tf_op jit(solution)/shard_map/ppermute | solution.py:16
  207.9 7.2 %collective-permute-start.40 = (f32[80,120]{0,1:T(8,128)S(1)}, f32[80,120]{0,1:T(8,128)S(1)}, u32[]{:S(2)}, u32[]{:S(2)}) collective-permute-start(f32[80,120]{0,1:T(8,128)S(1)} %fusion.17), channel_id=1, source_target_pairs={{0,1},{1,0},{2,3},{3,2},{4,5},{5,4},{6,7},{7,6},{8,9},{9,8},{10,11... | collective-permute-start | bytes 115208 | tf_op jit(solution)/shard_map/ppermute | solution.py:16
  215.0 1.4 collective-permute-start.32

commit v10 on v9

--- a/solution.py
+++ b/solution.py
@@ -466,38 +466,42 @@
 
 
 def put_body(count, places, *refs):
-    out = refs[count + 1]
+    arrived, out = refs[:count], refs[count + 1]
+    taken, made, in_sems, out_sems = refs[count + 2 :]
+    height = taken.shape[1]
+    fetches = [pltpu.make_async_copy(arrived[j], taken.at[j], in_sems.at[j]) for j in range(count)]
+    for fetch in fetches:
+        fetch.start()
+    stores = []
     for j in range(count):
-
-        @pl.when(pl.program_id(0) == j)
-        def _():
-            out[...] = refs[j][...].astype(out.dtype)
+        fetches[j].wait()
+        made[j] = taken[j].astype(made.dtype)
+        store = pltpu.make_async_copy(
+            made.at[j], out.at[pl.ds(places[j] * height, height)], out_sems.at[j]
+        )
+        store.start()
+        stores.append(store)
+    for store in stores:
+        store.wait()
 
 
 def put(places, arrived, whole_array):
     count = len(arrived)
-    height, depth, width = arrived[0].shape
-    rows = 8 if height % 8 == 0 else 1
-    steps = height // rows
-
-    def from_block(j):
-        def index(block, step, places):
-            return jnp.where(block == j, step, jnp.where(block < j, 0, steps - 1)), 0, 0
-
-        return pl.BlockSpec((rows, depth, width), index)
-
+    shape = (count, *arrived[0].shape)
     return pl.pallas_call(
         functools.partial(put_body, count),
-        grid_spec=pltpu.PrefetchScalarGridSpec(
-            num_scalar_prefetch=1,
-            grid=(count, steps),
-            in_specs=[from_block(j) for j in range(count)] + [pl.BlockSpec(memory_space=pl.ANY)],
-            out_specs=pl.BlockSpec(
-                (rows, depth, width), lambda block, step, places: (places[block] * steps + step, 0, 0)
-            ),
-        ),
+        in_specs=[pl.BlockSpec(memory_space=pltpu.SMEM)]
+        + [pl.BlockSpec(memory_space=pl.ANY)] * (count + 1),
+        out_specs=pl.BlockSpec(memory_space=pl.ANY),
         out_shape=jax.ShapeDtypeStruct(whole_array.shape, whole_array.dtype),
+        scratch_shapes=[
+            pltpu.VMEM(shape, arrived[0].dtype),
+            pltpu.VMEM(shape, whole_array.dtype),
+            pltpu.SemaphoreType.DMA((count,)),
+            pltpu.SemaphoreType.DMA((count,)),
+        ],
         input_output_aliases={count + 1: 0},
+        compiler_params=pltpu.CompilerParams(vmem_limit_bytes=VMEM_LIMIT),
         cost_estimate=pl.CostEstimate(flops=0, bytes_accessed=4 * 1024 * 1024, transcendentals=0),
         name="put_rows",
     )(places, *arrived, whole_array)

time: 218 us -> 216 us (level)
  Pallas kernels: 55.2 us -> 50.1 us
  waiting for transfers between devices: 71.2 us -> 73.8 us
    pallas_call x2, Pallas kernels: 10.7 us -> 5.64 us  [put(): pl.pallas_call(functools.partial(put_body, count), in_specs=[pl.BlockSpec...]
    ppermute x39, waiting for transfers between devices: 71.2 us -> 73.8 us  [receive(): lax.ppermute(block, axis, [(i, (i - ahead) % count) for i in range(count)])]
  transfers between devices with their start and end apart: 41 -> 41, of which waited for: 17 -> 17; matrix products, arithmetic and copies ran while one was open for 6% -> 6% of each run, Pallas kernels for 25% -> 23%
where the time goes in v10:
time: 216 us; the launch traced here: 215 us
  waiting for transfers between devices  73.8 us (34%)
  starting transfers between devices  70.1 us (32%)
  Pallas kernels  50.1 us (23%)
  local copies, waits for them, and re-layouts  11.6 us (5%)
  other arithmetic  8.15 us (4%)
    ppermute x39, waiting for transfers between devices, receive(): lax.ppermute(block, axis, [(i, (i - ahead) % count) for i in range(count)])  73.8 us
    ppermute x39, starting transfers between devices, receive(): lax.ppermute(block, axis, [(i, (i - ahead) % count) for i in range(count)])  67.5 us
    pallas_call x2, Pallas kernels, correlate(): results = call(turn, stacked, *operands)  16.5 us
    pallas_call x1, Pallas kernels, forward(): results = call(turns, *pieces, *rims, *halves)  12.9 us
    pallas_call x1, Pallas kernels, backward(): pl.pallas_call(functools.partial(backward_body, count, lax.axis_size('row...  10.6 us
    pallas_call x2, Pallas kernels, put(): pl.pallas_call(functools.partial(put_body, count), in_specs=[pl.BlockSpec...  5.64 us
    unnamed x36, local copies, waits for them, and re-layouts  5.59 us
    pallas_call x1, Pallas kernels, turned(): pl.pallas_call(functools.partial(turned_body, shares), grid=(blocks,), in...  4.47 us
  transfers between devices with their start and end apart: 41, of which 17 were waited for; matrix products, arithmetic and copies ran while one was open for 6% of the time, Pallas kernels for 23%

profile of v10, /device:TPU:0, one launch (start us, length us, event | category | flops | bytes accessed | tf_op | source)
XLA Modules:
  0.0 214.8 jit_solution(4844885433212329628)
XLA Ops:
  0.7 0.9 copy-done
  1.8 3.1 %collective-permute-start.9 = (bf16[40,720]{1,0:T(8,128)(2,1)S(1)}, bf16[40,720]{1,0:T(8,128)(2,1)S(1)}, u32[]{:S(2)}, u32[]{:S(2)}) collective-permute-start(bf16[40,720]{1,0:T(8,128)(2,1)S(1)} %copy.13), channel_id=1, source_target_pairs={{0,2},{2,4},{4,6},{6,0},{1,3},{3,5},{5,7},{7,1},{8,10},{10,12},{12... | collective-permute-start | bytes 172808 | tf_op jit(solution)/shard_map/ppermute | solution.py:16
  4.9 2.6 %collective-permute-start.8 = (bf16[40,720]{1,0:T(8,128)(2,1)S(1)}, bf16[40,720]{1,0:T(8,128)(2,1)S(1)}, u32[]{:S(2)}, u32[]{:S(2)}) collective-permute-start(bf16[40,720]{1,0:T(8,128)(2,1)S(1)} %copy.13), channel_id=1, source_target_pairs={{0,4},{2,6},{4,0},{6,2},{1,5},{3,7},{5,1},{7,3},{8,12},{10,14},{12... | collective-permute-start | bytes 172808 | tf_op jit(solution)/shard_map/ppermute | solution.py:16
  7.5 1.3 collective-permute-start.7
  9.3 2.5 %collective-permute-done.8 = bf16[40,720]{1,0:T(8,128)(2,1)S(1)} collective-permute-done((bf16[40,720]{1,0:T(8,128)(2,1)S(1)}, bf16[40,720]{1,0:T(8,128)(2,1)S(1)}, u32[]{:S(2)}, u32[]{:S(2)}) %collective-permute-start.8) | collective-permute-done | bytes 57632 | tf_op jit(solution)/shard_map/ppermute | solution.py:16
  12.1 1.5 collective-permute-start.12
  13.6 1.5 collective-permute-start.11
  15.1 1.4 collective-permute-start.10
  16.6 1.1 dynamic-slice_bitcast_fusion
  17.7 2.9 %collective-permute-start = (bf16[16,80,128]{2,1,0:T(8,128)(2,1)}, bf16[16,80,128]{2,1,0:T(8,128)(2,1)}, u32[]{:S(2)}, u32[]{:S(2)}) collective-permute-start(bf16[16,80,128]{2,1,0:T(8,128)(2,1)} %get-tuple-element.66), channel_id=1, source_target_pairs={{0,6},{2,0},{4,2},{6,4},{1,7},{3,1},{5,3},{7,5},{8,14},{10,8},{12,... | collective-permute-start | bytes 983048 | tf_op jit(solution)/shard_map/ppermute | solution.py:16
  21.2 0.7 collective-permute-done.12
  21.9 1.4 collective-permute-start.2
  23.3 2.0 collective-permute-done.11
  25.3 0.7 copy-done.9
  26.0 1.1 pad_maximum_fusion.refs_8_.refs_0_
  27.6 2.3 %dynamic-slice_bitcast_fusion.4 = (bf16[14,80,128]{2,1,0:T(8,128)(2,1)}, bf16[14,80,128]{2,1,0:T(8,128)(2,1)}, bf16[14,80,128]{2,1,0:T(8,128)(2,1)}, bf16[14,80,128]{2,1,0:T(8,128)(2,1)}) fusion(bf16[1,64,80,128]{3,2,1,0:T(8,128)(2,1)} %param.5, s32[]{:T(128)S(6)} %select_n.315, s32[]{:T(128)S(6)} %select_n.313, s32[]{:T(128)S(6)} %select_n.312, ...), kind=kLoop, calls=%fused_computation.18 | loop fusion | bytes 2293776 | tf_op jit(solution)/shard_map/dynamic_slice | solution.py:598
  29.9 1.5 dynamic-slice_bitcast_fusion.9
  32.0 0.7 bitcast_select_fusion.1
  32.7 0.8 pad_maximum_fusion.4
  33.5 2.2 %collective-permute-start.4 = (bf16[4,80,128]{2,1,0:T(8,128)(2,1)S(1)}, bf16[4,80,128]{2,1,0:T(8,128)(2,1)S(1)}, u32[]{:S(2)}, u32[]{:S(2)}) collective-permute-start(bf16[4,80,128]{2,1,0:T(8,128)(2,1)S(1)} %pad_maximum_fusion.4), channel_id=1, source_target_pairs={{0,6},{2,0},{4,2},{6,4},{1,7},{3,1},{5,3},{7,5},{8,14},{10,8},{12,... | collective-permute-start | bytes 245768 | tf_op jit(solution)/shard_map/ppermute | solution.py:16
  35.7 0.8 pad_maximum_fusion.5
  36.5 10.2 %collective-permute-done.4.refs_5_.refs_6_ = bf16[4,80,128]{2,1,0:T(8,128)(2,1)S(1)} collective-permute-done((bf16[4,80,128]{2,1,0:T(8,128)(2,1)S(1)}, bf16[4,80,128]{2,1,0:T(8,128)(2,1)S(1)}, u32[]{:S(2)}, u32[]{:S(2)}) %collective-permute-start.4) | collective-permute-done | bytes 81952 | tf_op jit(solution)/shard_map/ppermute | solution.py:16
  46.6 2.9 %collective-permute-start.5 = (bf16[4,80,128]{2,1,0:T(8,128)(2,1)S(1)}, bf16[4,80,128]{2,1,0:T(8,128)(2,1)S(1)}, u32[]{:S(2)}, u32[]{:S(2)}) collective-permute-start(bf16[4,80,128]{2,1,0:T(8,128)(2,1)S(1)} %pad_maximum_fusion.5), channel_id=1, source_target_pairs={{0,4},{2,6},{4,0},{6,2},{1,5},{3,7},{5,1},{7,3},{8,12},{10,14},{12... | collective-permute-start | bytes 245768 | tf_op jit(solution)/shard_map/ppermute | solution.py:16
  49.6 3.3 %collective-permute-done.5.refs_6_.refs_7_ = bf16[4,80,128]{2,1,0:T(8,128)(2,1)S(1)} collective-permute-done((bf16[4,80,128]{2,1,0:T(8,128)(2,1)S(1)}, bf16[4,80,128]{2,1,0:T(8,128)(2,1)S(1)}, u32[]{:S(2)}, u32[]{:S(2)}) %collective-permute-start.5) | collective-permute-done | bytes 81952 | tf_op jit(solution)/shard_map/ppermute | solution.py:16
  52.9 3.0 %collective-permute-start.6 = (bf16[4,80,128]{2,1,0:T(8,128)(2,1)S(1)}, bf16[4,80,128]{2,1,0:T(8,128)(2,1)S(1)}, u32[]{:S(2)}, u32[]{:S(2)}) collective-permute-start(bf16[4,80,128]{2,1,0:T(8,128)(2,1)S(1)} %pad_maximum_fusion.6), channel_id=1, source_target_pairs={{0,2},{2,4},{4,6},{6,0},{1,3},{3,5},{5,7},{7,1},{8,10},{10,12},{12... | collective-permute-start | bytes 245768 | tf_op jit(solution)/shard_map/ppermute | solution.py:16
  56.6 3.4 %collective-permute-done.6.refs_7_.refs_8_ = bf16[4,80,128]{2,1,0:T(8,128)(2,1)S(1)} collective-permute-done((bf16[4,80,128]{2,1,0:T(8,128)(2,1)S(1)}, bf16[4,80,128]{2,1,0:T(8,128)(2,1)S(1)}, u32[]{:S(2)}, u32[]{:S(2)}) %collective-permute-start.6) | collective-permute-done | bytes 81952 | tf_op jit(solution)/shard_map/ppermute | solution.py:16
  60.0 1.0 collective-permute-start.17
  61.0 1.5 collective-permute-start.18
  62.6 1.0 copy-done.4
  63.5 12.9 %conv_forward.1 = (bf16[64,80,128]{2,1,0:T(8,128)(2,1)}, bf16[16,80,128]{2,1,0:T(8,128)(2,1)}, bf16[16,80,128]{2,1,0:T(8,128)(2,1)}, bf16[16,80,128]{2,1,0:T(8,1...) custom-call(s32[5]{0:T(128)} %stack.68.turns, ...), custom_call_target="tpu_custom_call" | custom-call | flops 3774873600 | bytes 16777216 | tf_op jit(solution)/shard_map/conv_forward/pallas_call | solution.py:207
  76.5 2.1 collective-permute-start.14
  78.5 2.4 %collective-permute-start.15 = (bf16[16,80,128]{2,1,0:T(8,128)(2,1)}, bf16[16,80,128]{2,1,0:T(8,128)(2,1)S(1)}, u32[]{:S(2)}, u32[]{:S(2)}) collective-permute-start(bf16[16,80,128]{2,1,0:T(8,128)(2,1)} %get-tuple-element.23), channel_id=1, source_target_pairs={{0,4},{2,6},{4,0},{6,2},{1,5},{3,7},{5,1},{7,3},{8,12},{10,14},{12... | collective-permute-start | bytes 983048 | tf_op jit(solution)/shard_map/ppermute | solution.py:16
  80.9 1.0 collective-permute-start.16
  81.9 19.6 %collective-permute-done.18.refs_3_ = bf16[14,80,128]{2,1,0:T(8,128)(2,1)S(1)} collective-permute-done((bf16[14,80,128]{2,1,0:T(8,128)(2,1)}, bf16[14,80,128]{2,1,0:T(8,128)(2,1)S(1)}, u32[]{:S(2)}, u32[]{:S(2)}) %collective-permute-start.18) | collective-permute-done | bytes 286752 | tf_op jit(solution)/shard_map/ppermute | solution.py:16
  101.5 1.3 collective-permute-start.20
  102.8 1.3 collective-permute-start.21
  104.2 10.6 %shard_map.58 = (f32[4,6,40,320]{3,2,1,0:T(8,128)}, f32[4,6,40,320]{3,2,1,0:T(8,128)}, bf16[320,2048]{1,0:T(8,128)(2,1)}) custom-call(s32[1]{0:T(128)} %bitcast.4.turn, bf16[960,2304]{1,0:T(8,128)(2,1)} %get-tuple-element.26.stacked, f32[16,320,128]{2,1,0:T(8,128)} %get-tuple-element.27.refs_0_, bf16[14,80,128]{2,1,0:T(8,128)(2,1)} %get-tuple-element.54.refs_1_, ...), custom_call_target="tpu_custom_call" | custom-call | flops 2516582400 | bytes 8388608 | tf_op jit(solution)/shard_map/pallas_call | solution.py:302
  114.8 4.5 %turn_kernel.1.kernels = bf16[4,80,3456]{2,1,0:T(8,128)(2,1)} custom-call(bf16[4,160,720]{2,1,0:T(8,128)(2,1)} %copy-done.1, bf16[4,160,720]{2,1,0:T(8,128)(2,1)} %copy-done.4), custom_call_target="tpu_custom_call" | custom-call | flops 235929600 | bytes 4194304 | tf_op jit(solution)/shard_map/turn_kernel/pallas_call | solution.py:348
  120.0 10.6 %conv_backward.1 = (f32[64,80,128]{2,1,0:T(8,128)}, bf16[16,80,128]{2,1,0:T(8,128)(2,1)}, bf16[16,80,128]{2,1,0:T(8,128)(2,1)}, bf16[16,80,128]{2,1,0:T(8,128)(2,1)}) custom-call(s32[5]{0:T(128)} %stack.68.turns, bf16[320,2048]{1,0:T(8,128)(2,1)} %get-tuple-element.38.slope.refs_0_, bf16[1,320,128]{2,1,0:T(8,128)(2,1)} %copy-done.16, ...), custom_call_target="tpu_custom_call" | custom-call | flops 3774873600 | bytes 8388608 | tf_op jit(solution)/shard_map/conv_backward/pallas_call | solution.py:439
  130.6 5.9 %shard_map.59 = (f32[4,3,40,320]{3,2,1,0:T(8,128)}, f32[4,3,40,320]{3,2,1,0:T(8,128)}) custom-call(s32[1]{0:T(128)} %bitcast.4.turn, bf16[960,2304]{1,0:T(8,128)(2,1)} %get-tuple-element.26.stacked, bf16[320,2048]{1,0:T(8,128)(2,1)} %get-tuple-element.38.slope.refs_0_), custom_call_target="tpu_custom_call" | custom-call | flops 1258291200 | bytes 8388608 | tf_op jit(solution)/shard_map/pallas_call | solution.py:302
  137.0 2.6 %collective-permute-start.22 = (bf16[16,80,128]{2,1,0:T(8,128)(2,1)}, bf16[16,80,128]{2,1,0:T(8,128)(2,1)S(1)}, u32[]{:S(2)}, u32[]{:S(2)}) collective-permute-start(bf16[16,80,128]{2,1,0:T(8,128)(2,1)} %get-tuple-element.32), channel_id=1, source_target_pairs={{0,2},{2,4},{4,6},{6,0},{1,3},{3,5},{5,7},{7,1},{8,10},{10,12},{12... | collective-permute-start | bytes 983048 | tf_op jit(solution)/shard_map/ppermute | solution.py:16
  139.7 0.7 copy-done.8
  140.7 2.9 %collective-permute-start.24 = (bf16[16,80,128]{2,1,0:T(8,128)(2,1)}, bf16[16,80,128]{2,1,0:T(8,128)(2,1)}, u32[]{:S(2)}, u32[]{:S(2)}) collective-permute-start(bf16[16,80,128]{2,1,0:T(8,128)(2,1)} %get-tuple-element.34), channel_id=1, source_target_pairs={{0,6},{2,0},{4,2},{6,4},{1,7},{3,1},{5,3},{7,5},{8,14},{10,8},{12,... | collective-permute-start | bytes 983048 | tf_op jit(solution)/shard_map/ppermute | solution.py:16
  143.6 0.7 pad_add_fusion.places
  144.2 2.6 %put_rows.2 = bf16[64,80,128]{2,1,0:T(8,128)(2,1)} custom-call(s32[3]{0:T(128)} %pad_add_fusion.places, bf16[16,80,128]{2,1,0:T(8,128)(2,1)} %collective-permute-done.14.refs_0_, bf16[16,80,128]{2,1,0:T(8,128)(2,1)} %copy-done.8, bf16[16,80,128]{2,1,0:T(8,128)(2,1)} %collective-permute-done.16.refs_2_, ...), custom_call_target="tpu_custom_call", output_to_operand_aliasing={{}: (4, {})} | custom-call | bytes 4194304 | tf_op jit(solution)/shard_map/put_rows/pallas_call | solution.py:491
  146.9 2.8 %collective-permute-done.22.refs_0_ = bf16[16,80,128]{2,1,0:T(8,128)(2,1)S(1)} collective-permute-done((bf16[16,80,128]{2,1,0:T(8,128)(2,1)}, bf16[16,80,128]{2,1,0:T(8,128)(2,1)S(1)}, u32[]{:S(2)}, u32[]{:S(2)}) %collective-permute-start.22) | collective-permute-done | bytes 327712 | tf_op jit(solution)/shard_map/ppermute | solution.py:16
  149.7 13.1 %collective-permute-done.23.refs_1_ = bf16[16,80,128]{2,1,0:T(8,128)(2,1)S(1)} collective-permute-done((bf16[16,80,128]{2,1,0:T(8,128)(2,1)}, bf16[16,80,128]{2,1,0:T(8,128)(2,1)S(1)}, u32[]{:S(2)}, u32[]{:S(2)}) %collective-permute-start.23) | collective-permute-done | bytes 327712 | tf_op jit(solution)/shard_map/ppermute | solution.py:16
  162.9 0.7 copy-done.7
  163.6 3.0 %put_rows.3 = f32[64,80,128]{2,1,0:T(8,128)} custom-call(s32[3]{0:T(128)} %pad_add_fusion.places, bf16[16,80,128]{2,1,0:T(8,128)(2,1)} %copy-done.6, bf16[16,80,128]{2,1,0:T(8,128)(2,1)} %copy-done.7, bf16[16,80,128]{2,1,0:T(8,128)(2,1)} %collective-permute-done.24.refs_2_, f32[64,80,128]{2,1,0:T(8,128)} %get-tuple-element.35.refs_3_), custom_call_target="tpu_custom_call", output_to_operand_aliasing={{}: (4, {})} | custom-call | bytes 4194304 | tf_op jit(solution)/shard_map/put_rows/pallas_call | solution.py:491
  166.6 0.9 copy-done.5
  167.5 1.5 add.277
  170.2 2.6 %collective-permute-start.34 = (f32[3,40,320]{2,1,0:T(8,128)S(1)}, f32[3,40,320]{2,1,0:T(8,128)S(1)}, u32[]{:S(2)}, u32[]{:S(2)}) collective-permute-start(f32[3,40,320]{2,1,0:T(8,128)S(1)} %get-tuple-element.68), channel_id=1, source_target_pairs={{0,24},{8,0},{16,8},{24,16},{1,25},{9,1},{17,9},{25,17},{2,26},{10... | collective-permute-start | bytes 460808 | tf_op jit(solution)/shard_map/ppermute | solution.py:16
  173.2 1.3 collective-permute-start.27
  174.5 3.0 %collective-permute-done.36 = f32[3,40,320]{2,1,0:T(8,128)S(1)} collective-permute-done((f32[3,40,320]{2,1,0:T(8,128)S(1)}, f32[3,40,320]{2,1,0:T(8,128)S(1)}, u32[]{:S(2)}, u32[]{:S(2)}) %collective-permute-start.36) | collective-permute-done | bytes 153632 | tf_op jit(solution)/shard_map/ppermute | solution.py:16
  177.6 4.0 %collective-permute-done.35 = f32[3,40,320]{2,1,0:T(8,128)S(1)} collective-permute-done((f32[3,40,320]{2,1,0:T(8,128)S(1)}, f32[3,40,320]{2,1,0:T(8,128)S(1)}, u32[]{:S(2)}, u32[]{:S(2)}) %collective-permute-start.35) | collective-permute-done | bytes 153632 | tf_op jit(solution)/shard_map/ppermute | solution.py:16
  181.7 6.9 %collective-permute-start.39 = (f32[80,120]{0,1:T(8,128)S(1)}, f32[80,120]{0,1:T(8,128)S(1)}, u32[]{:S(2)}, u32[]{:S(2)}) collective-permute-start(f32[80,120]{0,1:T(8,128)S(1)} %bitcast.152), channel_id=1, source_target_pairs={{0,2},{2,4},{4,6},{6,0},{1,3},{3,5},{5,7},{7,1},{8,10},{10,12},{12... | collective-permute-start | bytes 115208 | tf_op jit(solution)/shard_map/ppermute | solution.py:16
  188.7 2.6 %collective-permute-start.38 = (f32[80,120]{0,1:T(8,128)S(1)}, f32[80,120]{0,1:T(8,128)S(1)}, u32[]{:S(2)}, u32[]{:S(2)}) collective-permute-start(f32[80,120]{0,1:T(8,128)S(1)} %bitcast.151), channel_id=1, source_target_pairs={{0,4},{2,6},{4,0},{6,2},{1,5},{3,7},{5,1},{7,3},{8,12},{10,14},{12... | collective-permute-start | bytes 115208 | tf_op jit(solution)/shard_map/ppermute | solution.py:16
  191.2 7.1 %collective-permute-start.37 = (f32[80,120]{0,1:T(8,128)S(1)}, f32[80,120]{0,1:T(8,128)S(1)}, u32[]{:S(2)}, u32[]{:S(2)}) collective-permute-start(f32[80,120]{0,1:T(8,128)S(1)} %bitcast.150), channel_id=1, source_target_pairs={{0,6},{2,0},{4,2},{6,4},{1,7},{3,1},{5,3},{7,5},{8,14},{10,8},{12,... | collective-permute-start | bytes 115208 | tf_op jit(solution)/shard_map/ppermute | solution.py:16
  198.6 4.3 %collective-permute-start.31 = (f32[80,240]{0,1:T(8,128)S(1)}, f32[80,240]{0,1:T(8,128)S(1)}, u32[]{:S(2)}, u32[]{:S(2)}) collective-permute-start(f32[80,240]{0,1:T(8,128)S(1)} %bitcast.148), channel_id=1, source_target_pairs={{0,2},{2,4},{4,6},{6,0},{1,3},{3,5},{5,7},{7,1},{8,10},{10,12},{12... | collective-permute-start | bytes 230408 | tf_op jit(solution)/shard_map/ppermute | solution.py:16
  202.9 1.8 collective-permute-start.30
  205.5 2.9 %collective-permute-done.31 = f32[80,240]{0,1:T(8,128)S(1)} collective-permute-done((f32[80,240]{0,1:T(8,128)S(1)}, f32[80,240]{0,1:T(8,128)S(1)}, u32[]{:S(2)}, u32[]{:S(2)}) %collective-permute-start.31) | collective-permute-done | bytes 76832 | tf_op jit(solution)/shard_map/ppermute | solution.py:16
  208.4 4.0 %collective-permute-done.30 = f32[80,240]{0,1:T(8,128)S(1)} collective-permute-done((f32[80,240]{0,1:T(8,128)S(1)}, f32[80,240]{0,1:T(8,128)S(1)}, u32[]{:S(2)}, u32[]{:S(2)}) %collective-permute-start.30) | collective-permute-done | bytes 76832 | tf_op jit(solution)/shard_map/ppermute | solution.py:16
  212.7 1.2 collective-permute-done.32
  214.1 0.8 pad_maximum_fusion.1
  (91 shorter events, 8.1 us)
Async XLA Ops:
  0.6 0.9 copy-start
  0.6 15.9 %copy-start.2 = (bf16[1,64,80,128]{3,2,1,0:T(8,128)(2,1)S(1)}, bf16[1,64,80,128]{3,2,1,0:T(8,128)(2,1)}, u32[]{:S(2)}) copy-start(bf16[1,64,80,128]{3,2,1,0:T(8,128)(2,1)} %param.3) | copy-start | bytes 3932164
  1.8 7.5 %collective-permute-start.9 = (bf16[40,720]{1,0:T(8,128)(2,1)S(1)}, bf16[40,720]{1,0:T(8,128)(2,1)S(1)}, u32[]{:S(2)}, u32[]{:S(2)}) collective-permute-start(bf16[40,720]{1,0:T(8,128)(2,1)S(1)} %copy.13), channel_id=1, source_target_pairs={{0,2},{2,4},{4,6},{6,0},{1,3},{3,5},{5,7},{7,1},{8,10},{10,12},{12... | collective-permute-start | bytes 172808 | tf_op jit(solution)/shard_map/ppermute | solution.py:16
  4.9 6.9 %collective-permute-start.8 = (bf16[40,720]{1,0:T(8,128)(2,1)S(1)}, bf16[40,720]{1,0:T(8,128)(2,1)S(1)}, u32[]{:S(2)}, u32[]{:S(2)}) collective-permute-start(bf16[40,720]{1,0:T(8,128)(2,1)S(1)} %copy.13), channel_id=1, source_target_pairs={{0,4},{2,6},{4,0},{6,2},{1,5},{3,7},{5,1},{7,3},{8,12},{10,14},{12... | collective-permute-start | bytes 172808 | tf_op jit(solution)/shard_map/ppermute | solution.py:16
  7.5 4.6 %collective-permute-start.7 = (bf16[40,720]{1,0:T(8,128)(2,1)S(1)}, bf16[40,720]{1,0:T(8,128)(2,1)S(1)}, u32[]{:S(2)}, u32[]{:S(2)}) collective-permute-start(bf16[40,720]{1,0:T(8,128)(2,1)S(1)} %copy.13), channel_id=1, source_target_pairs={{0,6},{2,0},{4,2},{6,4},{1,7},{3,1},{5,3},{7,5},{8,14},{10,8},{12,... | collective-permute-start | bytes 172808 | tf_op jit(solution)/shard_map/ppermute | solution.py:16
  12.1 9.8 %collective-permute-start.12 = (bf16[160,720]{1,0:T(8,128)(2,1)S(1)}, bf16[160,720]{1,0:T(8,128)(2,1)S(1)}, u32[]{:S(2)}, u32[]{:S(2)}) collective-permute-start(bf16[160,720]{1,0:T(8,128)(2,1)S(1)} %get-tuple-element.76), channel_id=1, source_target_pairs={{0,8},{8,16},{16,24},{24,0},{1,9},{9,17},{17,25},{25,1},{2,10},{10... | collective-permute-start | bytes 691208 | tf_op jit(solution)/shard_map/ppermute | solution.py:16
  13.6 11.6 %collective-permute-start.11 = (bf16[160,720]{1,0:T(8,128)(2,1)S(1)}, bf16[160,720]{1,0:T(8,128)(2,1)S(1)}, u32[]{:S(2)}, u32[]{:S(2)}) collective-permute-start(bf16[160,720]{1,0:T(8,128)(2,1)S(1)} %get-tuple-element.76), channel_id=1, source_target_pairs={{0,16},{8,24},{16,0},{24,8},{1,17},{9,25},{17,1},{25,9},{2,18},{10... | collective-permute-start | bytes 691208 | tf_op jit(solution)/shard_map/ppermute | solution.py:16
  15.1 10.1 %collective-permute-start.10 = (bf16[160,720]{1,0:T(8,128)(2,1)S(1)}, bf16[160,720]{1,0:T(8,128)(2,1)S(1)}, u32[]{:S(2)}, u32[]{:S(2)}) collective-permute-start(bf16[160,720]{1,0:T(8,128)(2,1)S(1)} %get-tuple-element.76), channel_id=1, source_target_pairs={{0,24},{8,0},{16,8},{24,16},{1,25},{9,1},{17,9},{25,17},{2,26},{10... | collective-permute-start | bytes 691208 | tf_op jit(solution)/shard_map/ppermute | solution.py:16
  17.7 43.4 %collective-permute-start = (bf16[16,80,128]{2,1,0:T(8,128)(2,1)}, bf16[16,80,128]{2,1,0:T(8,128)(2,1)}, u32[]{:S(2)}, u32[]{:S(2)}) collective-permute-start(bf16[16,80,128]{2,1,0:T(8,128)(2,1)} %get-tuple-element.66), channel_id=1, source_target_pairs={{0,6},{2,0},{4,2},{6,4},{1,7},{3,1},{5,3},{7,5},{8,14},{10,8},{12,... | collective-permute-start | bytes 983048 | tf_op jit(solution)/shard_map/ppermute | solution.py:16
  20.6 41.9 %collective-permute-start.1 = (bf16[16,80,128]{2,1,0:T(8,128)(2,1)}, bf16[16,80,128]{2,1,0:T(8,128)(2,1)}, u32[]{:S(2)}, u32[]{:S(2)}) collective-permute-start(bf16[16,80,128]{2,1,0:T(8,128)(2,1)} %get-tuple-element.65), channel_id=1, source_target_pairs={{0,4},{2,6},{4,0},{6,2},{1,5},{3,7},{5,1},{7,3},{8,12},{10,14},{12... | collective-permute-start | bytes 983048 | tf_op jit(solution)/shard_map/ppermute | solution.py:16
  21.9 40.6 %collective-permute-start.2 = (bf16[16,80,128]{2,1,0:T(8,128)(2,1)}, bf16[16,80,128]{2,1,0:T(8,128)(2,1)}, u32[]{:S(2)}, u32[]{:S(2)}) collective-permute-start(bf16[16,80,128]{2,1,0:T(8,128)(2,1)} %get-tuple-element.64), channel_id=1, source_target_pairs={{0,2},{2,4},{4,6},{6,0},{1,3},{3,5},{5,7},{7,1},{8,10},{10,12},{12... | collective-permute-start | bytes 983048 | tf_op jit(solution)/shard_map/ppermute | solution.py:16
  25.3 6.7 %collective-permute-start.3 = (bf16[1,80,128]{2,1,0:T(8,128)(2,1)}, bf16[1,80,128]{2,1,0:T(8,128)(2,1)}, u32[]{:S(2)}, u32[]{:S(2)}) collective-permute-start(bf16[1,80,128]{2,1,0:T(8,128)(2,1)} %select_bitcast_fusion), channel_id=1, source_target_pairs={{0,1},{1,0},{2,3},{3,2},{4,5},{5,4},{6,7},{7,6},{8,9},{9,8},{10,11... | collective-permute-start | bytes 61448 | tf_op jit(solution)/shard_map/ppermute | solution.py:16
  25.3 0.7 copy-start.9
  27.1 5.7 %copy-start.1 = (bf16[4,160,720]{2,1,0:T(8,128)(2,1)}, bf16[4,160,720]{2,1,0:T(8,128)(2,1)S(1)}, u32[]{:S(2)}) copy-start(bf16[4,160,720]{2,1,0:T(8,128)(2,1)S(1)} %pad_maximum_fusion.refs_8_.refs_0_) | copy-start | bytes 2764804
  27.1 35.4 %collective-permute-start.13 = (bf16[4,160,720]{2,1,0:T(8,128)(2,1)S(1)}, bf16[4,160,720]{2,1,0:T(8,128)(2,1)S(1)}, u32[]{:S(2)}, u32[]{:S(2)}) collective-permute-start(bf16[4,160,720]{2,1,0:T(8,128)(2,1)S(1)} %pad_maximum_fusion.refs_8_.refs_0_), channel_id=1, source_target_pairs={{0,1},{1,0},{2,3},{3,2},{4,5},{5,4},{6,7},{7,6},{8,9},{9,8},{10,11... | collective-permute-start | bytes 2764808 | tf_op jit(solution)/shard_map/ppermute | solution.py:16
  33.5 13.1 %collective-permute-start.4 = (bf16[4,80,128]{2,1,0:T(8,128)(2,1)S(1)}, bf16[4,80,128]{2,1,0:T(8,128)(2,1)S(1)}, u32[]{:S(2)}, u32[]{:S(2)}) collective-permute-start(bf16[4,80,128]{2,1,0:T(8,128)(2,1)S(1)} %pad_maximum_fusion.4), channel_id=1, source_target_pairs={{0,6},{2,0},{4,2},{6,4},{1,7},{3,1},{5,3},{7,5},{8,14},{10,8},{12,... | collective-permute-start | bytes 245768 | tf_op jit(solution)/shard_map/ppermute | solution.py:16
  46.6 15.9 %copy-start.13 = (bf16[4,80,128]{2,1,0:T(8,128)(2,1)}, bf16[4,80,128]{2,1,0:T(8,128)(2,1)S(1)}, u32[]{:S(2)}) copy-start(bf16[4,80,128]{2,1,0:T(8,128)(2,1)S(1)} %collective-permute-done.4.refs_5_.refs_6_) | copy-start | bytes 245764
  46.6 6.3 %collective-permute-start.5 = (bf16[4,80,128]{2,1,0:T(8,128)(2,1)S(1)}, bf16[4,80,128]{2,1,0:T(8,128)(2,1)S(1)}, u32[]{:S(2)}, u32[]{:S(2)}) collective-permute-start(bf16[4,80,128]{2,1,0:T(8,128)(2,1)S(1)} %pad_maximum_fusion.5), channel_id=1, source_target_pairs={{0,4},{2,6},{4,0},{6,2},{1,5},{3,7},{5,1},{7,3},{8,12},{10,14},{12... | collective-permute-start | bytes 245768 | tf_op jit(solution)/shard_map/ppermute | solution.py:16
  52.9 9.6 %copy-start.14 = (bf16[4,80,128]{2,1,0:T(8,128)(2,1)}, bf16[4,80,128]{2,1,0:T(8,128)(2,1)S(1)}, u32[]{:S(2)}) copy-start(bf16[4,80,128]{2,1,0:T(8,128)(2,1)S(1)} %collective-permute-done.5.refs_6_.refs_7_) | copy-start | bytes 245764
  52.9 7.1 %collective-permute-start.6 = (bf16[4,80,128]{2,1,0:T(8,128)(2,1)S(1)}, bf16[4,80,128]{2,1,0:T(8,128)(2,1)S(1)}, u32[]{:S(2)}, u32[]{:S(2)}) collective-permute-start(bf16[4,80,128]{2,1,0:T(8,128)(2,1)S(1)} %pad_maximum_fusion.6), channel_id=1, source_target_pairs={{0,2},{2,4},{4,6},{6,0},{1,3},{3,5},{5,7},{7,1},{8,10},{10,12},{12... | collective-permute-start | bytes 245768 | tf_op jit(solution)/shard_map/ppermute | solution.py:16
  60.0 2.5 %copy-start.15 = (bf16[4,80,128]{2,1,0:T(8,128)(2,1)}, bf16[4,80,128]{2,1,0:T(8,128)(2,1)S(1)}, u32[]{:S(2)}) copy-start(bf16[4,80,128]{2,1,0:T(8,128)(2,1)S(1)} %collective-permute-done.6.refs_7_.refs_8_) | copy-start | bytes 245764
  60.0 20.9 %collective-permute-start.17 = (bf16[14,80,128]{2,1,0:T(8,128)(2,1)}, bf16[14,80,128]{2,1,0:T(8,128)(2,1)S(1)}, u32[]{:S(2)}, u32[]{:S(2)}) collective-permute-start(bf16[14,80,128]{2,1,0:T(8,128)(2,1)} %get-tuple-element.53), channel_id=1, source_target_pairs={{0,6},{2,0},{4,2},{6,4},{1,7},{3,1},{5,3},{7,5},{8,14},{10,8},{12,... | collective-permute-start | bytes 860168 | tf_op jit(solution)/shard_map/ppermute | solution.py:16
  61.0 40.5 %collective-permute-start.18 = (bf16[14,80,128]{2,1,0:T(8,128)(2,1)}, bf16[14,80,128]{2,1,0:T(8,128)(2,1)S(1)}, u32[]{:S(2)}, u32[]{:S(2)}) collective-permute-start(bf16[14,80,128]{2,1,0:T(8,128)(2,1)} %get-tuple-element.55), channel_id=1, source_target_pairs={{0,4},{2,6},{4,0},{6,2},{1,5},{3,7},{5,1},{7,3},{8,12},{10,14},{12... | collective-permute-start | bytes 860168 | tf_op jit(solution)/shard_map/ppermute | solution.py:16
  62.5 40.3 %collective-permute-start.19 = (bf16[14,80,128]{2,1,0:T(8,128)(2,1)}, bf16[14,80,128]{2,1,0:T(8,128)(2,1)S(1)}, u32[]{:S(2)}, u32[]{:S(2)}) collective-permute-start(bf16[14,80,128]{2,1,0:T(8,128)(2,1)} %get-tuple-element.52), channel_id=1, source_target_pairs={{0,2},{2,4},{4,6},{6,0},{1,3},{3,5},{5,7},{7,1},{8,10},{10,12},{12... | collective-permute-start | bytes 860168 | tf_op jit(solution)/shard_map/ppermute | solution.py:16
  62.5 1.0 copy-start.4
  76.5 60.5 %collective-permute-start.14 = (bf16[16,80,128]{2,1,0:T(8,128)(2,1)}, bf16[16,80,128]{2,1,0:T(8,128)(2,1)}, u32[]{:S(2)}, u32[]{:S(2)}) collective-permute-start(bf16[16,80,128]{2,1,0:T(8,128)(2,1)} %get-tuple-element.22), channel_id=1, source_target_pairs={{0,2},{2,4},{4,6},{6,0},{1,3},{3,5},{5,7},{7,1},{8,10},{10,12},{12... | collective-permute-start | bytes 983048 | tf_op jit(solution)/shard_map/ppermute | solution.py:16
  78.5 61.1 %collective-permute-start.15 = (bf16[16,80,128]{2,1,0:T(8,128)(2,1)}, bf16[16,80,128]{2,1,0:T(8,128)(2,1)S(1)}, u32[]{:S(2)}, u32[]{:S(2)}) collective-permute-start(bf16[16,80,128]{2,1,0:T(8,128)(2,1)} %get-tuple-element.23), channel_id=1, source_target_pairs={{0,4},{2,6},{4,0},{6,2},{1,5},{3,7},{5,1},{7,3},{8,12},{10,14},{12... | collective-permute-start | bytes 983048 | tf_op jit(solution)/shard_map/ppermute | solution.py:16
  80.9 23.2 %copy-start.10 = (bf16[14,80,128]{2,1,0:T(8,128)(2,1)}, bf16[14,80,128]{2,1,0:T(8,128)(2,1)S(1)}, u32[]{:S(2)}) copy-start(bf16[14,80,128]{2,1,0:T(8,128)(2,1)S(1)} %collective-permute-done.17.refs_2_) | copy-start | bytes 860164
  80.9 59.8 %collective-permute-start.16 = (bf16[16,80,128]{2,1,0:T(8,128)(2,1)}, bf16[16,80,128]{2,1,0:T(8,128)(2,1)}, u32[]{:S(2)}, u32[]{:S(2)}) collective-permute-start(bf16[16,80,128]{2,1,0:T(8,128)(2,1)} %get-tuple-element.24), channel_id=1, source_target_pairs={{0,6},{2,0},{4,2},{6,4},{1,7},{3,1},{5,3},{7,5},{8,14},{10,8},{12,... | collective-permute-start | bytes 983048 | tf_op jit(solution)/shard_map/ppermute | solution.py:16
  101.5 2.6 %copy-start.11 = (bf16[14,80,128]{2,1,0:T(8,128)(2,1)}, bf16[14,80,128]{2,1,0:T(8,128)(2,1)S(1)}, u32[]{:S(2)}) copy-start(bf16[14,80,128]{2,1,0:T(8,128)(2,1)S(1)} %collective-permute-done.18.refs_3_) | copy-start | bytes 860164
  101.5 17.8 %collective-permute-start.20 = (bf16[1,320,128]{2,1,0:T(8,128)(2,1)}, bf16[1,320,128]{2,1,0:T(8,128)(2,1)S(1)}, u32[]{:S(2)}, u32[]{:S(2)}) collective-permute-start(bf16[1,320,128]{2,1,0:T(8,128)(2,1)} %get-tuple-element.29), channel_id=1, source_target_pairs={{0,2},{2,4},{4,6},{6,7},{7,5},{5,3},{3,1},{8,10},{10,12},{12,14},{... | collective-permute-start | bytes 245768 | tf_op jit(solution)/shard_map/ppermute | solution.py:618
  102.8 1.3 copy-start.12
  102.8 16.5 %collective-permute-start.21 = (bf16[1,320,128]{2,1,0:T(8,128)(2,1)}, bf16[1,320,128]{2,1,0:T(8,128)(2,1)S(1)}, u32[]{:S(2)}, u32[]{:S(2)}) collective-permute-start(bf16[1,320,128]{2,1,0:T(8,128)(2,1)} %get-tuple-element.30), channel_id=1, source_target_pairs={{2,0},{4,2},{6,4},{7,6},{5,7},{3,5},{1,3},{10,8},{12,10},{14,12},{... | collective-permute-start | bytes 245768 | tf_op jit(solution)/shard_map/ppermute | solution.py:619
  119.3 0.6 copy-start.16
  119.3 53.6 %collective-permute-start.25 = (f32[4,6,40,320]{3,2,1,0:T(8,128)}, f32[4,6,40,320]{3,2,1,0:T(8,128)S(1)}, u32[]{:S(2)}, u32[]{:S(2)}) collective-permute-start(f32[4,6,40,320]{3,2,1,0:T(8,128)} %get-tuple-element.37), channel_id=1, source_target_pairs={{0,1},{1,0},{2,3},{3,2},{4,5},{5,4},{6,7},{7,6},{8,9},{9,8},{10,11... | collective-permute-start | bytes 3686408 | tf_op jit(solution)/shard_map/ppermute | solution.py:16
  119.4 0.6 copy-start.17
  136.5 30.2 %collective-permute-start.33 = (f32[4,3,40,320]{3,2,1,0:T(8,128)}, f32[4,3,40,320]{3,2,1,0:T(8,128)S(1)}, u32[]{:S(2)}, u32[]{:S(2)}) collective-permute-start(f32[4,3,40,320]{3,2,1,0:T(8,128)} %get-tuple-element.40), channel_id=1, source_target_pairs={{0,1},{1,0},{2,3},{3,2},{4,5},{5,4},{6,7},{7,6},{8,9},{9,8},{10,11... | collective-permute-start | bytes 1843208 | tf_op jit(solution)/shard_map/ppermute | solution.py:16
  137.0 12.7 %collective-permute-start.22 = (bf16[16,80,128]{2,1,0:T(8,128)(2,1)}, bf16[16,80,128]{2,1,0:T(8,128)(2,1)S(1)}, u32[]{:S(2)}, u32[]{:S(2)}) collective-permute-start(bf16[16,80,128]{2,1,0:T(8,128)(2,1)} %get-tuple-element.32), channel_id=1, source_target_pairs={{0,2},{2,4},{4,6},{6,0},{1,3},{3,5},{5,7},{7,1},{8,10},{10,12},{12... | collective-permute-start | bytes 983048 | tf_op jit(solution)/shard_map/ppermute | solution.py:16
  139.6 0.7 copy-start.8
  140.4 22.5 %collective-permute-start.23 = (bf16[16,80,128]{2,1,0:T(8,128)(2,1)}, bf16[16,80,128]{2,1,0:T(8,128)(2,1)S(1)}, u32[]{:S(2)}, u32[]{:S(2)}) collective-permute-start(bf16[16,80,128]{2,1,0:T(8,128)(2,1)} %get-tuple-element.33), channel_id=1, source_target_pairs={{0,4},{2,6},{4,0},{6,2},{1,5},{3,7},{5,1},{7,3},{8,12},{10,14},{12... | collective-permute-start | bytes 983048 | tf_op jit(solution)/shard_map/ppermute | solution.py:16
  140.7 22.2 %collective-permute-start.24 = (bf16[16,80,128]{2,1,0:T(8,128)(2,1)}, bf16[16,80,128]{2,1,0:T(8,128)(2,1)}, u32[]{:S(2)}, u32[]{:S(2)}) collective-permute-start(bf16[16,80,128]{2,1,0:T(8,128)(2,1)} %get-tuple-element.34), channel_id=1, source_target_pairs={{0,6},{2,0},{4,2},{6,4},{1,7},{3,1},{5,3},{7,5},{8,14},{10,8},{12,... | collective-permute-start | bytes 983048 | tf_op jit(solution)/shard_map/ppermute | solution.py:16
  149.7 13.1 %copy-start.6 = (bf16[16,80,128]{2,1,0:T(8,128)(2,1)}, bf16[16,80,128]{2,1,0:T(8,128)(2,1)S(1)}, u32[]{:S(2)}) copy-start(bf16[16,80,128]{2,1,0:T(8,128)(2,1)S(1)} %collective-permute-done.22.refs_0_) | copy-start | bytes 983044
  162.9 0.8 copy-start.7
  166.6 0.9 copy-start.5
  167.5 5.4 %copy-start.3 = (f32[4,6,40,320]{3,2,1,0:T(8,128)S(1)}, f32[4,6,40,320]{3,2,1,0:T(8,128)}, u32[]{:S(2)}) copy-start(f32[4,6,40,320]{3,2,1,0:T(8,128)} %get-tuple-element.36) | copy-start | bytes 3686404
  169.1 8.5 %collective-permute-start.36 = (f32[3,40,320]{2,1,0:T(8,128)S(1)}, f32[3,40,320]{2,1,0:T(8,128)S(1)}, u32[]{:S(2)}, u32[]{:S(2)}) collective-permute-start(f32[3,40,320]{2,1,0:T(8,128)S(1)} %get-tuple-element.69), channel_id=1, source_target_pairs={{0,8},{8,16},{16,24},{24,0},{1,9},{9,17},{17,25},{25,1},{2,10},{10... | collective-permute-start | bytes 460808 | tf_op jit(solution)/shard_map/ppermute | solution.py:16
  169.7 11.8 %collective-permute-start.35 = (f32[3,40,320]{2,1,0:T(8,128)S(1)}, f32[3,40,320]{2,1,0:T(8,128)S(1)}, u32[]{:S(2)}, u32[]{:S(2)}) collective-permute-start(f32[3,40,320]{2,1,0:T(8,128)S(1)} %get-tuple-element.70), channel_id=1, source_target_pairs={{0,16},{8,24},{16,0},{24,8},{1,17},{9,25},{17,1},{25,9},{2,18},{10... | collective-permute-start | bytes 460808 | tf_op jit(solution)/shard_map/ppermute | solution.py:16
  170.2 11.3 %collective-permute-start.34 = (f32[3,40,320]{2,1,0:T(8,128)S(1)}, f32[3,40,320]{2,1,0:T(8,128)S(1)}, u32[]{:S(2)}, u32[]{:S(2)}) collective-permute-start(f32[3,40,320]{2,1,0:T(8,128)S(1)} %get-tuple-element.68), channel_id=1, source_target_pairs={{0,24},{8,0},{16,8},{24,16},{1,25},{9,1},{17,9},{25,17},{2,26},{10... | collective-permute-start | bytes 460808 | tf_op jit(solution)/shard_map/ppermute | solution.py:16
  173.1 18.1 %collective-permute-start.28 = (f32[6,40,320]{2,1,0:T(8,128)S(1)}, f32[6,40,320]{2,1,0:T(8,128)S(1)}, u32[]{:S(2)}, u32[]{:S(2)}) collective-permute-start(f32[6,40,320]{2,1,0:T(8,128)S(1)} %get-tuple-element.42), channel_id=1, source_target_pairs={{0,8},{8,16},{16,24},{24,0},{1,9},{9,17},{17,25},{25,1},{2,10},{10... | collective-permute-start | bytes 921608 | tf_op jit(solution)/shard_map/ppermute | solution.py:16
  173.2 25.1 %collective-permute-start.27 = (f32[6,40,320]{2,1,0:T(8,128)S(1)}, f32[6,40,320]{2,1,0:T(8,128)S(1)}, u32[]{:S(2)}, u32[]{:S(2)}) collective-permute-start(f32[6,40,320]{2,1,0:T(8,128)S(1)} %get-tuple-element.43), channel_id=1, source_target_pairs={{0,16},{8,24},{16,0},{24,8},{1,17},{9,25},{17,1},{25,9},{2,18},{10... | collective-permute-start | bytes 921608 | tf_op jit(solution)/shard_map/ppermute | solution.py:16
  177.5 20.8 %collective-permute-start.26 = (f32[6,40,320]{2,1,0:T(8,128)S(1)}, f32[6,40,320]{2,1,0:T(8,128)S(1)}, u32[]{:S(2)}, u32[]{:S(2)}) collective-permute-start(f32[6,40,320]{2,1,0:T(8,128)S(1)} %get-tuple-element.41), channel_id=1, source_target_pairs={{0,24},{8,0},{16,8},{24,16},{1,25},{9,1},{17,9},{25,17},{2,26},{10... | collective-permute-start | bytes 921608 | tf_op jit(solution)/shard_map/ppermute | solution.py:16
  181.7 23.0 %collective-permute-start.39 = (f32[80,120]{0,1:T(8,128)S(1)}, f32[80,120]{0,1:T(8,128)S(1)}, u32[]{:S(2)}, u32[]{:S(2)}) collective-permute-start(f32[80,120]{0,1:T(8,128)S(1)} %bitcast.152), channel_id=1, source_target_pairs={{0,2},{2,4},{4,6},{6,0},{1,3},{3,5},{5,7},{7,1},{8,10},{10,12},{12... | collective-permute-start | bytes 115208 | tf_op jit(solution)/shard_map/ppermute | solution.py:16
  188.7 16.7 %collective-permute-start.38 = (f32[80,120]{0,1:T(8,128)S(1)}, f32[80,120]{0,1:T(8,128)S(1)}, u32[]{:S(2)}, u32[]{:S(2)}) collective-permute-start(f32[80,120]{0,1:T(8,128)S(1)} %bitcast.151), channel_id=1, source_target_pairs={{0,4},{2,6},{4,0},{6,2},{1,5},{3,7},{5,1},{7,3},{8,12},{10,14},{12... | collective-permute-start | bytes 115208 | tf_op jit(solution)/shard_map/ppermute | solution.py:16
  191.2 14.1 %collective-permute-start.37 = (f32[80,120]{0,1:T(8,128)S(1)}, f32[80,120]{0,1:T(8,128)S(1)}, u32[]{:S(2)}, u32[]{:S(2)}) collective-permute-start(f32[80,120]{0,1:T(8,128)S(1)} %bitcast.150), channel_id=1, source_target_pairs={{0,6},{2,0},{4,2},{6,4},{1,7},{3,1},{5,3},{7,5},{8,14},{10,8},{12,... | collective-permute-start | bytes 115208 | tf_op jit(solution)/shard_map/ppermute | solution.py:16
  198.6 9.8 %collective-permute-start.31 = (f32[80,240]{0,1:T(8,128)S(1)}, f32[80,240]{0,1:T(8,128)S(1)}, u32[]{:S(2)}, u32[]{:S(2)}) collective-permute-start(f32[80,240]{0,1:T(8,128)S(1)} %bitcast.148), channel_id=1, source_target_pairs={{0,2},{2,4},{4,6},{6,0},{1,3},{3,5},{5,7},{7,1},{8,10},{10,12},{12... | collective-permute-start | bytes 230408 | tf_op jit(solution)/shard_map/ppermute | solution.py:16
  202.9 9.5 %collective-permute-start.30 = (f32[80,240]{0,1:T(8,128)S(1)}, f32[80,240]{0,1:T(8,128)S(1)}, u32[]{:S(2)}, u32[]{:S(2)}) collective-permute-start(f32[80,240]{0,1:T(8,128)S(1)} %bitcast.147), channel_id=1, source_target_pairs={{0,4},{2,6},{4,0},{6,2},{1,5},{3,7},{5,1},{7,3},{8,12},{10,14},{12... | collective-permute-start | bytes 230408 | tf_op jit(solution)/shard_map/ppermute | solution.py:16
  204.7 7.8 %collective-permute-start.29 = (f32[80,240]{0,1:T(8,128)S(1)}, f32[80,240]{0,1:T(8,128)S(1)}, u32[]{:S(2)}, u32[]{:S(2)}) collective-permute-start(f32[80,240]{0,1:T(8,128)S(1)} %bitcast.146), channel_id=1, source_target_pairs={{0,6},{2,0},{4,2},{6,4},{1,7},{3,1},{5,3},{7,5},{8,14},{10,8},{12,... | collective-permute-start | bytes 230408 | tf_op jit(solution)/shard_map/ppermute | solution.py:16
  205.4 7.2 %collective-permute-start.40 = (f32[80,120]{0,1:T(8,128)S(1)}, f32[80,120]{0,1:T(8,128)S(1)}, u32[]{:S(2)}, u32[]{:S(2)}) collective-permute-start(f32[80,120]{0,1:T(8,128)S(1)} %fusion.17), channel_id=1, source_target_pairs={{0,1},{1,0},{2,3},{3,2},{4,5},{5,4},{6,7},{7,6},{8,9},{9,8},{10,11... | collective-permute-start | bytes 115208 | tf_op jit(solution)/shard_map/ppermute | solution.py:16
  212.5 1.4 collective-permute-start.32

commit v11 on v10

--- a/solution.py
+++ b/solution.py
@@ -20,19 +20,29 @@
     return lax.ppermute(block, axis, [(i, i ^ bit) for i in range(lax.axis_size(axis))])
 
 
-def summed_over_chan(total, outer, in_steps):
+def summed_over_chan(lead, rest, outer):
     chans = lax.axis_size("chan")
-    blocks = [total[j * outer : (j + 1) * outer] for j in range(chans)]
-    if chans != 4 or not in_steps:
-        own = blocks[0]
-        for j in range(1, chans):
-            own = own + receive(blocks[chans - j], "chan", j)
-        return own
+
+    def blocks_of(total):
+        return [total[j * outer : (j + 1) * outer] for j in range(chans)]
+
+    lead, rest = blocks_of(lead), blocks_of(rest)
+    if chans != 4:
+        owns = []
+        for blocks in (lead, rest):
+            own = blocks[0]
+            for j in range(1, chans):
+                own = own + receive(blocks[chans - j], "chan", j)
+            owns.append(own)
+        return jnp.concatenate(owns, axis=1)
     odd = lax.axis_index("chan") % 2 == 1
-    beside = swapped(jnp.concatenate([blocks[1], blocks[3]]), "chan", 1)
+    beside = swapped(jnp.concatenate([lead[1], lead[3]]), "chan", 1)
     first, second = beside[:outer], beside[outer:]
-    other = blocks[2] + jnp.where(odd, second, first)
-    return blocks[0] + jnp.where(odd, first, second) + swapped(other, "chan", 2)
+    other = lead[2] + jnp.where(odd, second, first)
+    last = jnp.concatenate([other, rest[2]], axis=1)
+    near = rest[0] + receive(rest[3], "chan", 1) + receive(rest[1], "chan", 3)
+    mine = jnp.concatenate([lead[0] + jnp.where(odd, first, second), near], axis=1)
+    return mine + receive(last, "chan", 2)
 
 
 def home_of(row, chan, chans):
@@ -542,11 +552,15 @@
     return total
 
 
-def kernel_grad_of(total, inner, outer, in_steps):
+def kernel_grad_of(lead, rest, inner, outer):
     row, rows = lax.axis_index("row"), lax.axis_size("row")
-    taps, share, channels = total.shape
-    total = jnp.transpose(total, (2, 0, 1)).reshape(channels, taps * share)
-    own = summed_over_chan(total, outer, in_steps)
+    share, channels = lead.shape[1:]
+    taps = lead.shape[0] + rest.shape[0]
+
+    def turned_rows(total):
+        return jnp.transpose(total, (2, 0, 1)).reshape(channels, -1)
+
+    own = summed_over_chan(turned_rows(lead), turned_rows(rest), outer)
     both = jnp.stack([own] + [receive(own, "row", j) for j in range(1, rows)])
     both = rotated(both, (rows - row) % rows, 0).reshape(rows, outer, taps, share)
     return jnp.transpose(both, (2, 0, 3, 1)).reshape(taps, inner, outer)
@@ -625,9 +639,7 @@
     (rest,) = correlate((6, 3), stacked, slope)
     rest = summed_over_images(rest)
     inner, outer = kernel.shape[1:]
-    kernel_grad = jnp.concatenate(
-        [kernel_grad_of(lead, inner, outer, False), kernel_grad_of(rest, inner, outer, False)]
-    )
+    kernel_grad = kernel_grad_of(lead, rest, inner, outer)
 
     places = jnp.stack([home(-j) for j in range(1, chans)]).astype(jnp.int32)
 

time: 216 us -> 220 us (1.019)
  local copies, waits for them, and re-layouts: 11.6 us -> 14.6 us
    ppermute x39 -> x35, waiting for transfers between devices: 73.8 us -> 60.5 us  [receive(): lax.ppermute(block, axis, [(i, (i - ahead) % count) for i in range(count)])]
    ppermute x0 -> x1, waiting for transfers between devices: none -> 13.1 us  [swapped(): lax.ppermute(block, axis, [(i, i ^ bit) for i in range(lax.axis_size(axis...]
    ppermute x39 -> x35, starting transfers between devices: 67.5 us -> 61.3 us  [receive(): lax.ppermute(block, axis, [(i, (i - ahead) % count) for i in range(count)])]
    ppermute x1, starting transfers between devices: 1.28 us -> 4.76 us  [shards(): above = lax.ppermute(last, ('chan', 'row'), line)]
    ppermute x0 -> x1, starting transfers between devices: none -> 2.71 us  [swapped(): lax.ppermute(block, axis, [(i, i ^ bit) for i in range(lax.axis_size(axis...]
    unnamed x36 -> x46, local copies, waits for them, and re-layouts: 5.59 us -> 6.03 us
  transfers between devices with their start and end apart: 41 -> 38, of which waited for: 17 -> 17; matrix products, arithmetic and copies ran while one was open for 6% -> 8% of each run, Pallas kernels for 23% -> 23%
where the time goes in v11:
time: 220 us; the launch traced here: 219 us
  waiting for transfers between devices  73.6 us (33%)
  starting transfers between devices  70 us (32%)
  Pallas kernels  50.1 us (23%)
  local copies, waits for them, and re-layouts  14.6 us (7%)
  other arithmetic  9.79 us (4%)
    ppermute x35, starting transfers between devices, receive(): lax.ppermute(block, axis, [(i, (i - ahead) % count) for i in range(count)])  61.3 us
    ppermute x35, waiting for transfers between devices, receive(): lax.ppermute(block, axis, [(i, (i - ahead) % count) for i in range(count)])  60.5 us
    pallas_call x2, Pallas kernels, correlate(): results = call(turn, stacked, *operands)  16.5 us
    ppermute x1, waiting for transfers between devices, swapped(): lax.ppermute(block, axis, [(i, i ^ bit) for i in range(lax.axis_size(axis...  13.1 us
    pallas_call x1, Pallas kernels, forward(): results = call(turns, *pieces, *rims, *halves)  13 us
    pallas_call x1, Pallas kernels, backward(): pl.pallas_call(functools.partial(backward_body, count, lax.axis_size('row...  10.6 us
    unnamed x46, local copies, waits for them, and re-layouts  6.03 us
    pallas_call x2, Pallas kernels, put(): pl.pallas_call(functools.partial(put_body, count), in_specs=[pl.BlockSpec...  5.64 us
  transfers between devices with their start and end apart: 38, of which 17 were waited for; matrix products, arithmetic and copies ran while one was open for 8% of the time, Pallas kernels for 23%

profile of v11, /device:TPU:0, one launch (start us, length us, event | category | flops | bytes accessed | tf_op | source)
XLA Modules:
  0.0 219.2 jit_solution(6287373395123285409)
XLA Ops:
  0.7 0.9 copy-done
  1.8 3.1 %collective-permute-start.9 = (bf16[40,720]{1,0:T(8,128)(2,1)S(1)}, bf16[40,720]{1,0:T(8,128)(2,1)S(1)}, u32[]{:S(2)}, u32[]{:S(2)}) collective-permute-start(bf16[40,720]{1,0:T(8,128)(2,1)S(1)} %copy.12), channel_id=1, source_target_pairs={{0,2},{2,4},{4,6},{6,0},{1,3},{3,5},{5,7},{7,1},{8,10},{10,12},{12... | collective-permute-start | bytes 172808 | tf_op jit(solution)/shard_map/ppermute | solution.py:16
  4.9 2.6 %collective-permute-start.8 = (bf16[40,720]{1,0:T(8,128)(2,1)S(1)}, bf16[40,720]{1,0:T(8,128)(2,1)S(1)}, u32[]{:S(2)}, u32[]{:S(2)}) collective-permute-start(bf16[40,720]{1,0:T(8,128)(2,1)S(1)} %copy.12), channel_id=1, source_target_pairs={{0,4},{2,6},{4,0},{6,2},{1,5},{3,7},{5,1},{7,3},{8,12},{10,14},{12... | collective-permute-start | bytes 172808 | tf_op jit(solution)/shard_map/ppermute | solution.py:16
  7.5 1.3 collective-permute-start.7
  9.3 2.5 %collective-permute-done.8 = bf16[40,720]{1,0:T(8,128)(2,1)S(1)} collective-permute-done((bf16[40,720]{1,0:T(8,128)(2,1)S(1)}, bf16[40,720]{1,0:T(8,128)(2,1)S(1)}, u32[]{:S(2)}, u32[]{:S(2)}) %collective-permute-start.8) | collective-permute-done | bytes 57632 | tf_op jit(solution)/shard_map/ppermute | solution.py:16
  12.1 1.5 collective-permute-start.12
  13.6 1.5 collective-permute-start.11
  15.1 1.4 collective-permute-start.10
  16.6 1.1 dynamic-slice_bitcast_fusion
  17.7 2.9 %collective-permute-start = (bf16[16,80,128]{2,1,0:T(8,128)(2,1)}, bf16[16,80,128]{2,1,0:T(8,128)(2,1)}, u32[]{:S(2)}, u32[]{:S(2)}) collective-permute-start(bf16[16,80,128]{2,1,0:T(8,128)(2,1)} %get-tuple-element.66), channel_id=1, source_target_pairs={{0,6},{2,0},{4,2},{6,4},{1,7},{3,1},{5,3},{7,5},{8,14},{10,8},{12,... | collective-permute-start | bytes 983048 | tf_op jit(solution)/shard_map/ppermute | solution.py:16
  21.2 0.7 collective-permute-done.12
  21.9 1.4 collective-permute-start.2
  23.3 2.0 collective-permute-done.11
  26.0 2.3 %dynamic-slice_bitcast_fusion.4 = (bf16[14,80,128]{2,1,0:T(8,128)(2,1)}, bf16[14,80,128]{2,1,0:T(8,128)(2,1)}, bf16[14,80,128]{2,1,0:T(8,128)(2,1)}, bf16[14,80,128]{2,1,0:T(8,128)(2,1)}) fusion(bf16[1,64,80,128]{3,2,1,0:T(8,128)(2,1)} %param.5, s32[]{:T(128)S(6)} %select_n.328, s32[]{:T(128)S(6)} %select_n.326, s32[]{:T(128)S(6)} %select_n.325, ...), kind=kLoop, calls=%fused_computation.20 | loop fusion | bytes 2293776 | tf_op jit(solution)/shard_map/dynamic_slice | solution.py:612
  28.3 1.5 dynamic-slice_bitcast_fusion.9
  30.4 0.7 bitcast_select_fusion.1
  31.1 0.8 pad_maximum_fusion.5
  31.9 2.2 %collective-permute-start.4 = (bf16[4,80,128]{2,1,0:T(8,128)(2,1)S(1)}, bf16[4,80,128]{2,1,0:T(8,128)(2,1)S(1)}, u32[]{:S(2)}, u32[]{:S(2)}) collective-permute-start(bf16[4,80,128]{2,1,0:T(8,128)(2,1)S(1)} %pad_maximum_fusion.5), channel_id=1, source_target_pairs={{0,6},{2,0},{4,2},{6,4},{1,7},{3,1},{5,3},{7,5},{8,14},{10,8},{12,... | collective-permute-start | bytes 245768 | tf_op jit(solution)/shard_map/ppermute | solution.py:16
  34.1 0.8 pad_maximum_fusion.6
  34.9 7.8 %collective-permute-done.4.refs_5_.refs_6_ = bf16[4,80,128]{2,1,0:T(8,128)(2,1)S(1)} collective-permute-done((bf16[4,80,128]{2,1,0:T(8,128)(2,1)S(1)}, bf16[4,80,128]{2,1,0:T(8,128)(2,1)S(1)}, u32[]{:S(2)}, u32[]{:S(2)}) %collective-permute-start.4) | collective-permute-done | bytes 81952 | tf_op jit(solution)/shard_map/ppermute | solution.py:16
  42.7 7.8 %collective-permute-start.5 = (bf16[4,80,128]{2,1,0:T(8,128)(2,1)S(1)}, bf16[4,80,128]{2,1,0:T(8,128)(2,1)S(1)}, u32[]{:S(2)}, u32[]{:S(2)}) collective-permute-start(bf16[4,80,128]{2,1,0:T(8,128)(2,1)S(1)} %pad_maximum_fusion.6), channel_id=1, source_target_pairs={{0,4},{2,6},{4,0},{6,2},{1,5},{3,7},{5,1},{7,3},{8,12},{10,14},{12... | collective-permute-start | bytes 245768 | tf_op jit(solution)/shard_map/ppermute | solution.py:16
  50.5 2.5 %collective-permute-done.5.refs_6_.refs_7_ = bf16[4,80,128]{2,1,0:T(8,128)(2,1)S(1)} collective-permute-done((bf16[4,80,128]{2,1,0:T(8,128)(2,1)S(1)}, bf16[4,80,128]{2,1,0:T(8,128)(2,1)S(1)}, u32[]{:S(2)}, u32[]{:S(2)}) %collective-permute-start.5) | collective-permute-done | bytes 81952 | tf_op jit(solution)/shard_map/ppermute | solution.py:16
  53.0 3.8 %collective-permute-start.6 = (bf16[4,80,128]{2,1,0:T(8,128)(2,1)S(1)}, bf16[4,80,128]{2,1,0:T(8,128)(2,1)S(1)}, u32[]{:S(2)}, u32[]{:S(2)}) collective-permute-start(bf16[4,80,128]{2,1,0:T(8,128)(2,1)S(1)} %pad_maximum_fusion.7), channel_id=1, source_target_pairs={{0,2},{2,4},{4,6},{6,0},{1,3},{3,5},{5,7},{7,1},{8,10},{10,12},{12... | collective-permute-start | bytes 245768 | tf_op jit(solution)/shard_map/ppermute | solution.py:16
  57.5 3.5 %collective-permute-done.6.refs_7_.refs_8_ = bf16[4,80,128]{2,1,0:T(8,128)(2,1)S(1)} collective-permute-done((bf16[4,80,128]{2,1,0:T(8,128)(2,1)S(1)}, bf16[4,80,128]{2,1,0:T(8,128)(2,1)S(1)}, u32[]{:S(2)}, u32[]{:S(2)}) %collective-permute-start.6) | collective-permute-done | bytes 81952 | tf_op jit(solution)/shard_map/ppermute | solution.py:16
  61.0 5.5 %collective-permute-start.17 = (bf16[14,80,128]{2,1,0:T(8,128)(2,1)}, bf16[14,80,128]{2,1,0:T(8,128)(2,1)S(1)}, u32[]{:S(2)}, u32[]{:S(2)}) collective-permute-start(bf16[14,80,128]{2,1,0:T(8,128)(2,1)} %get-tuple-element.53), channel_id=1, source_target_pairs={{0,6},{2,0},{4,2},{6,4},{1,7},{3,1},{5,3},{7,5},{8,14},{10,8},{12,... | collective-permute-start | bytes 860168 | tf_op jit(solution)/shard_map/ppermute | solution.py:16
  67.1 1.0 copy-done.5
  68.1 13.0 %conv_forward.1 = (bf16[64,80,128]{2,1,0:T(8,128)(2,1)}, bf16[16,80,128]{2,1,0:T(8,128)(2,1)}, bf16[16,80,128]{2,1,0:T(8,128)(2,1)}, bf16[16,80,128]{2,1,0:T(8,1...) custom-call(s32[5]{0:T(128)} %stack.61.turns, ...), custom_call_target="tpu_custom_call" | custom-call | flops 3774873600 | bytes 16777216 | tf_op jit(solution)/shard_map/conv_forward/pallas_call | solution.py:217
  81.1 4.8 %collective-permute-start.20 = (bf16[1,320,128]{2,1,0:T(8,128)(2,1)}, bf16[1,320,128]{2,1,0:T(8,128)(2,1)S(1)}, u32[]{:S(2)}, u32[]{:S(2)}) collective-permute-start(bf16[1,320,128]{2,1,0:T(8,128)(2,1)} %get-tuple-element.29), channel_id=1, source_target_pairs={{0,2},{2,4},{4,6},{6,7},{7,5},{5,3},{3,1},{8,10},{10,12},{12,14},{... | collective-permute-start | bytes 245768 | tf_op jit(solution)/shard_map/ppermute | solution.py:632
  85.8 1.3 collective-permute-start.21
  88.1 10.6 %shard_map.58 = (f32[4,6,40,320]{3,2,1,0:T(8,128)}, f32[4,6,40,320]{3,2,1,0:T(8,128)}, bf16[320,2048]{1,0:T(8,128)(2,1)}) custom-call(s32[1]{0:T(128)} %bitcast.4.turn, bf16[960,2304]{1,0:T(8,128)(2,1)} %get-tuple-element.26.stacked, f32[16,320,128]{2,1,0:T(8,128)} %get-tuple-element.27.refs_0_, bf16[14,80,128]{2,1,0:T(8,128)(2,1)} %get-tuple-element.54.refs_1_, ...), custom_call_target="tpu_custom_call" | custom-call | flops 2516582400 | bytes 8388608 | tf_op jit(solution)/shard_map/pallas_call | solution.py:312
  98.7 4.5 %turn_kernel.1.kernels = bf16[4,80,3456]{2,1,0:T(8,128)(2,1)} custom-call(bf16[4,160,720]{2,1,0:T(8,128)(2,1)} %copy-done.1, bf16[4,160,720]{2,1,0:T(8,128)(2,1)} %copy-done.5), custom_call_target="tpu_custom_call" | custom-call | flops 235929600 | bytes 4194304 | tf_op jit(solution)/shard_map/turn_kernel/pallas_call | solution.py:358
  103.9 10.6 %conv_backward.1 = (f32[64,80,128]{2,1,0:T(8,128)}, bf16[16,80,128]{2,1,0:T(8,128)(2,1)}, bf16[16,80,128]{2,1,0:T(8,128)(2,1)}, bf16[16,80,128]{2,1,0:T(8,128)(2,1)}) custom-call(s32[5]{0:T(128)} %stack.61.turns, bf16[320,2048]{1,0:T(8,128)(2,1)} %get-tuple-element.38.slope.refs_0_, bf16[1,320,128]{2,1,0:T(8,128)(2,1)} %copy-done.21, ...), custom_call_target="tpu_custom_call" | custom-call | flops 3774873600 | bytes 8388608 | tf_op jit(solution)/shard_map/conv_backward/pallas_call | solution.py:449
  114.4 5.9 %shard_map.59 = (f32[4,3,40,320]{3,2,1,0:T(8,128)}, f32[4,3,40,320]{3,2,1,0:T(8,128)}) custom-call(s32[1]{0:T(128)} %bitcast.4.turn, bf16[960,2304]{1,0:T(8,128)(2,1)} %get-tuple-element.26.stacked, bf16[320,2048]{1,0:T(8,128)(2,1)} %get-tuple-element.38.slope.refs_0_), custom_call_target="tpu_custom_call" | custom-call | flops 1258291200 | bytes 8388608 | tf_op jit(solution)/shard_map/pallas_call | solution.py:312
  120.9 2.1 collective-permute-done.30
  122.9 1.4 add.272
  124.3 0.8 slice_bitcast_fusion.6
  125.7 2.6 %collective-permute-start.31 = (f32[3,40,320]{2,1,0:T(8,128)}, f32[3,40,320]{2,1,0:T(8,128)}, u32[]{:S(2)}, u32[]{:S(2)}) collective-permute-start(f32[3,40,320]{2,1,0:T(8,128)} %get-tuple-element.68), channel_id=1, source_target_pairs={{0,24},{8,0},{16,8},{24,16},{1,25},{9,1},{17,9},{25,17},{2,26},{10... | collective-permute-start | bytes 460808 | tf_op jit(solution)/shard_map/ppermute | solution.py:16
  128.2 1.1 copy-done.4
  129.4 1.5 add.266
  130.9 1.0 slice_bitcast_fusion.2
  132.3 1.5 collective-permute-start.27
  133.7 2.9 %collective-permute-start.26 = (f32[6,40,320]{2,1,0:T(8,128)}, f32[6,40,320]{2,1,0:T(8,128)}, u32[]{:S(2)}, u32[]{:S(2)}) collective-permute-start(f32[6,40,320]{2,1,0:T(8,128)} %get-tuple-element.41), channel_id=1, source_target_pairs={{0,24},{8,0},{16,8},{24,16},{1,25},{9,1},{17,9},{25,17},{2,26},{10... | collective-permute-start | bytes 921608 | tf_op jit(solution)/shard_map/ppermute | solution.py:16
  136.7 0.9 collective-permute-done.32
  137.5 2.6 %collective-permute-start.14 = (bf16[16,80,128]{2,1,0:T(8,128)(2,1)}, bf16[16,80,128]{2,1,0:T(8,128)(2,1)S(1)}, u32[]{:S(2)}, u32[]{:S(2)}) collective-permute-start(bf16[16,80,128]{2,1,0:T(8,128)(2,1)} %get-tuple-element.22), channel_id=1, source_target_pairs={{0,2},{2,4},{4,6},{6,0},{1,3},{3,5},{5,7},{7,1},{8,10},{10,12},{12... | collective-permute-start | bytes 983048 | tf_op jit(solution)/shard_map/ppermute | solution.py:16
  140.2 1.0 collective-permute-start.15
  141.1 1.1 fusion.10
  142.2 3.2 %collective-permute-done.28 = f32[6,40,320]{2,1,0:T(8,128)S(1)} collective-permute-done((f32[6,40,320]{2,1,0:T(8,128)}, f32[6,40,320]{2,1,0:T(8,128)S(1)}, u32[]{:S(2)}, u32[]{:S(2)}) %collective-permute-start.28) | collective-permute-done | bytes 307232 | tf_op jit(solution)/shard_map/ppermute | solution.py:16
  145.4 3.0 %collective-permute-start.16 = (bf16[16,80,128]{2,1,0:T(8,128)(2,1)}, bf16[16,80,128]{2,1,0:T(8,128)(2,1)}, u32[]{:S(2)}, u32[]{:S(2)}) collective-permute-start(bf16[16,80,128]{2,1,0:T(8,128)(2,1)} %get-tuple-element.24), channel_id=1, source_target_pairs={{0,6},{2,0},{4,2},{6,4},{1,7},{3,1},{5,3},{7,5},{8,14},{10,8},{12,... | collective-permute-start | bytes 983048 | tf_op jit(solution)/shard_map/ppermute | solution.py:16
  148.5 3.8 %collective-permute-done.27 = f32[6,40,320]{2,1,0:T(8,128)S(1)} collective-permute-done((f32[6,40,320]{2,1,0:T(8,128)}, f32[6,40,320]{2,1,0:T(8,128)S(1)}, u32[]{:S(2)}, u32[]{:S(2)}) %collective-permute-start.27) | collective-permute-done | bytes 307232 | tf_op jit(solution)/shard_map/ppermute | solution.py:16
  152.3 1.1 fusion.6
  153.7 2.7 %collective-permute-start.29 = (f32[160,240]{0,1:T(8,128)S(1)}, f32[160,240]{0,1:T(8,128)S(1)}, u32[]{:S(2)}, u32[]{:S(2)}) collective-permute-start(f32[160,240]{0,1:T(8,128)S(1)} %pad_maximum_fusion.2), channel_id=1, source_target_pairs={{0,2},{2,0},{4,6},{6,4},{1,3},{3,1},{5,7},{7,5},{8,10},{10,8},{12,... | collective-permute-start | bytes 460808 | tf_op jit(solution)/shard_map/ppermute | solution.py:20
  156.6 13.1 %collective-permute-done.29 = f32[160,240]{0,1:T(8,128)S(1)} collective-permute-done((f32[160,240]{0,1:T(8,128)S(1)}, f32[160,240]{0,1:T(8,128)S(1)}, u32[]{:S(2)}, u32[]{:S(2)}) %collective-permute-start.29) | collective-permute-done | bytes 153632 | tf_op jit(solution)/shard_map/ppermute | solution.py:20
  169.7 5.5 %collective-permute-start.34 = (f32[80,120]{0,1:T(8,128)S(1)}, f32[80,120]{0,1:T(8,128)S(1)}, u32[]{:S(2)}, u32[]{:S(2)}) collective-permute-start(f32[80,120]{0,1:T(8,128)S(1)} %bitcast.136), channel_id=1, source_target_pairs={{0,6},{2,0},{4,2},{6,4},{1,7},{3,1},{5,3},{7,5},{8,14},{10,8},{12,... | collective-permute-start | bytes 115208 | tf_op jit(solution)/shard_map/ppermute | solution.py:16
  175.4 2.2 collective-permute-done.34
  178.0 2.6 %collective-permute-start.23 = (bf16[16,80,128]{2,1,0:T(8,128)(2,1)S(1)}, bf16[16,80,128]{2,1,0:T(8,128)(2,1)S(1)}, u32[]{:S(2)}, u32[]{:S(2)}) collective-permute-start(bf16[16,80,128]{2,1,0:T(8,128)(2,1)S(1)} %copy-done.13), channel_id=1, source_target_pairs={{0,4},{2,6},{4,0},{6,2},{1,5},{3,7},{5,1},{7,3},{8,12},{10,14},{12... | collective-permute-start | bytes 983048 | tf_op jit(solution)/shard_map/ppermute | solution.py:16
  180.6 20.0 %collective-permute-done.36 = f32[80,360]{0,1:T(8,128)S(1)} collective-permute-done((f32[80,360]{0,1:T(8,128)S(1)}, f32[80,360]{0,1:T(8,128)S(1)}, u32[]{:S(2)}, u32[]{:S(2)}) %collective-permute-start.36) | collective-permute-done | bytes 115232 | tf_op jit(solution)/shard_map/ppermute | solution.py:16
  200.6 1.2 collective-permute-start.24
  201.8 0.7 copy-done.10
  203.2 2.6 %put_rows.2 = bf16[64,80,128]{2,1,0:T(8,128)(2,1)} custom-call(s32[3]{0:T(128)} %pad_add_fusion.places, bf16[16,80,128]{2,1,0:T(8,128)(2,1)} %copy-done.9, bf16[16,80,128]{2,1,0:T(8,128)(2,1)} %copy-done.10, bf16[16,80,128]{2,1,0:T(8,128)(2,1)} %collective-permute-done.16.refs_2_, ...), custom_call_target="tpu_custom_call", output_to_operand_aliasing={{}: (4, {})} | custom-call | bytes 4194304 | tf_op jit(solution)/shard_map/put_rows/pallas_call | solution.py:501
  205.9 1.8 collective-permute-done.23.refs_1_
  207.7 6.9 %collective-permute-done.24.refs_2_ = bf16[16,80,128]{2,1,0:T(8,128)(2,1)S(1)} collective-permute-done((bf16[16,80,128]{2,1,0:T(8,128)(2,1)S(1)}, bf16[16,80,128]{2,1,0:T(8,128)(2,1)S(1)}, u32[]{:S(2)}, u32[]{:S(2)}) %collective-permute-start.24) | collective-permute-done | bytes 327712 | tf_op jit(solution)/shard_map/ppermute | solution.py:16
  214.6 0.7 copy-done.8
  215.3 3.0 %put_rows.3 = f32[64,80,128]{2,1,0:T(8,128)} custom-call(s32[3]{0:T(128)} %pad_add_fusion.places, bf16[16,80,128]{2,1,0:T(8,128)(2,1)} %copy-done.6, bf16[16,80,128]{2,1,0:T(8,128)(2,1)} %copy-done.7, bf16[16,80,128]{2,1,0:T(8,128)(2,1)} %copy-done.8, f32[64,80,128]{2,1,0:T(8,128)} %get-tuple-element.35.refs_3_), custom_call_target="tpu_custom_call", output_to_operand_aliasing={{}: (4, {})} | custom-call | bytes 4194304 | tf_op jit(solution)/shard_map/put_rows/pallas_call | solution.py:501
  218.4 0.8 copy.11
  (95 shorter events, 9.2 us)
Async XLA Ops:
  0.6 0.9 copy-start
  0.6 15.9 %copy-start.2 = (bf16[1,64,80,128]{3,2,1,0:T(8,128)(2,1)S(1)}, bf16[1,64,80,128]{3,2,1,0:T(8,128)(2,1)}, u32[]{:S(2)}) copy-start(bf16[1,64,80,128]{3,2,1,0:T(8,128)(2,1)} %param.3) | copy-start | bytes 3932164
  1.8 7.5 %collective-permute-start.9 = (bf16[40,720]{1,0:T(8,128)(2,1)S(1)}, bf16[40,720]{1,0:T(8,128)(2,1)S(1)}, u32[]{:S(2)}, u32[]{:S(2)}) collective-permute-start(bf16[40,720]{1,0:T(8,128)(2,1)S(1)} %copy.12), channel_id=1, source_target_pairs={{0,2},{2,4},{4,6},{6,0},{1,3},{3,5},{5,7},{7,1},{8,10},{10,12},{12... | collective-permute-start | bytes 172808 | tf_op jit(solution)/shard_map/ppermute | solution.py:16
  4.9 6.9 %collective-permute-start.8 = (bf16[40,720]{1,0:T(8,128)(2,1)S(1)}, bf16[40,720]{1,0:T(8,128)(2,1)S(1)}, u32[]{:S(2)}, u32[]{:S(2)}) collective-permute-start(bf16[40,720]{1,0:T(8,128)(2,1)S(1)} %copy.12), channel_id=1, source_target_pairs={{0,4},{2,6},{4,0},{6,2},{1,5},{3,7},{5,1},{7,3},{8,12},{10,14},{12... | collective-permute-start | bytes 172808 | tf_op jit(solution)/shard_map/ppermute | solution.py:16
  7.5 4.6 %collective-permute-start.7 = (bf16[40,720]{1,0:T(8,128)(2,1)S(1)}, bf16[40,720]{1,0:T(8,128)(2,1)S(1)}, u32[]{:S(2)}, u32[]{:S(2)}) collective-permute-start(bf16[40,720]{1,0:T(8,128)(2,1)S(1)} %copy.12), channel_id=1, source_target_pairs={{0,6},{2,0},{4,2},{6,4},{1,7},{3,1},{5,3},{7,5},{8,14},{10,8},{12,... | collective-permute-start | bytes 172808 | tf_op jit(solution)/shard_map/ppermute | solution.py:16
  12.1 9.8 %collective-permute-start.12 = (bf16[160,720]{1,0:T(8,128)(2,1)S(1)}, bf16[160,720]{1,0:T(8,128)(2,1)S(1)}, u32[]{:S(2)}, u32[]{:S(2)}) collective-permute-start(bf16[160,720]{1,0:T(8,128)(2,1)S(1)} %get-tuple-element.78), channel_id=1, source_target_pairs={{0,8},{8,16},{16,24},{24,0},{1,9},{9,17},{17,25},{25,1},{2,10},{10... | collective-permute-start | bytes 691208 | tf_op jit(solution)/shard_map/ppermute | solution.py:16
  13.6 11.6 %collective-permute-start.11 = (bf16[160,720]{1,0:T(8,128)(2,1)S(1)}, bf16[160,720]{1,0:T(8,128)(2,1)S(1)}, u32[]{:S(2)}, u32[]{:S(2)}) collective-permute-start(bf16[160,720]{1,0:T(8,128)(2,1)S(1)} %get-tuple-element.78), channel_id=1, source_target_pairs={{0,16},{8,24},{16,0},{24,8},{1,17},{9,25},{17,1},{25,9},{2,18},{10... | collective-permute-start | bytes 691208 | tf_op jit(solution)/shard_map/ppermute | solution.py:16
  15.1 10.1 %collective-permute-start.10 = (bf16[160,720]{1,0:T(8,128)(2,1)S(1)}, bf16[160,720]{1,0:T(8,128)(2,1)S(1)}, u32[]{:S(2)}, u32[]{:S(2)}) collective-permute-start(bf16[160,720]{1,0:T(8,128)(2,1)S(1)} %get-tuple-element.78), channel_id=1, source_target_pairs={{0,24},{8,0},{16,8},{24,16},{1,25},{9,1},{17,9},{25,17},{2,26},{10... | collective-permute-start | bytes 691208 | tf_op jit(solution)/shard_map/ppermute | solution.py:16
  17.7 48.8 %collective-permute-start = (bf16[16,80,128]{2,1,0:T(8,128)(2,1)}, bf16[16,80,128]{2,1,0:T(8,128)(2,1)}, u32[]{:S(2)}, u32[]{:S(2)}) collective-permute-start(bf16[16,80,128]{2,1,0:T(8,128)(2,1)} %get-tuple-element.66), channel_id=1, source_target_pairs={{0,6},{2,0},{4,2},{6,4},{1,7},{3,1},{5,3},{7,5},{8,14},{10,8},{12,... | collective-permute-start | bytes 983048 | tf_op jit(solution)/shard_map/ppermute | solution.py:16
  20.6 45.9 %collective-permute-start.1 = (bf16[16,80,128]{2,1,0:T(8,128)(2,1)}, bf16[16,80,128]{2,1,0:T(8,128)(2,1)}, u32[]{:S(2)}, u32[]{:S(2)}) collective-permute-start(bf16[16,80,128]{2,1,0:T(8,128)(2,1)} %get-tuple-element.65), channel_id=1, source_target_pairs={{0,4},{2,6},{4,0},{6,2},{1,5},{3,7},{5,1},{7,3},{8,12},{10,14},{12... | collective-permute-start | bytes 983048 | tf_op jit(solution)/shard_map/ppermute | solution.py:16
  21.9 45.2 %collective-permute-start.2 = (bf16[16,80,128]{2,1,0:T(8,128)(2,1)}, bf16[16,80,128]{2,1,0:T(8,128)(2,1)}, u32[]{:S(2)}, u32[]{:S(2)}) collective-permute-start(bf16[16,80,128]{2,1,0:T(8,128)(2,1)} %get-tuple-element.64), channel_id=1, source_target_pairs={{0,2},{2,4},{4,6},{6,0},{1,3},{3,5},{5,7},{7,1},{8,10},{10,12},{12... | collective-permute-start | bytes 983048 | tf_op jit(solution)/shard_map/ppermute | solution.py:16
  25.3 5.1 %collective-permute-start.3 = (bf16[1,80,128]{2,1,0:T(8,128)(2,1)}, bf16[1,80,128]{2,1,0:T(8,128)(2,1)}, u32[]{:S(2)}, u32[]{:S(2)}) collective-permute-start(bf16[1,80,128]{2,1,0:T(8,128)(2,1)} %select_bitcast_fusion), channel_id=1, source_target_pairs={{0,1},{1,0},{2,3},{3,2},{4,5},{5,4},{6,7},{7,6},{8,9},{9,8},{10,11... | collective-permute-start | bytes 61448 | tf_op jit(solution)/shard_map/ppermute | solution.py:16
  25.4 5.7 %copy-start.1 = (bf16[4,160,720]{2,1,0:T(8,128)(2,1)}, bf16[4,160,720]{2,1,0:T(8,128)(2,1)S(1)}, u32[]{:S(2)}) copy-start(bf16[4,160,720]{2,1,0:T(8,128)(2,1)S(1)} %pad_maximum_fusion.refs_8_.refs_0_) | copy-start | bytes 2764804
  25.4 41.7 %collective-permute-start.13 = (bf16[4,160,720]{2,1,0:T(8,128)(2,1)S(1)}, bf16[4,160,720]{2,1,0:T(8,128)(2,1)S(1)}, u32[]{:S(2)}, u32[]{:S(2)}) collective-permute-start(bf16[4,160,720]{2,1,0:T(8,128)(2,1)S(1)} %pad_maximum_fusion.refs_8_.refs_0_), channel_id=1, source_target_pairs={{0,1},{1,0},{2,3},{3,2},{4,5},{5,4},{6,7},{7,6},{8,9},{9,8},{10,11... | collective-permute-start | bytes 2764808 | tf_op jit(solution)/shard_map/ppermute | solution.py:16
  31.9 10.8 %collective-permute-start.4 = (bf16[4,80,128]{2,1,0:T(8,128)(2,1)S(1)}, bf16[4,80,128]{2,1,0:T(8,128)(2,1)S(1)}, u32[]{:S(2)}, u32[]{:S(2)}) collective-permute-start(bf16[4,80,128]{2,1,0:T(8,128)(2,1)S(1)} %pad_maximum_fusion.5), channel_id=1, source_target_pairs={{0,6},{2,0},{4,2},{6,4},{1,7},{3,1},{5,3},{7,5},{8,14},{10,8},{12,... | collective-permute-start | bytes 245768 | tf_op jit(solution)/shard_map/ppermute | solution.py:16
  42.7 24.4 %copy-start.18 = (bf16[4,80,128]{2,1,0:T(8,128)(2,1)}, bf16[4,80,128]{2,1,0:T(8,128)(2,1)S(1)}, u32[]{:S(2)}) copy-start(bf16[4,80,128]{2,1,0:T(8,128)(2,1)S(1)} %collective-permute-done.4.refs_5_.refs_6_) | copy-start | bytes 245764
  42.7 10.3 %collective-permute-start.5 = (bf16[4,80,128]{2,1,0:T(8,128)(2,1)S(1)}, bf16[4,80,128]{2,1,0:T(8,128)(2,1)S(1)}, u32[]{:S(2)}, u32[]{:S(2)}) collective-permute-start(bf16[4,80,128]{2,1,0:T(8,128)(2,1)S(1)} %pad_maximum_fusion.6), channel_id=1, source_target_pairs={{0,4},{2,6},{4,0},{6,2},{1,5},{3,7},{5,1},{7,3},{8,12},{10,14},{12... | collective-permute-start | bytes 245768 | tf_op jit(solution)/shard_map/ppermute | solution.py:16
  53.0 14.1 %copy-start.19 = (bf16[4,80,128]{2,1,0:T(8,128)(2,1)}, bf16[4,80,128]{2,1,0:T(8,128)(2,1)S(1)}, u32[]{:S(2)}) copy-start(bf16[4,80,128]{2,1,0:T(8,128)(2,1)S(1)} %collective-permute-done.5.refs_6_.refs_7_) | copy-start | bytes 245764
  53.0 8.0 %collective-permute-start.6 = (bf16[4,80,128]{2,1,0:T(8,128)(2,1)S(1)}, bf16[4,80,128]{2,1,0:T(8,128)(2,1)S(1)}, u32[]{:S(2)}, u32[]{:S(2)}) collective-permute-start(bf16[4,80,128]{2,1,0:T(8,128)(2,1)S(1)} %pad_maximum_fusion.7), channel_id=1, source_target_pairs={{0,2},{2,4},{4,6},{6,0},{1,3},{3,5},{5,7},{7,1},{8,10},{10,12},{12... | collective-permute-start | bytes 245768 | tf_op jit(solution)/shard_map/ppermute | solution.py:16
  61.0 6.2 %copy-start.20 = (bf16[4,80,128]{2,1,0:T(8,128)(2,1)}, bf16[4,80,128]{2,1,0:T(8,128)(2,1)S(1)}, u32[]{:S(2)}) copy-start(bf16[4,80,128]{2,1,0:T(8,128)(2,1)S(1)} %collective-permute-done.6.refs_7_.refs_8_) | copy-start | bytes 245764
  61.0 26.2 %collective-permute-start.17 = (bf16[14,80,128]{2,1,0:T(8,128)(2,1)}, bf16[14,80,128]{2,1,0:T(8,128)(2,1)S(1)}, u32[]{:S(2)}, u32[]{:S(2)}) collective-permute-start(bf16[14,80,128]{2,1,0:T(8,128)(2,1)} %get-tuple-element.53), channel_id=1, source_target_pairs={{0,6},{2,0},{4,2},{6,4},{1,7},{3,1},{5,3},{7,5},{8,14},{10,8},{12,... | collective-permute-start | bytes 860168 | tf_op jit(solution)/shard_map/ppermute | solution.py:16
  66.5 20.7 %collective-permute-start.18 = (bf16[14,80,128]{2,1,0:T(8,128)(2,1)}, bf16[14,80,128]{2,1,0:T(8,128)(2,1)S(1)}, u32[]{:S(2)}, u32[]{:S(2)}) collective-permute-start(bf16[14,80,128]{2,1,0:T(8,128)(2,1)} %get-tuple-element.55), channel_id=1, source_target_pairs={{0,4},{2,6},{4,0},{6,2},{1,5},{3,7},{5,1},{7,3},{8,12},{10,14},{12... | collective-permute-start | bytes 860168 | tf_op jit(solution)/shard_map/ppermute | solution.py:16
  66.5 20.7 %collective-permute-start.19 = (bf16[14,80,128]{2,1,0:T(8,128)(2,1)}, bf16[14,80,128]{2,1,0:T(8,128)(2,1)S(1)}, u32[]{:S(2)}, u32[]{:S(2)}) collective-permute-start(bf16[14,80,128]{2,1,0:T(8,128)(2,1)} %get-tuple-element.52), channel_id=1, source_target_pairs={{0,2},{2,4},{4,6},{6,0},{1,3},{3,5},{5,7},{7,1},{8,10},{10,12},{12... | collective-permute-start | bytes 860168 | tf_op jit(solution)/shard_map/ppermute | solution.py:16
  67.1 1.0 copy-start.5
  81.1 22.1 %collective-permute-start.20 = (bf16[1,320,128]{2,1,0:T(8,128)(2,1)}, bf16[1,320,128]{2,1,0:T(8,128)(2,1)S(1)}, u32[]{:S(2)}, u32[]{:S(2)}) collective-permute-start(bf16[1,320,128]{2,1,0:T(8,128)(2,1)} %get-tuple-element.29), channel_id=1, source_target_pairs={{0,2},{2,4},{4,6},{6,7},{7,5},{5,3},{3,1},{8,10},{10,12},{12,14},{... | collective-permute-start | bytes 245768 | tf_op jit(solution)/shard_map/ppermute | solution.py:632
  85.8 17.3 %collective-permute-start.21 = (bf16[1,320,128]{2,1,0:T(8,128)(2,1)}, bf16[1,320,128]{2,1,0:T(8,128)(2,1)S(1)}, u32[]{:S(2)}, u32[]{:S(2)}) collective-permute-start(bf16[1,320,128]{2,1,0:T(8,128)(2,1)} %get-tuple-element.30), channel_id=1, source_target_pairs={{2,0},{4,2},{6,4},{7,6},{5,7},{3,5},{1,3},{10,8},{12,10},{14,12},{... | collective-permute-start | bytes 245768 | tf_op jit(solution)/shard_map/ppermute | solution.py:633
  87.2 0.7 copy-start.15
  87.2 0.8 copy-start.16
  87.2 0.9 copy-start.17
  98.6 29.6 %collective-permute-start.25 = (f32[4,6,40,320]{3,2,1,0:T(8,128)}, f32[4,6,40,320]{3,2,1,0:T(8,128)S(1)}, u32[]{:S(2)}, u32[]{:S(2)}) collective-permute-start(f32[4,6,40,320]{3,2,1,0:T(8,128)} %get-tuple-element.37), channel_id=1, source_target_pairs={{0,1},{1,0},{2,3},{3,2},{4,5},{5,4},{6,7},{7,6},{8,9},{9,8},{10,11... | collective-permute-start | bytes 3686408 | tf_op jit(solution)/shard_map/ppermute | solution.py:16
  103.2 0.6 copy-start.21
  103.2 0.7 copy-start.22
  120.4 2.6 %collective-permute-start.30 = (f32[4,3,40,320]{3,2,1,0:T(8,128)}, f32[4,3,40,320]{3,2,1,0:T(8,128)S(1)}, u32[]{:S(2)}, u32[]{:S(2)}) collective-permute-start(f32[4,3,40,320]{3,2,1,0:T(8,128)} %get-tuple-element.40), channel_id=1, source_target_pairs={{0,1},{1,0},{2,3},{3,2},{4,5},{5,4},{6,7},{7,6},{8,9},{9,8},{10,11... | collective-permute-start | bytes 1843208 | tf_op jit(solution)/shard_map/ppermute | solution.py:16
  122.9 6.5 %copy-start.3 = (f32[4,6,40,320]{3,2,1,0:T(8,128)S(1)}, f32[4,6,40,320]{3,2,1,0:T(8,128)}, u32[]{:S(2)}) copy-start(f32[4,6,40,320]{3,2,1,0:T(8,128)} %get-tuple-element.36) | copy-start | bytes 3686404
  125.1 8.7 %collective-permute-start.33 = (f32[3,40,320]{2,1,0:T(8,128)S(1)}, f32[3,40,320]{2,1,0:T(8,128)S(1)}, u32[]{:S(2)}, u32[]{:S(2)}) collective-permute-start(f32[3,40,320]{2,1,0:T(8,128)S(1)} %get-tuple-element.69), channel_id=1, source_target_pairs={{0,8},{8,16},{16,24},{24,0},{1,9},{9,17},{17,25},{25,1},{2,10},{10... | collective-permute-start | bytes 460808 | tf_op jit(solution)/shard_map/ppermute | solution.py:16
  125.7 11.9 %collective-permute-start.32 = (f32[3,40,320]{2,1,0:T(8,128)}, f32[3,40,320]{2,1,0:T(8,128)S(1)}, u32[]{:S(2)}, u32[]{:S(2)}) collective-permute-start(f32[3,40,320]{2,1,0:T(8,128)} %get-tuple-element.70), channel_id=1, source_target_pairs={{0,16},{8,24},{16,0},{24,8},{1,17},{9,25},{17,1},{25,9},{2,18},{10... | collective-permute-start | bytes 460808 | tf_op jit(solution)/shard_map/ppermute | solution.py:16
  125.7 14.5 %collective-permute-start.31 = (f32[3,40,320]{2,1,0:T(8,128)}, f32[3,40,320]{2,1,0:T(8,128)}, u32[]{:S(2)}, u32[]{:S(2)}) collective-permute-start(f32[3,40,320]{2,1,0:T(8,128)} %get-tuple-element.68), channel_id=1, source_target_pairs={{0,24},{8,0},{16,8},{24,16},{1,25},{9,1},{17,9},{25,17},{2,26},{10... | collective-permute-start | bytes 460808 | tf_op jit(solution)/shard_map/ppermute | solution.py:16
  128.2 1.1 copy-start.4
  131.9 13.5 %collective-permute-start.28 = (f32[6,40,320]{2,1,0:T(8,128)}, f32[6,40,320]{2,1,0:T(8,128)S(1)}, u32[]{:S(2)}, u32[]{:S(2)}) collective-permute-start(f32[6,40,320]{2,1,0:T(8,128)} %get-tuple-element.42), channel_id=1, source_target_pairs={{0,8},{8,16},{16,24},{24,0},{1,9},{9,17},{17,25},{25,1},{2,10},{10... | collective-permute-start | bytes 921608 | tf_op jit(solution)/shard_map/ppermute | solution.py:16
  132.3 20.0 %collective-permute-start.27 = (f32[6,40,320]{2,1,0:T(8,128)}, f32[6,40,320]{2,1,0:T(8,128)S(1)}, u32[]{:S(2)}, u32[]{:S(2)}) collective-permute-start(f32[6,40,320]{2,1,0:T(8,128)} %get-tuple-element.43), channel_id=1, source_target_pairs={{0,16},{8,24},{16,0},{24,8},{1,17},{9,25},{17,1},{25,9},{2,18},{10... | collective-permute-start | bytes 921608 | tf_op jit(solution)/shard_map/ppermute | solution.py:16
  133.7 18.5 %collective-permute-start.26 = (f32[6,40,320]{2,1,0:T(8,128)}, f32[6,40,320]{2,1,0:T(8,128)}, u32[]{:S(2)}, u32[]{:S(2)}) collective-permute-start(f32[6,40,320]{2,1,0:T(8,128)} %get-tuple-element.41), channel_id=1, source_target_pairs={{0,24},{8,0},{16,8},{24,16},{1,25},{9,1},{17,9},{25,17},{2,26},{10... | collective-permute-start | bytes 921608 | tf_op jit(solution)/shard_map/ppermute | solution.py:16
  137.5 2.6 %copy-start.11 = (f32[3,40,320]{2,1,0:T(8,128)}, f32[3,40,320]{2,1,0:T(8,128)S(1)}, u32[]{:S(2)}) copy-start(f32[3,40,320]{2,1,0:T(8,128)S(1)} %collective-permute-done.32) | copy-start | bytes 460804
  137.5 40.4 %collective-permute-start.14 = (bf16[16,80,128]{2,1,0:T(8,128)(2,1)}, bf16[16,80,128]{2,1,0:T(8,128)(2,1)S(1)}, u32[]{:S(2)}, u32[]{:S(2)}) collective-permute-start(bf16[16,80,128]{2,1,0:T(8,128)(2,1)} %get-tuple-element.22), channel_id=1, source_target_pairs={{0,2},{2,4},{4,6},{6,0},{1,3},{3,5},{5,7},{7,1},{8,10},{10,12},{12... | collective-permute-start | bytes 983048 | tf_op jit(solution)/shard_map/ppermute | solution.py:16
  140.2 61.6 %collective-permute-start.15 = (bf16[16,80,128]{2,1,0:T(8,128)(2,1)}, bf16[16,80,128]{2,1,0:T(8,128)(2,1)S(1)}, u32[]{:S(2)}, u32[]{:S(2)}) collective-permute-start(bf16[16,80,128]{2,1,0:T(8,128)(2,1)} %get-tuple-element.23), channel_id=1, source_target_pairs={{0,4},{2,6},{4,0},{6,2},{1,5},{3,7},{5,1},{7,3},{8,12},{10,14},{12... | collective-permute-start | bytes 983048 | tf_op jit(solution)/shard_map/ppermute | solution.py:16
  145.4 57.8 %collective-permute-start.16 = (bf16[16,80,128]{2,1,0:T(8,128)(2,1)}, bf16[16,80,128]{2,1,0:T(8,128)(2,1)}, u32[]{:S(2)}, u32[]{:S(2)}) collective-permute-start(bf16[16,80,128]{2,1,0:T(8,128)(2,1)} %get-tuple-element.24), channel_id=1, source_target_pairs={{0,6},{2,0},{4,2},{6,4},{1,7},{3,1},{5,3},{7,5},{8,14},{10,8},{12,... | collective-permute-start | bytes 983048 | tf_op jit(solution)/shard_map/ppermute | solution.py:16
  153.4 22.0 %copy-start.14 = (bf16[16,80,128]{2,1,0:T(8,128)(2,1)S(1)}, bf16[16,80,128]{2,1,0:T(8,128)(2,1)}, u32[]{:S(2)}) copy-start(bf16[16,80,128]{2,1,0:T(8,128)(2,1)} %get-tuple-element.32) | copy-start | bytes 983044
  153.4 24.6 %copy-start.13 = (bf16[16,80,128]{2,1,0:T(8,128)(2,1)S(1)}, bf16[16,80,128]{2,1,0:T(8,128)(2,1)}, u32[]{:S(2)}) copy-start(bf16[16,80,128]{2,1,0:T(8,128)(2,1)} %get-tuple-element.33) | copy-start | bytes 983044
  153.4 47.2 %copy-start.12 = (bf16[16,80,128]{2,1,0:T(8,128)(2,1)S(1)}, bf16[16,80,128]{2,1,0:T(8,128)(2,1)}, u32[]{:S(2)}) copy-start(bf16[16,80,128]{2,1,0:T(8,128)(2,1)} %get-tuple-element.34) | copy-start | bytes 983044
  153.7 16.0 %collective-permute-start.29 = (f32[160,240]{0,1:T(8,128)S(1)}, f32[160,240]{0,1:T(8,128)S(1)}, u32[]{:S(2)}, u32[]{:S(2)}) collective-permute-start(f32[160,240]{0,1:T(8,128)S(1)} %pad_maximum_fusion.2), channel_id=1, source_target_pairs={{0,2},{2,0},{4,6},{6,4},{1,3},{3,1},{5,7},{7,5},{8,10},{10,8},{12,... | collective-permute-start | bytes 460808 | tf_op jit(solution)/shard_map/ppermute | solution.py:20
  156.5 18.8 %collective-permute-start.35 = (f32[80,120]{0,1:T(8,128)S(1)}, f32[80,120]{0,1:T(8,128)S(1)}, u32[]{:S(2)}, u32[]{:S(2)}) collective-permute-start(f32[80,120]{0,1:T(8,128)S(1)} %bitcast.137), channel_id=1, source_target_pairs={{0,2},{2,4},{4,6},{6,0},{1,3},{3,5},{5,7},{7,1},{8,10},{10,12},{12... | collective-permute-start | bytes 115208 | tf_op jit(solution)/shard_map/ppermute | solution.py:16
  169.7 7.9 %collective-permute-start.34 = (f32[80,120]{0,1:T(8,128)S(1)}, f32[80,120]{0,1:T(8,128)S(1)}, u32[]{:S(2)}, u32[]{:S(2)}) collective-permute-start(f32[80,120]{0,1:T(8,128)S(1)} %bitcast.136), channel_id=1, source_target_pairs={{0,6},{2,0},{4,2},{6,4},{1,7},{3,1},{5,3},{7,5},{8,14},{10,8},{12,... | collective-permute-start | bytes 115208 | tf_op jit(solution)/shard_map/ppermute | solution.py:16
  175.3 30.5 %collective-permute-start.22 = (bf16[16,80,128]{2,1,0:T(8,128)(2,1)S(1)}, bf16[16,80,128]{2,1,0:T(8,128)(2,1)S(1)}, u32[]{:S(2)}, u32[]{:S(2)}) collective-permute-start(bf16[16,80,128]{2,1,0:T(8,128)(2,1)S(1)} %copy-done.14), channel_id=1, source_target_pairs={{0,2},{2,4},{4,6},{6,0},{1,3},{3,5},{5,7},{7,1},{8,10},{10,12},{12... | collective-permute-start | bytes 983048 | tf_op jit(solution)/shard_map/ppermute | solution.py:16
  177.6 23.0 %collective-permute-start.36 = (f32[80,360]{0,1:T(8,128)S(1)}, f32[80,360]{0,1:T(8,128)S(1)}, u32[]{:S(2)}, u32[]{:S(2)}) collective-permute-start(f32[80,360]{0,1:T(8,128)S(1)} %pad_maximum_fusion.3), channel_id=1, source_target_pairs={{0,4},{2,6},{4,0},{6,2},{1,5},{3,7},{5,1},{7,3},{8,12},{10,14},{12... | collective-permute-start | bytes 345608 | tf_op jit(solution)/shard_map/ppermute | solution.py:16
  178.0 23.8 %copy-start.9 = (bf16[16,80,128]{2,1,0:T(8,128)(2,1)}, bf16[16,80,128]{2,1,0:T(8,128)(2,1)S(1)}, u32[]{:S(2)}) copy-start(bf16[16,80,128]{2,1,0:T(8,128)(2,1)S(1)} %collective-permute-done.14.refs_0_) | copy-start | bytes 983044
  178.0 29.7 %collective-permute-start.23 = (bf16[16,80,128]{2,1,0:T(8,128)(2,1)S(1)}, bf16[16,80,128]{2,1,0:T(8,128)(2,1)S(1)}, u32[]{:S(2)}, u32[]{:S(2)}) collective-permute-start(bf16[16,80,128]{2,1,0:T(8,128)(2,1)S(1)} %copy-done.13), channel_id=1, source_target_pairs={{0,4},{2,6},{4,0},{6,2},{1,5},{3,7},{5,1},{7,3},{8,12},{10,14},{12... | collective-permute-start | bytes 983048 | tf_op jit(solution)/shard_map/ppermute | solution.py:16
  200.6 13.9 %collective-permute-start.24 = (bf16[16,80,128]{2,1,0:T(8,128)(2,1)S(1)}, bf16[16,80,128]{2,1,0:T(8,128)(2,1)S(1)}, u32[]{:S(2)}, u32[]{:S(2)}) collective-permute-start(bf16[16,80,128]{2,1,0:T(8,128)(2,1)S(1)} %copy-done.12), channel_id=1, source_target_pairs={{0,6},{2,0},{4,2},{6,4},{1,7},{3,1},{5,3},{7,5},{8,14},{10,8},{12,... | collective-permute-start | bytes 983048 | tf_op jit(solution)/shard_map/ppermute | solution.py:16
  201.8 0.8 copy-start.10
  202.6 15.7 %collective-permute-start.37 = (f32[80,360]{0,1:T(8,128)S(1)}, f32[80,360]{0,1:T(8,128)S(1)}, u32[]{:S(2)}, u32[]{:S(2)}) collective-permute-start(f32[80,360]{0,1:T(8,128)S(1)} %maximum_add_fusion), channel_id=1, source_target_pairs={{0,1},{1,0},{2,3},{3,2},{4,5},{5,4},{6,7},{7,6},{8,9},{9,8},{10,11... | collective-permute-start | bytes 345608 | tf_op jit(solution)/shard_map/ppermute | solution.py:16
  205.9 8.7 %copy-start.6 = (bf16[16,80,128]{2,1,0:T(8,128)(2,1)}, bf16[16,80,128]{2,1,0:T(8,128)(2,1)S(1)}, u32[]{:S(2)}) copy-start(bf16[16,80,128]{2,1,0:T(8,128)(2,1)S(1)} %collective-permute-done.22.refs_0_) | copy-start | bytes 983044
  207.7 6.9 %copy-start.7 = (bf16[16,80,128]{2,1,0:T(8,128)(2,1)}, bf16[16,80,128]{2,1,0:T(8,128)(2,1)S(1)}, u32[]{:S(2)}) copy-start(bf16[16,80,128]{2,1,0:T(8,128)(2,1)S(1)} %collective-permute-done.23.refs_1_) | copy-start | bytes 983044
  214.6 0.7 copy-start.8
